TPU v7x, 32 devices: a whole 2x2x4 slice. The times are simulated.
32 devices in a mesh: fsdp: 4 (over x, core), context: 4 (over z), tensor: 2 (over y).
Axes of the slice: x: 2, y: 2, z: 4, core: 2. Of those that a mesh axis runs over, the one named last changes fastest.
Arguments:
- tokens: bfloat16 [4096, 1536], P(('fsdp', 'context')), may hold values from -6 to 6
- cotangent: bfloat16 [4096, 1536], P(('fsdp', 'context')), may hold values from -6 to 6
- lengths: int32 [4, 3], P('fsdp'), may hold values from 256 to 384, as said below
- span_order: int32 [4, 4, 4], P('fsdp'), may hold values from 0 to 3, each once within a row
- attn_gain: float32 [1536], P('fsdp'), may hold values from 0.5 to 1.5
- w_q: float32 [1536, 1536], P('fsdp', 'tensor'), may hold values from -0.15625 to 0.15625
- b_q: float32 [12, 128], P('tensor', 'fsdp'), may hold values from -3 to 3
- w_k: float32 [1536, 256], P('fsdp', 'tensor'), may hold values from -0.15625 to 0.15625
- b_k: float32 [2, 128], P('tensor', 'fsdp'), may hold values from -3 to 3
- w_v: float32 [1536, 256], P('fsdp', 'tensor'), may hold values from -0.15625 to 0.15625
- b_v: float32 [2, 128], P('tensor', 'fsdp'), may hold values from -3 to 3
- w_o: float32 [1536, 1536], P('tensor', 'fsdp'), may hold values from -1.75 to 1.75
- mlp_gain: float32 [1536], P('fsdp'), may hold values from 0.5 to 1.5
- w_gate: float32 [1536, 8960], P('fsdp', 'tensor'), may hold values from -0.15625 to 0.15625
- w_up: float32 [1536, 8960], P('fsdp', 'tensor'), may hold values from -0.15625 to 0.15625
- w_down: float32 [8960, 1536], P('tensor', 'fsdp'), may hold values from -0.0625 to 0.0625
Outputs:
- out: float32 [4096, 1536], P(('fsdp', 'context'))
- grad_tokens: float32 [4096, 1536], P(('fsdp', 'context'))
- grad_attn_gain: float32 [1536], P('fsdp')
- grad_w_q: float32 [1536, 1536], P('fsdp', 'tensor')
- grad_b_q: float32 [12, 128], P('tensor', 'fsdp')
- grad_w_k: float32 [1536, 256], P('fsdp', 'tensor')
- grad_b_k: float32 [2, 128], P('tensor', 'fsdp')
- grad_w_v: float32 [1536, 256], P('fsdp', 'tensor')
- grad_b_v: float32 [2, 128], P('tensor', 'fsdp')
- grad_w_o: float32 [1536, 1536], P('tensor', 'fsdp')
- grad_mlp_gain: float32 [1536], P('fsdp')
- grad_w_gate: float32 [1536, 8960], P('fsdp', 'tensor')
- grad_w_up: float32 [1536, 8960], P('fsdp', 'tensor')
- grad_w_down: float32 [8960, 1536], P('tensor', 'fsdp')
Inputs may be any that keep to these rules, and one draw needn't show every extreme that they name: Row f lists the lengths of the 3 sequences packed in order into the 1024 rows of group f; they sum to 1024, and one of them is exactly 384 long. Each row span_order[f, c] is a permutation of 0 to 3.
All inputs are finite; a program needn't handle non-finite values.
Results may differ from a plain program's by a relative error of at most 0.018.
Values may be sent and summed in bfloat16 or wider, within the bound.
No kernel may reach another device: no remote copies, remote signals or barrier semaphores. Data moves between devices by JAX's collectives and lax.ppermute only.
A program may use at most 256 MiB of HBM per device.

v0:
```python
import jax
import jax.numpy as jnp
from jax import lax
from jax.sharding import PartitionSpec as P

D = 1536
HD = 128


epsilon = 1e-06
rope_base = 10000.0
neg_big = -1e30


def rms_scale(values):
    return lax.rsqrt(jnp.mean(values * values, axis=-1, keepdims=True) + epsilon)


def rotary_tables(position):
    half_dim = HD // 2
    frequency = rope_base ** (-(jnp.arange(half_dim, dtype=jnp.float32) * 2.0) / HD)
    angles = position.astype(jnp.float32)[:, None] * frequency[None, :]
    angles = jnp.concatenate([angles, angles], axis=1)
    return (jnp.cos(angles), jnp.sin(angles))


def rotate(values, cos_table, sin_table):
    half_dim = HD // 2
    turned = jnp.concatenate([-values[..., half_dim:], values[..., :half_dim]], axis=-1)
    return values * cos_table[:, None, :] + turned * sin_table[:, None, :]


def rotate_back(grad_in, cos_table, sin_table):
    half_dim = HD // 2
    scaled = grad_in * sin_table[:, None, :]
    turned = jnp.concatenate([scaled[..., half_dim:], -scaled[..., :half_dim]], axis=-1)
    return grad_in * cos_table[:, None, :] + turned


def locate(packed, seq_lengths):
    seq_ends = jnp.cumsum(seq_lengths)
    seq_starts = seq_ends - seq_lengths
    segment = jnp.sum((packed[:, None] >= seq_ends[None, :]).astype(jnp.int32), axis=1)
    inside = segment[:, None] == jnp.arange(seq_lengths.shape[0], dtype=jnp.int32)[None, :]
    offset = jnp.sum(jnp.where(inside, seq_starts[None, :], 0), axis=1)
    return (segment, packed - offset)


def dot_plain(left_op, right_op):
    return jnp.dot(left_op, right_op, preferred_element_type=jnp.float32)


def dot_rows(left_op, right_op):
    return lax.dot_general(
        left_op, right_op, (((0,), (0,)), ((), ())), preferred_element_type=jnp.float32
    )


def dot_cols(left_op, right_op):
    return lax.dot_general(
        left_op, right_op, (((1,), (1,)), ((), ())), preferred_element_type=jnp.float32
    )


def score_block(q_block, key_block, q_seg, q_pack, k_seg, k_pack):
    scores = jnp.einsum(
        "qngd,knd->ngqk", q_block, key_block, preferred_element_type=jnp.float32
    ) * HD ** (-0.5)
    allowed = (q_seg[:, None] == k_seg[None, :]) & (k_pack[None, :] <= q_pack[:, None])
    return jnp.where(allowed[None, None], scores, neg_big)


def key_split(kv_all, key_seg, key_pack, kv_local):
    key_size = min(1024, kv_all.shape[0])
    key_count = kv_all.shape[0] // key_size
    return (
        kv_all.reshape(key_count, key_size, 2, kv_local, HD),
        key_seg.reshape(key_count, key_size),
        key_pack.reshape(key_count, key_size),
    )


def query_split(arrays, row_count):
    query_size = min(512, row_count)
    return tuple(
        (
            member.reshape((row_count // query_size, query_size) + member.shape[1:])
            for member in arrays
        )
    )


def attend_forward(queries, kv_all, own_seg, own_pack, key_seg, key_pack):
    row_count, kv_local, grouped = (queries.shape[0], queries.shape[1], queries.shape[2])
    key_parts = key_split(kv_all, key_seg, key_pack, kv_local)
    query_parts = query_split((queries, own_seg, own_pack), row_count)
    query_size = query_parts[1].shape[1]

    def one_block(block_args):
        q_block, q_seg, q_pack = block_args

        def stat_step(running, key_args):
            run_top, run_sum = running
            kv_block, k_seg, k_pack = key_args
            scores = score_block(q_block, kv_block[:, 0], q_seg, q_pack, k_seg, k_pack)
            new_top = jnp.maximum(run_top, jnp.max(scores, axis=-1))
            run_sum = run_sum * jnp.exp(run_top - new_top) + jnp.sum(
                jnp.exp(scores - new_top[..., None]), axis=-1
            )
            return ((new_top, run_sum), None)

        start_top = jnp.full((kv_local, grouped, query_size), neg_big, jnp.float32)
        start_sum = jnp.zeros((kv_local, grouped, query_size), jnp.float32)
        run_top, run_sum = lax.scan(stat_step, (start_top, start_sum), key_parts)[0]
        log_sum = run_top + jnp.log(run_sum)

        def out_step(running, key_args):
            kv_block, k_seg, k_pack = key_args
            scores = score_block(q_block, kv_block[:, 0], q_seg, q_pack, k_seg, k_pack)
            weights = jnp.exp(scores - log_sum[..., None]).astype(jnp.bfloat16)
            return (
                running
                + jnp.einsum(
                    "ngqk,knd->qngd", weights, kv_block[:, 1], preferred_element_type=jnp.float32
                ),
                None,
            )

        start_out = jnp.zeros((query_size, kv_local, grouped, HD), jnp.float32)
        return (lax.scan(out_step, start_out, key_parts)[0], log_sum)

    attended, log_sum = lax.map(one_block, query_parts)
    return (attended.reshape(row_count, kv_local, grouped, HD), log_sum)


def attend_backward(queries, grad_out, log_sum, kv_all, own_seg, own_pack, key_seg, key_pack):
    row_count, kv_local, grouped = (queries.shape[0], queries.shape[1], queries.shape[2])
    key_parts = key_split(kv_all, key_seg, key_pack, kv_local)
    query_parts = query_split((queries, grad_out, own_seg, own_pack), row_count)
    score_scale = HD ** (-0.5)

    def one_block(dkv_sum, block_args):
        q_block, g_block, q_seg, q_pack, lse_block = block_args

        def delta_step(running, key_args):
            kv_block, k_seg, k_pack = key_args
            prob_block = jnp.exp(
                score_block(q_block, kv_block[:, 0], q_seg, q_pack, k_seg, k_pack)
                - lse_block[..., None]
            )
            dprobs = jnp.einsum(
                "qngd,knd->ngqk", g_block, kv_block[:, 1], preferred_element_type=jnp.float32
            )
            return (running + jnp.sum(prob_block * dprobs, axis=-1), None)

        row_delta = lax.scan(delta_step, jnp.zeros(lse_block.shape, jnp.float32), key_parts)[0]

        def grad_step(dq_sum, key_args):
            kv_block, k_seg, k_pack = key_args
            prob_block = jnp.exp(
                score_block(q_block, kv_block[:, 0], q_seg, q_pack, k_seg, k_pack)
                - lse_block[..., None]
            )
            dprobs = jnp.einsum(
                "qngd,knd->ngqk", g_block, kv_block[:, 1], preferred_element_type=jnp.float32
            )
            dscores = (prob_block * (dprobs - row_delta[..., None])).astype(jnp.bfloat16)
            dq_sum = (
                dq_sum
                + jnp.einsum(
                    "ngqk,knd->qngd", dscores, kv_block[:, 0], preferred_element_type=jnp.float32
                )
                * score_scale
            )
            d_keys = (
                jnp.einsum("ngqk,qngd->knd", dscores, q_block, preferred_element_type=jnp.float32)
                * score_scale
            )
            dvalues = jnp.einsum(
                "ngqk,qngd->knd",
                prob_block.astype(jnp.bfloat16),
                g_block,
                preferred_element_type=jnp.float32,
            )
            return (dq_sum, jnp.stack([d_keys, dvalues], axis=1))

        dq_block, dkv_blocks = lax.scan(grad_step, jnp.zeros(q_block.shape, jnp.float32), key_parts)
        return (dkv_sum + dkv_blocks.reshape(dkv_sum.shape), dq_block)

    dkv_start = jnp.zeros((kv_all.shape[0], kv_all.shape[1]), jnp.float32)
    dkv_all, dq_blocks = lax.scan(one_block, dkv_start, query_parts + (log_sum,))
    return (dq_blocks.reshape(row_count, kv_local, grouped, HD), dkv_all)


def swiglu_grads(gate_proj, up_proj, d_hidden):
    gate_sig = jax.nn.sigmoid(gate_proj)
    activated = gate_proj * gate_sig
    hidden = (activated * up_proj).astype(jnp.bfloat16)
    d_gate = (d_hidden * up_proj * gate_sig * (1.0 + gate_proj * (1.0 - gate_sig))).astype(
        jnp.bfloat16
    )
    d_up = (d_hidden * activated).astype(jnp.bfloat16)
    return (hidden, d_gate, d_up)


def head_total(values):
    return lax.psum(values, "tensor")


def per_device(
    tokens,
    cotangent,
    lengths,
    span_order,
    attn_gain,
    w_q,
    b_q,
    w_k,
    b_k,
    w_v,
    b_v,
    w_o,
    mlp_gain,
    w_gate,
    w_up,
    w_down,
):
    ctx_size = lax.axis_size("context")
    my_context = lax.axis_index("context")
    row_count = tokens.shape[0]
    piece_rows = row_count // ctx_size
    span_owner = lax.dynamic_index_in_dim(span_order[0], my_context, 0, keepdims=False)
    placing = span_owner[None, :] == jnp.arange(ctx_size, dtype=jnp.int32)[:, None]
    stacked = jnp.stack([tokens, cotangent]).reshape(2, ctx_size, piece_rows, D)
    outgoing = jnp.einsum(
        "dk,skrm->sdrm", placing.astype(jnp.bfloat16), stacked, preferred_element_type=jnp.float32
    ).astype(jnp.bfloat16)
    arrived = lax.all_to_all(outgoing, "context", split_axis=1, concat_axis=1, tiled=True).reshape(
        2, row_count, D
    )
    own_tokens = arrived[0]
    own_grad = arrived[1]
    seq_lengths = lengths[0]
    local_row = jnp.arange(row_count, dtype=jnp.int32)
    own_pack = (
        local_row // piece_rows * row_count + my_context * piece_rows + local_row % piece_rows
    )
    key_row = jnp.arange(ctx_size * row_count, dtype=jnp.int32)
    key_inner = key_row % row_count
    key_pack = (
        key_inner // piece_rows * row_count
        + key_row // row_count * piece_rows
        + key_inner % piece_rows
    )
    own_seg, own_pos = locate(own_pack, seq_lengths)
    key_seg = locate(key_pack, seq_lengths)[0]
    cos_table, sin_table = rotary_tables(own_pos)
    gain_one, gain_two, query_w, key_w, value_w, query_b, key_b, value_b, out_w = (
        lax.all_gather(attn_gain.astype(jnp.bfloat16), "fsdp", axis=0, tiled=True),
        lax.all_gather(mlp_gain.astype(jnp.bfloat16), "fsdp", axis=0, tiled=True),
        lax.all_gather(w_q.astype(jnp.bfloat16), "fsdp", axis=0, tiled=True),
        lax.all_gather(w_k.astype(jnp.bfloat16), "fsdp", axis=0, tiled=True),
        lax.all_gather(w_v.astype(jnp.bfloat16), "fsdp", axis=0, tiled=True),
        lax.all_gather(b_q.astype(jnp.bfloat16), "fsdp", axis=1, tiled=True),
        lax.all_gather(b_k.astype(jnp.bfloat16), "fsdp", axis=1, tiled=True),
        lax.all_gather(b_v.astype(jnp.bfloat16), "fsdp", axis=1, tiled=True),
        lax.all_gather(w_o.astype(jnp.bfloat16), "fsdp", axis=1, tiled=True),
    )
    heads_local = query_b.shape[0]
    kv_local = key_b.shape[0]
    grouped = heads_local // kv_local
    inputs = own_tokens.astype(jnp.float32)
    scale_one = rms_scale(inputs)
    normed = (inputs * scale_one * gain_one.astype(jnp.float32)).astype(jnp.bfloat16)
    query_pre = dot_plain(normed, query_w) + query_b.reshape(-1).astype(jnp.float32)
    key_pre = dot_plain(normed, key_w) + key_b.reshape(-1).astype(jnp.float32)
    value_pre = dot_plain(normed, value_w) + value_b.reshape(-1).astype(jnp.float32)
    queries = rotate(query_pre.reshape(row_count, heads_local, HD), cos_table, sin_table).astype(
        jnp.bfloat16
    )
    keys_rot = rotate(key_pre.reshape(row_count, kv_local, HD), cos_table, sin_table).astype(
        jnp.bfloat16
    )
    kv_local_rows = jnp.concatenate(
        [keys_rot.reshape(row_count, kv_local * HD), value_pre.astype(jnp.bfloat16)], axis=1
    )
    kv_all = lax.all_gather(kv_local_rows, "context", axis=0, tiled=True)
    queries_grouped = queries.reshape(row_count, kv_local, grouped, HD)
    attended, log_sum = attend_forward(
        queries_grouped, kv_all, own_seg, own_pack, key_seg, key_pack
    )
    attended_low = attended.reshape(row_count, heads_local * HD).astype(jnp.bfloat16)
    middle = inputs + head_total(dot_plain(attended_low, out_w))
    middle_scale = rms_scale(middle)
    normed_two = (middle * middle_scale * gain_two.astype(jnp.float32)).astype(jnp.bfloat16)
    gate_w, up_w, down_w = (
        lax.all_gather(w_gate.astype(jnp.bfloat16), "fsdp", axis=0, tiled=True),
        lax.all_gather(w_up.astype(jnp.bfloat16), "fsdp", axis=0, tiled=True),
        lax.all_gather(w_down.astype(jnp.bfloat16), "fsdp", axis=1, tiled=True),
    )
    gate_proj = dot_plain(normed_two, gate_w)
    up_proj = dot_plain(normed_two, up_w)
    hidden, d_gate, d_up = swiglu_grads(gate_proj, up_proj, dot_cols(own_grad, down_w))
    branch_part = dot_plain(hidden, down_w)
    normed_part = dot_cols(d_gate, gate_w) + dot_cols(d_up, up_w)
    mlp_grads = (
        lax.psum_scatter(
            dot_rows(normed_two, d_gate), ("fsdp", "context"), scatter_dimension=0, tiled=True
        ),
        lax.psum_scatter(
            dot_rows(normed_two, d_up), ("fsdp", "context"), scatter_dimension=0, tiled=True
        ),
        lax.psum_scatter(
            dot_rows(hidden, own_grad), ("fsdp", "context"), scatter_dimension=1, tiled=True
        ),
    )
    branch_out, d_normed_two = lax.psum((branch_part, normed_part), "tensor")
    grad_gain_two = jnp.sum(d_normed_two * middle * middle_scale, axis=0)
    weighted_two = d_normed_two * gain_two.astype(jnp.float32)
    d_middle = (
        own_grad.astype(jnp.float32)
        + middle_scale * weighted_two
        - middle * middle_scale**3 * jnp.mean(weighted_two * middle, axis=-1, keepdims=True)
    )
    d_branch = d_middle.astype(jnp.bfloat16)
    grad_o_w = dot_rows(attended_low, d_branch)
    d_attended = dot_cols(d_branch, out_w).astype(jnp.bfloat16)
    dq_rot, dkv_all = attend_backward(
        queries_grouped,
        d_attended.reshape(row_count, kv_local, grouped, HD),
        log_sum,
        kv_all,
        own_seg,
        own_pack,
        key_seg,
        key_pack,
    )
    dkv_own = lax.psum_scatter(dkv_all, "context", scatter_dimension=0, tiled=True)
    dq_low = (
        rotate_back(dq_rot.reshape(row_count, heads_local, HD), cos_table, sin_table)
        .reshape(row_count, heads_local * HD)
        .astype(jnp.bfloat16)
    )
    dk_low = (
        rotate_back(
            dkv_own[:, : kv_local * HD].reshape(row_count, kv_local, HD), cos_table, sin_table
        )
        .reshape(row_count, kv_local * HD)
        .astype(jnp.bfloat16)
    )
    dv_low = dkv_own[:, kv_local * HD :].astype(jnp.bfloat16)
    grad_q_w = dot_rows(normed, dq_low)
    grad_k_w = dot_rows(normed, dk_low)
    grad_v_w = dot_rows(normed, dv_low)
    grad_q_b = jnp.sum(dq_low.astype(jnp.float32), axis=0).reshape(heads_local, HD)
    grad_k_b = jnp.sum(dk_low.astype(jnp.float32), axis=0).reshape(kv_local, HD)
    grad_v_b = jnp.sum(dv_low.astype(jnp.float32), axis=0).reshape(kv_local, HD)
    d_normed_one = head_total(
        dot_cols(dq_low, query_w) + dot_cols(dk_low, key_w) + dot_cols(dv_low, value_w)
    )
    grad_gain_one = jnp.sum(d_normed_one * inputs * scale_one, axis=0)
    weighted_one = d_normed_one * gain_one.astype(jnp.float32)
    d_inputs = (
        d_middle
        + scale_one * weighted_one
        - inputs * scale_one**3 * jnp.mean(weighted_one * inputs, axis=-1, keepdims=True)
    )
    attn_grads = (
        lax.psum_scatter(grad_gain_one, ("fsdp", "context"), scatter_dimension=0, tiled=True),
        lax.psum_scatter(grad_gain_two, ("fsdp", "context"), scatter_dimension=0, tiled=True),
        lax.psum_scatter(grad_q_w, ("fsdp", "context"), scatter_dimension=0, tiled=True),
        lax.psum_scatter(grad_k_w, ("fsdp", "context"), scatter_dimension=0, tiled=True),
        lax.psum_scatter(grad_v_w, ("fsdp", "context"), scatter_dimension=0, tiled=True),
        lax.psum_scatter(grad_q_b, ("fsdp", "context"), scatter_dimension=1, tiled=True),
        lax.psum_scatter(grad_k_b, ("fsdp", "context"), scatter_dimension=1, tiled=True),
        lax.psum_scatter(grad_v_b, ("fsdp", "context"), scatter_dimension=1, tiled=True),
        lax.psum_scatter(grad_o_w, ("fsdp", "context"), scatter_dimension=1, tiled=True),
    )
    shared = (
        lax.all_gather(attn_grads[0].astype(jnp.bfloat16), "context", axis=0, tiled=True).astype(
            jnp.float32
        ),
        lax.all_gather(attn_grads[1].astype(jnp.bfloat16), "context", axis=0, tiled=True).astype(
            jnp.float32
        ),
        lax.all_gather(attn_grads[2].astype(jnp.bfloat16), "context", axis=0, tiled=True).astype(
            jnp.float32
        ),
        lax.all_gather(attn_grads[3].astype(jnp.bfloat16), "context", axis=0, tiled=True).astype(
            jnp.float32
        ),
        lax.all_gather(attn_grads[4].astype(jnp.bfloat16), "context", axis=0, tiled=True).astype(
            jnp.float32
        ),
        lax.all_gather(attn_grads[5].astype(jnp.bfloat16), "context", axis=1, tiled=True).astype(
            jnp.float32
        ),
        lax.all_gather(attn_grads[6].astype(jnp.bfloat16), "context", axis=1, tiled=True).astype(
            jnp.float32
        ),
        lax.all_gather(attn_grads[7].astype(jnp.bfloat16), "context", axis=1, tiled=True).astype(
            jnp.float32
        ),
        lax.all_gather(attn_grads[8].astype(jnp.bfloat16), "context", axis=1, tiled=True).astype(
            jnp.float32
        ),
        lax.all_gather(mlp_grads[0].astype(jnp.bfloat16), "context", axis=0, tiled=True).astype(
            jnp.float32
        ),
        lax.all_gather(mlp_grads[1].astype(jnp.bfloat16), "context", axis=0, tiled=True).astype(
            jnp.float32
        ),
        lax.all_gather(mlp_grads[2].astype(jnp.bfloat16), "context", axis=1, tiled=True).astype(
            jnp.float32
        ),
    )
    results = jnp.stack([middle + branch_out, d_inputs]).reshape(2, ctx_size, piece_rows, D)
    returned = lax.all_to_all(
        results.astype(jnp.bfloat16), "context", split_axis=1, concat_axis=1, tiled=True
    ).astype(results.dtype)
    restored = jnp.einsum(
        "dk,sdrm->skrm",
        placing.astype(jnp.float32),
        returned,
        precision=lax.Precision.HIGHEST,
        preferred_element_type=jnp.float32,
    ).reshape(2, row_count, D)
    return (
        restored[0],
        restored[1],
        shared[0],
        shared[2],
        shared[5],
        shared[3],
        shared[6],
        shared[4],
        shared[7],
        shared[8],
        shared[1],
        shared[9],
        shared[10],
        shared[11],
    )


def solution(mesh):
    in_specs = (
        P(("fsdp", "context"), None),
        P(("fsdp", "context"), None),
        P("fsdp", None),
        P("fsdp", None, None),
        P("fsdp"),
        P("fsdp", "tensor"),
        P("tensor", "fsdp"),
        P("fsdp", "tensor"),
        P("tensor", "fsdp"),
        P("fsdp", "tensor"),
        P("tensor", "fsdp"),
        P("tensor", "fsdp"),
        P("fsdp"),
        P("fsdp", "tensor"),
        P("fsdp", "tensor"),
        P("tensor", "fsdp"),
    )
    out_specs = (
        P(("fsdp", "context"), None),
        P(("fsdp", "context"), None),
        P("fsdp"),
        P("fsdp", "tensor"),
        P("tensor", "fsdp"),
        P("fsdp", "tensor"),
        P("tensor", "fsdp"),
        P("fsdp", "tensor"),
        P("tensor", "fsdp"),
        P("tensor", "fsdp"),
        P("fsdp"),
        P("fsdp", "tensor"),
        P("fsdp", "tensor"),
        P("tensor", "fsdp"),
    )
    return jax.shard_map(
        per_device, mesh=mesh, in_specs=in_specs, out_specs=out_specs, check_vma=False
    )
```

profile of v0, /device:TPU:0, one launch (start us, length us, event | category | flops | bytes accessed | tf_op | source)
XLA Modules:
  0.0 1950.7 jit_solution(576891917013980563)
XLA Ops:
  13.4 6.5 all-to-all-start
  20.9 5.2 all-gather
  27.9 7.5 all-reduce.14
  35.7 5.2 all-gather.1
  41.2 6.5 all_gather.78
  47.8 9.1 all_gather.76
  64.8 17.2 all_gather.80
  97.6 3.7 fusion.85
  101.4 5.1 convert_element_type.300
  106.6 5.6 convert_element_type.303
  112.3 5.1 convert_element_type.301
  118.1 5.5 all-gather.2
  124.6 29.2 %all-reduce.19.cloned.1.call-done = f32[256,1536]{1,0:T(8,128)} async-done(((f32[256,1536]{1,0:T(8,128)}), f32[256,1536]{1,0:T(8,128)}) %all-reduce.19.cloned.1.call-update) | async-done | bytes 1572880 | tf_op jit(solution)/shard_map/psum | solution.py:207
  155.8 88.9 %all-gather.16.cloned.1.call-done = bf16[1536,4480]{1,0:T(8,128)(2,1)} async-done(((bf16[384,4480]{1,0:T(8,128)(2,1)}), bf16[1536,4480]{1,0:T(8,128)(2,1)}) %all-gather.16.cloned.1.call-update) | async-done | bytes 13762576 | tf_op jit(solution)/shard_map/all_gather | solution.py:297
  244.7 10.5 fusion.86
  255.2 80.2 %all-gather.20.cloned.1.call-done = bf16[4480,1536]{1,0:T(8,128)(2,1)} async-done(((bf16[4480,384]{1,0:T(8,128)(2,1)}), bf16[4480,1536]{1,0:T(8,128)(2,1)}) %all-gather.20.cloned.1.call-update) | async-done | bytes 13762576 | tf_op jit(solution)/shard_map/all_gather | solution.py:299
  335.4 15.5 fusion.88
  350.9 74.9 %all-gather.18.cloned.1.call-done = bf16[1536,4480]{1,0:T(8,128)(2,1)} async-done(((bf16[384,4480]{1,0:T(8,128)(2,1)}), bf16[1536,4480]{1,0:T(8,128)(2,1)}) %all-gather.18.cloned.1.call-update) | async-done | bytes 13762576 | tf_op jit(solution)/shard_map/all_gather | solution.py:298
  425.7 13.0 multiply_convert_fusion.2
  438.7 8.7 fusion.89
  447.5 8.4 convolution_add_fusion.2
  456.1 51.4 %all-reduce.21.cloned.1.call-done = f32[256,1536]{1,0:T(8,128)} async-done(((f32[256,1536]{1,0:T(8,128)}), f32[256,1536]{1,0:T(8,128)}) %all-reduce.21.cloned.1.call-update) | async-done | bytes 1572880 | tf_op jit(solution)/shard_map/psum | solution.py:317
  515.0 4.9 fusion
  529.8 11.2 fusion.93
  542.7 11.1 fusion.94
  555.7 12.9 fusion.95
  568.7 14.5 fusion.87
  607.4 214.7 %reduce-scatter.22.cloned.1.call-done = f32[96,4480]{1,0:T(8,128)} async-done(((f32[1536,4480]{1,0:T(8,128)}), f32[96,4480]{1,0:T(8,128)}) %reduce-scatter.22.cloned.1.call-update) | async-done | bytes 1720336 | tf_op jit(solution)/shard_map/reduce_scatter | solution.py:307
  824.6 263.4 %reduce-scatter.24.cloned.1.call-done = f32[96,4480]{1,0:T(8,128)} async-done(((f32[1536,4480]{1,0:T(8,128)}), f32[96,4480]{1,0:T(8,128)}) %reduce-scatter.24.cloned.1.call-update) | async-done | bytes 1720336 | tf_op jit(solution)/shard_map/reduce_scatter | solution.py:310
  1090.6 264.1 %reduce-scatter.26.cloned.1.call-done = f32[4480,96]{0,1:T(8,128)} async-done(((f32[4480,1536]{0,1:T(8,128)}), f32[4480,96]{0,1:T(8,128)}) %reduce-scatter.26.cloned.1.call-update) | async-done | bytes 1720336 | tf_op jit(solution)/shard_map/reduce_scatter | solution.py:313
  1357.2 86.0 %all-reduce.23.cloned.1.call-done = (f32[256,1536]{1,0:T(8,128)}, f32[256,1536]{1,0:T(8,128)}) async-done(((f32[256,1536]{1,0:T(8,128)}, f32[256,1536]{1,0:T(8,128)}), (f32[256,1536]{1,0:T(8,128)}, f32[256,1536]{1,0:T(8,128)})) %all-reduce.23.cloned.1.call-update) | async-done | bytes 3145744 | tf_op jit(solution)/shard_map/psum | solution.py:207
  1448.8 4.7 all-to-all-start.1
  1457.3 53.4 %reduce-scatter.16.cloned.1.call-done = f32[96,128]{1,0:T(8,128)} async-done(((f32[1536,128]{1,0:T(8,128)}), f32[96,128]{1,0:T(8,128)}) %reduce-scatter.16.cloned.1.call-update) | async-done | bytes 49168 | tf_op jit(solution)/shard_map/reduce_scatter | solution.py:372
  1511.5 13.7 all_gather.91
  1525.9 44.3 %reduce-scatter.18.cloned.1.call-done = f32[96,128]{1,0:T(8,128)} async-done(((f32[1536,128]{1,0:T(8,128)}), f32[96,128]{1,0:T(8,128)}) %reduce-scatter.18.cloned.1.call-update) | async-done | bytes 49168 | tf_op jit(solution)/shard_map/reduce_scatter | solution.py:373
  1571.0 13.4 all_gather.93
  1585.2 59.6 %all-reduce.11 = (bf16[6,128]{1,0:T(8,128)(2,1)S(1)}, bf16[1536]{0:T(1024)(128)(2,1)S(1)}, bf16[1,128]{1,0:T(2,128)(2,1)S(1)}, bf16[1,128]{1,0:T(2,128)(2,1)S(1)}, bf16[1536]{0:T(1024)(128)(2,1)S(1)}) all-reduce(f32[6,128]{1,0:T(8,128)S(1)} %get-tuple-element.323, ...), channel_id=5, replica_groups=mesh['fsdp'=4,'context'=4,'tensor'=2] {'fsdp','context'}, use_global_device_ids=true, to_apply=%region_20.21.clone | all-reduce | flops 4096 | bytes 24576
  1645.9 8.3 all-reduce.13
  1655.0 11.9 all_gather.90
  1670.1 16.2 all_gather.89
  1687.4 41.7 %reduce-scatter.20.cloned.1.call-done = f32[768,96]{0,1:T(8,128)} async-done(((f32[768,1536]{0,1:T(8,128)}), f32[768,96]{0,1:T(8,128)}) %reduce-scatter.20.cloned.1.call-update) | async-done | bytes 294928 | tf_op jit(solution)/shard_map/reduce_scatter | solution.py:377
  1730.1 18.9 all_gather.95
  1755.1 45.0 %all-gather.22.cloned.1.call-done = bf16[384,4480]{1,0:T(8,128)(2,1)} async-done(((bf16[96,4480]{1,0:T(8,128)(2,1)}), bf16[384,4480]{1,0:T(8,128)(2,1)}) %all-gather.22.cloned.1.call-update) | async-done | bytes 3440656 | tf_op jit(solution)/shard_map/all_gather | solution.py:407
  1800.1 5.3 convert_element_type.339
  1805.4 63.5 %all-gather.24.cloned.1.call-done = bf16[384,4480]{1,0:T(8,128)(2,1)} async-done(((bf16[96,4480]{1,0:T(8,128)(2,1)}), bf16[384,4480]{1,0:T(8,128)(2,1)}) %all-gather.24.cloned.1.call-update) | async-done | bytes 3440656 | tf_op jit(solution)/shard_map/all_gather | solution.py:410
  1868.9 5.3 convert_element_type.341
  1874.2 63.3 %all-gather.26.cloned.1.call-done = bf16[4480,384]{0,1:T(8,128)(2,1)} async-done(((bf16[4480,96]{0,1:T(8,128)(2,1)}), bf16[4480,384]{0,1:T(8,128)(2,1)}) %all-gather.26.cloned.1.call-update) | async-done | bytes 3440656 | tf_op jit(solution)/shard_map/all_gather | solution.py:413
  1937.5 6.2 copy.182
  (333 shorter events, 111.4 us)
Async XLA Ops:
  7.2 74.7 %all-gather.12.cloned.1.call-start = ((), (), s32[]{:S(2)}) async-start(), calls=%async_computation.10 | async-start | bytes 2949120 | tf_op jit(solution)/shard_map/all_gather | solution.py:261
  13.4 7.5 copy-start.66
  13.4 12.7 copy-start.70
  13.4 12.7 copy-start.54
  13.4 12.8 copy-start.75
  13.4 14.3 copy-start.71
  13.4 22.0 %copy-start.72 = (s32[1,3]{1,0:T(1,128)S(1)}, s32[1,3]{1,0:T(1,128)}, u32[]{:S(2)}) copy-start(s32[1,3]{1,0:T(1,128)} %param.18) | copy-start | bytes 40
  13.4 22.2 %copy-start.55 = (f32[384,128]{1,0:T(8,128)S(1)}, f32[384,128]{1,0:T(8,128)}, u32[]{:S(2)}) copy-start(f32[384,128]{1,0:T(8,128)} %param.23) | copy-start | bytes 589828
  13.4 44.5 %all-to-all-start = ((bf16[2,4,64,1536]{3,2,0,1:T(8,128)(2,1)}), bf16[2,4,64,1536]{3,2,0,1:T(8,128)(2,1)S(1)}, u32[]{:S(2)}, u32[]{:S(2)}) async-start(bf16[2,4,64,1536]{3,2,0,1:T(8,128)(2,1)} %copy.153), calls=%async_computation | async-start | bytes 3145728 | tf_op jit(solution)/shard_map/all_to_all | solution.py:238
  19.9 15.8 copy-start.63
  19.9 77.7 %all-gather.14.cloned.1.call-start = ((), (), s32[]{:S(2)}) async-start(), calls=%async_computation.11 | async-start | bytes 2949120 | tf_op jit(solution)/shard_map/all_gather | solution.py:267
  20.8 133.0 %all-reduce.19.cloned.1.call-start = ((), (), s32[]{:S(2)}) async-start(), calls=%async_computation.12 | async-start | bytes 3145728 | tf_op jit(solution)/shard_map/psum | solution.py:207
  26.1 33.7 %copy-start.52 = (f32[1536]{0:T(1024)}, f32[1536]{0:T(1024)S(1)}, u32[]{:S(2)}) copy-start(f32[1536]{0:T(1024)S(1)} %reshape.576) | copy-start | bytes 18436
  47.8 16.6 copy-start.25
  58.0 95.8 %copy-start.5 = (bf16[2,4,64,1536]{3,2,0,1:T(8,128)(2,1)}, bf16[2,4,64,1536]{3,2,0,1:T(8,128)(2,1)S(1)}, u32[]{:S(2)}) copy-start(bf16[2,4,64,1536]{3,2,0,1:T(8,128)(2,1)S(1)} %all-to-all-done) | copy-start | bytes 4718596
  59.4 22.6 %copy-start.12 = (bf16[256,1536]{1,0:T(8,128)(2,1)}, bf16[256,1536]{1,0:T(8,128)(2,1)S(1)}, u32[]{:S(2)}) copy-start(bf16[256,1536]{1,0:T(8,128)(2,1)S(1)} %fusion.16) | copy-start | bytes 2359300
  101.4 143.3 %all-gather.16.cloned.1.call-start = ((), (), s32[]{:S(2)}) async-start(), calls=%async_computation.13 | async-start | bytes 17203200 | tf_op jit(solution)/shard_map/all_gather | solution.py:297
  106.5 228.9 %all-gather.20.cloned.1.call-start = ((), (), s32[]{:S(2)}) async-start(), calls=%async_computation.15 | async-start | bytes 17203200 | tf_op jit(solution)/shard_map/all_gather | solution.py:299
  112.2 313.5 %all-gather.18.cloned.1.call-start = ((), (), s32[]{:S(2)}) async-start(), calls=%async_computation.14 | async-start | bytes 17203200 | tf_op jit(solution)/shard_map/all_gather | solution.py:298
  117.4 390.1 %all-reduce.21.cloned.1.call-start = ((), (), s32[]{:S(2)}) async-start(), calls=%async_computation.16 | async-start | bytes 3145728 | tf_op jit(solution)/shard_map/psum | solution.py:317
  155.5 354.6 %copy-start.3 = (f32[256,1536]{1,0:T(8,128)}, f32[256,1536]{1,0:T(8,128)S(1)}, u32[]{:S(2)}) copy-start(f32[256,1536]{1,0:T(8,128)S(1)} %get-tuple-element.326) | copy-start | bytes 4718596
  155.7 270.0 %copy-start.20 = (bf16[256,1536]{1,0:T(8,128)(2,1)}, bf16[256,1536]{1,0:T(8,128)(2,1)S(1)}, u32[]{:S(2)}) copy-start(bf16[256,1536]{1,0:T(8,128)(2,1)S(1)} %multiply_convert_fusion.3) | copy-start | bytes 2359300
  155.7 179.7 %copy-start.18 = (bf16[1,4,64,1536]{3,2,0,1:T(8,128)(2,1)S(1)}, bf16[1,4,64,1536]{3,2,0,1:T(8,128)(2,1)}, u32[]{:S(2)}) copy-start(bf16[1,4,64,1536]{3,2,0,1:T(8,128)(2,1)} %slice.96) | copy-start | bytes 2359300
  438.7 8.7 copy-start.38
  438.7 8.7 copy-start.36
  455.9 131.3 %reduce-scatter.12.cloned.1.call-start = ((), (), s32[]{:S(2)}) async-start(), calls=%async_computation.17 | async-start | bytes 1310720 | tf_op jit(solution)/shard_map/reduce_scatter | solution.py:338
  512.2 7.7 slice-start
  528.6 293.5 %reduce-scatter.22.cloned.1.call-start = ((), (), s32[]{:S(2)}) async-start(), calls=%async_computation.22 | async-start | bytes 29245440 | tf_op jit(solution)/shard_map/reduce_scatter | solution.py:307
  541.0 547.0 %reduce-scatter.24.cloned.1.call-start = ((), (), s32[]{:S(2)}) async-start(), calls=%async_computation.24 | async-start | bytes 29245440 | tf_op jit(solution)/shard_map/reduce_scatter | solution.py:310
  553.8 800.9 %reduce-scatter.26.cloned.1.call-start = ((), (), s32[]{:S(2)}) async-start(), calls=%async_computation.26 | async-start | bytes 29245440 | tf_op jit(solution)/shard_map/reduce_scatter | solution.py:313
  568.6 14.6 copy-start.8
  568.6 14.6 copy-start.44
  568.6 874.5 %all-reduce.23.cloned.1.call-start = ((), (), s32[]{:S(2)}) async-start(), calls=%async_computation.28 | async-start | bytes 6291456 | tf_op jit(solution)/shard_map/psum | solution.py:207
  568.7 14.5 copy-start.31
  593.5 917.2 %reduce-scatter.16.cloned.1.call-start = ((), (), s32[]{:S(2)}) async-start(), calls=%async_computation.19 | async-start | bytes 835584 | tf_op jit(solution)/shard_map/reduce_scatter | solution.py:372
  597.4 972.8 %reduce-scatter.18.cloned.1.call-start = ((), (), s32[]{:S(2)}) async-start(), calls=%async_computation.20 | async-start | bytes 835584 | tf_op jit(solution)/shard_map/reduce_scatter | solution.py:373
  599.7 1069.4 %reduce-scatter.14.cloned.1.call-start = ((), (), s32[]{:S(2)}) async-start(), calls=%async_computation.18 | async-start | bytes 5013504 | tf_op jit(solution)/shard_map/reduce_scatter | solution.py:371
  602.8 1126.3 %reduce-scatter.20.cloned.1.call-start = ((), (), s32[]{:S(2)}) async-start(), calls=%async_computation.21 | async-start | bytes 5013504 | tf_op jit(solution)/shard_map/reduce_scatter | solution.py:377
  607.3 1192.8 %all-gather.22.cloned.1.call-start = ((), (), s32[]{:S(2)}) async-start(), calls=%async_computation.23 | async-start | bytes 4300800 | tf_op jit(solution)/shard_map/all_gather | solution.py:407
  824.5 266.0 %copy-start.60 = (f32[256]{0:T(256)S(1)}, f32[256]{0:T(256)}, u32[]{:S(2)}) copy-start(f32[256]{0:T(256)} %copy-done.59) | copy-start | bytes 3076
  824.6 1044.3 %all-gather.24.cloned.1.call-start = ((), (), s32[]{:S(2)}) async-start(), calls=%async_computation.25 | async-start | bytes 4300800 | tf_op jit(solution)/shard_map/all_gather | solution.py:410
  1090.5 847.0 %all-gather.26.cloned.1.call-start = ((), (), s32[]{:S(2)}) async-start(), calls=%async_computation.27 | async-start | bytes 4300800 | tf_op jit(solution)/shard_map/all_gather | solution.py:413
  1090.6 354.6 %copy-start.4 = (f32[256,1536]{1,0:T(8,128)S(1)}, f32[256,1536]{1,0:T(8,128)}, u32[]{:S(2)}) copy-start(f32[256,1536]{1,0:T(8,128)} %copy-done.3) | copy-start | bytes 4718596
  1448.8 136.4 %copy-start.58 = (f32[1536]{0:T(1024)S(1)}, f32[1536]{0:T(1024)}, u32[]{:S(2)}) copy-start(f32[1536]{0:T(1024)} %get-tuple-element.304) | copy-start | bytes 18436
  1448.8 136.4 %copy-start.64 = (f32[128]{0:T(128)S(1)}, f32[128]{0:T(128)}, u32[]{:S(2)}) copy-start(f32[128]{0:T(128)} %get-tuple-element.337) | copy-start | bytes 1540
  1448.8 136.4 %copy-start.65 = (f32[128]{0:T(128)S(1)}, f32[128]{0:T(128)}, u32[]{:S(2)}) copy-start(f32[128]{0:T(128)} %get-tuple-element.321) | copy-start | bytes 1540
  1448.8 301.5 %all-to-all-start.1 = ((bf16[2,4,64,1536]{3,2,0,1:T(8,128)(2,1)}), bf16[2,4,64,1536]{3,2,0,1:T(8,128)(2,1)S(1)}, u32[]{:S(2)}, u32[]{:S(2)}) async-start(bf16[2,4,64,1536]{3,2,0,1:T(8,128)(2,1)} %pad_maximum_fusion), calls=%async_computation.2 | async-start | bytes 3145728 | tf_op jit(solution)/shard_map/all_to_all | solution.py:418
  1686.3 64.0 %copy-start.69 = (s32[4]{0:T(128)S(1)}, s32[4]{0:T(128)}, u32[]{:S(2)}) copy-start(s32[4]{0:T(128)} %copy-done.68) | copy-start | bytes 52
  (51 other events, 138.9 us)
Sparse Core Ops, SparseCore 0:
  10.2 26.9 all-gather.11
  39.3 26.1 all-gather.13
  101.5 52.2 all-reduce.18
  155.9 88.7 all-gather.15
  246.8 88.5 all-gather.19
  336.9 88.7 all-gather.17
  456.0 51.4 all-reduce.20
  528.7 27.1 reduce-scatter.11
  560.5 261.5 reduce-scatter.21
  826.0 261.9 reduce-scatter.23
  1092.7 261.9 reduce-scatter.25
  1358.1 85.0 all-reduce.22
  1447.7 62.9 reduce-scatter.15
  1514.7 55.4 reduce-scatter.17
  1575.0 75.1 reduce-scatter.13
  1654.5 74.5 reduce-scatter.19
  1730.6 69.4 all-gather.21
  1801.6 67.2 all-gather.23
  1870.5 66.9 all-gather.25
where the time goes:
time: 1960 us; the launch traced here: 1950 us
  waiting for transfers between devices  1460 us (74%)
  blocking collectives  198 us (10%)
  matrix products  145 us (7%)
  other arithmetic  70.6 us (4%)
  local copies, waits for them, and re-layouts  41.5 us (2%)
    reduce_scatter x1, waiting for transfers between devices, per_device(): lax.psum_scatter(dot_rows(hidden, own_grad), ('fsdp', 'context'), scatter...  264 us
    reduce_scatter x1, waiting for transfers between devices, per_device(): lax.psum_scatter(dot_rows(normed_two, d_up), ('fsdp', 'context'), scatter...  263 us
    reduce_scatter x1, waiting for transfers between devices, per_device(): lax.psum_scatter(dot_rows(normed_two, d_gate), ('fsdp', 'context'), scatt...  215 us
    psum x2, waiting for transfers between devices, head_total(): return lax.psum(values, 'tensor')  115 us
    all_gather x1, waiting for transfers between devices, per_device(): lax.all_gather(w_gate.astype(jnp.bfloat16), 'fsdp', axis=0, tiled=True)  88.9 us
    all_gather x1, waiting for transfers between devices, per_device(): lax.all_gather(w_down.astype(jnp.bfloat16), 'fsdp', axis=1, tiled=True)  80.2 us
    unnamed x3, blocking collectives  75.5 us
    all_gather x1, waiting for transfers between devices, per_device(): lax.all_gather(w_up.astype(jnp.bfloat16), 'fsdp', axis=0, tiled=True)  74.9 us
  transfers between devices with their start and end apart: 21, of which 15 were waited for; matrix products, arithmetic and copies ran while one was open for 9% of the time, Pallas kernels for 0%

commit v1 on v0

v1 whole, which is shorter than its diff:
```python
import functools

import jax
import jax.numpy as jnp
from jax import lax
from jax.experimental import pallas as pl
from jax.experimental.pallas import tpu as pltpu
from jax.sharding import PartitionSpec as P

D = 1536
HD = 128
LANES = 128
TEAM = 2
PARTS = 2

epsilon = 1e-06
rope_base = 10000.0
neg_big = -1e30
far_away = 1 << 29
bf16 = jnp.bfloat16
f32 = jnp.float32


def dot_plain(left_op, right_op):
    return jnp.dot(left_op, right_op, preferred_element_type=f32)


def dot_rows(left_op, right_op):
    return lax.dot_general(
        left_op, right_op, (((0,), (0,)), ((), ())), preferred_element_type=f32
    )


def dot_cols(left_op, right_op):
    return lax.dot_general(
        left_op, right_op, (((1,), (1,)), ((), ())), preferred_element_type=f32
    )


def swap(values, axis_name, bit):
    size = lax.axis_size(axis_name)
    return lax.ppermute(values, axis_name, [(i, i ^ bit) for i in range(size)])


def shift(values, axis_name, step):
    size = lax.axis_size(axis_name)
    pairs = [(i, i + step) for i in range(size) if 0 <= i + step < size]
    return lax.ppermute(values, axis_name, pairs)


def bits_of(size):
    found = []
    bit = 1
    while bit < size:
        found.append(bit)
        bit *= 2
    return found


def fsdp_order(size):
    order = [0]
    for bit in reversed(bits_of(size)):
        order = order + [held ^ bit for held in order]
    return order


def gather_pieces(piece):
    pieces = [piece]
    for bit in reversed(bits_of(lax.axis_size("fsdp"))):
        pieces = pieces + [swap(held, "fsdp", bit) for held in pieces]
    return pieces


def xor_blocks(blocks, index, size):
    for bit in bits_of(size):
        on = (index & bit) != 0
        blocks = [jnp.where(on, blocks[i ^ bit], blocks[i]) for i in range(size)]
    return blocks


def to_relative(values, index, size):
    width = values.shape[-1] // size
    blocks = [values[..., i * width : (i + 1) * width] for i in range(size)]
    blocks = xor_blocks(blocks, index, size)
    return jnp.concatenate([blocks[i] for i in fsdp_order(size)], axis=-1)


def from_relative(values, index, size):
    width = values.shape[-1] // size
    order = fsdp_order(size)
    blocks = [None] * size
    for place, i in enumerate(order):
        blocks[i] = values[..., place * width : (place + 1) * width]
    return jnp.concatenate(xor_blocks(blocks, index, size), axis=-1)


def reduce_fsdp(values, axis):
    for bit in bits_of(lax.axis_size("fsdp")):
        half = values.shape[axis] // 2
        kept = lax.slice_in_dim(values, 0, half, axis=axis)
        sent = lax.slice_in_dim(values, half, 2 * half, axis=axis).astype(bf16)
        values = kept.astype(f32) + swap(sent, "fsdp", bit).astype(f32)
    return values


def sum_context(values):
    index = lax.axis_index("context")
    bits = bits_of(lax.axis_size("context"))
    for bit in bits:
        half = values.shape[0] // 2
        on = (index & bit) != 0
        kept = jnp.where(on, values[half:], values[:half])
        sent = jnp.where(on, values[:half], values[half:]).astype(bf16)
        values = kept + swap(sent, "context", bit).astype(f32)
    values = values.astype(bf16)
    for bit in reversed(bits):
        on = (index & bit) != 0
        other = swap(values, "context", bit)
        values = jnp.concatenate(
            [jnp.where(on, other, values), jnp.where(on, values, other)], axis=0
        )
    return values.astype(f32)


def turn_sign(shape):
    lane = lax.broadcasted_iota(jnp.int32, shape, 1)
    return jnp.where(lane < HD // 2, -1.0, 1.0)


def attend_body(q_ref, kv_ref, low_ref, high_ref, key_ref, o_ref):
    scores = dot_cols(q_ref[...], kv_ref[:, :HD]) * HD ** (-0.5)
    key_at = key_ref[...]
    allowed = (key_at >= low_ref[...]) & (key_at <= high_ref[...])
    scores = jnp.where(allowed, scores, neg_big)
    top = jnp.max(scores, axis=-1, keepdims=True)
    raised = jnp.exp(scores - top)
    weights = raised * (1.0 / jnp.sum(raised, axis=-1, keepdims=True))
    o_ref[...] = dot_plain(weights.astype(bf16), kv_ref[:, HD:]).astype(bf16)


def attend_back_body(
    q_ref, g_ref, kv_ref, low_ref, high_ref, key_ref, cos_ref, sin_ref, dq_ref, dkv_ref
):
    scale = HD ** (-0.5)
    queries = q_ref[...]
    grad = g_ref[...]
    keys = kv_ref[:, :HD]
    scores = dot_cols(queries, keys) * scale
    key_at = key_ref[...]
    allowed = (key_at >= low_ref[...]) & (key_at <= high_ref[...])
    scores = jnp.where(allowed, scores, neg_big)
    top = jnp.max(scores, axis=-1, keepdims=True)
    raised = jnp.exp(scores - top)
    weights = raised * (1.0 / jnp.sum(raised, axis=-1, keepdims=True))
    dweights = dot_cols(grad, kv_ref[:, HD:])
    delta = jnp.sum(weights * dweights, axis=-1, keepdims=True)
    dscores = (weights * (dweights - delta)).astype(bf16)
    dq_rot = dot_plain(dscores, keys) * scale
    turned = pltpu.roll(dq_rot, HD // 2, 1)
    dq_ref[...] = (dq_rot * cos_ref[...] - turned * sin_ref[...]).astype(bf16)
    dkeys = dot_rows(dscores, queries) * scale
    dvalues = dot_rows(weights.astype(bf16), grad)

    @pl.when(pl.program_id(0) == 0)
    def _():
        dkv_ref[:, :HD] = dkeys
        dkv_ref[:, HD:] = dvalues

    @pl.when(pl.program_id(0) != 0)
    def _():
        dkv_ref[:, :HD] += dkeys
        dkv_ref[:, HD:] += dvalues


def whole_spec(array):
    return pl.BlockSpec(array.shape, lambda h: (0,) * array.ndim)


def attend(queries, kv_all, low, high, key_at):
    rows, width = queries.shape
    head = pl.BlockSpec((rows, HD), lambda h: (0, h))
    keys = kv_all.shape[0]
    return pl.pallas_call(
        attend_body,
        out_shape=jax.ShapeDtypeStruct(queries.shape, bf16),
        grid=(width // HD,),
        in_specs=[head] + [whole_spec(a) for a in (kv_all, low, high, key_at)],
        out_specs=head,
        compiler_params=pltpu.CompilerParams(vmem_limit_bytes=32 << 20),
        cost_estimate=pl.CostEstimate(
            flops=4 * rows * width * keys,
            transcendentals=rows * keys * (width // HD),
            bytes_accessed=4 * rows * width + 4 * keys * HD,
        ),
    )(queries, kv_all, low, high, key_at)


def attend_back(queries, grad, kv_all, low, high, key_at, cos_table, sin_table):
    rows, width = queries.shape
    head = pl.BlockSpec((rows, HD), lambda h: (0, h))
    keys = kv_all.shape[0]
    rest = (kv_all, low, high, key_at, cos_table, sin_table)
    return pl.pallas_call(
        attend_back_body,
        out_shape=(
            jax.ShapeDtypeStruct(queries.shape, bf16),
            jax.ShapeDtypeStruct(kv_all.shape, f32),
        ),
        grid=(width // HD,),
        in_specs=[head, head] + [whole_spec(a) for a in rest],
        out_specs=(head, whole_spec(kv_all)),
        compiler_params=pltpu.CompilerParams(vmem_limit_bytes=48 << 20),
        cost_estimate=pl.CostEstimate(
            flops=10 * rows * width * keys,
            transcendentals=rows * keys * (width // HD),
            bytes_accessed=6 * rows * width + 12 * keys * HD,
        ),
    )(queries, grad, *rest)


def swiglu_grads(gate_proj, up_proj, d_hidden, shown):
    gate_sig = jax.nn.sigmoid(gate_proj)
    activated = gate_proj * gate_sig
    hidden = activated * up_proj
    d_gate = d_hidden * up_proj * gate_sig * (1.0 + gate_proj * (1.0 - gate_sig))
    d_up = d_hidden * activated
    if shown is not None:
        hidden, d_gate, d_up = (jnp.where(shown, v, 0.0) for v in (hidden, d_gate, d_up))
    return hidden.astype(bf16), d_gate.astype(bf16), d_up.astype(bf16)


def rms_scale(values):
    return lax.rsqrt(jnp.mean(values * values, axis=-1, keepdims=True) + epsilon)


def per_device(
    tokens,
    cotangent,
    lengths,
    span_order,
    attn_gain,
    w_q,
    b_q,
    w_k,
    b_k,
    w_v,
    b_v,
    w_o,
    mlp_gain,
    w_gate,
    w_up,
    w_down,
):
    n_fsdp = lax.axis_size("fsdp")
    n_ctx = lax.axis_size("context")
    my_fsdp = lax.axis_index("fsdp")
    my_ctx = lax.axis_index("context")
    my_tensor = lax.axis_index("tensor")
    member = my_ctx % TEAM
    rows = tokens.shape[0]
    half = rows // 2
    piece_rows = rows // n_ctx
    shard = D // n_fsdp
    q_width = w_q.shape[1]
    kv_width = w_k.shape[1]
    qkv_width = q_width + 2 * kv_width
    heads_local = q_width // HD
    all_heads = qkv_width // HD
    flipped = my_tensor != 0

    def mine_first(values):
        first, second = values[:half], values[half:]
        return jnp.concatenate(
            [jnp.where(flipped, second, first), jnp.where(flipped, first, second)], axis=0
        )

    extras = jnp.concatenate(
        [
            attn_gain.astype(bf16),
            mlp_gain.astype(bf16),
            jnp.concatenate([b_q, b_k, b_v], axis=0).astype(bf16).reshape(-1),
        ]
    )
    extras = jnp.pad(extras, (0, qkv_width - extras.shape[0]))
    extra_rows = jnp.pad(extras[None, :], ((0, 15), (0, 0)))
    qkv_pack = jnp.concatenate(
        [jnp.concatenate([w_q, w_k, w_v], axis=1).astype(bf16), extra_rows], axis=0
    )
    qkv_pieces = gather_pieces(qkv_pack)
    qkv_w = jnp.concatenate([p[:shard] for p in qkv_pieces], axis=0)
    gain_one = jnp.concatenate([p[shard, :shard] for p in qkv_pieces]).astype(f32)[None, :]
    gain_two = (
        jnp.concatenate([p[shard, shard : 2 * shard] for p in qkv_pieces]).astype(f32)[None, :]
    )
    bias_cols = HD // n_fsdp
    bias_size = all_heads * bias_cols
    order = fsdp_order(n_fsdp)
    bias_blocks = [None] * n_fsdp
    for place, i in enumerate(order):
        bias_blocks[i] = (
            qkv_pieces[place][shard, 2 * shard : 2 * shard + bias_size]
            .astype(f32)
            .reshape(all_heads, bias_cols)
        )
    bias = jnp.concatenate(xor_blocks(bias_blocks, my_fsdp, n_fsdp), axis=1).reshape(1, -1)
    out_w = jnp.concatenate(gather_pieces(w_o.astype(bf16)), axis=1)

    ff_local = w_gate.shape[1]
    tiles = ff_local // LANES
    slice_tiles = -(-tiles // (TEAM * PARTS)) * PARTS
    part = slice_tiles // PARTS * LANES
    starts = [min(s * slice_tiles, tiles - slice_tiles) * LANES for s in range(TEAM)]
    fresh = [s * slice_tiles * LANES - starts[s] for s in range(TEAM)]

    def own_part(values, axis, index):
        chosen = lax.slice_in_dim(values, starts[0] + index * part, starts[0] + (index + 1) * part, axis=axis)
        for s in range(1, TEAM):
            other = lax.slice_in_dim(values, starts[s] + index * part, starts[s] + (index + 1) * part, axis=axis)
            chosen = jnp.where(member == s, other, chosen)
        return chosen.astype(bf16)

    up_gate_w, down_w = [], []
    for index in range(PARTS):
        both = jnp.concatenate([own_part(w_gate, 1, index), own_part(w_up, 1, index)], axis=1)
        up_gate_w.append(jnp.concatenate(gather_pieces(both), axis=0))
        down_w.append(jnp.concatenate(gather_pieces(own_part(w_down, 0, index)), axis=1))

    own_tokens = to_relative(mine_first(tokens), my_fsdp, n_fsdp)
    own_grad = to_relative(mine_first(cotangent), my_fsdp, n_fsdp)

    def gather_rows(mine):
        held = jnp.concatenate([mine, swap(mine, "context", 1)], axis=0)
        team = jnp.concatenate([held, swap(held, "tensor", 1)], axis=0)
        others = []
        for bit in bits_of(n_ctx)[1:]:
            arrived = swap(held, "context", bit)
            others.append(arrived)
            held = jnp.concatenate([held, arrived], axis=0)
        remote = jnp.concatenate(others, axis=0)
        return team, jnp.concatenate([remote, swap(remote, "tensor", 1)], axis=0)

    grad_team, grad_remote = gather_rows(own_grad[:half])

    seq_lengths = lengths[0]
    seq_ends = jnp.cumsum(seq_lengths)
    seq_starts = seq_ends - seq_lengths
    row = jnp.arange(rows, dtype=jnp.int32)
    stored = jnp.where(flipped, (row + half) % rows, row)

    def packed_of(context):
        owner = lax.dynamic_index_in_dim(span_order[0], context, 0, keepdims=False)
        span = stored // piece_rows
        hot = span[:, None] == jnp.arange(n_ctx, dtype=jnp.int32)[None, :]
        place = jnp.sum(jnp.where(hot, owner[None, :], 0), axis=1)
        return context * rows + place * piece_rows + stored % piece_rows

    own_at = packed_of(my_ctx)
    passed = own_at[:, None] >= seq_ends[None, :]
    begin = jnp.max(jnp.where(passed, seq_ends[None, :], 0), axis=1)
    position = own_at - begin
    longest = 3 * n_ctx * rows // 8
    behind = min(n_ctx - 1, (longest - 1 + rows - 1) // rows)
    key_at = [own_at]
    for step in range(1, behind + 1):
        there = packed_of(jnp.maximum(my_ctx - step, 0))
        key_at.append(jnp.where(my_ctx >= step, there, far_away))
    key_at = jnp.concatenate(key_at)[None, :]
    low, high = begin[:, None], own_at[:, None]

    half_dim = HD // 2
    frequency = rope_base ** (-(jnp.arange(half_dim, dtype=f32) * 2.0) / HD)
    angles = position.astype(f32)[:, None] * frequency[None, :]
    cosine, sine = jnp.cos(angles), jnp.sin(angles)
    cos_table = jnp.concatenate([cosine, cosine], axis=1)
    sin_table = jnp.concatenate([-sine, sine], axis=1)

    def rotate(values):
        count = values.shape[1] // HD
        shaped = values.reshape(rows, count, HD)
        turned = jnp.concatenate([shaped[..., half_dim:], shaped[..., :half_dim]], axis=-1)
        return (shaped * cos_table[:, None, :] + turned * sin_table[:, None, :]).reshape(
            values.shape
        )

    inputs = own_tokens.astype(f32)
    scale_one = rms_scale(inputs)
    normed = (inputs * scale_one * gain_one).astype(bf16)
    qkv = dot_plain(normed, qkv_w) + bias
    rotated = rotate(qkv[:, : q_width + kv_width]).astype(bf16)
    queries = rotated[:, :q_width]
    kv_own = jnp.concatenate([rotated[:, q_width:], qkv[:, q_width + kv_width :].astype(bf16)], axis=1)
    kv_all = jnp.concatenate(
        [kv_own] + [shift(kv_own, "context", step) for step in range(1, behind + 1)], axis=0
    )
    attended = attend(queries, kv_all, low, high, key_at)
    branch = dot_plain(attended, out_w)
    middle = (
        inputs[:half]
        + branch[:half]
        + swap(branch[half:].astype(bf16), "tensor", 1).astype(f32)
    )
    middle_scale = rms_scale(middle)
    normed_two = (middle * middle_scale * gain_two).astype(bf16)
    team_rows, remote_rows = gather_rows(normed_two)

    def feed(index, rows_in, grads_in):
        both = dot_plain(rows_in, up_gate_w[index])
        d_hidden = dot_cols(grads_in, down_w[index])
        shown = None
        overlap = max(fresh)
        if index == 0 and overlap:
            column = jnp.arange(part, dtype=jnp.int32)[None, :]
            limit = jnp.int32(0)
            for s in range(TEAM):
                limit = jnp.where(member == s, fresh[s], limit)
            shown = column >= limit
        hidden, d_gate, d_up = swiglu_grads(both[:, :part], both[:, part:], d_hidden, shown)
        return hidden, jnp.concatenate([d_gate, d_up], axis=1)

    team_out, remote_out = [], []
    d_rows, out_rows = 0.0, 0.0
    for index in range(PARTS):
        hidden, d_both = feed(index, team_rows, grad_team)
        team_out.append((hidden, d_both))
        d_rows = d_rows + dot_cols(d_both, up_gate_w[index])
        out_rows = out_rows + dot_plain(hidden, down_w[index])
    for index in range(PARTS):
        remote_out.append(feed(index, remote_rows, grad_remote))

    def give_back(partial):
        mid_rows = partial.shape[0] // 2
        mine = partial[:mid_rows] + swap(partial[mid_rows:].astype(bf16), "tensor", 1).astype(f32)
        return mine[:half] + swap(mine[half:].astype(bf16), "context", 1).astype(f32)

    d_normed_two = give_back(d_rows)
    branch_out = give_back(out_rows)

    all_rows = jnp.concatenate([team_rows, remote_rows], axis=0)
    all_grads = jnp.concatenate([grad_team, grad_remote], axis=0)
    both_parts, down_parts = [], []
    for index in range(PARTS):
        hidden = jnp.concatenate([team_out[index][0], remote_out[index][0]], axis=0)
        d_both = jnp.concatenate([team_out[index][1], remote_out[index][1]], axis=0)
        grad_both = dot_rows(all_rows, d_both).astype(bf16)
        grad_down = dot_rows(hidden, all_grads).astype(bf16)
        both_own = reduce_fsdp(grad_both, 0).astype(bf16)
        down_own = reduce_fsdp(grad_down, 1).astype(bf16)
        both_parts.append((both_own, swap(both_own, "context", 1)))
        down_parts.append((down_own, swap(down_own, "context", 1)))

    def assemble(parts, axis):
        own = jnp.concatenate([p[0] for p in parts], axis=axis)
        other = jnp.concatenate([p[1] for p in parts], axis=axis)
        pieces = []
        for s in range(TEAM):
            full = jnp.where(member == s, own, other)
            pieces.append(lax.slice_in_dim(full, fresh[s], full.shape[axis], axis=axis))
        return jnp.concatenate(pieces, axis=axis).astype(f32)

    grad_gate = assemble([(a[:, :part], b[:, :part]) for a, b in both_parts], 1)
    grad_up = assemble([(a[:, part:], b[:, part:]) for a, b in both_parts], 1)
    grad_down = assemble(down_parts, 0)

    grad_gain_two = jnp.sum(d_normed_two * middle * middle_scale, axis=0)
    weighted_two = d_normed_two * gain_two
    d_middle = (
        own_grad[:half].astype(f32)
        + middle_scale * weighted_two
        - middle * middle_scale**3 * jnp.mean(weighted_two * middle, axis=-1, keepdims=True)
    )
    d_branch_half = d_middle.astype(bf16)
    d_branch = jnp.concatenate([d_branch_half, swap(d_branch_half, "tensor", 1)], axis=0)
    d_attended = dot_cols(d_branch, out_w).astype(bf16)
    dq_low, dkv_all = attend_back(
        queries, d_attended, kv_all, low, high, key_at, cos_table, sin_table
    )
    dkv = dkv_all[:rows]
    for step in range(1, behind + 1):
        sent = dkv_all[step * rows : (step + 1) * rows].astype(bf16)
        dkv = dkv + shift(sent, "context", -step).astype(f32)
    dk = dkv[:, :HD]
    dk_turned = jnp.concatenate([dk[:, half_dim:], dk[:, :half_dim]], axis=1)
    dk = dk * cos_table - dk_turned * sin_table
    d_qkv = jnp.concatenate([dq_low, dk.astype(bf16), dkv[:, HD:].astype(bf16)], axis=1)
    d_normed_part = dot_cols(d_qkv, qkv_w)
    d_normed = d_normed_part[:half] + swap(
        d_normed_part[half:].astype(bf16), "tensor", 1
    ).astype(f32)
    grad_gain_one = jnp.sum(d_normed * inputs[:half] * scale_one[:half], axis=0)
    weighted_one = d_normed * gain_one
    d_inputs = (
        d_middle
        + scale_one[:half] * weighted_one
        - inputs[:half]
        * scale_one[:half] ** 3
        * jnp.mean(weighted_one * inputs[:half], axis=-1, keepdims=True)
    )

    grad_o = sum_context(reduce_fsdp(dot_rows(attended, d_branch).astype(bf16), 1))
    grad_qkv = sum_context(reduce_fsdp(dot_rows(normed, d_qkv).astype(bf16), 0))

    gains = jnp.stack([grad_gain_one, grad_gain_two])
    gains = gains + swap(gains, "tensor", 1)
    grad_bias = jnp.sum(d_qkv.astype(f32), axis=0).reshape(all_heads, n_fsdp, bias_cols)
    bias_rel = xor_blocks([grad_bias[:, i] for i in range(n_fsdp)], my_fsdp, n_fsdp)
    small = jnp.stack(
        [
            jnp.concatenate(
                [gains[:, place * shard : (place + 1) * shard].reshape(-1), bias_rel[i].reshape(-1)]
            )
            for place, i in enumerate(order)
        ]
    )
    for bit in bits_of(n_fsdp):
        kept = small.shape[0] // 2
        small = small[:kept] + swap(small[kept:], "fsdp", bit)
    for bit in bits_of(n_ctx):
        small = small + swap(small, "context", bit)
    small = small[0]
    grad_biases = small[2 * shard :].reshape(all_heads, bias_cols)

    def restore(mine):
        low_half = mine.astype(bf16)
        both = mine_first(jnp.concatenate([low_half, swap(low_half, "tensor", 1)], axis=0))
        return from_relative(both, my_fsdp, n_fsdp).astype(f32)

    return (
        restore(middle + branch_out),
        restore(d_inputs),
        small[:shard],
        grad_qkv[:, :q_width],
        grad_biases[:heads_local],
        grad_qkv[:, q_width : q_width + kv_width],
        grad_biases[heads_local : heads_local + 1],
        grad_qkv[:, q_width + kv_width :],
        grad_biases[heads_local + 1 :],
        grad_o,
        small[shard : 2 * shard],
        grad_gate,
        grad_up,
        grad_down,
    )


def solution(mesh):
    in_specs = (
        P(("fsdp", "context"), None),
        P(("fsdp", "context"), None),
        P("fsdp", None),
        P("fsdp", None, None),
        P("fsdp"),
        P("fsdp", "tensor"),
        P("tensor", "fsdp"),
        P("fsdp", "tensor"),
        P("tensor", "fsdp"),
        P("fsdp", "tensor"),
        P("tensor", "fsdp"),
        P("tensor", "fsdp"),
        P("fsdp"),
        P("fsdp", "tensor"),
        P("fsdp", "tensor"),
        P("tensor", "fsdp"),
    )
    out_specs = (
        P(("fsdp", "context"), None),
        P(("fsdp", "context"), None),
        P("fsdp"),
        P("fsdp", "tensor"),
        P("tensor", "fsdp"),
        P("fsdp", "tensor"),
        P("tensor", "fsdp"),
        P("fsdp", "tensor"),
        P("tensor", "fsdp"),
        P("tensor", "fsdp"),
        P("fsdp"),
        P("fsdp", "tensor"),
        P("fsdp", "tensor"),
        P("tensor", "fsdp"),
    )
    return jax.shard_map(
        per_device, mesh=mesh, in_specs=in_specs, out_specs=out_specs, check_vma=False
    )
```

time: 1960 us -> 669 us (0.34)
  waiting for transfers between devices: 1460 us -> 290 us
  blocking collectives: 198 us -> 0 us
  starting transfers between devices: 12.3 us -> 58.4 us
    reduce_scatter x8 -> x0, waiting for transfers between devices: 882 us -> none  [the longest x1 264 us: per_device(): lax.psum_scatter(dot_rows(hidden, own_grad), ('fsdp', 'context'), scatter...]
    all_gather x8 -> x0, waiting for transfers between devices: 416 us -> none  [the longest x1 88.9 us: per_device(): lax.all_gather(w_gate.astype(jnp.bfloat16), 'fsdp', axis=0, tiled=True)]
    ppermute x0 -> x68, waiting for transfers between devices: none -> 290 us  [the longest x64 283 us: swap(): return lax.ppermute(values, axis_name, [(i, i ^ bit) for i in range(size)])]
    psum x3 -> x0, waiting for transfers between devices: 167 us -> none  [the longest x2 115 us: head_total(): return lax.psum(values, 'tensor')]
    all_gather x11 -> x0, blocking collectives: 123 us -> none  [the longest x1 18.9 us: per_device(): lax.all_gather(attn_grads[8].astype(jnp.bfloat16), 'context', axis=1, til...]
    unnamed x3 -> x0, blocking collectives: 75.5 us -> none
    ppermute x0 -> x68, starting transfers between devices: none -> 58.4 us  [the longest x64 48.4 us: swap(): return lax.ppermute(values, axis_name, [(i, i ^ bit) for i in range(size)])]
    slice x4 -> x46, local copies, waits for them, and re-layouts: 4.39 us -> 30 us  [the longest x12 13.9 us: reduce_fsdp(): sent = lax.slice_in_dim(values, half, 2 * half, axis=axis).astype(bf16)]
  transfers between devices with their start and end apart: 21 -> 68, of which waited for: 15 -> 33; matrix products, arithmetic and copies ran while one was open for 9% -> 38% of each run, Pallas kernels for 0% -> 2%
where the time goes in v1:
time: 669 us; the launch traced here: 659 us
  waiting for transfers between devices  290 us (43%)
  matrix products  155 us (23%)
  other arithmetic  87.2 us (13%)
  starting transfers between devices  58.4 us (9%)
  local copies, waits for them, and re-layouts  53.2 us (8%)
  Pallas kernels  12.2 us (2%)
    ppermute x64, waiting for transfers between devices, swap(): return lax.ppermute(values, axis_name, [(i, i ^ bit) for i in range(size)])  283 us
    dot_general x8, matrix products, dot_plain(): return jnp.dot(left_op, right_op, preferred_element_type=f32)  60.6 us
    dot_general x8, matrix products, dot_cols(): lax.dot_general(left_op, right_op, (((1,), (1,)), ((), ())), preferred_el...  58.8 us
    ppermute x64, starting transfers between devices, swap(): return lax.ppermute(values, axis_name, [(i, i ^ bit) for i in range(size)])  48.4 us
    dot_general x6, matrix products, dot_rows(): lax.dot_general(left_op, right_op, (((0,), (0,)), ((), ())), preferred_el...  35.9 us
    add x8, other arithmetic, reduce_fsdp(): values = kept.astype(f32) + swap(sent, 'fsdp', bit).astype(f32)  15.9 us
    slice x12, local copies, waits for them, and re-layouts, reduce_fsdp(): sent = lax.slice_in_dim(values, half, 2 * half, axis=axis).astype(bf16)  13.9 us
  transfers between devices with their start and end apart: 68, of which 33 were waited for; matrix products, arithmetic and copies ran while one was open for 38% of the time, Pallas kernels for 2%

profile of v1, /device:TPU:0, one launch (start us, length us, event | category | flops | bytes accessed | tf_op | source)
XLA Modules:
  0.0 659.5 jit_solution(3510138531066468153)
XLA Ops:
  12.9 4.6 select_convert_fusion.9
  23.5 5.8 select_convert_fusion.10
  32.3 5.4 collective-permute-done
  49.7 6.4 pad_maximum_fusion.4
  65.0 4.5 collective-permute-start.4
  77.1 4.8 shard_map.263
  81.9 5.2 collective-permute-start.54
  92.7 3.5 collective-permute-done.14
  97.7 23.3 %collective-permute-done.54 = bf16[256,1536]{1,0:T(8,128)(2,1)} collective-permute-done((bf16[256,1536]{1,0:T(8,128)(2,1)S(1)}, bf16[256,1536]{1,0:T(8,128)(2,1)}, u32[]{:S(2)}, u32[]{:S(2)}) %collective-permute-start.54) | collective-permute-done | bytes 786464 | tf_op jit(solution)/shard_map/ppermute | solution.py:42
  125.8 10.0 %collective-permute-done.9 = bf16[128,1536]{1,0:T(8,128)(2,1)S(1)} collective-permute-done((bf16[128,1536]{1,0:T(8,128)(2,1)S(1)}, bf16[128,1536]{1,0:T(8,128)(2,1)S(1)}, u32[]{:S(2)}, u32[]{:S(2)}) %collective-permute-start.9) | collective-permute-done | bytes 393248 | tf_op jit(solution)/shard_map/ppermute | solution.py:42
  141.6 5.6 fusion.52
  147.1 10.9 %collective-permute-done.10 = bf16[256,1536]{1,0:T(8,128)(2,1)S(1)} collective-permute-done((bf16[256,1536]{1,0:T(8,128)(2,1)S(1)}, bf16[256,1536]{1,0:T(8,128)(2,1)S(1)}, u32[]{:S(2)}, u32[]{:S(2)}) %collective-permute-start.10) | collective-permute-done | bytes 786464 | tf_op jit(solution)/shard_map/ppermute | solution.py:42
  158.8 17.6 %collective-permute-done.52 = bf16[256,1536]{1,0:T(8,128)(2,1)S(1)} collective-permute-done((bf16[256,1536]{1,0:T(8,128)(2,1)S(1)}, bf16[256,1536]{1,0:T(8,128)(2,1)S(1)}, u32[]{:S(2)}, u32[]{:S(2)}) %collective-permute-start.52) | collective-permute-done | bytes 786464 | tf_op jit(solution)/shard_map/ppermute | solution.py:42
  176.6 19.4 %collective-permute-done.20 = bf16[1152,384]{1,0:T(8,128)(2,1)S(1)} collective-permute-done((bf16[1152,384]{1,0:T(8,128)(2,1)S(1)}, bf16[1152,384]{1,0:T(8,128)(2,1)S(1)}, u32[]{:S(2)}, u32[]{:S(2)}) %collective-permute-start.20) | collective-permute-done | bytes 884768 | tf_op jit(solution)/shard_map/ppermute | solution.py:42
  198.5 12.0 %fusion.53 = f32[512,2304]{1,0:T(8,128)} fusion(bf16[256,1536]{1,0:T(8,128)(2,1)S(1)} %collective-permute-done.10, bf16[128,1536]{1,0:T(8,128)(2,1)S(1)} %collective-permute-done.9, bf16[128,1536]{1,0:T(8,128)(2,1)S(1)} %get-tuple-element.46, bf16[384,2304]{1,0:T(8,128)(2,1)} %copy-done.93, bf16[384,2304]{1,0:T(8,128)(2,1)S(1)} %collective-permute-done.18, ...), kind=kOutput, calls=%fused_computation.190 | convolution fusion | flops 3663986688 | bytes 13369344 | tf_op jit(solution)/shard_map/dot_general | solution.py:25
  210.6 7.5 %multiply_convert_fusion.4 = (bf16[512,1152]{1,0:T(8,128)(2,1)S(1)}, bf16[512,1152]{1,0:T(8,128)(2,1)}, bf16[512,1152]{1,0:T(8,128)(2,1)}) fusion(f32[512,2304]{1,0:T(8,128)} %fusion.53, bf16[1152,384]{1,0:T(8,128)(2,1)S(1)} %collective-permute-done.22, bf16[1152,384]{1,0:T(8,128)(2,1)S(1)} %collective-permute-done.21, ...), kind=kOutput, calls=%fused_computation.67 | convolution fusion | flops 1839661056 | bytes 13369344 | tf_op jit(solution)/shard_map/dot_general | solution.py:35
  219.1 12.9 %fusion.19 = f32[512,1536]{1,0:T(8,128)} fusion(bf16[512,1152]{1,0:T(8,128)(2,1)} %get-tuple-element.80, bf16[512,1152]{1,0:T(8,128)(2,1)S(1)} %get-tuple-element.79, bf16[384,2304]{1,0:T(8,128)(2,1)} %copy-done.93, bf16[384,2304]{1,0:T(8,128)(2,1)} %copy-done.91, bf16[384,2304]{1,0:T(8,128)(2,1)} %collective-permute-done.17, ...), kind=kOutput, calls=%fused_computation.45 | convolution fusion | flops 3663986688 | bytes 12582912 | tf_op jit(solution)/shard_map/dot_general | solution.py:35
  232.0 12.2 %fusion.54 = f32[512,2304]{1,0:T(8,128)} fusion(bf16[256,1536]{1,0:T(8,128)(2,1)S(1)} %collective-permute-done.10, bf16[128,1536]{1,0:T(8,128)(2,1)S(1)} %collective-permute-done.9, bf16[128,1536]{1,0:T(8,128)(2,1)S(1)} %get-tuple-element.46, bf16[384,2304]{1,0:T(8,128)(2,1)} %collective-permute-done.13, bf16[384,2304]{1,0:T(8,128)(2,1)} %collective-permute-done.12, ...), kind=kOutput, calls=%fused_computation.191 | convolution fusion | flops 3663986688 | bytes 13369344 | tf_op jit(solution)/shard_map/dot_general | solution.py:25
  248.2 11.9 %fusion.112 = f32[512,2304]{1,0:T(8,128)} fusion(bf16[512,1536]{1,0:T(8,128)(2,1)S(1)} %get-tuple-element.105, bf16[384,2304]{1,0:T(8,128)(2,1)S(1)} %copy-done.94, bf16[384,2304]{1,0:T(8,128)(2,1)S(1)} %copy-done.92, bf16[384,2304]{1,0:T(8,128)(2,1)} %collective-permute-done.17, bf16[384,1152]{1,0:T(8,128)(2,1)S(1)} %copy-done.31, ...), kind=kOutput, calls=%fused_computation.424 | convolution fusion | flops 3659268096 | bytes 13369344 | tf_op jit(solution)/shard_map/dot_general | solution.py:25
  260.1 6.5 multiply_convert_fusion.2
  266.6 4.2 convolution_convert_fusion.2
  274.2 12.2 %fusion.111 = f32[512,2304]{1,0:T(8,128)} fusion(bf16[512,1536]{1,0:T(8,128)(2,1)S(1)} %get-tuple-element.105, bf16[384,2304]{1,0:T(8,128)(2,1)} %collective-permute-done.13, bf16[384,2304]{1,0:T(8,128)(2,1)} %collective-permute-done.12, bf16[384,2304]{1,0:T(8,128)(2,1)S(1)} %collective-permute-done.11, bf16[384,1152]{1,0:T(8,128)(2,1)S(1)} %copy-done.27, ...), kind=kOutput, calls=%fused_computation.423 | convolution fusion | flops 3659268096 | bytes 13369344 | tf_op jit(solution)/shard_map/dot_general | solution.py:25
  286.4 9.3 %select_convert_fusion.2 = (bf16[512,1152]{1,0:T(8,128)(2,1)}, bf16[512,1152]{1,0:T(8,128)(2,1)}, bf16[512,1152]{1,0:T(8,128)(2,1)S(1)}, bf16[512,1152]{1,0:T(8,...) fusion(f32[512,2304]{1,0:T(8,128)} %fusion.111, pred[1152]{0:T(1024)(128)(4,1)S(1)} %iota_compare_fusion.1, ...), kind=kOutput, calls=%fused_computation.62 | convolution fusion | flops 1847328768 | bytes 23987328 | tf_op jit(solution)/shard_map/dot_general | solution.py:35
  295.7 4.2 convolution_convert_fusion.3
  299.9 5.8 convolution_add_fusion.1
  305.8 11.6 %convolution_add_fusion = f32[512,1536]{1,0:T(8,128)S(1)} fusion(f32[512,1536]{1,0:T(8,128)} %fusion.19, bf16[512,1152]{1,0:T(8,128)(2,1)S(1)} %copy-done.106, bf16[512,1152]{1,0:T(8,128)(2,1)} %get-tuple-element.152, bf16[384,2304]{1,0:T(8,128)(2,1)} %collective-permute-done.13, bf16[384,2304]{1,0:T(8,128)(2,1)} %collective-permute-done.12, ...), kind=kOutput, calls=%fused_computation.37 | convolution fusion | flops 3664773120 | bytes 15728640 | tf_op jit(solution)/shard_map/dot_general | solution.py:35
  321.0 10.5 %convolution_convert_fusion = bf16[1536,2304]{1,0:T(8,128)(2,1)S(1)} fusion(bf16[1024,1536]{1,0:T(8,128)(2,1)} %get-tuple-element.106, bf16[512,1152]{1,0:T(8,128)(2,1)} %get-tuple-element.78, bf16[512,1152]{1,0:T(8,128)(2,1)} %get-tuple-element.77, bf16[512,1152]{1,0:T(8,128)(2,1)} %get-tuple-element.80, bf16[512,1152]{1,0:T(8,128)(2,1)S(1)} %copy-done.108), kind=kOutput, calls=%fused_computation | convolution fusion | flops 7270170624 | bytes 14942208 | tf_op jit(solution)/shard_map/dot_general | solution.py:29
  331.5 6.5 collective-permute-done.28
  338.6 15.4 %collective-permute-done.23 = bf16[256,1536]{1,0:T(8,128)(2,1)S(1)} collective-permute-done((bf16[256,1536]{1,0:T(8,128)(2,1)S(1)}, bf16[256,1536]{1,0:T(8,128)(2,1)S(1)}, u32[]{:S(2)}, u32[]{:S(2)}) %collective-permute-start.23) | collective-permute-done | bytes 786464 | tf_op jit(solution)/shard_map/ppermute | solution.py:42
  355.0 9.7 %collective-permute-done.24 = bf16[128,1536]{1,0:T(8,128)(2,1)S(1)} collective-permute-done((bf16[128,1536]{1,0:T(8,128)(2,1)S(1)}, bf16[128,1536]{1,0:T(8,128)(2,1)S(1)}, u32[]{:S(2)}, u32[]{:S(2)}) %collective-permute-start.24) | collective-permute-done | bytes 393248 | tf_op jit(solution)/shard_map/ppermute | solution.py:42
  368.7 15.1 %convolution_convert_fusion.1 = bf16[1536,2304]{1,0:T(8,128)(2,1)S(1)} fusion(bf16[1024,1536]{1,0:T(8,128)(2,1)S(1)} %copy-done.79, bf16[512,1152]{1,0:T(8,128)(2,1)S(1)} %copy-done.105, bf16[512,1152]{1,0:T(8,128)(2,1)S(1)} %copy-done.104, bf16[512,1152]{1,0:T(8,128)(2,1)} %get-tuple-element.151, bf16[512,1152]{1,0:T(8,128)(2,1)} %get-tuple-element.152), kind=kOutput, calls=%fused_computation.1 | convolution fusion | flops 7270170624 | bytes 14942208 | tf_op jit(solution)/shard_map/dot_general | solution.py:29
  392.9 7.4 %shard_map.264 = (bf16[256,768]{1,0:T(8,128)(2,1)S(1)}, f32[768,256]{1,0:T(8,128)S(1)}) custom-call(bf16[256,768]{1,0:T(8,128)(2,1)S(1)} %copy-done.3, bf16[256,768]{1,0:T(8,128)(2,1)S(1)} %convolution_convert_fusion.6.g_ref, bf16[768,256]{1,0:T(8,128)(2,1)S(1)} %copy-done.5, s32[256,1]{1,0:T(8,128)S(1)} %copy-done.7, s32[256,1]{1,0:T(8,128)S(1)} %copy-done.9, ...), custom_call_target="tpu_custom_call" | custom-call | flops 1509949440 | bytes 2359296 | tf_op jit(solution)/shard_map/pallas_call | solution.py:203
  409.6 3.7 collective-permute-done.32
  424.4 4.2 collective-permute-done.33
  445.9 3.6 collective-permute-done.38
  450.6 3.4 collective-permute-done.39
  457.4 5.4 collective-permute-done.34
  467.1 15.7 %collective-permute-done.65 = bf16[1152,384]{1,0:T(8,128)(2,1)S(1)} collective-permute-done((bf16[1152,384]{1,0:T(8,128)(2,1)}, bf16[1152,384]{1,0:T(8,128)(2,1)S(1)}, u32[]{:S(2)}, u32[]{:S(2)}) %collective-permute-start.65) | collective-permute-done | bytes 884768 | tf_op jit(solution)/shard_map/ppermute | solution.py:42
  486.7 15.9 %collective-permute-done.63 = bf16[1152,384]{1,0:T(8,128)(2,1)S(1)} collective-permute-done((bf16[1152,384]{1,0:T(8,128)(2,1)S(1)}, bf16[1152,384]{1,0:T(8,128)(2,1)S(1)}, u32[]{:S(2)}, u32[]{:S(2)}) %collective-permute-start.63) | collective-permute-done | bytes 884768 | tf_op jit(solution)/shard_map/ppermute | solution.py:42
  508.1 7.8 %collective-permute-done.47 = bf16[768,384]{1,0:T(8,128)(2,1)S(1)} collective-permute-done((bf16[768,384]{1,0:T(8,128)(2,1)S(1)}, bf16[768,384]{1,0:T(8,128)(2,1)S(1)}, u32[]{:S(2)}, u32[]{:S(2)}) %collective-permute-start.47) | collective-permute-done | bytes 589856 | tf_op jit(solution)/shard_map/ppermute | solution.py:42
  530.4 6.3 collective-permute-done.41
  539.4 14.5 %collective-permute-done.42 = bf16[192,1024]{1,0:T(8,128)(2,1)S(1)} collective-permute-done((bf16[192,1024]{1,0:T(8,128)(2,1)S(1)}, bf16[192,1024]{1,0:T(8,128)(2,1)S(1)}, u32[]{:S(2)}, u32[]{:S(2)}) %collective-permute-start.42) | collective-permute-done | bytes 393248 | tf_op jit(solution)/shard_map/ppermute | solution.py:42
  557.3 6.3 collective-permute-done.43
  566.3 5.7 collective-permute-done.44
  578.2 7.2 %collective-permute-done.45 = bf16[192,1024]{1,0:T(8,128)(2,1)S(1)} collective-permute-done((bf16[192,1024]{1,0:T(8,128)(2,1)S(1)}, bf16[192,1024]{1,0:T(8,128)(2,1)S(1)}, u32[]{:S(2)}, u32[]{:S(2)}) %collective-permute-start.45) | collective-permute-done | bytes 393248 | tf_op jit(solution)/shard_map/ppermute | solution.py:42
  589.7 15.7 %collective-permute-done.57 = bf16[384,2304]{1,0:T(8,128)(2,1)S(1)} collective-permute-done((bf16[384,2304]{1,0:T(8,128)(2,1)S(1)}, bf16[384,2304]{1,0:T(8,128)(2,1)S(1)}, u32[]{:S(2)}, u32[]{:S(2)}) %collective-permute-start.57) | collective-permute-done | bytes 1769504 | tf_op jit(solution)/shard_map/ppermute | solution.py:42
  607.4 16.2 %collective-permute-done.61 = bf16[384,2304]{1,0:T(8,128)(2,1)S(1)} collective-permute-done((bf16[384,2304]{1,0:T(8,128)(2,1)S(1)}, bf16[384,2304]{1,0:T(8,128)(2,1)S(1)}, u32[]{:S(2)}, u32[]{:S(2)}) %collective-permute-start.61) | collective-permute-done | bytes 1769504 | tf_op jit(solution)/shard_map/ppermute | solution.py:42
  623.8 26.7 %collective-permute-done.60 = bf16[384,2304]{1,0:T(8,128)(2,1)S(1)} collective-permute-done((bf16[384,2304]{1,0:T(8,128)(2,1)S(1)}, bf16[384,2304]{1,0:T(8,128)(2,1)S(1)}, u32[]{:S(2)}, u32[]{:S(2)}) %collective-permute-start.60) | collective-permute-done | bytes 1769504 | tf_op jit(solution)/shard_map/ppermute | solution.py:42
  (546 shorter events, 195.8 us)
Async XLA Ops:
  2.9 79.0 %collective-permute-start.6 = (bf16[768,384]{1,0:T(8,128)(2,1)}, bf16[768,384]{1,0:T(8,128)(2,1)}, u32[]{:S(2)}, u32[]{:S(2)}) collective-permute-start(bf16[768,384]{1,0:T(8,128)(2,1)} %convert_element_type.332), channel_id=1, source_target_pairs={{0,8},{8,0},{16,24},{24,16},{1,9},{9,1},{17,25},{25,17},{2,10},{10... | collective-permute-start | bytes 1769480 | tf_op jit(solution)/shard_map/ppermute | solution.py:42
  3.4 37.5 %collective-permute-start.5 = (bf16[768,384]{1,0:T(8,128)(2,1)}, bf16[768,384]{1,0:T(8,128)(2,1)}, u32[]{:S(2)}, u32[]{:S(2)}) collective-permute-start(bf16[768,384]{1,0:T(8,128)(2,1)} %convert_element_type.332), channel_id=1, source_target_pairs={{0,16},{8,24},{16,0},{24,8},{1,17},{9,25},{17,1},{25,9},{2,18},{10... | collective-permute-start | bytes 1769480 | tf_op jit(solution)/shard_map/ppermute | solution.py:42
  12.4 30.4 %collective-permute-start.1 = (bf16[400,1024]{1,0:T(8,128)(2,1)}, bf16[400,1024]{1,0:T(8,128)(2,1)}, u32[]{:S(2)}, u32[]{:S(2)}) collective-permute-start(bf16[400,1024]{1,0:T(8,128)(2,1)} %fusion.47), channel_id=1, source_target_pairs={{0,8},{8,0},{16,24},{24,16},{1,9},{9,1},{17,25},{25,17},{2,10},{10... | collective-permute-start | bytes 2457608 | tf_op jit(solution)/shard_map/ppermute | solution.py:42
  12.6 25.1 %collective-permute-start = (bf16[400,1024]{1,0:T(8,128)(2,1)}, bf16[400,1024]{1,0:T(8,128)(2,1)}, u32[]{:S(2)}, u32[]{:S(2)}) collective-permute-start(bf16[400,1024]{1,0:T(8,128)(2,1)} %fusion.47), channel_id=1, source_target_pairs={{0,16},{8,24},{16,0},{24,8},{1,17},{9,25},{17,1},{25,9},{2,18},{10... | collective-permute-start | bytes 2457608 | tf_op jit(solution)/shard_map/ppermute | solution.py:42
  17.6 118.3 %collective-permute-start.15 = (bf16[1152,384]{1,0:T(8,128)(2,1)}, bf16[1152,384]{1,0:T(8,128)(2,1)}, u32[]{:S(2)}, u32[]{:S(2)}) collective-permute-start(bf16[1152,384]{1,0:T(8,128)(2,1)} %get-tuple-element.81), channel_id=1, source_target_pairs={{0,8},{8,0},{16,24},{24,16},{1,9},{9,1},{17,25},{25,17},{2,10},{10... | collective-permute-start | bytes 2654216 | tf_op jit(solution)/shard_map/ppermute | solution.py:42
  40.9 28.6 %collective-permute-start.26 = (bf16[128,1536]{1,0:T(8,128)(2,1)}, bf16[128,1536]{1,0:T(8,128)(2,1)}, u32[]{:S(2)}, u32[]{:S(2)}) collective-permute-start(bf16[128,1536]{1,0:T(8,128)(2,1)} %get-tuple-element.44), channel_id=1, source_target_pairs={{0,2},{2,0},{4,6},{6,4},{1,3},{3,1},{5,7},{7,5},{8,10},{10,8},{12,... | collective-permute-start | bytes 1179656 | tf_op jit(solution)/shard_map/ppermute | solution.py:42
  42.8 44.4 %collective-permute-start.7 = (bf16[768,384]{1,0:T(8,128)(2,1)}, bf16[768,384]{1,0:T(8,128)(2,1)}, u32[]{:S(2)}, u32[]{:S(2)}) collective-permute-start(bf16[768,384]{1,0:T(8,128)(2,1)} %collective-permute-done.5), channel_id=1, source_target_pairs={{0,8},{8,0},{16,24},{24,16},{1,9},{9,1},{17,25},{25,17},{2,10},{10... | collective-permute-start | bytes 1769480 | tf_op jit(solution)/shard_map/ppermute | solution.py:42
  73.3 22.9 %collective-permute-start.14 = (bf16[1152,384]{1,0:T(8,128)(2,1)}, bf16[1152,384]{1,0:T(8,128)(2,1)}, u32[]{:S(2)}, u32[]{:S(2)}) collective-permute-start(bf16[1152,384]{1,0:T(8,128)(2,1)} %get-tuple-element.81), channel_id=1, source_target_pairs={{0,16},{8,24},{16,0},{24,8},{1,17},{9,25},{17,1},{25,9},{2,18},{10... | collective-permute-start | bytes 2654216 | tf_op jit(solution)/shard_map/ppermute | solution.py:42
  75.5 61.0 %collective-permute-start.17 = (bf16[384,2304]{1,0:T(8,128)(2,1)}, bf16[384,2304]{1,0:T(8,128)(2,1)}, u32[]{:S(2)}, u32[]{:S(2)}) collective-permute-start(bf16[384,2304]{1,0:T(8,128)(2,1)} %pad_maximum_fusion.12), channel_id=1, source_target_pairs={{0,16},{8,24},{16,0},{24,8},{1,17},{9,25},{17,1},{25,9},{2,18},{10... | collective-permute-start | bytes 5308424 | tf_op jit(solution)/shard_map/ppermute | solution.py:42
  81.9 39.1 %collective-permute-start.54 = (bf16[256,1536]{1,0:T(8,128)(2,1)S(1)}, bf16[256,1536]{1,0:T(8,128)(2,1)}, u32[]{:S(2)}, u32[]{:S(2)}) collective-permute-start(bf16[256,1536]{1,0:T(8,128)(2,1)S(1)} %pad_maximum_fusion.16), channel_id=1, source_target_pairs={{0,4},{2,6},{4,0},{6,2},{1,5},{3,7},{5,1},{7,3},{8,12},{10,14},{12... | collective-permute-start | bytes 2359304 | tf_op jit(solution)/shard_map/ppermute | solution.py:42
  90.3 30.7 %collective-permute-start.8 = (bf16[128,1536]{1,0:T(8,128)(2,1)}, bf16[128,1536]{1,0:T(8,128)(2,1)}, u32[]{:S(2)}, u32[]{:S(2)}) collective-permute-start(bf16[128,1536]{1,0:T(8,128)(2,1)} %slice.1143), channel_id=1, source_target_pairs={{0,1},{1,0},{2,3},{3,2},{4,5},{5,4},{6,7},{7,6},{8,9},{9,8},{10,11... | collective-permute-start | bytes 1179656 | tf_op jit(solution)/shard_map/ppermute | solution.py:42
  96.2 28.3 %collective-permute-start.27 = (bf16[256,1536]{1,0:T(8,128)(2,1)S(1)}, bf16[256,1536]{1,0:T(8,128)(2,1)S(1)}, u32[]{:S(2)}, u32[]{:S(2)}) collective-permute-start(bf16[256,1536]{1,0:T(8,128)(2,1)S(1)} %pad_maximum_fusion.16), channel_id=1, source_target_pairs={{0,1},{1,0},{2,3},{3,2},{4,5},{5,4},{6,7},{7,6},{8,9},{9,8},{10,11... | collective-permute-start | bytes 2359304 | tf_op jit(solution)/shard_map/ppermute | solution.py:42
  121.0 15.7 %collective-permute-start.16 = (bf16[1152,384]{1,0:T(8,128)(2,1)}, bf16[1152,384]{1,0:T(8,128)(2,1)S(1)}, u32[]{:S(2)}, u32[]{:S(2)}) collective-permute-start(bf16[1152,384]{1,0:T(8,128)(2,1)} %collective-permute-done.14), channel_id=1, source_target_pairs={{0,8},{8,0},{16,24},{24,16},{1,9},{9,1},{17,25},{25,17},{2,10},{10... | collective-permute-start | bytes 2654216 | tf_op jit(solution)/shard_map/ppermute | solution.py:42
  121.0 20.5 %collective-permute-start.55 = (bf16[256,1536]{1,0:T(8,128)(2,1)}, bf16[256,1536]{1,0:T(8,128)(2,1)S(1)}, u32[]{:S(2)}, u32[]{:S(2)}) collective-permute-start(bf16[256,1536]{1,0:T(8,128)(2,1)} %collective-permute-done.54), channel_id=1, source_target_pairs={{0,1},{1,0},{2,3},{3,2},{4,5},{5,4},{6,7},{7,6},{8,9},{9,8},{10,11... | collective-permute-start | bytes 2359304 | tf_op jit(solution)/shard_map/ppermute | solution.py:42
  135.8 60.1 %collective-permute-start.18 = (bf16[384,2304]{1,0:T(8,128)(2,1)}, bf16[384,2304]{1,0:T(8,128)(2,1)S(1)}, u32[]{:S(2)}, u32[]{:S(2)}) collective-permute-start(bf16[384,2304]{1,0:T(8,128)(2,1)} %pad_maximum_fusion.12), channel_id=1, source_target_pairs={{0,8},{8,0},{16,24},{24,16},{1,9},{9,1},{17,25},{25,17},{2,10},{10... | collective-permute-start | bytes 5308424 | tf_op jit(solution)/shard_map/ppermute | solution.py:42
  135.9 60.6 %collective-permute-start.11 = (bf16[384,2304]{1,0:T(8,128)(2,1)S(1)}, bf16[384,2304]{1,0:T(8,128)(2,1)S(1)}, u32[]{:S(2)}, u32[]{:S(2)}) collective-permute-start(bf16[384,2304]{1,0:T(8,128)(2,1)S(1)} %copy-done.40), channel_id=1, source_target_pairs={{0,16},{8,24},{16,0},{24,8},{1,17},{9,25},{17,1},{25,9},{2,18},{10... | collective-permute-start | bytes 5308424 | tf_op jit(solution)/shard_map/ppermute | solution.py:42
  136.5 60.1 %collective-permute-start.19 = (bf16[384,2304]{1,0:T(8,128)(2,1)}, bf16[384,2304]{1,0:T(8,128)(2,1)S(1)}, u32[]{:S(2)}, u32[]{:S(2)}) collective-permute-start(bf16[384,2304]{1,0:T(8,128)(2,1)} %collective-permute-done.17), channel_id=1, source_target_pairs={{0,8},{8,0},{16,24},{24,16},{1,9},{9,1},{17,25},{25,17},{2,10},{10... | collective-permute-start | bytes 5308424 | tf_op jit(solution)/shard_map/ppermute | solution.py:42
  136.7 21.3 %collective-permute-start.10 = (bf16[256,1536]{1,0:T(8,128)(2,1)S(1)}, bf16[256,1536]{1,0:T(8,128)(2,1)S(1)}, u32[]{:S(2)}, u32[]{:S(2)}) collective-permute-start(bf16[256,1536]{1,0:T(8,128)(2,1)S(1)} %pad_maximum_fusion.15), channel_id=1, source_target_pairs={{0,1},{1,0},{2,3},{3,2},{4,5},{5,4},{6,7},{7,6},{8,9},{9,8},{10,11... | collective-permute-start | bytes 2359304 | tf_op jit(solution)/shard_map/ppermute | solution.py:42
  141.6 34.9 %collective-permute-start.52 = (bf16[256,1536]{1,0:T(8,128)(2,1)S(1)}, bf16[256,1536]{1,0:T(8,128)(2,1)S(1)}, u32[]{:S(2)}, u32[]{:S(2)}) collective-permute-start(bf16[256,1536]{1,0:T(8,128)(2,1)S(1)} %pad_maximum_fusion.15), channel_id=1, source_target_pairs={{0,4},{2,6},{4,0},{6,2},{1,5},{3,7},{5,1},{7,3},{8,12},{10,14},{12... | collective-permute-start | bytes 2359304 | tf_op jit(solution)/shard_map/ppermute | solution.py:42
  158.0 37.9 %collective-permute-start.20 = (bf16[1152,384]{1,0:T(8,128)(2,1)S(1)}, bf16[1152,384]{1,0:T(8,128)(2,1)S(1)}, u32[]{:S(2)}, u32[]{:S(2)}) collective-permute-start(bf16[1152,384]{1,0:T(8,128)(2,1)S(1)} %copy-done.68), channel_id=1, source_target_pairs={{0,16},{8,24},{16,0},{24,8},{1,17},{9,25},{17,1},{25,9},{2,18},{10... | collective-permute-start | bytes 2654216 | tf_op jit(solution)/shard_map/ppermute | solution.py:42
  176.4 34.1 %collective-permute-start.21 = (bf16[1152,384]{1,0:T(8,128)(2,1)S(1)}, bf16[1152,384]{1,0:T(8,128)(2,1)S(1)}, u32[]{:S(2)}, u32[]{:S(2)}) collective-permute-start(bf16[1152,384]{1,0:T(8,128)(2,1)S(1)} %copy-done.68), channel_id=1, source_target_pairs={{0,8},{8,0},{16,24},{24,16},{1,9},{9,1},{17,25},{25,17},{2,10},{10... | collective-permute-start | bytes 2654216 | tf_op jit(solution)/shard_map/ppermute | solution.py:42
  196.0 36.0 %collective-permute-start.12 = (bf16[384,2304]{1,0:T(8,128)(2,1)S(1)}, bf16[384,2304]{1,0:T(8,128)(2,1)}, u32[]{:S(2)}, u32[]{:S(2)}) collective-permute-start(bf16[384,2304]{1,0:T(8,128)(2,1)S(1)} %copy-done.40), channel_id=1, source_target_pairs={{0,8},{8,0},{16,24},{24,16},{1,9},{9,1},{17,25},{25,17},{2,10},{10... | collective-permute-start | bytes 5308424 | tf_op jit(solution)/shard_map/ppermute | solution.py:42
  196.0 14.6 %collective-permute-start.22 = (bf16[1152,384]{1,0:T(8,128)(2,1)S(1)}, bf16[1152,384]{1,0:T(8,128)(2,1)S(1)}, u32[]{:S(2)}, u32[]{:S(2)}) collective-permute-start(bf16[1152,384]{1,0:T(8,128)(2,1)S(1)} %collective-permute-done.20), channel_id=1, source_target_pairs={{0,8},{8,0},{16,24},{24,16},{1,9},{9,1},{17,25},{25,17},{2,10},{10... | collective-permute-start | bytes 2654216 | tf_op jit(solution)/shard_map/ppermute | solution.py:42
  196.5 35.5 %collective-permute-start.13 = (bf16[384,2304]{1,0:T(8,128)(2,1)S(1)}, bf16[384,2304]{1,0:T(8,128)(2,1)}, u32[]{:S(2)}, u32[]{:S(2)}) collective-permute-start(bf16[384,2304]{1,0:T(8,128)(2,1)S(1)} %collective-permute-done.11), channel_id=1, source_target_pairs={{0,8},{8,0},{16,24},{24,16},{1,9},{9,1},{17,25},{25,17},{2,10},{10... | collective-permute-start | bytes 5308424 | tf_op jit(solution)/shard_map/ppermute | solution.py:42
  198.0 48.4 %collective-permute-start.53 = (bf16[256,1536]{1,0:T(8,128)(2,1)S(1)}, bf16[256,1536]{1,0:T(8,128)(2,1)S(1)}, u32[]{:S(2)}, u32[]{:S(2)}) collective-permute-start(bf16[256,1536]{1,0:T(8,128)(2,1)S(1)} %collective-permute-done.52), channel_id=1, source_target_pairs={{0,1},{1,0},{2,3},{3,2},{4,5},{5,4},{6,7},{7,6},{8,9},{9,8},{10,11... | collective-permute-start | bytes 2359304 | tf_op jit(solution)/shard_map/ppermute | solution.py:42
  273.9 155.6 %collective-permute-start.64 = (bf16[1152,768]{1,0:T(8,128)(2,1)}, bf16[1152,768]{1,0:T(8,128)(2,1)}, u32[]{:S(2)}, u32[]{:S(2)}) collective-permute-start(bf16[1152,768]{1,0:T(8,128)(2,1)} %slice.771), channel_id=1, source_target_pairs={{0,8},{8,0},{16,24},{24,16},{1,9},{9,1},{17,25},{25,17},{2,10},{10... | collective-permute-start | bytes 5308424 | tf_op jit(solution)/shard_map/ppermute | solution.py:42
  317.5 20.4 %collective-permute-start.28 = (bf16[256,1536]{1,0:T(8,128)(2,1)S(1)}, bf16[256,1536]{1,0:T(8,128)(2,1)S(1)}, u32[]{:S(2)}, u32[]{:S(2)}) collective-permute-start(bf16[256,1536]{1,0:T(8,128)(2,1)S(1)} %slice.1137), channel_id=1, source_target_pairs={{0,1},{1,0},{2,3},{3,2},{4,5},{5,4},{6,7},{7,6},{8,9},{9,8},{10,11... | collective-permute-start | bytes 2359304 | tf_op jit(solution)/shard_map/ppermute | solution.py:42
  319.1 34.9 %collective-permute-start.23 = (bf16[256,1536]{1,0:T(8,128)(2,1)S(1)}, bf16[256,1536]{1,0:T(8,128)(2,1)S(1)}, u32[]{:S(2)}, u32[]{:S(2)}) collective-permute-start(bf16[256,1536]{1,0:T(8,128)(2,1)S(1)} %slice.1138), channel_id=1, source_target_pairs={{0,1},{1,0},{2,3},{3,2},{4,5},{5,4},{6,7},{7,6},{8,9},{9,8},{10,11... | collective-permute-start | bytes 2359304 | tf_op jit(solution)/shard_map/ppermute | solution.py:42
  321.0 119.6 %collective-permute-start.62 = (bf16[1152,768]{1,0:T(8,128)(2,1)}, bf16[1152,768]{1,0:T(8,128)(2,1)}, u32[]{:S(2)}, u32[]{:S(2)}) collective-permute-start(bf16[1152,768]{1,0:T(8,128)(2,1)} %slice.767), channel_id=1, source_target_pairs={{0,8},{8,0},{16,24},{24,16},{1,9},{9,1},{17,25},{25,17},{2,10},{10... | collective-permute-start | bytes 5308424 | tf_op jit(solution)/shard_map/ppermute | solution.py:42
  338.3 16.4 %collective-permute-start.29 = (bf16[128,1536]{1,0:T(8,128)(2,1)S(1)}, bf16[128,1536]{1,0:T(8,128)(2,1)S(1)}, u32[]{:S(2)}, u32[]{:S(2)}) collective-permute-start(bf16[128,1536]{1,0:T(8,128)(2,1)S(1)} %slice.1141), channel_id=1, source_target_pairs={{0,2},{2,0},{4,6},{6,4},{1,3},{3,1},{5,7},{7,5},{8,10},{10,8},{12,... | collective-permute-start | bytes 1179656 | tf_op jit(solution)/shard_map/ppermute | solution.py:42
  367.2 23.2 %collective-permute-start.30 = (bf16[128,1536]{1,0:T(8,128)(2,1)S(1)}, bf16[128,1536]{1,0:T(8,128)(2,1)S(1)}, u32[]{:S(2)}, u32[]{:S(2)}) collective-permute-start(bf16[128,1536]{1,0:T(8,128)(2,1)S(1)} %get-tuple-element.52), channel_id=1, source_target_pairs={{0,1},{1,0},{2,3},{3,2},{4,5},{5,4},{6,7},{7,6},{8,9},{9,8},{10,11... | collective-permute-start | bytes 1179656 | tf_op jit(solution)/shard_map/ppermute | solution.py:42
  389.8 127.8 %collective-permute-start.58 = (bf16[768,2304]{1,0:T(8,128)(2,1)}, bf16[768,2304]{1,0:T(8,128)(2,1)}, u32[]{:S(2)}, u32[]{:S(2)}) collective-permute-start(bf16[768,2304]{1,0:T(8,128)(2,1)} %slice.748), channel_id=1, source_target_pairs={{0,8},{8,0},{16,24},{24,16},{1,9},{9,1},{17,25},{25,17},{2,10},{10... | collective-permute-start | bytes 10616840 | tf_op jit(solution)/shard_map/ppermute | solution.py:42
  409.6 113.0 %collective-permute-start.56 = (bf16[768,2304]{1,0:T(8,128)(2,1)}, bf16[768,2304]{1,0:T(8,128)(2,1)}, u32[]{:S(2)}, u32[]{:S(2)}) collective-permute-start(bf16[768,2304]{1,0:T(8,128)(2,1)} %slice.741), channel_id=1, source_target_pairs={{0,8},{8,0},{16,24},{24,16},{1,9},{9,1},{17,25},{25,17},{2,10},{10... | collective-permute-start | bytes 10616840 | tf_op jit(solution)/shard_map/ppermute | solution.py:42
  428.6 56.0 %collective-permute-start.46 = (bf16[768,768]{1,0:T(8,128)(2,1)}, bf16[768,768]{1,0:T(8,128)(2,1)}, u32[]{:S(2)}, u32[]{:S(2)}) collective-permute-start(bf16[768,768]{1,0:T(8,128)(2,1)} %slice.730), channel_id=1, source_target_pairs={{0,8},{8,0},{16,24},{24,16},{1,9},{9,1},{17,25},{25,17},{2,10},{10... | collective-permute-start | bytes 3538952 | tf_op jit(solution)/shard_map/ppermute | solution.py:42
  440.0 64.4 %collective-permute-start.40 = (bf16[768,1024]{1,0:T(8,128)(2,1)}, bf16[768,1024]{1,0:T(8,128)(2,1)}, u32[]{:S(2)}, u32[]{:S(2)}) collective-permute-start(bf16[768,1024]{1,0:T(8,128)(2,1)} %slice.718), channel_id=1, source_target_pairs={{0,8},{8,0},{16,24},{24,16},{1,9},{9,1},{17,25},{25,17},{2,10},{10... | collective-permute-start | bytes 4718600 | tf_op jit(solution)/shard_map/ppermute | solution.py:42
  462.8 20.0 %collective-permute-start.65 = (bf16[1152,384]{1,0:T(8,128)(2,1)}, bf16[1152,384]{1,0:T(8,128)(2,1)S(1)}, u32[]{:S(2)}, u32[]{:S(2)}) collective-permute-start(bf16[1152,384]{1,0:T(8,128)(2,1)} %slice.1134), channel_id=1, source_target_pairs={{0,16},{8,24},{16,0},{24,8},{1,17},{9,25},{17,1},{25,9},{2,18},{10... | collective-permute-start | bytes 2654216 | tf_op jit(solution)/shard_map/ppermute | solution.py:42
  482.8 19.8 %collective-permute-start.63 = (bf16[1152,384]{1,0:T(8,128)(2,1)S(1)}, bf16[1152,384]{1,0:T(8,128)(2,1)S(1)}, u32[]{:S(2)}, u32[]{:S(2)}) collective-permute-start(bf16[1152,384]{1,0:T(8,128)(2,1)S(1)} %copy-done.63), channel_id=1, source_target_pairs={{0,16},{8,24},{16,0},{24,8},{1,17},{9,25},{17,1},{25,9},{2,18},{10... | collective-permute-start | bytes 2654216 | tf_op jit(solution)/shard_map/ppermute | solution.py:42
  484.6 44.4 %collective-permute-start.67 = (bf16[1152,384]{1,0:T(8,128)(2,1)S(1)}, bf16[1152,384]{1,0:T(8,128)(2,1)S(1)}, u32[]{:S(2)}, u32[]{:S(2)}) collective-permute-start(bf16[1152,384]{1,0:T(8,128)(2,1)S(1)} %fusion.36), channel_id=1, source_target_pairs={{0,2},{2,0},{4,6},{6,4},{1,3},{3,1},{5,7},{7,5},{8,10},{10,8},{12,... | collective-permute-start | bytes 2654216 | tf_op jit(solution)/shard_map/ppermute | solution.py:42
  504.4 21.8 %collective-permute-start.66 = (bf16[1152,384]{1,0:T(8,128)(2,1)S(1)}, bf16[1152,384]{1,0:T(8,128)(2,1)}, u32[]{:S(2)}, u32[]{:S(2)}) collective-permute-start(bf16[1152,384]{1,0:T(8,128)(2,1)S(1)} %fusion.37), channel_id=1, source_target_pairs={{0,2},{2,0},{4,6},{6,4},{1,3},{3,1},{5,7},{7,5},{8,10},{10,8},{12,... | collective-permute-start | bytes 2654216 | tf_op jit(solution)/shard_map/ppermute | solution.py:42
  515.9 20.8 %collective-permute-start.41 = (bf16[384,1024]{1,0:T(8,128)(2,1)}, bf16[384,1024]{1,0:T(8,128)(2,1)}, u32[]{:S(2)}, u32[]{:S(2)}) collective-permute-start(bf16[384,1024]{1,0:T(8,128)(2,1)} %slice.1136), channel_id=1, source_target_pairs={{0,16},{8,24},{16,0},{24,8},{1,17},{9,25},{17,1},{25,9},{2,18},{10... | collective-permute-start | bytes 2359304 | tf_op jit(solution)/shard_map/ppermute | solution.py:42
  517.6 20.9 %collective-permute-start.48 = (bf16[384,384]{1,0:T(8,128)(2,1)S(1)}, bf16[384,384]{1,0:T(8,128)(2,1)S(1)}, u32[]{:S(2)}, u32[]{:S(2)}) collective-permute-start(bf16[384,384]{1,0:T(8,128)(2,1)S(1)} %select_convert_fusion.13), channel_id=1, source_target_pairs={{0,2},{2,0},{4,6},{6,4},{1,3},{3,1},{5,7},{7,5},{8,10},{10,8},{12,... | collective-permute-start | bytes 884744 | tf_op jit(solution)/shard_map/ppermute | solution.py:42
  522.5 64.4 %collective-permute-start.59 = (bf16[384,2304]{1,0:T(8,128)(2,1)}, bf16[384,2304]{1,0:T(8,128)(2,1)}, u32[]{:S(2)}, u32[]{:S(2)}) collective-permute-start(bf16[384,2304]{1,0:T(8,128)(2,1)} %slice.1132), channel_id=1, source_target_pairs={{0,16},{8,24},{16,0},{24,8},{1,17},{9,25},{17,1},{25,9},{2,18},{10... | collective-permute-start | bytes 5308424 | tf_op jit(solution)/shard_map/ppermute | solution.py:42
  526.2 79.2 %collective-permute-start.57 = (bf16[384,2304]{1,0:T(8,128)(2,1)S(1)}, bf16[384,2304]{1,0:T(8,128)(2,1)S(1)}, u32[]{:S(2)}, u32[]{:S(2)}) collective-permute-start(bf16[384,2304]{1,0:T(8,128)(2,1)S(1)} %slice.1133), channel_id=1, source_target_pairs={{0,16},{8,24},{16,0},{24,8},{1,17},{9,25},{17,1},{25,9},{2,18},{10... | collective-permute-start | bytes 5308424 | tf_op jit(solution)/shard_map/ppermute | solution.py:42
  538.2 15.8 %collective-permute-start.42 = (bf16[192,1024]{1,0:T(8,128)(2,1)S(1)}, bf16[192,1024]{1,0:T(8,128)(2,1)S(1)}, u32[]{:S(2)}, u32[]{:S(2)}) collective-permute-start(bf16[192,1024]{1,0:T(8,128)(2,1)S(1)} %select_convert_fusion.12), channel_id=1, source_target_pairs={{0,2},{2,0},{4,6},{6,4},{1,3},{3,1},{5,7},{7,5},{8,10},{10,8},{12,... | collective-permute-start | bytes 1179656 | tf_op jit(solution)/shard_map/ppermute | solution.py:42
  538.6 15.7 %collective-permute-start.49 = (bf16[192,384]{1,0:T(8,128)(2,1)S(1)}, bf16[192,384]{1,0:T(8,128)(2,1)S(1)}, u32[]{:S(2)}, u32[]{:S(2)}) collective-permute-start(bf16[192,384]{1,0:T(8,128)(2,1)S(1)} %select_convert_fusion.15), channel_id=1, source_target_pairs={{0,4},{2,6},{4,0},{6,2},{1,5},{3,7},{5,1},{7,3},{8,12},{10,14},{12... | collective-permute-start | bytes 442376 | tf_op jit(solution)/shard_map/ppermute | solution.py:42
  572.1 13.4 %collective-permute-start.45 = (bf16[192,1024]{1,0:T(8,128)(2,1)S(1)}, bf16[192,1024]{1,0:T(8,128)(2,1)S(1)}, u32[]{:S(2)}, u32[]{:S(2)}) collective-permute-start(bf16[192,1024]{1,0:T(8,128)(2,1)S(1)} %pad_maximum_fusion.31), channel_id=1, source_target_pairs={{0,2},{2,0},{4,6},{6,4},{1,3},{3,1},{5,7},{7,5},{8,10},{10,8},{12,... | collective-permute-start | bytes 1179656 | tf_op jit(solution)/shard_map/ppermute | solution.py:42
  588.8 34.8 %collective-permute-start.61 = (bf16[384,2304]{1,0:T(8,128)(2,1)S(1)}, bf16[384,2304]{1,0:T(8,128)(2,1)S(1)}, u32[]{:S(2)}, u32[]{:S(2)}) collective-permute-start(bf16[384,2304]{1,0:T(8,128)(2,1)S(1)} %fusion.14), channel_id=1, source_target_pairs={{0,2},{2,0},{4,6},{6,4},{1,3},{3,1},{5,7},{7,5},{8,10},{10,8},{12,... | collective-permute-start | bytes 5308424 | tf_op jit(solution)/shard_map/ppermute | solution.py:42
  605.7 44.7 %collective-permute-start.60 = (bf16[384,2304]{1,0:T(8,128)(2,1)S(1)}, bf16[384,2304]{1,0:T(8,128)(2,1)S(1)}, u32[]{:S(2)}, u32[]{:S(2)}) collective-permute-start(bf16[384,2304]{1,0:T(8,128)(2,1)S(1)} %fusion.15), channel_id=1, source_target_pairs={{0,2},{2,0},{4,6},{6,4},{1,3},{3,1},{5,7},{7,5},{8,10},{10,8},{12,... | collective-permute-start | bytes 5308424 | tf_op jit(solution)/shard_map/ppermute | solution.py:42
  (133 other events, 1601.4 us)

commit v2 on v1

v2 whole, which is shorter than its diff:
```python
import functools

import jax
import jax.numpy as jnp
from jax import lax
from jax.experimental import pallas as pl
from jax.experimental.pallas import tpu as pltpu
from jax.sharding import PartitionSpec as P

D = 1536
HD = 128
LANES = 128
TEAM = 2
PARTS = 3
WIDE = 256
SHARED_PARTS = 1

epsilon = 1e-06
rope_base = 10000.0
neg_big = -1e30
far_away = 1 << 29
bf16 = jnp.bfloat16
f32 = jnp.float32


def dot_plain(left_op, right_op):
    return jnp.dot(left_op, right_op, preferred_element_type=f32)


def dot_rows(left_op, right_op):
    return lax.dot_general(
        left_op, right_op, (((0,), (0,)), ((), ())), preferred_element_type=f32
    )


def dot_cols(left_op, right_op):
    return lax.dot_general(
        left_op, right_op, (((1,), (1,)), ((), ())), preferred_element_type=f32
    )


def swap(values, axis_name, bit):
    size = lax.axis_size(axis_name)
    return lax.ppermute(values, axis_name, [(i, i ^ bit) for i in range(size)])


def shift(values, axis_name, step):
    size = lax.axis_size(axis_name)
    pairs = [(i, i + step) for i in range(size) if 0 <= i + step < size]
    return lax.ppermute(values, axis_name, pairs)


def bits_of(size):
    found = []
    bit = 1
    while bit < size:
        found.append(bit)
        bit *= 2
    return found


def fsdp_order(size):
    order = [0]
    for bit in reversed(bits_of(size)):
        order = order + [held ^ bit for held in order]
    return order


def gather_pieces(piece):
    pieces = [piece]
    for bit in reversed(bits_of(lax.axis_size("fsdp"))):
        pieces = pieces + [swap(held, "fsdp", bit) for held in pieces]
    return pieces


def xor_blocks(blocks, index, size):
    for bit in bits_of(size):
        on = (index & bit) != 0
        blocks = [jnp.where(on, blocks[i ^ bit], blocks[i]) for i in range(size)]
    return blocks


def to_relative(values, index, size):
    width = values.shape[-1] // size
    blocks = [values[..., i * width : (i + 1) * width] for i in range(size)]
    blocks = xor_blocks(blocks, index, size)
    return jnp.concatenate([blocks[i] for i in fsdp_order(size)], axis=-1)


def from_relative(values, index, size):
    width = values.shape[-1] // size
    order = fsdp_order(size)
    blocks = [None] * size
    for place, i in enumerate(order):
        blocks[i] = values[..., place * width : (place + 1) * width]
    return jnp.concatenate(xor_blocks(blocks, index, size), axis=-1)


def reduce_fsdp(values, axis):
    for bit in bits_of(lax.axis_size("fsdp")):
        half = values.shape[axis] // 2
        kept = lax.slice_in_dim(values, 0, half, axis=axis)
        sent = lax.slice_in_dim(values, half, 2 * half, axis=axis).astype(bf16)
        values = kept.astype(f32) + swap(sent, "fsdp", bit).astype(f32)
    return values


def sum_context(values):
    index = lax.axis_index("context")
    bits = bits_of(lax.axis_size("context"))
    for bit in bits:
        half = values.shape[0] // 2
        on = (index & bit) != 0
        kept = jnp.where(on, values[half:], values[:half])
        sent = jnp.where(on, values[:half], values[half:]).astype(bf16)
        values = kept + swap(sent, "context", bit).astype(f32)
    values = values.astype(bf16)
    for bit in reversed(bits):
        on = (index & bit) != 0
        other = swap(values, "context", bit)
        values = jnp.concatenate(
            [jnp.where(on, other, values), jnp.where(on, values, other)], axis=0
        )
    return values.astype(f32)


def whole(array):
    return pl.BlockSpec(array.shape, lambda *ids: (0,) * array.ndim)


def wide_enough(pieces, axis):
    if pieces[0].shape[axis] % LANES:
        return [jnp.concatenate(pieces, axis=axis)]
    return pieces


def cost(us=1):
    return pl.CostEstimate(
        flops=int(us * 0.55e9), bytes_accessed=int(us * 1.8e6), transcendentals=0
    )


def joined(refs, index_ref, axis, cut=None):
    blocks = [r[...] if cut is None else r[cut] for r in refs]
    if len(blocks) > 1:
        order = fsdp_order(len(blocks))
        blocks = [blocks[order.index(i)] for i in range(len(blocks))]
        blocks = xor_blocks(blocks, index_ref[0], len(blocks))
    return jnp.concatenate(blocks, axis=axis)


def params(mib):
    return pltpu.CompilerParams(vmem_limit_bytes=mib << 20)


def pack_body(count, start_ref, *refs):
    out_ref = refs[-1]
    for i in range(count):
        at = slice(i * LANES, (i + 1) * LANES)
        out_ref[0, :, at] = refs[i][...].astype(bf16)
        out_ref[1, :, at] = refs[count + i][...].astype(bf16)
        out_ref[2, :, at] = refs[2 * count + i][...].T.astype(bf16)


def pack(w_gate, w_up, w_down, start, width):
    shard = w_gate.shape[0]
    count = width // LANES
    columns = [pl.BlockSpec((shard, LANES), lambda j, s, i=i: (0, s[0] + i)) for i in range(count)]
    lines = [pl.BlockSpec((LANES, shard), lambda j, s, i=i: (s[0] + i, 0)) for i in range(count)]
    spec = pltpu.PrefetchScalarGridSpec(
        num_scalar_prefetch=1,
        grid=(1,),
        in_specs=columns + columns + lines,
        out_specs=pl.BlockSpec((3, shard, width), lambda j, s: (0, 0, 0)),
    )
    return pl.pallas_call(
        functools.partial(pack_body, count),
        out_shape=jax.ShapeDtypeStruct((3, shard, width), bf16),
        grid_spec=spec,
        cost_estimate=cost(),
        compiler_params=params(60),
    )(start, *[w_gate] * count, *[w_up] * count, *[w_down] * count)


def vectors_body(count, heads, index_ref, *refs):
    gain_ref, bias_ref = refs[count:]
    width = D // count
    gain_ref[...] = joined(refs[:count], index_ref, 1, (slice(0, 2), slice(0, width)))
    bias_ref[...] = sum(r[8 : 8 + heads, :HD].astype(f32) for r in refs[:count])


def vectors(index, pieces, heads):
    shard = D // len(pieces)
    if shard % LANES:
        order = fsdp_order(len(pieces))
        blocks = [pieces[order.index(i)][shard : shard + 2, :shard] for i in range(len(pieces))]
        gains = jnp.concatenate(xor_blocks(blocks, index[0], len(pieces)), axis=1)
        return gains, sum(p[shard + 8 : shard + 8 + heads, :HD].astype(f32) for p in pieces)
    rows = pl.BlockSpec((16, pieces[0].shape[1]), lambda i: (shard // 16, 0))
    outs = (jax.ShapeDtypeStruct((2, D), bf16), jax.ShapeDtypeStruct((heads, HD), f32))
    return pl.pallas_call(
        functools.partial(vectors_body, len(pieces), heads),
        out_shape=outs,
        grid=(1,),
        in_specs=[pl.BlockSpec(memory_space=pltpu.SMEM)] + [rows] * len(pieces),
        out_specs=tuple(whole(a) for a in outs),
        cost_estimate=cost(),
        compiler_params=params(60),
    )(index, *pieces)


def project_body(count, q_width, index_ref, a_ref, b_ref, gain_ref, bias_ref, cos_ref, sin_ref, *refs):
    w_refs, (q_ref, kv_ref, h_ref) = refs[:count], refs[count:]
    x = jnp.concatenate([a_ref[...], b_ref[...]], axis=0).astype(f32)
    scale = lax.rsqrt(jnp.mean(x * x, axis=-1, keepdims=True) + epsilon)
    normed = (x * scale * gain_ref[0:1].astype(f32)).astype(bf16)
    h_ref[...] = normed
    total = w_refs[0].shape[1]
    depth = D // count
    for at in range(0, total, WIDE):
        weights = joined(w_refs, index_ref, 0, (slice(0, depth), slice(at, at + WIDE)))
        both = dot_plain(normed, weights)
        for inner in range(0, WIDE, HD):
            place = at + inner
            head = place // HD
            values = both[:, inner : inner + HD] + bias_ref[head : head + 1]
            if place < total - HD:
                turned = pltpu.roll(values, HD // 2, 1)
                values = values * cos_ref[...] + turned * sin_ref[...]
            if place < q_width:
                q_ref[:, place : place + HD] = values.astype(bf16)
            else:
                kv_ref[:, place - q_width : place - q_width + HD] = values.astype(bf16)


def project(index, first, second, gain, bias, cos_table, sin_table, weights, q_width):
    rows = 2 * first.shape[0]
    total = weights[0].shape[1]
    return pl.pallas_call(
        functools.partial(project_body, len(weights), q_width),
        out_shape=(
            jax.ShapeDtypeStruct((rows, q_width), bf16),
            jax.ShapeDtypeStruct((rows, total - q_width), bf16),
            jax.ShapeDtypeStruct((rows, D), bf16),
        ),
        in_specs=[pl.BlockSpec(memory_space=pltpu.SMEM)] + [pl.BlockSpec(memory_space=pltpu.VMEM)] * (6 + len(weights)),
        cost_estimate=cost(4),
        compiler_params=params(60),
    )(index, first, second, gain, bias, cos_table, sin_table, *weights)


def masked_weights(queries, keys, low_ref, high_ref, key_ref):
    scores = dot_cols(queries, keys) * HD ** (-0.5)
    key_at = key_ref[...]
    allowed = (key_at >= low_ref[...]) & (key_at <= high_ref[...])
    scores = jnp.where(allowed, scores, neg_big)
    top = jnp.max(scores, axis=-1, keepdims=True)
    raised = jnp.exp(scores - top)
    return raised * (1.0 / jnp.sum(raised, axis=-1, keepdims=True))


def attend_body(count, ahead, index_ref, q_ref, low_ref, high_ref, key_ref, *refs):
    w_refs, kv_refs = refs[:count], refs[count : count + ahead]
    o_ref, mine_ref, other_ref = refs[count + ahead :]
    keys = jnp.concatenate([kv[:, :HD] for kv in kv_refs], axis=0)
    values = jnp.concatenate([kv[:, HD:] for kv in kv_refs], axis=0)
    weights = masked_weights(q_ref[...], keys, low_ref, high_ref, key_ref)
    head = pl.program_id(0)
    out = dot_plain(weights.astype(bf16), values).astype(bf16)
    o_ref[:, pl.ds(pl.multiple_of(head * HD, HD), HD)] = out

    @pl.when(head == pl.num_programs(0) - 1)
    def _():
        half = mine_ref.shape[0]
        out_w = joined(w_refs, index_ref, 1)
        branch = dot_plain(o_ref[...], out_w)
        mine_ref[...] = branch[:half]
        other_ref[...] = branch[half:].astype(bf16)


def attend(index, queries, low, high, key_at, weights, kv_parts):
    rows, width = queries.shape
    head = pl.BlockSpec((rows, HD), lambda h: (0, h))
    keys = key_at.shape[1]
    rest = (low, high, key_at, *weights, *kv_parts)
    outs = (
        jax.ShapeDtypeStruct(queries.shape, bf16),
        jax.ShapeDtypeStruct((rows // 2, D), f32),
        jax.ShapeDtypeStruct((rows // 2, D), bf16),
    )
    return pl.pallas_call(
        functools.partial(attend_body, len(weights), len(kv_parts)),
        out_shape=outs,
        grid=(width // HD,),
        in_specs=[pl.BlockSpec(memory_space=pltpu.SMEM), head] + [whole(a) for a in rest],
        out_specs=tuple(whole(a) for a in outs),
        compiler_params=params(60),
        cost_estimate=cost(8),
    )(index, queries, *rest)


def middle_body(x_ref, mine_ref, other_ref, gain_ref, mid_ref, h_ref):
    middle = x_ref[...].astype(f32) + mine_ref[...] + other_ref[...].astype(f32)
    scale = lax.rsqrt(jnp.mean(middle * middle, axis=-1, keepdims=True) + epsilon)
    mid_ref[...] = middle
    h_ref[...] = (middle * scale * gain_ref[1:2].astype(f32)).astype(bf16)


def middle_norm(x, mine, other, gain):
    return pl.pallas_call(
        middle_body,
        out_shape=(jax.ShapeDtypeStruct(mine.shape, f32), jax.ShapeDtypeStruct(mine.shape, bf16)),
        cost_estimate=cost(),
        compiler_params=params(60),
    )(x, mine, other, gain)


def feed_body(count, base, back, carried, last, filled, at_row, limit_ref, ctx_ref, *refs):
    (h_own, h_across, g_own, g_across, w_ref), refs = refs[:5], refs[5:]
    carry, refs = refs[: 2 * carried], refs[2 * carried + filled :]
    outs, (act_ref, sem) = refs[:-2], refs[-2:]
    gate_w, up_w, down_w = (
        jnp.concatenate([w_ref[i, k] for i in range(count)], axis=0) for k in range(3)
    )
    rows = act_ref.shape[1]
    lane = lax.broadcasted_iota(jnp.int32, (1, act_ref.shape[2]), 1)
    shown = lane >= limit_ref[0]
    half = g_own.shape[1]
    chunk = 2 * half
    at = 0
    for h_ref, g_ref in ((h_own, g_own), (h_across, g_across)):
        for j in range(h_ref.shape[0] // chunk):
            rows_in = h_ref[j * chunk : (j + 1) * chunk]
            grads_in = jnp.concatenate(
                [g_ref[ctx_ref[0] ^ (base + 2 * j + k)] for k in range(2)], axis=0
            )
            gate = dot_plain(rows_in, gate_w)
            up = dot_plain(rows_in, up_w)
            d_hidden = dot_plain(grads_in, down_w)
            gate_sig = jax.nn.sigmoid(gate)
            activated = gate * gate_sig
            hidden = activated * up
            d_gate = d_hidden * up * gate_sig * (1.0 + gate * (1.0 - gate_sig))
            d_up = d_hidden * activated
            act_ref[0, at : at + chunk] = jnp.where(shown, d_gate, 0.0).astype(bf16)
            act_ref[1, at : at + chunk] = jnp.where(shown, d_up, 0.0).astype(bf16)
            act_ref[2, at : at + chunk] = jnp.where(shown, hidden, 0.0).astype(bf16)
            at += chunk
    copy = pltpu.make_async_copy(act_ref, outs[0].at[:, pl.ds(at_row, rows), :], sem)
    copy.start()
    if back:
        d_rows = dot_cols(act_ref[0], gate_w) + dot_cols(act_ref[1], up_w)
        out_rows = dot_cols(act_ref[2], down_w)
        if carried:
            d_rows = d_rows + carry[0][...]
            out_rows = out_rows + carry[1][...]
        if last:
            cuts = [(i * half, (i + 1) * half) for i in range(4)]
            for ref, (low, high) in zip(outs[1:5], cuts):
                ref[...] = d_rows[low:high].astype(ref.dtype)
            cuts = cuts[:2] + [(2 * half, 4 * half)]
            for ref, (low, high) in zip(outs[5:], cuts):
                ref[...] = out_rows[low:high].astype(ref.dtype)
        else:
            outs[1][...] = d_rows
            outs[2][...] = out_rows
    copy.wait()


def feed(limit, ctx, rows_in, grads_in, weights, total, back, carry=(), last=False, act=None):
    some = sum(r.shape[0] for r in rows_in)
    width = weights.shape[3]
    outs = [jax.ShapeDtypeStruct((3, total, width), bf16)]
    half = grads_in[0].shape[1]
    if back and last:
        outs += [jax.ShapeDtypeStruct((half, D), f32)] * 2
        outs += [jax.ShapeDtypeStruct((half, D), bf16)] * 2
        outs += [jax.ShapeDtypeStruct((half, D), f32)] * 2
        outs += [jax.ShapeDtypeStruct((2 * half, D), bf16)]
    elif back:
        outs += [jax.ShapeDtypeStruct((some, D), f32)] * 2
    vmem = pl.BlockSpec(memory_space=pltpu.VMEM)
    smem = pl.BlockSpec(memory_space=pltpu.SMEM)
    hbm = pl.BlockSpec(memory_space=pl.ANY)
    inputs = (*rows_in, *grads_in, weights, *carry)
    filled = () if act is None else (act,)
    return pl.pallas_call(
        functools.partial(
            feed_body, weights.shape[0], 0 if back else TEAM, back, len(carry) // 2, last,
            len(filled), 0 if back else total - some,
        ),
        out_shape=tuple(outs),
        in_specs=[smem, smem] + [vmem] * len(inputs) + [hbm] * len(filled),
        out_specs=tuple([hbm] + [vmem] * (len(outs) - 1)),
        scratch_shapes=[pltpu.VMEM((3, some, width), bf16), pltpu.SemaphoreType.DMA],
        input_output_aliases={2 + len(inputs): 0} if filled else {},
        compiler_params=params(60),
        cost_estimate=cost((6 if back else 0) + 9 * some / 512),
    )(limit, ctx, *inputs, *filled)


def turn_body(contexts, blocks, index_ref, ctx_ref, *refs):
    lines, (g_own, g_across, kept_ref, sent_ref) = refs[:-4], refs[-4:]
    width = D // blocks
    order = fsdp_order(blocks)
    half = g_own.shape[1]

    def put(which, at, value):
        here = slice(at, at + value.shape[0])
        parts = [value[:, i * width : (i + 1) * width] for i in range(blocks)]
        if blocks > 2:
            parts = xor_blocks(parts, index_ref[0], blocks)
            parts = [parts[i] for i in order]
        for spot in range(blocks // 2):
            lines_at = slice(spot * width, (spot + 1) * width)
            kept_ref[which, lines_at, here] = parts[spot].T
            sent_ref[which, lines_at, here] = parts[blocks // 2 + spot].T

    at = 0
    for ref in lines:
        put(0, at, ref[...])
        at += ref.shape[0]
    at = 0
    for group in (range(TEAM), range(TEAM, contexts)):
        for ref in (g_own, g_across):
            for k in group:
                put(1, at, ref[ctx_ref[0] ^ k])
                at += half


def turn_rows(index, ctx, rows, grads, n_fsdp):
    total = sum(r.shape[0] for r in rows)
    blocks = n_fsdp
    if D // n_fsdp % LANES:
        blocks = 2
        rows, grads = (
            [to_relative(v, index[0], n_fsdp) for v in some] for some in (rows, grads)
        )
    smem = pl.BlockSpec(memory_space=pltpu.SMEM)
    return pl.pallas_call(
        functools.partial(turn_body, grads[0].shape[0], blocks),
        out_shape=(jax.ShapeDtypeStruct((2, D // 2, total), bf16),) * 2,
        in_specs=[smem, smem] + [pl.BlockSpec(memory_space=pltpu.VMEM)] * (len(rows) + 2),
        cost_estimate=cost(7),
        compiler_params=params(60),
    )(index, ctx, *rows, *grads)


def weight_body(own_ref, beside_ref, act_ref, act_beside_ref, near_ref, far_ref):
    cut = near_ref.shape[1]
    value = dot_plain(own_ref[0], act_ref[0]) + dot_plain(beside_ref[0], act_beside_ref[0])
    near_ref[0] = value[:cut].astype(bf16)
    far_ref[0] = value[cut:].astype(bf16)


def weight_grads(own, beside, act, act_beside):
    total, width = act.shape[1:]
    cut = D // 4
    left = pl.BlockSpec((1, D // 2, total), lambda k: (k // 2, 0, 0))
    right = pl.BlockSpec((1, total, width), lambda k: (k, 0, 0))
    out = pl.BlockSpec((1, cut, width), lambda k: (k, 0, 0))
    return pl.pallas_call(
        weight_body,
        out_shape=(jax.ShapeDtypeStruct((3, cut, width), bf16),) * 2,
        grid=(3,),
        in_specs=[left, left, right, right],
        out_specs=(out, out),
        compiler_params=params(60),
        cost_estimate=cost(12),
    )(own, beside, act, act_beside)


def middle_back_body(
    near_ref, across_ref, far_ref, mid_ref, gain_ref, g_ref, d_ref, low_ref, gain_out
):
    d_normed = near_ref[...] + across_ref[...].astype(f32) + far_ref[...].astype(f32)
    middle = mid_ref[...]
    scale = lax.rsqrt(jnp.mean(middle * middle, axis=-1, keepdims=True) + epsilon)
    gain_out[...] = jnp.sum(d_normed * middle * scale, axis=0, keepdims=True)
    weighted = d_normed * gain_ref[1:2].astype(f32)
    inner = jnp.mean(weighted * middle, axis=-1, keepdims=True)
    d_middle = g_ref[...].astype(f32) + scale * weighted - middle * scale**3 * inner
    d_ref[...] = d_middle
    low_ref[...] = d_middle.astype(bf16)


def middle_back(near, across, far, middle, gain, grads):
    return pl.pallas_call(
        middle_back_body,
        out_shape=(
            jax.ShapeDtypeStruct(near.shape, f32),
            jax.ShapeDtypeStruct(near.shape, bf16),
            jax.ShapeDtypeStruct((1, D), f32),
        ),
        cost_estimate=cost(),
        compiler_params=params(60),
    )(near, across, far, middle, gain, grads)


def attend_back_body(count, ahead, index_ref, q_ref, low_ref, high_ref, key_ref, cos_ref, sin_ref, *refs):
    scale = HD ** (-0.5)
    mine_ref, other_ref = refs[:2]
    w_refs, kv_refs = refs[2 : 2 + count], refs[2 + count : 2 + count + ahead]
    outs = refs[2 + count + ahead :]
    dq_ref, dkv_refs, (d_o, sums) = outs[0], outs[1 : 1 + ahead], outs[1 + ahead :]
    head = pl.program_id(0)

    @pl.when(head == 0)
    def _():
        d_branch = jnp.concatenate([mine_ref[...], other_ref[...]], axis=0)
        out_w = joined(w_refs, index_ref, 1)
        d_o[...] = dot_cols(d_branch, out_w).astype(bf16)
        sums[...] = jnp.zeros_like(sums)

    queries = q_ref[...]
    grad = d_o[:, pl.ds(pl.multiple_of(head * HD, HD), HD)]
    keys = jnp.concatenate([kv[:, :HD] for kv in kv_refs], axis=0)
    values = jnp.concatenate([kv[:, HD:] for kv in kv_refs], axis=0)
    weights = masked_weights(queries, keys, low_ref, high_ref, key_ref)
    dweights = dot_cols(grad, values)
    delta = jnp.sum(weights * dweights, axis=-1, keepdims=True)
    dscores = (weights * (dweights - delta)).astype(bf16)
    dq_rot = dot_plain(dscores, keys) * scale
    turned = pltpu.roll(dq_rot, HD // 2, 1)
    dq_ref[...] = (dq_rot * cos_ref[...] - turned * sin_ref[...]).astype(bf16)
    sums[:, :HD] += dot_rows(dscores, queries) * scale
    sums[:, HD:] += dot_rows(weights.astype(bf16), grad)

    @pl.when(head == pl.num_programs(0) - 1)
    def _():
        rows = q_ref.shape[0]
        for i, out in enumerate(dkv_refs):
            out[...] = sums[i * rows : (i + 1) * rows].astype(out.dtype)


def attend_back(index, queries, low, high, key_at, cos_table, sin_table, grads, weights, kv_parts):
    rows, width = queries.shape
    head = pl.BlockSpec((rows, HD), lambda h: (0, h))
    keys = key_at.shape[1]
    rest = (low, high, key_at, cos_table, sin_table, *grads, *weights, *kv_parts)
    outs = [jax.ShapeDtypeStruct(queries.shape, bf16)]
    outs += [
        jax.ShapeDtypeStruct(kv.shape, bf16 if i else f32) for i, kv in enumerate(kv_parts)
    ]
    return pl.pallas_call(
        functools.partial(attend_back_body, len(weights), len(kv_parts)),
        out_shape=tuple(outs),
        grid=(width // HD,),
        in_specs=[pl.BlockSpec(memory_space=pltpu.SMEM), head] + [whole(a) for a in rest],
        out_specs=tuple([head] + [whole(a) for a in outs[1:]]),
        scratch_shapes=[pltpu.VMEM((rows, width), bf16), pltpu.VMEM((keys, 2 * HD), f32)],
        compiler_params=params(60),
        cost_estimate=cost(10),
    )(index, queries, *rest)


def project_back_body(count, ahead, index_ref, dq_ref, cos_ref, sin_ref, *refs):
    w_refs, dkv_refs = refs[:count], refs[count : count + ahead]
    d_ref, mine_ref, other_ref, bias_ref = refs[count + ahead :]
    total = dkv_refs[0][...]
    for extra in dkv_refs[1:]:
        total = total + extra[...].astype(f32)
    dk = total[:, :HD]
    dk = dk * cos_ref[...] - pltpu.roll(dk, HD // 2, 1) * sin_ref[...]
    d_low = jnp.concatenate([dq_ref[...], dk.astype(bf16), total[:, HD:].astype(bf16)], axis=1)
    d_ref[...] = d_low
    bias_ref[...] = jnp.sum(d_low.astype(f32), axis=0, keepdims=True)
    weights = joined(w_refs, index_ref, 0, slice(0, D // count))
    d_normed = dot_cols(d_low, weights)
    half = mine_ref.shape[0]
    mine_ref[...] = d_normed[:half]
    other_ref[...] = d_normed[half:].astype(bf16)


def project_back(index, dq, cos_table, sin_table, weights, dkv_parts):
    rows = dq.shape[0]
    total = weights[0].shape[1]
    return pl.pallas_call(
        functools.partial(project_back_body, len(weights), len(dkv_parts)),
        out_shape=(
            jax.ShapeDtypeStruct((rows, total), bf16),
            jax.ShapeDtypeStruct((rows // 2, D), f32),
            jax.ShapeDtypeStruct((rows // 2, D), bf16),
            jax.ShapeDtypeStruct((1, total), f32),
        ),
        in_specs=[pl.BlockSpec(memory_space=pltpu.SMEM)] + [pl.BlockSpec(memory_space=pltpu.VMEM)] * (3 + len(weights) + len(dkv_parts)),
        cost_estimate=cost(4),
        compiler_params=params(60),
    )(index, dq, cos_table, sin_table, *weights, *dkv_parts)


def input_back_body(mine_ref, other_ref, x_ref, gain_ref, mid_ref, d_ref, gain_out):
    d_normed = mine_ref[...] + other_ref[...].astype(f32)
    x = x_ref[...].astype(f32)
    scale = lax.rsqrt(jnp.mean(x * x, axis=-1, keepdims=True) + epsilon)
    gain_out[...] = jnp.sum(d_normed * x * scale, axis=0, keepdims=True)
    weighted = d_normed * gain_ref[0:1].astype(f32)
    inner = jnp.mean(weighted * x, axis=-1, keepdims=True)
    d_ref[...] = (mid_ref[...] + scale * weighted - x * scale**3 * inner).astype(bf16)


def input_back(mine, other, x, gain, d_middle):
    return pl.pallas_call(
        input_back_body,
        out_shape=(jax.ShapeDtypeStruct(mine.shape, bf16), jax.ShapeDtypeStruct((1, D), f32)),
        cost_estimate=cost(),
        compiler_params=params(60),
    )(mine, other, x, gain, d_middle)


def place_body(plan, carried, member_ref, *refs):
    own_ref, other_ref, refs = refs[0], refs[1], refs[2:]
    outs = refs[carried : carried + 3]
    wide_buf, tall_buf, sems = refs[carried + 3 :]
    width = own_ref.shape[2]

    def copies(team):
        skip, at = plan[team]
        size = width - skip
        for k in range(2):
            yield pltpu.make_async_copy(
                wide_buf.at[team, k, :, pl.ds(skip, size)],
                outs[k].at[:, pl.ds(at + skip, size)],
                sems.at[team, k],
            )
        yield pltpu.make_async_copy(
            tall_buf.at[team, pl.ds(skip, size)],
            outs[2].at[pl.ds(at + skip, size)],
            sems.at[team, 2],
        )

    for team in range(len(plan)):
        def put(ref, team=team):
            wide_buf[team, 0] = ref[0].astype(f32)
            wide_buf[team, 1] = ref[1].astype(f32)
            tall_buf[team] = ref[2].astype(f32).T

        @pl.when(member_ref[0] == team)
        def _():
            put(own_ref)

        @pl.when(member_ref[0] != team)
        def _():
            put(other_ref)

        for copy in copies(team):
            copy.start()
    for team in range(len(plan)):
        for copy in copies(team):
            copy.wait()


def place(member, own, other, index, starts, fresh, ff_local, carry):
    shard, width = own.shape[1:]
    plan = tuple(
        (min(max(fresh[s] - index * width, 0), width), starts[s] + index * width)
        for s in range(TEAM)
    )
    hbm = pl.BlockSpec(memory_space=pl.ANY)
    vmem = pl.BlockSpec(memory_space=pltpu.VMEM)
    return pl.pallas_call(
        functools.partial(place_body, plan, len(carry)),
        out_shape=(
            jax.ShapeDtypeStruct((shard, ff_local), f32),
            jax.ShapeDtypeStruct((shard, ff_local), f32),
            jax.ShapeDtypeStruct((ff_local, shard), f32),
        ),
        in_specs=[pl.BlockSpec(memory_space=pltpu.SMEM)] + [vmem] * 2 + [hbm] * len(carry),
        out_specs=(hbm, hbm, hbm),
        scratch_shapes=[
            pltpu.VMEM((TEAM, 2, shard, width), f32),
            pltpu.VMEM((TEAM, width, shard), f32),
            pltpu.SemaphoreType.DMA((TEAM, 3)),
        ],
        input_output_aliases={3 + i: i for i in range(len(carry))},
        cost_estimate=cost(),
        compiler_params=params(60),
    )(member, own, other, *carry)


def after(values, *first):
    return lax.optimization_barrier((values, first))[0]


class Order:
    def __init__(self):
        self.last = ()

    def __call__(self, step, *args):
        args, _ = lax.optimization_barrier((args, self.last))
        result = step(*args)
        self.last = (jax.tree.leaves(result)[0],)
        return result

    def pin(self, values):
        values, _ = lax.optimization_barrier((values, self.last))
        self.last = (jax.tree.leaves(values)[0],)
        return values


def stack(*pieces):
    return jnp.concatenate(pieces, axis=0)


class Pieces:
    def __init__(self, run, full, *first):
        bits = list(reversed(bits_of(lax.axis_size("fsdp"))))
        self.run, self.near = run, bits[-1]
        self.held = [full]
        gate = after(full, *first)
        for bit in bits[:-1]:
            self.held = self.held + [swap(p, "fsdp", bit) for p in [gate] + self.held[1:]]

    def turn(self):
        self.held = self.held[:1] + list(self.run.pin(tuple(self.held[1:])))
        self.sent = swap(self.run(lambda *a: jnp.stack(a), *self.held), "fsdp", self.near)
        return self.held[-1]

    def finish(self):
        self.sent = self.run.pin(self.sent)

    def pieces(self):
        return self.held + [self.sent[i] for i in range(len(self.held))]


def per_device(
    tokens,
    cotangent,
    lengths,
    span_order,
    attn_gain,
    w_q,
    b_q,
    w_k,
    b_k,
    w_v,
    b_v,
    w_o,
    mlp_gain,
    w_gate,
    w_up,
    w_down,
):
    n_fsdp = lax.axis_size("fsdp")
    n_ctx = lax.axis_size("context")
    my_fsdp = lax.axis_index("fsdp")
    my_ctx = lax.axis_index("context")
    my_tensor = lax.axis_index("tensor")
    member = my_ctx % TEAM
    rows = tokens.shape[0]
    half = rows // 2
    piece_rows = rows // n_ctx
    shard = D // n_fsdp
    q_width = w_q.shape[1]
    kv_width = w_k.shape[1]
    qkv_width = q_width + 2 * kv_width
    heads_local = q_width // HD
    all_heads = qkv_width // HD
    flipped = my_tensor != 0
    run = Order()
    sharing = n_fsdp == 4 and n_ctx % 2 == 0

    def mine_first(values):
        first, second = values[:half], values[half:]
        return stack(jnp.where(flipped, second, first), jnp.where(flipped, first, second))

    bias_cols = HD // n_fsdp

    def qkv_pack(g1, g2, b_q, b_k, b_v, *w):
        biases = jnp.concatenate([b_q, b_k, b_v], axis=0).astype(bf16)
        spread = jnp.concatenate([biases] * n_fsdp, axis=1)
        lane = jnp.arange(HD, dtype=jnp.int32)[None, :] // bias_cols
        spread = jnp.where(lane == my_fsdp, spread, jnp.zeros_like(spread))
        gains = jnp.pad(jnp.stack([g1, g2]).astype(bf16), ((0, 6), (0, qkv_width - shard)))
        spread = jnp.pad(spread, ((0, 8 - all_heads), (0, qkv_width - HD)))
        return stack(jnp.concatenate(w, axis=1).astype(bf16), gains, spread)

    qkv_h = Pieces(run, run(qkv_pack, attn_gain, mlp_gain, b_q, b_k, b_v, w_q, w_k, w_v))
    out_cast = run(lambda w: w.astype(bf16), w_o)

    def arrange(values):
        both = mine_first(values)
        return both[:half], both[half:]

    pair = n_ctx == 4

    class Rows:
        def __init__(self, mine):
            self.mine = mine
            self.beside = swap(mine, "context", 1)

        def early(self):
            if pair:
                self.remote_mine = swap(self.mine, "context", 2)

        def turn(self):
            self.beside = run.pin(self.beside)

        def across_team(self):
            self.held = run(stack, self.mine, self.beside)
            self.held_across = swap(self.held, "tensor", 1)

        def pin_early(self):
            if pair:
                self.remote_mine = run.pin(self.remote_mine)

        def late(self):
            if pair:
                self.remote_beside = swap(self.beside, "context", 2)
                return
            held, others = self.held, []
            for bit in bits_of(n_ctx)[1:]:
                there = swap(held, "context", bit)
                others.append(there)
                held = stack(held, there)
            self.remote = stack(*others)

        def across_rest(self):
            if pair:
                self.remote = run(stack, self.remote_mine, self.remote_beside)
            self.remote_across = swap(self.remote, "tensor", 1)

        def pin_team(self):
            self.held_across = run.pin(self.held_across)

        def pin_rest(self):
            self.remote_across = run.pin(self.remote_across)

        def team(self):
            return (self.held, self.held_across)

        def rest(self):
            return (self.remote, self.remote_across)

    grad_mine, _ = run(arrange, cotangent)
    grads_own = run(lambda v: jnp.broadcast_to(v[None], (n_ctx,) + v.shape), grad_mine)
    grads_own = lax.all_to_all(grads_own, "context", split_axis=0, concat_axis=0)

    ff_local = w_gate.shape[1]
    tiles = ff_local // LANES
    unit = PARTS * WIDE // LANES
    slice_tiles = -(-tiles // (TEAM * unit)) * unit
    part = slice_tiles // PARTS * LANES
    starts = [min(s * slice_tiles, tiles - slice_tiles) * LANES for s in range(TEAM)]
    fresh = [s * slice_tiles * LANES - starts[s] for s in range(TEAM)]
    my_start = jnp.int32(starts[0] // LANES)
    limit = jnp.int32(fresh[0])
    for s in range(1, TEAM):
        my_start = jnp.where(member == s, starts[s] // LANES, my_start)
        limit = jnp.where(member == s, fresh[s], limit)

    def packed(index):
        start = (my_start + index * (part // LANES)).reshape(1)
        return run(lambda *a: pack(*a, part), w_gate, w_up, w_down, start)

    longest = 3 * n_ctx * rows // 8
    behind = min(n_ctx - 1, (longest - 1 + rows - 1) // rows)
    half_dim = HD // 2

    def places(lengths, span_order):
        seq_ends = jnp.cumsum(lengths[0])
        row = jnp.arange(rows, dtype=jnp.int32)
        stored = jnp.where(flipped, (row + half) % rows, row)

        def packed_of(context):
            owner = lax.dynamic_index_in_dim(span_order[0], context, 0, keepdims=False)
            span = stored // piece_rows
            hot = span[:, None] == jnp.arange(n_ctx, dtype=jnp.int32)[None, :]
            spot = jnp.sum(jnp.where(hot, owner[None, :], 0), axis=1)
            return context * rows + spot * piece_rows + stored % piece_rows

        own_at = packed_of(my_ctx)
        passed = own_at[:, None] >= seq_ends[None, :]
        begin = jnp.max(jnp.where(passed, seq_ends[None, :], 0), axis=1)
        position = own_at - begin
        key_at = [own_at]
        for step in range(1, behind + 1):
            there = packed_of(jnp.maximum(my_ctx - step, 0))
            key_at.append(jnp.where(my_ctx >= step, there, far_away))
        frequency = rope_base ** (-(jnp.arange(half_dim, dtype=f32) * 2.0) / HD)
        angles = position.astype(f32)[:, None] * frequency[None, :]
        cosine, sine = jnp.cos(angles), jnp.sin(angles)
        return (
            begin[:, None],
            own_at[:, None],
            jnp.concatenate(key_at)[None, :],
            jnp.concatenate([cosine, cosine], axis=1),
            jnp.concatenate([-sine, sine], axis=1),
        )

    index = my_fsdp.astype(jnp.int32).reshape(1)
    ctx = my_ctx.astype(jnp.int32).reshape(1)
    feed_in = [packed(0)]
    mine_tokens, other_tokens = run(arrange, tokens)
    feed_in.append(packed(1))
    far = qkv_h.turn()
    out_h = Pieces(run, out_cast, far)
    feed_in += [packed(i) for i in range(2, PARTS)]
    low, high, key_at, cos_table, sin_table = run(places, lengths, span_order)
    qkv_h.finish()

    def in_order(pieces, axis, cut=None):
        if shard % LANES == 0:
            return pieces
        order = fsdp_order(n_fsdp)
        blocks = [pieces[order.index(i)] for i in range(n_fsdp)]
        blocks = [b if cut is None else b[:cut] for b in blocks]
        return [jnp.concatenate(xor_blocks(blocks, my_fsdp, n_fsdp), axis=axis)]

    gains, bias = run(lambda i, p: vectors(i, p, all_heads), index, qkv_h.pieces())
    qkv_w = in_order(qkv_h.pieces(), 0, shard)

    queries, kv_own, normed = run(
        lambda *a: project(*a, q_width),
        index, mine_tokens, other_tokens, gains, bias, cos_table, sin_table, qkv_w,
    )
    kv_parts = [kv_own] + [shift(kv_own, "context", step) for step in range(1, behind + 1)]
    normed_rel = run(lambda v: to_relative(v, my_fsdp, n_fsdp), normed)
    grads_own = run.pin(grads_own)
    grads = (grads_own, swap(grads_own, "tensor", 1))
    far = out_h.turn()
    feed_w = [lax.all_gather(after(v, far), "fsdp") for v in feed_in]
    kv_parts = [kv_own] + list(run.pin(tuple(kv_parts[1:])))
    out_h.finish()
    out_w = in_order(out_h.pieces(), 1)
    branch_mine, attended, branch_other = run(
        lambda *a: (lambda o, m, s: (m, o, s))(*attend(*a)),
        index, queries, low, high, key_at, out_w, kv_parts,
    )
    branch_other = swap(branch_other, "tensor", 1)
    sent = run(lambda a, b: jnp.concatenate([a, b[:, D // 2 :]], axis=1), attended, normed_rel)
    early_beside = swap(sent, "fsdp", 1)
    grads = run.pin(grads)
    middle, normed_two = run(
        middle_norm, mine_tokens, branch_mine, branch_other, gains
    )
    lines = Rows(normed_two)
    lines.early()
    early_beside = run.pin(early_beside)
    attended_beside, normed_beside = early_beside[:, :q_width], early_beside[:, q_width:]
    lines.turn()
    lines.across_team()
    lines.pin_early()
    lines.late()
    lines.pin_team()
    lines.across_rest()

    limits = [limit.reshape(1)] + [jnp.zeros((1,), jnp.int32)] * (PARTS - 1)
    acts, acts_beside = {}, {}
    total_rows = n_ctx * rows

    def feed_team(index, carry, last=False):
        acts[index], *carry = run(
            lambda *a: feed(*a[:5], total_rows, True, a[5], last),
            limits[index], ctx, lines.team(), grads, feed_w[index], carry,
        )
        return tuple(carry)

    def feed_rest(index):
        (acts[index],) = run(
            lambda *a: feed(*a[:5], total_rows, False, act=a[5]),
            limits[index], ctx, lines.rest(), grads, feed_w[index], acts[index],
        )
        acts_beside[index] = swap(acts[index], "fsdp", 1)

    waiting, reduced, other_parts = {}, {}, {}

    def grads_of(index):
        far, near = run(
            lambda *a: weight_grads(*a)[::-1],
            turned, turned_beside, acts[index], acts_beside[index],
        )
        bits = bits_of(n_fsdp)[1:]
        for bit in bits[:-1]:
            total = near.astype(f32) + swap(far, "fsdp", bit).astype(f32)
            cut = total.shape[1] // 2
            far, near = total[:, cut:].astype(bf16), total[:, :cut].astype(bf16)
        waiting[index] = (near, swap(far, "fsdp", bits[-1]))

    def give(near, arrived):
        return (near.astype(f32) + arrived.astype(f32)).astype(bf16)

    def add_far(index):
        reduced[index] = run(give, *waiting[index])
        other_parts[index] = swap(reduced[index], "context", 1)

    carry = feed_team(0, ())
    lines.pin_rest()
    turned, turned_sent = run(
        lambda *a: turn_rows(*a, n_fsdp), index, ctx, lines.team() + lines.rest(), grads
    )
    turned_beside = swap(turned_sent, "fsdp", 1)
    feed_rest(0)
    carry = feed_team(1, carry)
    grads_of(0)
    feed_rest(1)
    given = feed_team(2, carry, True)
    d_near, d_beside, d_far, d_far_beside = given[:4]
    out_near, out_beside, out_far = given[4:]
    d_far_beside, d_far = swap(d_far_beside, "tensor", 1), swap(d_far, "tensor", 1)
    feed_rest(2)
    d_beside = swap(run(give, d_beside, d_far_beside), "context", 1)
    d_far = run.pin(d_far)
    grads_of(1)
    add_far(0)
    d_middle, d_branch, grad_gain_two = run(
        middle_back, d_near, d_far, d_beside, middle, gains, grad_mine
    )
    d_branch_other = swap(d_branch, "tensor", 1)
    grads_of(2)
    d_branch_other = run.pin(d_branch_other)
    d_all = run(lambda *a: to_relative(stack(*a), my_fsdp, n_fsdp), d_branch, d_branch_other)
    d_all_beside = swap(d_all[:, D // 2 :], "fsdp", 1)
    d_all_beside = run.pin(d_all_beside)
    dq_low, *dkv_parts = run(
        attend_back,
        index, queries, low, high, key_at, cos_table, sin_table,
        (d_branch, d_branch_other), out_w, kv_parts,
    )
    dkv_parts = [dkv_parts[0]] + [
        shift(p, "context", -step - 1) for step, p in enumerate(dkv_parts[1:])
    ]
    add_far(1)
    other_parts[0] = run.pin(other_parts[0])

    def halves(values, axis):
        cut = values.shape[axis] // 2
        return (
            lax.slice_in_dim(values, 0, cut, axis=axis),
            lax.slice_in_dim(values, cut, 2 * cut, axis=axis),
        )

    class Reduce:
        def __init__(self, axis, full, full_beside, split, split_beside):
            self.axis, self.other = axis, 1 - axis
            self.full, self.full_beside = full, full_beside
            self.kept, self.kept_beside = split[:, : D // 2], split_beside
            self.todo = [("fsdp", bit) for bit in bits_of(n_fsdp)[1:]]
            self.todo += [("context", bit) for bit in bits_of(n_ctx)]
            self.back = [bit for bit in reversed(bits_of(n_ctx))]
            self.value = None

        def cut(self, total):
            name, bit = self.todo[0]
            if name == "fsdp":
                keep, send = halves(total, self.axis)
                return keep, send.astype(bf16)
            first, second = halves(total, self.other)
            on = (my_ctx & bit) != 0
            return jnp.where(on, second, first), jnp.where(on, first, second).astype(bf16)

        def send(self, pair):
            name, bit = self.todo.pop(0)
            self.keep, sent = pair
            self.sent = swap(sent, name, bit)

        def first(self):
            def product(full, kept, full_beside, kept_beside):
                left, right = stack(kept, kept_beside), stack(full, full_beside)
                if self.axis == 1:
                    left, right = right, left
                return self.cut(dot_rows(left, right))

            self.send(run(product, self.full, self.kept, self.full_beside, self.kept_beside))

        def step(self):
            if self.todo:
                self.send(run(lambda a, b: self.cut(a + b.astype(f32)), self.keep, self.sent))
                return
            if self.value is None:
                self.value = run(give, self.keep, self.sent)
            else:
                self.value = self.join()
            self.bit = self.back.pop(0)
            self.sent = swap(self.value, "context", self.bit)

        def join(self):
            on = (my_ctx & self.bit) != 0

            def both(mine, other):
                return jnp.concatenate(
                    [jnp.where(on, other, mine), jnp.where(on, mine, other)], axis=self.other
                )

            return run(both, self.value, self.sent)

    reduce_o = Reduce(1, attended, attended_beside, d_all, d_all_beside)
    reduce_o.first()
    d_qkv, dn_mine, dn_other, grad_bias = run(
        project_back, index, dq_low, cos_table, sin_table, qkv_w, dkv_parts
    )
    d_qkv_beside = swap(d_qkv, "fsdp", 1)
    dn_other = swap(dn_other, "tensor", 1)
    placed = ()

    def place_part(index, placed):
        return run(
            lambda m, a, b, c: place(m, a, b, index, starts, fresh, ff_local, c),
            member.reshape(1), reduced[index], other_parts[index], placed,
        )

    placed = place_part(0, placed)
    reduce_qkv = Reduce(0, d_qkv, d_qkv_beside, normed_rel, normed_beside)
    reduce_qkv.first()
    d_inputs, grad_gain_one = run(
        input_back, dn_mine, dn_other, mine_tokens, gains, d_middle
    )
    reduce_o.step()
    add_far(2)
    d_inputs_other = swap(d_inputs, "tensor", 1)
    reduce_qkv.step()
    d_inputs_other = run.pin(d_inputs_other)
    out_far = swap(out_far, "tensor", 1)
    reduce_o.step()
    other_parts[1] = run.pin(other_parts[1])
    reduce_qkv.step()
    out_mine, out_beside = run(
        lambda a, b, c: (a + c[:half].astype(f32), give(b, c[half:])), out_near, out_beside, out_far
    )
    out_beside = swap(out_beside, "context", 1)
    reduce_o.step()
    reduce_qkv.step()
    placed = place_part(1, placed)
    out_half = run(
        lambda a, b, c: (a + b + c.astype(f32)).astype(bf16), middle, out_mine, out_beside
    )
    out_half_other = swap(out_half, "tensor", 1)

    gain_rows = run(stack, grad_gain_one, grad_gain_two)
    gain_other = swap(gain_rows, "tensor", 1)

    def smalls(gain_rows, gain_other, grad_bias):
        gain_rows = jnp.pad(gain_rows + gain_other, ((0, 6), (0, 0)))
        biases = jnp.pad(grad_bias.reshape(all_heads, HD), ((0, 0), (0, D - HD)))
        return stack(gain_rows, biases)

    reduce_o.step()
    reduce_qkv.step()
    small = run(smalls, gain_rows, gain_other, grad_bias)
    steps = [("fsdp", bit) for bit in bits_of(n_fsdp)] + [("context", bit) for bit in bits_of(n_ctx)]

    def small_step(small):
        name, bit = steps.pop(0)
        return run(jnp.add, small, swap(small, name, bit))

    small = small_step(small)
    while reduce_o.back:
        reduce_o.step()
        reduce_qkv.step()
        small = small_step(small)
    while steps:
        small = small_step(small)
    grad_o = reduce_o.join().astype(f32)
    grad_qkv = reduce_qkv.join().astype(f32)
    grad_gate, grad_up, grad_down = place_part(2, placed)
    grad_biases = small[8 : 8 + all_heads, :bias_cols]
    small_gains = small[:2, :shard]
    for f in range(1, n_fsdp):
        there = small[8 : 8 + all_heads, f * bias_cols : (f + 1) * bias_cols]
        grad_biases = jnp.where(my_fsdp == f, there, grad_biases)
        small_gains = jnp.where(my_fsdp == f, small[:2, f * shard : (f + 1) * shard], small_gains)
    def restore(low_half, other_half):
        both = mine_first(stack(low_half, other_half))
        return both.astype(f32)

    return (
        restore(out_half, out_half_other),
        restore(d_inputs, d_inputs_other),
        small_gains[0],
        grad_qkv[:, :q_width],
        grad_biases[:heads_local],
        grad_qkv[:, q_width : q_width + kv_width],
        grad_biases[heads_local : heads_local + 1],
        grad_qkv[:, q_width + kv_width :],
        grad_biases[heads_local + 1 :],
        grad_o,
        small_gains[1],
        grad_gate,
        grad_up,
        grad_down,
    )


def solution(mesh):
    in_specs = (
        P(("fsdp", "context"), None),
        P(("fsdp", "context"), None),
        P("fsdp", None),
        P("fsdp", None, None),
        P("fsdp"),
        P("fsdp", "tensor"),
        P("tensor", "fsdp"),
        P("fsdp", "tensor"),
        P("tensor", "fsdp"),
        P("fsdp", "tensor"),
        P("tensor", "fsdp"),
        P("tensor", "fsdp"),
        P("fsdp"),
        P("fsdp", "tensor"),
        P("fsdp", "tensor"),
        P("tensor", "fsdp"),
    )
    out_specs = (
        P(("fsdp", "context"), None),
        P(("fsdp", "context"), None),
        P("fsdp"),
        P("fsdp", "tensor"),
        P("tensor", "fsdp"),
        P("fsdp", "tensor"),
        P("tensor", "fsdp"),
        P("fsdp", "tensor"),
        P("tensor", "fsdp"),
        P("tensor", "fsdp"),
        P("fsdp"),
        P("fsdp", "tensor"),
        P("fsdp", "tensor"),
        P("tensor", "fsdp"),
    )
    return jax.shard_map(
        per_device, mesh=mesh, in_specs=in_specs, out_specs=out_specs, check_vma=False
    )
```

time: 669 us -> 566 us (0.85)
  Pallas kernels: 12.2 us -> 190 us
  matrix products: 155 us -> 4.15 us
  waiting for transfers between devices: 290 us -> 225 us
  other arithmetic: 87.2 us -> 42.2 us
  local copies, waits for them, and re-layouts: 53.2 us -> 29.3 us
  between operations: 3.31 us -> 15.4 us
    pallas_call x2 -> x24, Pallas kernels: 12.2 us -> 190 us  [the longest x6 79 us: feed(): pl.pallas_call(functools.partial(feed_body, weights.shape[0], 0 if back e...]
    dot_general x16 -> x0, matrix products: 119 us -> none  [the longest x8 60.6 us: dot_plain(): return jnp.dot(left_op, right_op, preferred_element_type=f32)]
    ppermute x64 -> x48, waiting for transfers between devices: 283 us -> 199 us  [swap(): return lax.ppermute(values, axis_name, [(i, i ^ bit) for i in range(size)])]
    dot_general x6 -> x2, matrix products: 35.9 us -> 4.15 us  [dot_rows(): lax.dot_general(left_op, right_op, (((0,), (0,)), ((), ())), preferred_el...]
    slice x44 -> x11, local copies, waits for them, and re-layouts: 28.3 us -> 5.76 us  [the longest x2 2.33 us: halves(): lax.slice_in_dim(values, cut, 2 * cut, axis=axis)]
    convert_element_type x30 -> x18, other arithmetic: 36.5 us -> 15.9 us  [the longest x7 9.82 us: give(): return (near.astype(f32) + arrived.astype(f32)).astype(bf16)]
    all_to_all x0 -> x1, waiting for transfers between devices: none -> 19.4 us  [per_device(): lax.all_to_all(grads_own, 'context', split_axis=0, concat_axis=0)]
    add x21 -> x11, other arithmetic: 16.8 us -> 3.5 us  [the longest x4 2.7 us: step(): a + b.astype(f32)]
  transfers between devices with their start and end apart: 68 -> 56, of which waited for: 33 -> 23; matrix products, arithmetic and copies ran while one was open for 38% -> 10% of each run, Pallas kernels for 2% -> 34%
where the time goes in v2:
time: 566 us; the launch traced here: 558 us
  waiting for transfers between devices  225 us (40%)
  Pallas kernels  190 us (34%)
  starting transfers between devices  52.7 us (9%)
  other arithmetic  42.2 us (7%)
  local copies, waits for them, and re-layouts  29.3 us (5%)
  between operations  15.4 us (3%)
    ppermute x48, waiting for transfers between devices, swap(): return lax.ppermute(values, axis_name, [(i, i ^ bit) for i in range(size)])  199 us
    pallas_call x6, Pallas kernels, feed(): pl.pallas_call(functools.partial(feed_body, weights.shape[0], 0 if back e...  79 us
    ppermute x48, starting transfers between devices, swap(): return lax.ppermute(values, axis_name, [(i, i ^ bit) for i in range(size)])  38.4 us
    pallas_call x3, Pallas kernels, weight_grads(): pl.pallas_call(weight_body, out_shape=(jax.ShapeDtypeStruct((3, cut, widt...  36.6 us
    all_to_all x1, waiting for transfers between devices, per_device(): lax.all_to_all(grads_own, 'context', split_axis=0, concat_axis=0)  19.4 us
    pallas_call x3, Pallas kernels, place(): pl.pallas_call(functools.partial(place_body, plan, len(carry)), out_shape...  15.9 us
    unnamed x105, local copies, waits for them, and re-layouts  12.1 us
  transfers between devices with their start and end apart: 56, of which 23 were waited for; matrix products, arithmetic and copies ran while one was open for 10% of the time, Pallas kernels for 34%

profile of v2, /device:TPU:0, one launch (start us, length us, event | category | flops | bytes accessed | tf_op | source)
XLA Modules:
  0.0 558.4 jit_solution(191220648716368934)
XLA Ops:
  12.4 3.0 collective-permute-start
  18.1 3.6 shard_map.263
  23.9 3.6 shard_map.264
  27.5 6.1 %collective-permute-done.refs_1_ = bf16[400,1024]{1,0:T(8,128)(2,1)S(1)} collective-permute-done((bf16[400,1024]{1,0:T(8,128)(2,1)S(1)}, bf16[400,1024]{1,0:T(8,128)(2,1)S(1)}, u32[]{:S(2)}, u32[]{:S(2)}) %collective-permute-start) | collective-permute-done | bytes 819232 | tf_op jit(solution)/shard_map/ppermute | solution.py:44
  35.1 5.1 all-to-all-start
  40.3 3.7 shard_map.265
  47.2 2.7 slice_bitcast_fusion
  51.3 4.7 shard_map.267
  58.4 19.4 %all-to-all-done.refs_2_.refs_4_ = bf16[4,128,1536]{2,1,0:T(8,128)(2,1)S(1)} async-done(((bf16[4,128,1536]{2,1,0:T(8,128)(2,1)}), bf16[4,128,1536]{2,1,0:T(8,128)(2,1)S(1)}, u32[]{:S(2)}, u32[]{:S(2)}) %all-to-all-start) | async-done | bytes 1572896 | tf_op jit(solution)/shard_map/all_to_all | solution.py:837
  85.2 4.6 collective-permute-start.5
  95.2 8.9 %shard_map.268 = (bf16[256,768]{1,0:T(8,128)(2,1)}, f32[128,1536]{1,0:T(8,128)}, bf16[128,1536]{1,0:T(8,128)(2,1)}) custom-call(s32[1]{0:T(128)} %bitcast.1.index_ref, bf16[256,768]{1,0:T(8,128)(2,1)} %get-tuple-element.542.q_ref, s32[256,1]{1,0:T(8,128)} %copy.46.low_ref, s32[256,1]{1,0:T(8,128)} %fusion.19.high_ref, s32[1,768]{1,0:T(1,128)} %broadcast_in_dim.97.key_ref, ...), custom_call_target="tpu_custom_call" | custom-call | flops 4400000000 | bytes 14400000 | tf_op jit(solution)/shard_map/pallas_call | solution.py:291
  106.6 11.6 %collective-permute-done.7.refs_3_.refs_5_ = bf16[4,128,1536]{2,1,0:T(8,128)(2,1)S(1)} collective-permute-done((bf16[4,128,1536]{2,1,0:T(8,128)(2,1)S(1)}, bf16[4,128,1536]{2,1,0:T(8,128)(2,1)S(1)}, u32[]{:S(2)}, u32[]{:S(2)}) %collective-permute-start.7) | collective-permute-done | bytes 1572896 | tf_op jit(solution)/shard_map/ppermute | solution.py:44
  118.2 8.0 %collective-permute-done.6.other_ref = bf16[128,1536]{1,0:T(8,128)(2,1)S(1)} collective-permute-done((bf16[128,1536]{1,0:T(8,128)(2,1)}, bf16[128,1536]{1,0:T(8,128)(2,1)S(1)}, u32[]{:S(2)}, u32[]{:S(2)}) %collective-permute-start.6) | collective-permute-done | bytes 393248 | tf_op jit(solution)/shard_map/ppermute | solution.py:44
  129.5 11.1 %collective-permute-done.8 = bf16[128,1536]{1,0:T(8,128)(2,1)S(1)} collective-permute-done((bf16[128,1536]{1,0:T(8,128)(2,1)}, bf16[128,1536]{1,0:T(8,128)(2,1)S(1)}, u32[]{:S(2)}, u32[]{:S(2)}) %collective-permute-start.8) | collective-permute-done | bytes 393248 | tf_op jit(solution)/shard_map/ppermute | solution.py:44
  143.6 2.6 collective-permute-start.12
  146.2 24.9 %collective-permute-done.11 = bf16[128,1536]{1,0:T(8,128)(2,1)S(1)} collective-permute-done((bf16[128,1536]{1,0:T(8,128)(2,1)}, bf16[128,1536]{1,0:T(8,128)(2,1)S(1)}, u32[]{:S(2)}, u32[]{:S(2)}) %collective-permute-start.11) | collective-permute-done | bytes 393248 | tf_op jit(solution)/shard_map/ppermute | solution.py:44
  172.0 7.4 %collective-permute-done.12 = bf16[128,1536]{1,0:T(8,128)(2,1)S(1)} collective-permute-done((bf16[128,1536]{1,0:T(8,128)(2,1)S(1)}, bf16[128,1536]{1,0:T(8,128)(2,1)S(1)}, u32[]{:S(2)}, u32[]{:S(2)}) %collective-permute-start.12) | collective-permute-done | bytes 393248 | tf_op jit(solution)/shard_map/ppermute | solution.py:44
  180.0 15.1 %shard_map.270 = (bf16[3,1024,768]{2,1,0:T(8,128)(2,1)}, f32[512,1536]{1,0:T(8,128)}, f32[512,1536]{1,0:T(8,128)}) custom-call(s32[1]{0:T(128)} %bitcast.22.limit_ref, s32[1]{0:T(128)} %bitcast.19.ctx_ref, bf16[256,1536]{1,0:T(8,128)(2,1)} %copy-done.33, bf16[256,1536]{1,0:T(8,128)(2,1)} %copy-done.42, bf16[4,128,1536]{2,1,0:T(8,128)(2,1)} %copy-done, ...), custom_call_target="tpu_custom_call" | custom-call | flops 8249999872 | bytes 27000000 | tf_op jit(solution)/shard_map/pallas_call | solution.py:387
  195.1 3.8 collective-permute-done.13.refs_3_.refs_1_
  199.9 8.0 %shard_map.271 = (bf16[2,768,1024]{2,1,0:T(8,128)(2,1)}, bf16[2,768,1024]{2,1,0:T(8,128)(2,1)}) custom-call(s32[1]{0:T(128)} %bitcast.1.index_ref, s32[1]{0:T(128)} %bitcast.19.ctx_ref, bf16[256,1536]{1,0:T(8,128)(2,1)} %copy-done.33, bf16[256,1536]{1,0:T(8,128)(2,1)} %copy-done.42, bf16[256,1536]{1,0:T(8,128)(2,1)} %copy-done.2, ...), custom_call_target="tpu_custom_call" | custom-call | flops 3849999872 | bytes 12600000 | tf_op jit(solution)/shard_map/pallas_call | solution.py:440
  207.9 10.5 %shard_map.272.act_ref = bf16[3,1024,768]{2,1,0:T(8,128)(2,1)} custom-call(s32[1]{0:T(128)} %bitcast.22.limit_ref, s32[1]{0:T(128)} %bitcast.19.ctx_ref, bf16[256,1536]{1,0:T(8,128)(2,1)} %copy-done.2, bf16[256,1536]{1,0:T(8,128)(2,1)} %copy-done.7, bf16[4,128,1536]{2,1,0:T(8,128)(2,1)} %copy-done, ...), custom_call_target="tpu_custom_call", output_to_operand_aliasing={{}: (7, {})} | custom-call | flops 4950000128 | bytes 16200000 | tf_op jit(solution)/shard_map/pallas_call | solution.py:387
  218.9 16.8 %shard_map.273 = (bf16[3,1024,768]{2,1,0:T(8,128)(2,1)}, f32[512,1536]{1,0:T(8,128)}, f32[512,1536]{1,0:T(8,128)}) custom-call(s32[1]{0:T(128)} %constant.138.clone.1.limit_ref, s32[1]{0:T(128)} %bitcast.19.ctx_ref, bf16[256,1536]{1,0:T(8,128)(2,1)} %copy-done.33, bf16[256,1536]{1,0:T(8,128)(2,1)} %copy-done.42, bf16[4,128,1536]{2,1,0:T(8,128)(2,1)} %copy-done, ...), custom_call_target="tpu_custom_call" | custom-call | flops 8249999872 | bytes 27000000 | tf_op jit(solution)/shard_map/pallas_call | solution.py:387
  237.4 12.3 %shard_map.274 = (bf16[3,384,768]{2,1,0:T(8,128)(2,1)}, bf16[3,384,768]{2,1,0:T(8,128)(2,1)}) custom-call(bf16[2,768,1024]{2,1,0:T(8,128)(2,1)} %get-tuple-element.533.own_ref, bf16[2,768,1024]{2,1,0:T(8,128)(2,1)} %copy-done.41, bf16[3,1024,768]{2,1,0:T(8,128)(2,1)} %shard_map.272.act_ref, bf16[3,1024,768]{2,1,0:T(8,128)(2,1)} %collective-permute-done.15.act_beside_ref), custom_call_target="tpu_custom_call" | custom-call | flops 6600000000 | bytes 21600000 | tf_op jit(solution)/shard_map/pallas_call | solution.py:462
  249.7 10.0 %shard_map.275.act_ref = bf16[3,1024,768]{2,1,0:T(8,128)(2,1)} custom-call(s32[1]{0:T(128)} %constant.138.clone.1.limit_ref, s32[1]{0:T(128)} %bitcast.19.ctx_ref, bf16[256,1536]{1,0:T(8,128)(2,1)} %copy-done.2, bf16[256,1536]{1,0:T(8,128)(2,1)} %copy-done.7, bf16[4,128,1536]{2,1,0:T(8,128)(2,1)} %copy-done, ...), custom_call_target="tpu_custom_call", output_to_operand_aliasing={{}: (7, {})} | custom-call | flops 4950000128 | bytes 16200000 | tf_op jit(solution)/shard_map/pallas_call | solution.py:387
  259.9 16.3 %shard_map.276 = (bf16[3,1024,768]{2,1,0:T(8,128)(2,1)}, f32[128,1536]{1,0:T(8,128)}, f32[128,1536]{1,0:T(8,128)}, bf16[128,1536]{1,0:T(8,128)(2,1)}, bf16[128,1...) custom-call(s32[1]{0:T(128)} %constant.138.clone.1.limit_ref, ...), custom_call_target="tpu_custom_call" | custom-call | flops 8249999872 | bytes 27000000 | tf_op jit(solution)/shard_map/pallas_call | solution.py:387
  276.2 10.3 %shard_map.277.act_ref = bf16[3,1024,768]{2,1,0:T(8,128)(2,1)} custom-call(s32[1]{0:T(128)} %constant.138.clone.1.limit_ref, s32[1]{0:T(128)} %bitcast.19.ctx_ref, bf16[256,1536]{1,0:T(8,128)(2,1)} %copy-done.2, bf16[256,1536]{1,0:T(8,128)(2,1)} %copy-done.7, bf16[4,128,1536]{2,1,0:T(8,128)(2,1)} %copy-done, ...), custom_call_target="tpu_custom_call", output_to_operand_aliasing={{}: (7, {})} | custom-call | flops 4950000128 | bytes 16200000 | tf_op jit(solution)/shard_map/pallas_call | solution.py:387
  290.3 10.0 %collective-permute-done.18 = bf16[128,1536]{1,0:T(8,128)(2,1)S(1)} collective-permute-done((bf16[128,1536]{1,0:T(8,128)(2,1)S(1)}, bf16[128,1536]{1,0:T(8,128)(2,1)S(1)}, u32[]{:S(2)}, u32[]{:S(2)}) %collective-permute-start.18) | collective-permute-done | bytes 393248 | tf_op jit(solution)/shard_map/ppermute | solution.py:44
  301.1 6.5 %collective-permute-done.17.across_ref = bf16[128,1536]{1,0:T(8,128)(2,1)} collective-permute-done((bf16[128,1536]{1,0:T(8,128)(2,1)S(1)}, bf16[128,1536]{1,0:T(8,128)(2,1)}, u32[]{:S(2)}, u32[]{:S(2)}) %collective-permute-start.17) | collective-permute-done | bytes 393248 | tf_op jit(solution)/shard_map/ppermute | solution.py:44
  307.6 12.1 %shard_map.278 = (bf16[3,384,768]{2,1,0:T(8,128)(2,1)}, bf16[3,384,768]{2,1,0:T(8,128)(2,1)}) custom-call(bf16[2,768,1024]{2,1,0:T(8,128)(2,1)} %get-tuple-element.533.own_ref, bf16[2,768,1024]{2,1,0:T(8,128)(2,1)} %copy-done.41, bf16[3,1024,768]{2,1,0:T(8,128)(2,1)} %shard_map.275.act_ref, bf16[3,1024,768]{2,1,0:T(8,128)(2,1)} %collective-permute-done.21.act_beside_ref), custom_call_target="tpu_custom_call" | custom-call | flops 6600000000 | bytes 21600000 | tf_op jit(solution)/shard_map/pallas_call | solution.py:462
  320.5 8.1 %collective-permute-done.20 = bf16[3,384,768]{2,1,0:T(8,128)(2,1)S(1)} collective-permute-done((bf16[3,384,768]{2,1,0:T(8,128)(2,1)}, bf16[3,384,768]{2,1,0:T(8,128)(2,1)S(1)}, u32[]{:S(2)}, u32[]{:S(2)}) %collective-permute-start.20) | collective-permute-done | bytes 1769504 | tf_op jit(solution)/shard_map/ppermute | solution.py:44
  332.4 3.9 shard_map.279
  337.0 12.1 %shard_map.280 = (bf16[3,384,768]{2,1,0:T(8,128)(2,1)}, bf16[3,384,768]{2,1,0:T(8,128)(2,1)}) custom-call(bf16[2,768,1024]{2,1,0:T(8,128)(2,1)} %get-tuple-element.533.own_ref, bf16[2,768,1024]{2,1,0:T(8,128)(2,1)} %copy-done.41, bf16[3,1024,768]{2,1,0:T(8,128)(2,1)} %shard_map.277.act_ref, bf16[3,1024,768]{2,1,0:T(8,128)(2,1)} %collective-permute-done.23.act_beside_ref), custom_call_target="tpu_custom_call" | custom-call | flops 6600000000 | bytes 21600000 | tf_op jit(solution)/shard_map/pallas_call | solution.py:462
  355.3 10.7 %shard_map.281 = (bf16[256,768]{1,0:T(8,128)(2,1)}, f32[256,256]{1,0:T(8,128)}, bf16[256,256]{1,0:T(8,128)(2,1)}, bf16[256,256]{1,0:T(8,128)(2,1)}) custom-call(s32[1]{0:T(128)} %bitcast.1.index_ref, bf16[256,768]{1,0:T(8,128)(2,1)} %get-tuple-element.542.q_ref, s32[256,1]{1,0:T(8,128)} %copy.47.low_ref, s32[256,1]{1,0:T(8,128)} %fusion.19.high_ref, ...), custom_call_target="tpu_custom_call" | custom-call | flops 5500000256 | bytes 18000000 | tf_op jit(solution)/shard_map/pallas_call | solution.py:545
  376.0 4.3 collective-permute-done.26.refs_6_
  380.9 4.7 shard_map.282
  389.9 5.2 shard_map.283
  401.3 2.8 shard_map.284
  404.1 13.2 %collective-permute-done.32 = bf16[768,384]{1,0:T(8,128)(2,1)} collective-permute-done((bf16[768,384]{1,0:T(8,128)(2,1)S(1)}, bf16[768,384]{1,0:T(8,128)(2,1)}, u32[]{:S(2)}, u32[]{:S(2)}) %collective-permute-start.32) | collective-permute-done | bytes 589856 | tf_op jit(solution)/shard_map/ppermute | solution.py:44
  422.4 10.8 %collective-permute-done.30 = bf16[384,1024]{1,0:T(8,128)(2,1)} collective-permute-done((bf16[384,1024]{1,0:T(8,128)(2,1)}, bf16[384,1024]{1,0:T(8,128)(2,1)}, u32[]{:S(2)}, u32[]{:S(2)}) %collective-permute-start.30) | collective-permute-done | bytes 786464 | tf_op jit(solution)/shard_map/ppermute | solution.py:44
  434.8 8.3 %collective-permute-done.36 = bf16[384,384]{1,0:T(8,128)(2,1)S(1)} collective-permute-done((bf16[384,384]{1,0:T(8,128)(2,1)S(1)}, bf16[384,384]{1,0:T(8,128)(2,1)S(1)}, u32[]{:S(2)}, u32[]{:S(2)}) %collective-permute-start.36) | collective-permute-done | bytes 294944 | tf_op jit(solution)/shard_map/ppermute | solution.py:44
  445.3 45.9 %collective-permute-done.34 = bf16[384,512]{1,0:T(8,128)(2,1)S(1)} collective-permute-done((bf16[384,512]{1,0:T(8,128)(2,1)S(1)}, bf16[384,512]{1,0:T(8,128)(2,1)S(1)}, u32[]{:S(2)}, u32[]{:S(2)}) %collective-permute-start.34) | collective-permute-done | bytes 393248 | tf_op jit(solution)/shard_map/ppermute | solution.py:44
  496.6 7.3 %collective-permute-done.39 = bf16[384,256]{1,0:T(8,128)(2,1)S(1)} collective-permute-done((bf16[384,256]{1,0:T(8,128)(2,1)S(1)}, bf16[384,256]{1,0:T(8,128)(2,1)S(1)}, u32[]{:S(2)}, u32[]{:S(2)}) %collective-permute-start.39) | collective-permute-done | bytes 196640 | tf_op jit(solution)/shard_map/ppermute | solution.py:44
  504.1 5.4 shard_map.285
  509.5 2.8 collective-permute-done.38
  522.2 2.5 collective-permute-done.46
  528.2 5.3 shard_map.286
  533.6 2.8 collective-permute-start.48
  537.8 8.2 %collective-permute-done.49 = bf16[384,512]{1,0:T(8,128)(2,1)S(1)} collective-permute-done((bf16[384,512]{1,0:T(8,128)(2,1)S(1)}, bf16[384,512]{1,0:T(8,128)(2,1)S(1)}, u32[]{:S(2)}, u32[]{:S(2)}) %collective-permute-start.49) | collective-permute-done | bytes 393248 | tf_op jit(solution)/shard_map/ppermute | solution.py:44
  (301 shorter events, 115.8 us)
Async XLA Ops:
  12.4 21.2 %collective-permute-start = (bf16[400,1024]{1,0:T(8,128)(2,1)S(1)}, bf16[400,1024]{1,0:T(8,128)(2,1)S(1)}, u32[]{:S(2)}, u32[]{:S(2)}) collective-permute-start(bf16[400,1024]{1,0:T(8,128)(2,1)S(1)} %fusion.5.refs_0_), channel_id=1, source_target_pairs={{0,16},{8,24},{16,0},{24,8},{1,17},{9,25},{17,1},{25,9},{2,18},{10... | collective-permute-start | bytes 2457608 | tf_op jit(solution)/shard_map/ppermute | solution.py:44
  35.1 12.1 %collective-permute-start.1 = (bf16[2,400,1024]{2,1,0:T(8,128)(2,1)}, bf16[2,400,1024]{2,1,0:T(8,128)(2,1)}, u32[]{:S(2)}, u32[]{:S(2)}) collective-permute-start(bf16[2,400,1024]{2,1,0:T(8,128)(2,1)} %pad_maximum_fusion), channel_id=1, source_target_pairs={{0,8},{8,0},{16,24},{24,16},{1,9},{9,1},{17,25},{25,17},{2,10},{10... | collective-permute-start | bytes 4915208 | tf_op jit(solution)/shard_map/ppermute | solution.py:44
  35.1 42.8 %all-to-all-start = ((bf16[4,128,1536]{2,1,0:T(8,128)(2,1)}), bf16[4,128,1536]{2,1,0:T(8,128)(2,1)S(1)}, u32[]{:S(2)}, u32[]{:S(2)}) async-start(bf16[4,128,1536]{2,1,0:T(8,128)(2,1)} %broadcast_in_dim.86), calls=%async_computation | async-start | bytes 3145728 | tf_op jit(solution)/shard_map/all_to_all | solution.py:837
  40.2 139.8 %all-gather.11.cloned.1.call-start = ((), (), s32[]{:S(2)}) async-start(), calls=%async_computation.3 | async-start | bytes 8847360 | tf_op jit(solution)/shard_map/all_gather | solution.py:922
  44.1 33.7 %collective-permute-start.2 = (bf16[768,384]{1,0:T(8,128)(2,1)S(1)}, bf16[768,384]{1,0:T(8,128)(2,1)}, u32[]{:S(2)}, u32[]{:S(2)}) collective-permute-start(bf16[768,384]{1,0:T(8,128)(2,1)S(1)} %convert_element_type.119.refs_0_.refs_2_), channel_id=1, source_target_pairs={{0,16},{8,24},{16,0},{24,8},{1,17},{9,25},{17,1},{25,9},{2,18},{10... | collective-permute-start | bytes 1769480 | tf_op jit(solution)/shard_map/ppermute | solution.py:44
  77.9 141.1 %all-gather.9.cloned.1.call-start = ((), (), s32[]{:S(2)}) async-start(), calls=%async_computation.2 | async-start | bytes 8847360 | tf_op jit(solution)/shard_map/all_gather | solution.py:922
  78.6 181.2 %all-gather.7.cloned.1.call-start = ((), (), s32[]{:S(2)}) async-start(), calls=%async_computation.1 | async-start | bytes 8847360 | tf_op jit(solution)/shard_map/all_gather | solution.py:922
  80.9 11.1 %collective-permute-start.3 = (bf16[2,768,384]{2,1,0:T(8,128)(2,1)}, bf16[2,768,384]{2,1,0:T(8,128)(2,1)}, u32[]{:S(2)}, u32[]{:S(2)}) collective-permute-start(bf16[2,768,384]{2,1,0:T(8,128)(2,1)} %pad_maximum_fusion.1), channel_id=1, source_target_pairs={{0,8},{8,0},{16,24},{24,16},{1,9},{9,1},{17,25},{25,17},{2,10},{10... | collective-permute-start | bytes 3538952 | tf_op jit(solution)/shard_map/ppermute | solution.py:44
  80.9 37.3 %collective-permute-start.7 = (bf16[4,128,1536]{2,1,0:T(8,128)(2,1)S(1)}, bf16[4,128,1536]{2,1,0:T(8,128)(2,1)S(1)}, u32[]{:S(2)}, u32[]{:S(2)}) collective-permute-start(bf16[4,128,1536]{2,1,0:T(8,128)(2,1)S(1)} %all-to-all-done.refs_2_.refs_4_), channel_id=1, source_target_pairs={{0,1},{1,0},{2,3},{3,2},{4,5},{5,4},{6,7},{7,6},{8,9},{9,8},{10,11... | collective-permute-start | bytes 4718600 | tf_op jit(solution)/shard_map/ppermute | solution.py:44
  104.1 22.1 %collective-permute-start.6 = (bf16[128,1536]{1,0:T(8,128)(2,1)}, bf16[128,1536]{1,0:T(8,128)(2,1)S(1)}, u32[]{:S(2)}, u32[]{:S(2)}) collective-permute-start(bf16[128,1536]{1,0:T(8,128)(2,1)} %get-tuple-element.412), channel_id=1, source_target_pairs={{0,1},{1,0},{2,3},{3,2},{4,5},{5,4},{6,7},{7,6},{8,9},{9,8},{10,11... | collective-permute-start | bytes 1179656 | tf_op jit(solution)/shard_map/ppermute | solution.py:44
  106.6 22.9 %collective-permute-start.9 = (bf16[256,1536]{1,0:T(8,128)(2,1)}, bf16[256,1536]{1,0:T(8,128)(2,1)}, u32[]{:S(2)}, u32[]{:S(2)}) collective-permute-start(bf16[256,1536]{1,0:T(8,128)(2,1)} %pad_maximum_fusion.3), channel_id=1, source_target_pairs={{0,8},{8,0},{16,24},{24,16},{1,9},{9,1},{17,25},{25,17},{2,10},{10... | collective-permute-start | bytes 2359304 | tf_op jit(solution)/shard_map/ppermute | solution.py:44
  129.5 11.1 %collective-permute-start.8 = (bf16[128,1536]{1,0:T(8,128)(2,1)}, bf16[128,1536]{1,0:T(8,128)(2,1)S(1)}, u32[]{:S(2)}, u32[]{:S(2)}) collective-permute-start(bf16[128,1536]{1,0:T(8,128)(2,1)} %get-tuple-element.425), channel_id=1, source_target_pairs={{0,2},{2,0},{4,6},{6,4},{1,3},{3,1},{5,7},{7,5},{8,10},{10,8},{12,... | collective-permute-start | bytes 1179656 | tf_op jit(solution)/shard_map/ppermute | solution.py:44
  141.7 29.4 %collective-permute-start.10 = (bf16[256,1536]{1,0:T(8,128)(2,1)S(1)}, bf16[256,1536]{1,0:T(8,128)(2,1)S(1)}, u32[]{:S(2)}, u32[]{:S(2)}) collective-permute-start(bf16[256,1536]{1,0:T(8,128)(2,1)S(1)} %constant_dynamic-update-slice_fusion.refs_0_), channel_id=1, source_target_pairs={{0,1},{1,0},{2,3},{3,2},{4,5},{5,4},{6,7},{7,6},{8,9},{9,8},{10,11... | collective-permute-start | bytes 2359304 | tf_op jit(solution)/shard_map/ppermute | solution.py:44
  143.3 27.8 %collective-permute-start.11 = (bf16[128,1536]{1,0:T(8,128)(2,1)}, bf16[128,1536]{1,0:T(8,128)(2,1)S(1)}, u32[]{:S(2)}, u32[]{:S(2)}) collective-permute-start(bf16[128,1536]{1,0:T(8,128)(2,1)} %get-tuple-element.425), channel_id=1, source_target_pairs={{0,4},{2,6},{4,0},{6,2},{1,5},{3,7},{5,1},{7,3},{8,12},{10,14},{12... | collective-permute-start | bytes 1179656 | tf_op jit(solution)/shard_map/ppermute | solution.py:44
  143.6 35.8 %collective-permute-start.12 = (bf16[128,1536]{1,0:T(8,128)(2,1)S(1)}, bf16[128,1536]{1,0:T(8,128)(2,1)S(1)}, u32[]{:S(2)}, u32[]{:S(2)}) collective-permute-start(bf16[128,1536]{1,0:T(8,128)(2,1)S(1)} %collective-permute-done.8), channel_id=1, source_target_pairs={{0,4},{2,6},{4,0},{6,2},{1,5},{3,7},{5,1},{7,3},{8,12},{10,14},{12... | collective-permute-start | bytes 1179656 | tf_op jit(solution)/shard_map/ppermute | solution.py:44
  179.5 19.5 %collective-permute-start.13 = (bf16[256,1536]{1,0:T(8,128)(2,1)S(1)}, bf16[256,1536]{1,0:T(8,128)(2,1)S(1)}, u32[]{:S(2)}, u32[]{:S(2)}) collective-permute-start(bf16[256,1536]{1,0:T(8,128)(2,1)S(1)} %constant_dynamic-update-slice_fusion.2.refs_2_.refs_0_), channel_id=1, source_target_pairs={{0,1},{1,0},{2,3},{3,2},{4,5},{5,4},{6,7},{7,6},{8,9},{9,8},{10,11... | collective-permute-start | bytes 2359304 | tf_op jit(solution)/shard_map/ppermute | solution.py:44
  218.4 17.4 %collective-permute-start.15 = (bf16[3,1024,768]{2,1,0:T(8,128)(2,1)}, bf16[3,1024,768]{2,1,0:T(8,128)(2,1)}, u32[]{:S(2)}, u32[]{:S(2)}) collective-permute-start(bf16[3,1024,768]{2,1,0:T(8,128)(2,1)} %shard_map.272.act_ref), channel_id=1, source_target_pairs={{0,8},{8,0},{16,24},{24,16},{1,9},{9,1},{17,25},{25,17},{2,10},{10... | collective-permute-start | bytes 14155784 | tf_op jit(solution)/shard_map/ppermute | solution.py:44
  218.4 17.3 %collective-permute-start.14 = (bf16[2,768,1024]{2,1,0:T(8,128)(2,1)}, bf16[2,768,1024]{2,1,0:T(8,128)(2,1)S(1)}, u32[]{:S(2)}, u32[]{:S(2)}) collective-permute-start(bf16[2,768,1024]{2,1,0:T(8,128)(2,1)} %get-tuple-element.475), channel_id=1, source_target_pairs={{0,8},{8,0},{16,24},{24,16},{1,9},{9,1},{17,25},{25,17},{2,10},{10... | collective-permute-start | bytes 9437192 | tf_op jit(solution)/shard_map/ppermute | solution.py:44
  259.7 47.9 %collective-permute-start.21 = (bf16[3,1024,768]{2,1,0:T(8,128)(2,1)}, bf16[3,1024,768]{2,1,0:T(8,128)(2,1)}, u32[]{:S(2)}, u32[]{:S(2)}) collective-permute-start(bf16[3,1024,768]{2,1,0:T(8,128)(2,1)} %shard_map.275.act_ref), channel_id=1, source_target_pairs={{0,8},{8,0},{16,24},{24,16},{1,9},{9,1},{17,25},{25,17},{2,10},{10... | collective-permute-start | bytes 14155784 | tf_op jit(solution)/shard_map/ppermute | solution.py:44
  286.5 49.8 %collective-permute-start.23 = (bf16[3,1024,768]{2,1,0:T(8,128)(2,1)}, bf16[3,1024,768]{2,1,0:T(8,128)(2,1)}, u32[]{:S(2)}, u32[]{:S(2)}) collective-permute-start(bf16[3,1024,768]{2,1,0:T(8,128)(2,1)} %shard_map.277.act_ref), channel_id=1, source_target_pairs={{0,8},{8,0},{16,24},{24,16},{1,9},{9,1},{17,25},{25,17},{2,10},{10... | collective-permute-start | bytes 14155784 | tf_op jit(solution)/shard_map/ppermute | solution.py:44
  287.0 41.7 %collective-permute-start.20 = (bf16[3,384,768]{2,1,0:T(8,128)(2,1)}, bf16[3,384,768]{2,1,0:T(8,128)(2,1)S(1)}, u32[]{:S(2)}, u32[]{:S(2)}) collective-permute-start(bf16[3,384,768]{2,1,0:T(8,128)(2,1)} %get-tuple-element.480), channel_id=1, source_target_pairs={{0,16},{8,24},{16,0},{24,8},{1,17},{9,25},{17,1},{25,9},{2,18},{10... | collective-permute-start | bytes 5308424 | tf_op jit(solution)/shard_map/ppermute | solution.py:44
  288.2 12.0 %collective-permute-start.18 = (bf16[128,1536]{1,0:T(8,128)(2,1)S(1)}, bf16[128,1536]{1,0:T(8,128)(2,1)S(1)}, u32[]{:S(2)}, u32[]{:S(2)}) collective-permute-start(bf16[128,1536]{1,0:T(8,128)(2,1)S(1)} %copy-done.45), channel_id=1, source_target_pairs={{0,1},{1,0},{2,3},{3,2},{4,5},{5,4},{6,7},{7,6},{8,9},{9,8},{10,11... | collective-permute-start | bytes 1179656 | tf_op jit(solution)/shard_map/ppermute | solution.py:44
  288.8 18.7 %collective-permute-start.17 = (bf16[128,1536]{1,0:T(8,128)(2,1)S(1)}, bf16[128,1536]{1,0:T(8,128)(2,1)}, u32[]{:S(2)}, u32[]{:S(2)}) collective-permute-start(bf16[128,1536]{1,0:T(8,128)(2,1)S(1)} %copy-done.44), channel_id=1, source_target_pairs={{0,1},{1,0},{2,3},{3,2},{4,5},{5,4},{6,7},{7,6},{8,9},{9,8},{10,11... | collective-permute-start | bytes 1179656 | tf_op jit(solution)/shard_map/ppermute | solution.py:44
  301.1 31.3 %collective-permute-start.19 = (bf16[128,1536]{1,0:T(8,128)(2,1)}, bf16[128,1536]{1,0:T(8,128)(2,1)}, u32[]{:S(2)}, u32[]{:S(2)}) collective-permute-start(bf16[128,1536]{1,0:T(8,128)(2,1)} %add_convert_fusion.5), channel_id=1, source_target_pairs={{0,2},{2,0},{4,6},{6,4},{1,3},{3,1},{5,7},{7,5},{8,10},{10,8},{12,... | collective-permute-start | bytes 1179656 | tf_op jit(solution)/shard_map/ppermute | solution.py:44
  319.7 48.9 %collective-permute-start.28 = (bf16[3,384,768]{2,1,0:T(8,128)(2,1)}, bf16[3,384,768]{2,1,0:T(8,128)(2,1)S(1)}, u32[]{:S(2)}, u32[]{:S(2)}) collective-permute-start(bf16[3,384,768]{2,1,0:T(8,128)(2,1)} %get-tuple-element.522), channel_id=1, source_target_pairs={{0,16},{8,24},{16,0},{24,8},{1,17},{9,25},{17,1},{25,9},{2,18},{10... | collective-permute-start | bytes 5308424 | tf_op jit(solution)/shard_map/ppermute | solution.py:44
  332.3 40.1 %collective-permute-start.27 = (bf16[3,384,768]{2,1,0:T(8,128)(2,1)S(1)}, bf16[3,384,768]{2,1,0:T(8,128)(2,1)}, u32[]{:S(2)}, u32[]{:S(2)}) collective-permute-start(bf16[3,384,768]{2,1,0:T(8,128)(2,1)S(1)} %add_convert_fusion.2.refs_0_), channel_id=1, source_target_pairs={{0,2},{2,0},{4,6},{6,4},{1,3},{3,1},{5,7},{7,5},{8,10},{10,8},{12,... | collective-permute-start | bytes 5308424 | tf_op jit(solution)/shard_map/ppermute | solution.py:44
  336.3 12.8 %collective-permute-start.22 = (bf16[128,1536]{1,0:T(8,128)(2,1)}, bf16[128,1536]{1,0:T(8,128)(2,1)}, u32[]{:S(2)}, u32[]{:S(2)}) collective-permute-start(bf16[128,1536]{1,0:T(8,128)(2,1)} %get-tuple-element.548.refs_0_), channel_id=1, source_target_pairs={{0,1},{1,0},{2,3},{3,2},{4,5},{5,4},{6,7},{7,6},{8,9},{9,8},{10,11... | collective-permute-start | bytes 1179656 | tf_op jit(solution)/shard_map/ppermute | solution.py:44
  352.5 66.6 %collective-permute-start.31 = (bf16[3,384,768]{2,1,0:T(8,128)(2,1)}, bf16[3,384,768]{2,1,0:T(8,128)(2,1)}, u32[]{:S(2)}, u32[]{:S(2)}) collective-permute-start(bf16[3,384,768]{2,1,0:T(8,128)(2,1)} %get-tuple-element.537), channel_id=1, source_target_pairs={{0,16},{8,24},{16,0},{24,8},{1,17},{9,25},{17,1},{25,9},{2,18},{10... | collective-permute-start | bytes 5308424 | tf_op jit(solution)/shard_map/ppermute | solution.py:44
  366.0 9.9 %collective-permute-start.25 = (bf16[256,256]{1,0:T(8,128)(2,1)}, bf16[256,256]{1,0:T(8,128)(2,1)S(1)}, u32[]{:S(2)}, u32[]{:S(2)}) collective-permute-start(bf16[256,256]{1,0:T(8,128)(2,1)} %get-tuple-element.559), channel_id=1, source_target_pairs={{2,0},{4,2},{6,4},{3,1},{5,3},{7,5},{10,8},{12,10},{14,12},{11,9},... | collective-permute-start | bytes 393224 | tf_op jit(solution)/shard_map/ppermute | solution.py:50
  367.3 12.9 %collective-permute-start.26 = (bf16[256,256]{1,0:T(8,128)(2,1)}, bf16[256,256]{1,0:T(8,128)(2,1)S(1)}, u32[]{:S(2)}, u32[]{:S(2)}) collective-permute-start(bf16[256,256]{1,0:T(8,128)(2,1)} %get-tuple-element.560), channel_id=1, source_target_pairs={{4,0},{6,2},{5,1},{7,3},{12,8},{14,10},{13,9},{15,11},{20,16},{22,... | collective-permute-start | bytes 393224 | tf_op jit(solution)/shard_map/ppermute | solution.py:50
  386.9 30.3 %collective-permute-start.32 = (bf16[768,384]{1,0:T(8,128)(2,1)S(1)}, bf16[768,384]{1,0:T(8,128)(2,1)}, u32[]{:S(2)}, u32[]{:S(2)}) collective-permute-start(bf16[768,384]{1,0:T(8,128)(2,1)S(1)} %slice.364), channel_id=1, source_target_pairs={{0,16},{8,24},{16,0},{24,8},{1,17},{9,25},{17,1},{25,9},{2,18},{10... | collective-permute-start | bytes 1769480 | tf_op jit(solution)/shard_map/ppermute | solution.py:44
  387.8 12.3 %collective-permute-start.33 = (bf16[128,1536]{1,0:T(8,128)(2,1)}, bf16[128,1536]{1,0:T(8,128)(2,1)}, u32[]{:S(2)}, u32[]{:S(2)}) collective-permute-start(bf16[128,1536]{1,0:T(8,128)(2,1)} %get-tuple-element.591), channel_id=1, source_target_pairs={{0,1},{1,0},{2,3},{3,2},{4,5},{5,4},{6,7},{7,6},{8,9},{9,8},{10,11... | collective-permute-start | bytes 1179656 | tf_op jit(solution)/shard_map/ppermute | solution.py:44
  389.3 102.1 %collective-permute-start.16 = (bf16[256,1536]{1,0:T(8,128)(2,1)}, bf16[256,1536]{1,0:T(8,128)(2,1)}, u32[]{:S(2)}, u32[]{:S(2)}) collective-permute-start(bf16[256,1536]{1,0:T(8,128)(2,1)} %get-tuple-element.500), channel_id=1, source_target_pairs={{0,1},{1,0},{2,3},{3,2},{4,5},{5,4},{6,7},{7,6},{8,9},{9,8},{10,11... | collective-permute-start | bytes 2359304 | tf_op jit(solution)/shard_map/ppermute | solution.py:44
  395.2 50.2 %collective-permute-start.35 = (bf16[3,384,768]{2,1,0:T(8,128)(2,1)S(1)}, bf16[3,384,768]{2,1,0:T(8,128)(2,1)}, u32[]{:S(2)}, u32[]{:S(2)}) collective-permute-start(bf16[3,384,768]{2,1,0:T(8,128)(2,1)S(1)} %add_convert_fusion.1.refs_0_), channel_id=1, source_target_pairs={{0,2},{2,0},{4,6},{6,4},{1,3},{3,1},{5,7},{7,5},{8,10},{10,8},{12,... | collective-permute-start | bytes 5308424 | tf_op jit(solution)/shard_map/ppermute | solution.py:44
  400.0 33.2 %collective-permute-start.30 = (bf16[384,1024]{1,0:T(8,128)(2,1)}, bf16[384,1024]{1,0:T(8,128)(2,1)}, u32[]{:S(2)}, u32[]{:S(2)}) collective-permute-start(bf16[384,1024]{1,0:T(8,128)(2,1)} %slice.363), channel_id=1, source_target_pairs={{0,16},{8,24},{16,0},{24,8},{1,17},{9,25},{17,1},{25,9},{2,18},{10... | collective-permute-start | bytes 2359304 | tf_op jit(solution)/shard_map/ppermute | solution.py:44
  417.3 17.5 %collective-permute-start.37 = (bf16[128,1536]{1,0:T(8,128)(2,1)}, bf16[128,1536]{1,0:T(8,128)(2,1)S(1)}, u32[]{:S(2)}, u32[]{:S(2)}) collective-permute-start(bf16[128,1536]{1,0:T(8,128)(2,1)} %get-tuple-element.597), channel_id=1, source_target_pairs={{0,1},{1,0},{2,3},{3,2},{4,5},{5,4},{6,7},{7,6},{8,9},{9,8},{10,11... | collective-permute-start | bytes 1179656 | tf_op jit(solution)/shard_map/ppermute | solution.py:44
  419.2 23.9 %collective-permute-start.36 = (bf16[384,384]{1,0:T(8,128)(2,1)S(1)}, bf16[384,384]{1,0:T(8,128)(2,1)S(1)}, u32[]{:S(2)}, u32[]{:S(2)}) collective-permute-start(bf16[384,384]{1,0:T(8,128)(2,1)S(1)} %select_convert_fusion.1), channel_id=1, source_target_pairs={{0,2},{2,0},{4,6},{6,4},{1,3},{3,1},{5,7},{7,5},{8,10},{10,8},{12,... | collective-permute-start | bytes 884744 | tf_op jit(solution)/shard_map/ppermute | solution.py:44
  433.2 95.0 %collective-permute-start.51 = (bf16[3,384,768]{2,1,0:T(8,128)(2,1)S(1)}, bf16[3,384,768]{2,1,0:T(8,128)(2,1)}, u32[]{:S(2)}, u32[]{:S(2)}) collective-permute-start(bf16[3,384,768]{2,1,0:T(8,128)(2,1)S(1)} %add_convert_fusion.refs_0_), channel_id=1, source_target_pairs={{0,2},{2,0},{4,6},{6,4},{1,3},{3,1},{5,7},{7,5},{8,10},{10,8},{12,... | collective-permute-start | bytes 5308424 | tf_op jit(solution)/shard_map/ppermute | solution.py:44
  443.1 48.1 %collective-permute-start.34 = (bf16[384,512]{1,0:T(8,128)(2,1)S(1)}, bf16[384,512]{1,0:T(8,128)(2,1)S(1)}, u32[]{:S(2)}, u32[]{:S(2)}) collective-permute-start(bf16[384,512]{1,0:T(8,128)(2,1)S(1)} %select_convert_fusion), channel_id=1, source_target_pairs={{0,2},{2,0},{4,6},{6,4},{1,3},{3,1},{5,7},{7,5},{8,10},{10,8},{12,... | collective-permute-start | bytes 1179656 | tf_op jit(solution)/shard_map/ppermute | solution.py:44
  443.3 50.2 %collective-permute-start.40 = (bf16[192,384]{1,0:T(8,128)(2,1)S(1)}, bf16[192,384]{1,0:T(8,128)(2,1)S(1)}, u32[]{:S(2)}, u32[]{:S(2)}) collective-permute-start(bf16[192,384]{1,0:T(8,128)(2,1)S(1)} %select_convert_fusion.3), channel_id=1, source_target_pairs={{0,4},{2,6},{4,0},{6,2},{1,5},{3,7},{5,1},{7,3},{8,12},{10,14},{12... | collective-permute-start | bytes 442376 | tf_op jit(solution)/shard_map/ppermute | solution.py:44
  493.5 10.4 %collective-permute-start.39 = (bf16[384,256]{1,0:T(8,128)(2,1)S(1)}, bf16[384,256]{1,0:T(8,128)(2,1)S(1)}, u32[]{:S(2)}, u32[]{:S(2)}) collective-permute-start(bf16[384,256]{1,0:T(8,128)(2,1)S(1)} %select_convert_fusion.2), channel_id=1, source_target_pairs={{0,4},{2,6},{4,0},{6,2},{1,5},{3,7},{5,1},{7,3},{8,12},{10,14},{12... | collective-permute-start | bytes 589832 | tf_op jit(solution)/shard_map/ppermute | solution.py:44
  493.6 18.7 %collective-permute-start.38 = (bf16[128,1536]{1,0:T(8,128)(2,1)}, bf16[128,1536]{1,0:T(8,128)(2,1)}, u32[]{:S(2)}, u32[]{:S(2)}) collective-permute-start(bf16[128,1536]{1,0:T(8,128)(2,1)} %get-tuple-element.683), channel_id=1, source_target_pairs={{0,2},{2,0},{4,6},{6,4},{1,3},{3,1},{5,7},{7,5},{8,10},{10,8},{12,... | collective-permute-start | bytes 1179656 | tf_op jit(solution)/shard_map/ppermute | solution.py:44
  495.6 20.2 %collective-permute-start.44 = (bf16[192,384]{1,0:T(8,128)(2,1)S(1)}, bf16[192,384]{1,0:T(8,128)(2,1)}, u32[]{:S(2)}, u32[]{:S(2)}) collective-permute-start(bf16[192,384]{1,0:T(8,128)(2,1)S(1)} %add_convert_fusion.7), channel_id=1, source_target_pairs={{0,4},{2,6},{4,0},{6,2},{1,5},{3,7},{5,1},{7,3},{8,12},{10,14},{12... | collective-permute-start | bytes 442376 | tf_op jit(solution)/shard_map/ppermute | solution.py:44
  504.0 14.1 %collective-permute-start.43 = (bf16[384,256]{1,0:T(8,128)(2,1)S(1)}, bf16[384,256]{1,0:T(8,128)(2,1)S(1)}, u32[]{:S(2)}, u32[]{:S(2)}) collective-permute-start(bf16[384,256]{1,0:T(8,128)(2,1)S(1)} %add_convert_fusion.6), channel_id=1, source_target_pairs={{0,4},{2,6},{4,0},{6,2},{1,5},{3,7},{5,1},{7,3},{8,12},{10,14},{12... | collective-permute-start | bytes 589832 | tf_op jit(solution)/shard_map/ppermute | solution.py:44
  518.3 18.1 %collective-permute-start.41 = (bf16[128,1536]{1,0:T(8,128)(2,1)S(1)}, bf16[128,1536]{1,0:T(8,128)(2,1)S(1)}, u32[]{:S(2)}, u32[]{:S(2)}) collective-permute-start(bf16[128,1536]{1,0:T(8,128)(2,1)S(1)} %copy-done.21), channel_id=1, source_target_pairs={{0,1},{1,0},{2,3},{3,2},{4,5},{5,4},{6,7},{7,6},{8,9},{9,8},{10,11... | collective-permute-start | bytes 1179656 | tf_op jit(solution)/shard_map/ppermute | solution.py:44
  526.2 22.1 %collective-permute-start.50 = (bf16[384,384]{1,0:T(8,128)(2,1)S(1)}, bf16[384,384]{1,0:T(8,128)(2,1)}, u32[]{:S(2)}, u32[]{:S(2)}) collective-permute-start(bf16[384,384]{1,0:T(8,128)(2,1)S(1)} %pad_maximum_fusion.10), channel_id=1, source_target_pairs={{0,2},{2,0},{4,6},{6,4},{1,3},{3,1},{5,7},{7,5},{8,10},{10,8},{12,... | collective-permute-start | bytes 884744 | tf_op jit(solution)/shard_map/ppermute | solution.py:44
  528.2 17.8 %collective-permute-start.49 = (bf16[384,512]{1,0:T(8,128)(2,1)S(1)}, bf16[384,512]{1,0:T(8,128)(2,1)S(1)}, u32[]{:S(2)}, u32[]{:S(2)}) collective-permute-start(bf16[384,512]{1,0:T(8,128)(2,1)S(1)} %pad_maximum_fusion.9), channel_id=1, source_target_pairs={{0,2},{2,0},{4,6},{6,4},{1,3},{3,1},{5,7},{7,5},{8,10},{10,8},{12,... | collective-permute-start | bytes 1179656 | tf_op jit(solution)/shard_map/ppermute | solution.py:44
  533.6 14.5 %collective-permute-start.48 = (f32[16,1536]{1,0:T(8,128)S(1)}, f32[16,1536]{1,0:T(8,128)S(1)}, u32[]{:S(2)}, u32[]{:S(2)}) collective-permute-start(f32[16,1536]{1,0:T(8,128)S(1)} %add.255), channel_id=1, source_target_pairs={{0,4},{2,6},{4,0},{6,2},{1,5},{3,7},{5,1},{7,3},{8,12},{10,14},{12... | collective-permute-start | bytes 294920 | tf_op jit(solution)/shard_map/ppermute | solution.py:44
  (62 other events, 634.5 us)
Sparse Core Ops, SparseCore 0:
  78.0 49.9 all-gather.10
  130.1 50.8 all-gather.8
  182.5 50.8 all-gather.6

commit v3 on v2

--- a/solution.py
+++ b/solution.py
@@ -134,9 +134,12 @@
     return pieces
 
 
+SCALE = 0.5
+
+
 def cost(us=1):
     return pl.CostEstimate(
-        flops=int(us * 0.55e9), bytes_accessed=int(us * 1.8e6), transcendentals=0
+        flops=int(us * SCALE * 1.1e9), bytes_accessed=int(us * SCALE * 3.6e6), transcendentals=0
     )
 
 
@@ -315,10 +318,13 @@
     )(x, mine, other, gain)
 
 
-def feed_body(count, base, back, carried, last, filled, at_row, limit_ref, ctx_ref, *refs):
-    (h_own, h_across, g_own, g_across, w_ref), refs = refs[:5], refs[5:]
+def feed_body(
+    count, bases, back, carried, last, filled, at_row, limit_ref, ctx_ref, *refs
+):
+    h_refs, refs = refs[: 2 * len(bases)], refs[2 * len(bases) :]
+    (g_own, g_across, w_ref), refs = refs[:3], refs[3:]
     carry, refs = refs[: 2 * carried], refs[2 * carried + filled :]
-    outs, (act_ref, sem) = refs[:-2], refs[-2:]
+    outs, (act_ref, sems) = refs[:-2], refs[-2:]
     gate_w, up_w, down_w = (
         jnp.concatenate([w_ref[i, k] for i in range(count)], axis=0) for k in range(3)
     )
@@ -328,7 +334,8 @@
     half = g_own.shape[1]
     chunk = 2 * half
     at = 0
-    for h_ref, g_ref in ((h_own, g_own), (h_across, g_across)):
+    for which, h_ref in enumerate(h_refs):
+        base, g_ref = bases[which // 2], (g_own, g_across)[which % 2]
         for j in range(h_ref.shape[0] // chunk):
             rows_in = h_ref[j * chunk : (j + 1) * chunk]
             grads_in = jnp.concatenate(
@@ -346,54 +353,57 @@
             act_ref[1, at : at + chunk] = jnp.where(shown, d_up, 0.0).astype(bf16)
             act_ref[2, at : at + chunk] = jnp.where(shown, hidden, 0.0).astype(bf16)
             at += chunk
-    copy = pltpu.make_async_copy(act_ref, outs[0].at[:, pl.ds(at_row, rows), :], sem)
-    copy.start()
+    copies = [
+        pltpu.make_async_copy(act_ref.at[k], outs[k].at[pl.ds(at_row, rows)], sems.at[k])
+        for k in range(3)
+    ]
+    for copy in copies:
+        copy.start()
     if back:
-        d_rows = dot_cols(act_ref[0], gate_w) + dot_cols(act_ref[1], up_w)
-        out_rows = dot_cols(act_ref[2], down_w)
+        team = slice(0, 2 * chunk)
+        d_rows = dot_cols(act_ref[0, team], gate_w) + dot_cols(act_ref[1, team], up_w)
+        out_rows = dot_cols(act_ref[2, team], down_w)
         if carried:
             d_rows = d_rows + carry[0][...]
             out_rows = out_rows + carry[1][...]
         if last:
-            cuts = [(i * half, (i + 1) * half) for i in range(4)]
-            for ref, (low, high) in zip(outs[1:5], cuts):
-                ref[...] = d_rows[low:high].astype(ref.dtype)
-            cuts = cuts[:2] + [(2 * half, 4 * half)]
-            for ref, (low, high) in zip(outs[5:], cuts):
-                ref[...] = out_rows[low:high].astype(ref.dtype)
+            cuts = ((0, half), (half, 2 * half), (2 * half, 4 * half))
+            for group, total in ((outs[3:6], d_rows), (outs[6:], out_rows)):
+                for ref, (low, high) in zip(group, cuts):
+                    ref[...] = total[low:high].astype(ref.dtype)
         else:
-            outs[1][...] = d_rows
-            outs[2][...] = out_rows
-    copy.wait()
+            outs[3][...] = d_rows
+            outs[4][...] = out_rows
+    for copy in copies:
+        copy.wait()
 
 
 def feed(limit, ctx, rows_in, grads_in, weights, total, back, carry=(), last=False, act=None):
     some = sum(r.shape[0] for r in rows_in)
     width = weights.shape[3]
-    outs = [jax.ShapeDtypeStruct((3, total, width), bf16)]
+    outs = [jax.ShapeDtypeStruct((total, width), bf16)] * 3
     half = grads_in[0].shape[1]
     if back and last:
-        outs += [jax.ShapeDtypeStruct((half, D), f32)] * 2
-        outs += [jax.ShapeDtypeStruct((half, D), bf16)] * 2
-        outs += [jax.ShapeDtypeStruct((half, D), f32)] * 2
-        outs += [jax.ShapeDtypeStruct((2 * half, D), bf16)]
+        group = [jax.ShapeDtypeStruct((half, D), f32)] * 2
+        outs += (group + [jax.ShapeDtypeStruct((2 * half, D), bf16)]) * 2
     elif back:
-        outs += [jax.ShapeDtypeStruct((some, D), f32)] * 2
+        outs += [jax.ShapeDtypeStruct((4 * half, D), f32)] * 2
     vmem = pl.BlockSpec(memory_space=pltpu.VMEM)
     smem = pl.BlockSpec(memory_space=pltpu.SMEM)
     hbm = pl.BlockSpec(memory_space=pl.ANY)
     inputs = (*rows_in, *grads_in, weights, *carry)
-    filled = () if act is None else (act,)
+    filled = () if act is None else tuple(act)
     return pl.pallas_call(
         functools.partial(
-            feed_body, weights.shape[0], 0 if back else TEAM, back, len(carry) // 2, last,
-            len(filled), 0 if back else total - some,
+            feed_body, weights.shape[0],
+            ((0,) if back else ()) + ((TEAM,) if some == total or not back else ()),
+            back, len(carry) // 2, last, len(filled), 0 if back else total - some,
         ),
         out_shape=tuple(outs),
         in_specs=[smem, smem] + [vmem] * len(inputs) + [hbm] * len(filled),
-        out_specs=tuple([hbm] + [vmem] * (len(outs) - 1)),
-        scratch_shapes=[pltpu.VMEM((3, some, width), bf16), pltpu.SemaphoreType.DMA],
-        input_output_aliases={2 + len(inputs): 0} if filled else {},
+        out_specs=tuple([hbm] * 3 + [vmem] * (len(outs) - 3)),
+        scratch_shapes=[pltpu.VMEM((3, some, width), bf16), pltpu.SemaphoreType.DMA((3,))],
+        input_output_aliases={2 + len(inputs) + k: k for k in range(len(filled))},
         compiler_params=params(60),
         cost_estimate=cost((6 if back else 0) + 9 * some / 512),
     )(limit, ctx, *inputs, *filled)
@@ -446,28 +456,30 @@
     )(index, ctx, *rows, *grads)
 
 
-def weight_body(own_ref, beside_ref, act_ref, act_beside_ref, near_ref, far_ref):
+def weight_body(own_ref, beside_ref, *refs):
+    acts, acts_beside, (near_ref, far_ref) = refs[:3], refs[3:6], refs[6:]
     cut = near_ref.shape[1]
-    value = dot_plain(own_ref[0], act_ref[0]) + dot_plain(beside_ref[0], act_beside_ref[0])
-    near_ref[0] = value[:cut].astype(bf16)
-    far_ref[0] = value[cut:].astype(bf16)
-
-
-def weight_grads(own, beside, act, act_beside):
-    total, width = act.shape[1:]
-    cut = D // 4
-    left = pl.BlockSpec((1, D // 2, total), lambda k: (k // 2, 0, 0))
-    right = pl.BlockSpec((1, total, width), lambda k: (k, 0, 0))
-    out = pl.BlockSpec((1, cut, width), lambda k: (k, 0, 0))
+    for k in range(3):
+        value = dot_plain(own_ref[k // 2], acts[k][...])
+        value = value + dot_plain(beside_ref[k // 2], acts_beside[k][...])
+        near_ref[k] = value[:cut].astype(bf16)
+        far_ref[k] = value[cut:].astype(bf16)
+
+
+def weight_grads(own, beside, acts, acts_beside):
+    total, width = acts[0].shape
+    left = pl.BlockSpec(own.shape, lambda j: (0, 0, 0), pipeline_mode=pl.Buffered(1))
+    right = pl.BlockSpec((total, WIDE), lambda j: (0, j))
+    out = pl.BlockSpec((3, D // 4, WIDE), lambda j: (0, 0, j))
     return pl.pallas_call(
         weight_body,
-        out_shape=(jax.ShapeDtypeStruct((3, cut, width), bf16),) * 2,
-        grid=(3,),
-        in_specs=[left, left, right, right],
+        out_shape=(jax.ShapeDtypeStruct((3, D // 4, width), bf16),) * 2,
+        grid=(width // WIDE,),
+        in_specs=[left, left] + [right] * 6,
         out_specs=(out, out),
         compiler_params=params(60),
         cost_estimate=cost(12),
-    )(own, beside, act, act_beside)
+    )(own, beside, *acts, *acts_beside)
 
 
 def middle_back_body(
@@ -782,42 +794,24 @@
         both = mine_first(values)
         return both[:half], both[half:]
 
-    pair = n_ctx == 4
-
     class Rows:
         def __init__(self, mine):
             self.mine = mine
             self.beside = swap(mine, "context", 1)
 
-        def early(self):
-            if pair:
-                self.remote_mine = swap(self.mine, "context", 2)
-
         def turn(self):
             self.beside = run.pin(self.beside)
-
-        def across_team(self):
             self.held = run(stack, self.mine, self.beside)
             self.held_across = swap(self.held, "tensor", 1)
-
-        def pin_early(self):
-            if pair:
-                self.remote_mine = run.pin(self.remote_mine)
-
-        def late(self):
-            if pair:
-                self.remote_beside = swap(self.beside, "context", 2)
-                return
             held, others = self.held, []
             for bit in bits_of(n_ctx)[1:]:
                 there = swap(held, "context", bit)
                 others.append(there)
                 held = stack(held, there)
-            self.remote = stack(*others)
+            self.remote = others[0] if len(others) == 1 else stack(*others)
 
         def across_rest(self):
-            if pair:
-                self.remote = run(stack, self.remote_mine, self.remote_beside)
+            self.remote = run.pin(self.remote)
             self.remote_across = swap(self.remote, "tensor", 1)
 
         def pin_team(self):
@@ -833,8 +827,7 @@
             return (self.remote, self.remote_across)
 
     grad_mine, _ = run(arrange, cotangent)
-    grads_own = run(lambda v: jnp.broadcast_to(v[None], (n_ctx,) + v.shape), grad_mine)
-    grads_own = lax.all_to_all(grads_own, "context", split_axis=0, concat_axis=0)
+    grads_own = lax.all_gather(grad_mine, "context")
 
     ff_local = w_gate.shape[1]
     tiles = ff_local // LANES
@@ -896,6 +889,7 @@
     far = qkv_h.turn()
     out_h = Pieces(run, out_cast, far)
     feed_in += [packed(i) for i in range(2, PARTS)]
+    feed_w = [lax.all_gather(after(v, far), "fsdp") for v in feed_in]
     low, high, key_at, cos_table, sin_table = run(places, lengths, span_order)
     qkv_h.finish()
 
@@ -915,11 +909,10 @@
         index, mine_tokens, other_tokens, gains, bias, cos_table, sin_table, qkv_w,
     )
     kv_parts = [kv_own] + [shift(kv_own, "context", step) for step in range(1, behind + 1)]
-    normed_rel = run(lambda v: to_relative(v, my_fsdp, n_fsdp), normed)
     grads_own = run.pin(grads_own)
     grads = (grads_own, swap(grads_own, "tensor", 1))
-    far = out_h.turn()
-    feed_w = [lax.all_gather(after(v, far), "fsdp") for v in feed_in]
+    normed_rel = run(lambda v: to_relative(v, my_fsdp, n_fsdp), normed)
+    out_h.turn()
     kv_parts = [kv_own] + list(run.pin(tuple(kv_parts[1:])))
     out_h.finish()
     out_w = in_order(out_h.pieces(), 1)
@@ -935,33 +928,32 @@
         middle_norm, mine_tokens, branch_mine, branch_other, gains
     )
     lines = Rows(normed_two)
-    lines.early()
     early_beside = run.pin(early_beside)
     attended_beside, normed_beside = early_beside[:, :q_width], early_beside[:, q_width:]
     lines.turn()
-    lines.across_team()
-    lines.pin_early()
-    lines.late()
     lines.pin_team()
-    lines.across_rest()
 
     limits = [limit.reshape(1)] + [jnp.zeros((1,), jnp.int32)] * (PARTS - 1)
     acts, acts_beside = {}, {}
     total_rows = n_ctx * rows
 
-    def feed_team(index, carry, last=False):
-        acts[index], *carry = run(
+    def feed_team(index, carry, last=False, every=False):
+        rows_in = lines.team() + lines.rest() if every else lines.team()
+        results = run(
             lambda *a: feed(*a[:5], total_rows, True, a[5], last),
-            limits[index], ctx, lines.team(), grads, feed_w[index], carry,
+            limits[index], ctx, rows_in, grads, feed_w[index], carry,
         )
-        return tuple(carry)
+        acts[index] = tuple(results[:3])
+        if every:
+            acts_beside[index] = tuple(swap(a, "fsdp", 1) for a in acts[index])
+        return tuple(results[3:])
 
     def feed_rest(index):
-        (acts[index],) = run(
+        acts[index] = run(
             lambda *a: feed(*a[:5], total_rows, False, act=a[5]),
             limits[index], ctx, lines.rest(), grads, feed_w[index], acts[index],
         )
-        acts_beside[index] = swap(acts[index], "fsdp", 1)
+        acts_beside[index] = tuple(swap(a, "fsdp", 1) for a in acts[index])
 
     waiting, reduced, other_parts = {}, {}, {}
 
@@ -985,26 +977,26 @@
         other_parts[index] = swap(reduced[index], "context", 1)
 
     carry = feed_team(0, ())
+    lines.across_rest()
+    carry = feed_team(1, carry)
     lines.pin_rest()
     turned, turned_sent = run(
         lambda *a: turn_rows(*a, n_fsdp), index, ctx, lines.team() + lines.rest(), grads
     )
     turned_beside = swap(turned_sent, "fsdp", 1)
     feed_rest(0)
-    carry = feed_team(1, carry)
+    feed_rest(1)
     grads_of(0)
-    feed_rest(1)
     given = feed_team(2, carry, True)
-    d_near, d_beside, d_far, d_far_beside = given[:4]
-    out_near, out_beside, out_far = given[4:]
-    d_far_beside, d_far = swap(d_far_beside, "tensor", 1), swap(d_far, "tensor", 1)
+    d_near, d_beside, d_far, out_near, out_beside, out_far = given
+    d_far = swap(d_far, "tensor", 1)
     feed_rest(2)
-    d_beside = swap(run(give, d_beside, d_far_beside), "context", 1)
-    d_far = run.pin(d_far)
     grads_of(1)
+    d_beside = swap(run(lambda a, b: give(a, b[half:]), d_beside, d_far), "context", 1)
     add_far(0)
     d_middle, d_branch, grad_gain_two = run(
-        middle_back, d_near, d_far, d_beside, middle, gains, grad_mine
+        lambda a, b, *c: middle_back(a, b[:half], *c),
+        d_near, d_far, d_beside, middle, gains, grad_mine,
     )
     d_branch_other = swap(d_branch, "tensor", 1)
     grads_of(2)
@@ -1020,8 +1012,8 @@
     dkv_parts = [dkv_parts[0]] + [
         shift(p, "context", -step - 1) for step, p in enumerate(dkv_parts[1:])
     ]
-    add_far(1)
     other_parts[0] = run.pin(other_parts[0])
+    reduced[1] = run(give, *waiting[1])
 
     def halves(values, axis):
         cut = values.shape[axis] // 2
@@ -1084,75 +1076,77 @@
 
             return run(both, self.value, self.sent)
 
-    reduce_o = Reduce(1, attended, attended_beside, d_all, d_all_beside)
-    reduce_o.first()
-    d_qkv, dn_mine, dn_other, grad_bias = run(
-        project_back, index, dq_low, cos_table, sin_table, qkv_w, dkv_parts
-    )
-    d_qkv_beside = swap(d_qkv, "fsdp", 1)
-    dn_other = swap(dn_other, "tensor", 1)
-    placed = ()
-
     def place_part(index, placed):
         return run(
             lambda m, a, b, c: place(m, a, b, index, starts, fresh, ff_local, c),
             member.reshape(1), reduced[index], other_parts[index], placed,
         )
 
-    placed = place_part(0, placed)
+    def smalls(gain_rows, gain_other, grad_bias):
+        gain_rows = jnp.pad(gain_rows + gain_other, ((0, 6), (0, 0)))
+        biases = jnp.pad(grad_bias.reshape(all_heads, HD), ((0, 0), (0, D - HD)))
+        return stack(gain_rows, biases)
+
+    steps = [("fsdp", bit) for bit in bits_of(n_fsdp)] + [("context", bit) for bit in bits_of(n_ctx)]
+
+    def small_step(small):
+        name, bit = steps.pop(0)
+        return run(jnp.add, small, swap(small, name, bit))
+
+    reduce_o = Reduce(1, attended, attended_beside, d_all, d_all_beside)
+    reduce_o.first()
+    dkv_parts = dkv_parts[:1] + list(run.pin(tuple(dkv_parts[1:])))
+    other_parts[1] = swap(after(reduced[1], dkv_parts[-1]), "context", 1)
+    d_qkv, dn_mine, dn_other, grad_bias = run(
+        project_back, index, dq_low, cos_table, sin_table, qkv_w, dkv_parts
+    )
+    d_qkv_beside = swap(d_qkv, "fsdp", 1)
+    dn_other = swap(dn_other, "tensor", 1)
+    placed = place_part(0, ())
     reduce_qkv = Reduce(0, d_qkv, d_qkv_beside, normed_rel, normed_beside)
     reduce_qkv.first()
     d_inputs, grad_gain_one = run(
         input_back, dn_mine, dn_other, mine_tokens, gains, d_middle
     )
+    d_inputs_other = swap(d_inputs, "tensor", 1)
+    add_far(2)
+    d_inputs_other = run.pin(d_inputs_other)
+    other_parts[1] = run.pin(other_parts[1])
     reduce_o.step()
-    add_far(2)
-    d_inputs_other = swap(d_inputs, "tensor", 1)
+    gain_rows = run(stack, grad_gain_one, grad_gain_two)
+    gain_other = swap(gain_rows, "tensor", 1)
+    out_far = swap(after(out_far, other_parts[1]), "tensor", 1)
     reduce_qkv.step()
-    d_inputs_other = run.pin(d_inputs_other)
-    out_far = swap(out_far, "tensor", 1)
-    reduce_o.step()
-    other_parts[1] = run.pin(other_parts[1])
-    reduce_qkv.step()
+    small = run(smalls, gain_rows, gain_other, grad_bias)
+    placed = place_part(1, placed)
     out_mine, out_beside = run(
         lambda a, b, c: (a + c[:half].astype(f32), give(b, c[half:])), out_near, out_beside, out_far
     )
-    out_beside = swap(out_beside, "context", 1)
+    small = small_step(small)
+    small = small_step(small)
     reduce_o.step()
     reduce_qkv.step()
-    placed = place_part(1, placed)
+    out_beside = swap(out_beside, "context", 1)
+    other_parts[2] = run.pin(other_parts[2])
+    reduce_o.step()
+    reduce_qkv.step()
+    small = small_step(small)
+    reduce_o.step()
     out_half = run(
         lambda a, b, c: (a + b + c.astype(f32)).astype(bf16), middle, out_mine, out_beside
     )
     out_half_other = swap(out_half, "tensor", 1)
-
-    gain_rows = run(stack, grad_gain_one, grad_gain_two)
-    gain_other = swap(gain_rows, "tensor", 1)
-
-    def smalls(gain_rows, gain_other, grad_bias):
-        gain_rows = jnp.pad(gain_rows + gain_other, ((0, 6), (0, 0)))
-        biases = jnp.pad(grad_bias.reshape(all_heads, HD), ((0, 0), (0, D - HD)))
-        return stack(gain_rows, biases)
-
-    reduce_o.step()
     reduce_qkv.step()
-    small = run(smalls, gain_rows, gain_other, grad_bias)
-    steps = [("fsdp", bit) for bit in bits_of(n_fsdp)] + [("context", bit) for bit in bits_of(n_ctx)]
-
-    def small_step(small):
-        name, bit = steps.pop(0)
-        return run(jnp.add, small, swap(small, name, bit))
-
     small = small_step(small)
+    placed = place_part(2, placed)
     while reduce_o.back:
         reduce_o.step()
         reduce_qkv.step()
-        small = small_step(small)
     while steps:
         small = small_step(small)
+    grad_gate, grad_up, grad_down = placed
     grad_o = reduce_o.join().astype(f32)
     grad_qkv = reduce_qkv.join().astype(f32)
-    grad_gate, grad_up, grad_down = place_part(2, placed)
     grad_biases = small[8 : 8 + all_heads, :bias_cols]
     small_gains = small[:2, :shard]
     for f in range(1, n_fsdp):

time: 566 us -> 498 us (0.88)
  waiting for transfers between devices: 225 us -> 159 us
  local copies, waits for them, and re-layouts: 29.3 us -> 22.7 us
  starting transfers between devices: 52.7 us -> 59.3 us
    ppermute x48 -> x52, waiting for transfers between devices: 199 us -> 149 us  [swap(): return lax.ppermute(values, axis_name, [(i, i ^ bit) for i in range(size)])]
    all_to_all x1 -> x0, waiting for transfers between devices: 19.4 us -> none  [per_device(): lax.all_to_all(grads_own, 'context', split_axis=0, concat_axis=0)]
    ppermute x48 -> x52, starting transfers between devices: 38.4 us -> 48.5 us  [swap(): return lax.ppermute(values, axis_name, [(i, i ^ bit) for i in range(size)])]
    unnamed x105 -> x96, local copies, waits for them, and re-layouts: 12.1 us -> 9.22 us
  transfers between devices with their start and end apart: 56 -> 60, of which waited for: 23 -> 26; matrix products, arithmetic and copies ran while one was open for 10% -> 10% of each run, Pallas kernels for 34% -> 39%
where the time goes in v3:
time: 498 us; the launch traced here: 491 us
  Pallas kernels  192 us (39%)
  waiting for transfers between devices  159 us (32%)
  starting transfers between devices  59.3 us (12%)
  other arithmetic  38.7 us (8%)
  local copies, waits for them, and re-layouts  22.7 us (5%)
  between operations  15.3 us (3%)
    ppermute x52, waiting for transfers between devices, swap(): return lax.ppermute(values, axis_name, [(i, i ^ bit) for i in range(size)])  149 us
    pallas_call x6, Pallas kernels, feed(): pl.pallas_call(functools.partial(feed_body, weights.shape[0], ((0,) if ba...  78.6 us
    ppermute x52, starting transfers between devices, swap(): return lax.ppermute(values, axis_name, [(i, i ^ bit) for i in range(size)])  48.5 us
    pallas_call x3, Pallas kernels, weight_grads(): pl.pallas_call(weight_body, out_shape=(jax.ShapeDtypeStruct((3, D // 4, w...  39.8 us
    pallas_call x3, Pallas kernels, place(): pl.pallas_call(functools.partial(place_body, plan, len(carry)), out_shape...  15.8 us
    convert_element_type x7, other arithmetic, give(): return (near.astype(f32) + arrived.astype(f32)).astype(bf16)  11.3 us
    pallas_call x3, Pallas kernels, pack(): pl.pallas_call(functools.partial(pack_body, count), out_shape=jax.ShapeDt...  11.2 us
    pallas_call x1, Pallas kernels, attend_back(): pl.pallas_call(functools.partial(attend_back_body, len(weights), len(kv_p...  10.7 us
  transfers between devices with their start and end apart: 60, of which 26 were waited for; matrix products, arithmetic and copies ran while one was open for 10% of the time, Pallas kernels for 39%

profile of v3, /device:TPU:0, one launch (start us, length us, event | category | flops | bytes accessed | tf_op | source)
XLA Modules:
  0.0 491.0 jit_solution(13652159833464611779)
XLA Ops:
  15.0 3.0 collective-permute-start
  18.0 3.7 shard_map.263
  22.6 3.7 shard_map.264
  26.4 9.8 %collective-permute-done.refs_1_ = bf16[400,1024]{1,0:T(8,128)(2,1)S(1)} collective-permute-done((bf16[400,1024]{1,0:T(8,128)(2,1)S(1)}, bf16[400,1024]{1,0:T(8,128)(2,1)S(1)}, u32[]{:S(2)}, u32[]{:S(2)}) %collective-permute-start) | collective-permute-done | bytes 819232 | tf_op jit(solution)/shard_map/ppermute | solution.py:44
  38.4 3.7 shard_map.265
  48.4 4.7 shard_map.267
  62.7 3.5 collective-permute-start.4
  66.1 4.5 collective-permute-start.5
  75.5 8.9 %shard_map.268 = (bf16[256,768]{1,0:T(8,128)(2,1)}, f32[128,1536]{1,0:T(8,128)}, bf16[128,1536]{1,0:T(8,128)(2,1)}) custom-call(s32[1]{0:T(128)} %bitcast.1.index_ref, bf16[256,768]{1,0:T(8,128)(2,1)} %get-tuple-element.604.q_ref, s32[256,1]{1,0:T(8,128)} %copy.52.low_ref, s32[256,1]{1,0:T(8,128)} %fusion.19.high_ref, s32[1,768]{1,0:T(1,128)} %broadcast_in_dim.90.key_ref, ...), custom_call_target="tpu_custom_call" | custom-call | flops 4400000000 | bytes 14400000 | tf_op jit(solution)/shard_map/pallas_call | solution.py:294
  86.1 11.6 %collective-permute-done.7.refs_3_.refs_5_ = bf16[4,128,1536]{2,1,0:T(8,128)(2,1)} collective-permute-done((bf16[4,128,1536]{2,1,0:T(8,128)(2,1)}, bf16[4,128,1536]{2,1,0:T(8,128)(2,1)}, u32[]{:S(2)}, u32[]{:S(2)}) %collective-permute-start.7) | collective-permute-done | bytes 1572896 | tf_op jit(solution)/shard_map/ppermute | solution.py:44
  97.7 7.9 %collective-permute-done.6.other_ref = bf16[128,1536]{1,0:T(8,128)(2,1)S(1)} collective-permute-done((bf16[128,1536]{1,0:T(8,128)(2,1)}, bf16[128,1536]{1,0:T(8,128)(2,1)S(1)}, u32[]{:S(2)}, u32[]{:S(2)}) %collective-permute-start.6) | collective-permute-done | bytes 393248 | tf_op jit(solution)/shard_map/ppermute | solution.py:44
  110.6 9.2 %collective-permute-done.8 = bf16[128,1536]{1,0:T(8,128)(2,1)S(1)} collective-permute-done((bf16[128,1536]{1,0:T(8,128)(2,1)}, bf16[128,1536]{1,0:T(8,128)(2,1)S(1)}, u32[]{:S(2)}, u32[]{:S(2)}) %collective-permute-start.8) | collective-permute-done | bytes 393248 | tf_op jit(solution)/shard_map/ppermute | solution.py:44
  125.3 14.1 %collective-permute-done.10.refs_1_ = bf16[256,1536]{1,0:T(8,128)(2,1)S(1)} collective-permute-done((bf16[256,1536]{1,0:T(8,128)(2,1)S(1)}, bf16[256,1536]{1,0:T(8,128)(2,1)S(1)}, u32[]{:S(2)}, u32[]{:S(2)}) %collective-permute-start.10) | collective-permute-done | bytes 786464 | tf_op jit(solution)/shard_map/ppermute | solution.py:44
  140.3 15.0 %shard_map.270 = (bf16[1024,768]{1,0:T(8,128)(2,1)}, bf16[1024,768]{1,0:T(8,128)(2,1)}, bf16[1024,768]{1,0:T(8,128)(2,1)}, f32[512,1536]{1,0:T(8,128)}, f32[512,1536]{1,0:T(8,128)}) custom-call(s32[1]{0:T(128)} %bitcast.23.limit_ref, s32[1]{0:T(128)} %bitcast.20.ctx_ref, bf16[256,1536]{1,0:T(8,128)(2,1)} %copy-done.27, bf16[256,1536]{1,0:T(8,128)(2,1)} %copy-done.37, ...), custom_call_target="tpu_custom_call" | custom-call | flops 8249999872 | bytes 27000000 | tf_op jit(solution)/shard_map/pallas_call | solution.py:396
  155.3 3.3 collective-permute-done.11.refs_2_.refs_0_
  159.8 17.2 %shard_map.271 = (bf16[1024,768]{1,0:T(8,128)(2,1)}, bf16[1024,768]{1,0:T(8,128)(2,1)}, bf16[1024,768]{1,0:T(8,128)(2,1)}, f32[512,1536]{1,0:T(8,128)}, f32[512,1536]{1,0:T(8,128)}) custom-call(s32[1]{0:T(128)} %constant.138.clone.1.limit_ref, s32[1]{0:T(128)} %bitcast.20.ctx_ref, bf16[256,1536]{1,0:T(8,128)(2,1)} %copy-done.27, ...), custom_call_target="tpu_custom_call" | custom-call | flops 8249999872 | bytes 27000000 | tf_op jit(solution)/shard_map/pallas_call | solution.py:396
  177.9 7.9 %shard_map.272 = (bf16[2,768,1024]{2,1,0:T(8,128)(2,1)}, bf16[2,768,1024]{2,1,0:T(8,128)(2,1)}) custom-call(s32[1]{0:T(128)} %bitcast.1.index_ref, s32[1]{0:T(128)} %bitcast.20.ctx_ref, bf16[256,1536]{1,0:T(8,128)(2,1)} %copy-done.27, bf16[256,1536]{1,0:T(8,128)(2,1)} %copy-done.37, bf16[256,1536]{1,0:T(8,128)(2,1)} %copy-done.36, ...), custom_call_target="tpu_custom_call" | custom-call | flops 3849999872 | bytes 12600000 | tf_op jit(solution)/shard_map/pallas_call | solution.py:450
  186.0 10.1 %shard_map.273 = (bf16[1024,768]{1,0:T(8,128)(2,1)}, bf16[1024,768]{1,0:T(8,128)(2,1)}, bf16[1024,768]{1,0:T(8,128)(2,1)}) custom-call(s32[1]{0:T(128)} %bitcast.23.limit_ref, s32[1]{0:T(128)} %bitcast.20.ctx_ref, bf16[256,1536]{1,0:T(8,128)(2,1)} %copy-done.36, ...), custom_call_target="tpu_custom_call", output_to_operand_aliasing={{0}: (7, {}), {1}: (8, {}), {2}: (9, {})} | custom-call | flops 4950000128 | bytes 16200000 | tf_op jit(solution)/shard_map/pallas_call | solution.py:396
  197.0 10.0 %shard_map.274 = (bf16[1024,768]{1,0:T(8,128)(2,1)}, bf16[1024,768]{1,0:T(8,128)(2,1)}, bf16[1024,768]{1,0:T(8,128)(2,1)}) custom-call(s32[1]{0:T(128)} %constant.138.clone.1.limit_ref, s32[1]{0:T(128)} %bitcast.20.ctx_ref, bf16[256,1536]{1,0:T(8,128)(2,1)} %copy-done.36, ...), custom_call_target="tpu_custom_call", output_to_operand_aliasing={{0}: (7, {}), {1}: (8, {}), {2}: (9, {})} | custom-call | flops 4950000128 | bytes 16200000 | tf_op jit(solution)/shard_map/pallas_call | solution.py:396
  209.6 13.3 %shard_map.275 = (bf16[3,384,768]{2,1,0:T(8,128)(2,1)}, bf16[3,384,768]{2,1,0:T(8,128)(2,1)}) custom-call(bf16[2,768,1024]{2,1,0:T(8,128)(2,1)} %get-tuple-element.591.own_ref, bf16[2,768,1024]{2,1,0:T(8,128)(2,1)} %copy-done.35, bf16[1024,768]{1,0:T(8,128)(2,1)} %get-tuple-element.528.refs_0_, bf16[1024,768]{1,0:T(8,128)(2,1)} %get-tuple-element.529.refs_1_, ...), custom_call_target="tpu_custom_call" | custom-call | flops 6600000000 | bytes 21600000 | tf_op jit(solution)/shard_map/pallas_call | solution.py:474
  224.3 16.2 %shard_map.276 = (bf16[1024,768]{1,0:T(8,128)(2,1)}, bf16[1024,768]{1,0:T(8,128)(2,1)}, bf16[1024,768]{1,0:T(8,128)(2,1)}, f32[128,1536]{1,0:T(8,128)}, f32[128,...) custom-call(s32[1]{0:T(128)} %constant.138.clone.1.limit_ref, ...), custom_call_target="tpu_custom_call" | custom-call | flops 8249999872 | bytes 27000000 | tf_op jit(solution)/shard_map/pallas_call | solution.py:396
  241.4 10.0 %shard_map.277 = (bf16[1024,768]{1,0:T(8,128)(2,1)}, bf16[1024,768]{1,0:T(8,128)(2,1)}, bf16[1024,768]{1,0:T(8,128)(2,1)}) custom-call(s32[1]{0:T(128)} %constant.138.clone.1.limit_ref, s32[1]{0:T(128)} %bitcast.20.ctx_ref, bf16[256,1536]{1,0:T(8,128)(2,1)} %copy-done.36, ...), custom_call_target="tpu_custom_call", output_to_operand_aliasing={{0}: (7, {}), {1}: (8, {}), {2}: (9, {})} | custom-call | flops 4950000128 | bytes 16200000 | tf_op jit(solution)/shard_map/pallas_call | solution.py:396
  252.1 13.3 %shard_map.278 = (bf16[3,384,768]{2,1,0:T(8,128)(2,1)}, bf16[3,384,768]{2,1,0:T(8,128)(2,1)}) custom-call(bf16[2,768,1024]{2,1,0:T(8,128)(2,1)} %get-tuple-element.591.own_ref, bf16[2,768,1024]{2,1,0:T(8,128)(2,1)} %copy-done.35, bf16[1024,768]{1,0:T(8,128)(2,1)} %get-tuple-element.565.refs_0_, bf16[1024,768]{1,0:T(8,128)(2,1)} %get-tuple-element.566.refs_1_, ...), custom_call_target="tpu_custom_call" | custom-call | flops 6600000000 | bytes 21600000 | tf_op jit(solution)/shard_map/pallas_call | solution.py:474
  271.6 6.7 %collective-permute-done.24.far_ref = bf16[128,1536]{1,0:T(8,128)(2,1)S(1)} collective-permute-done((bf16[128,1536]{1,0:T(8,128)(2,1)S(1)}, bf16[128,1536]{1,0:T(8,128)(2,1)S(1)}, u32[]{:S(2)}, u32[]{:S(2)}) %collective-permute-start.24) | collective-permute-done | bytes 393248 | tf_op jit(solution)/shard_map/ppermute | solution.py:44
  281.5 3.4 shard_map.279
  286.4 13.2 %shard_map.280 = (bf16[3,384,768]{2,1,0:T(8,128)(2,1)}, bf16[3,384,768]{2,1,0:T(8,128)(2,1)}) custom-call(bf16[2,768,1024]{2,1,0:T(8,128)(2,1)} %get-tuple-element.591.own_ref, bf16[2,768,1024]{2,1,0:T(8,128)(2,1)} %copy-done.35, bf16[1024,768]{1,0:T(8,128)(2,1)} %get-tuple-element.593.refs_0_, bf16[1024,768]{1,0:T(8,128)(2,1)} %get-tuple-element.594.refs_1_, ...), custom_call_target="tpu_custom_call" | custom-call | flops 6600000000 | bytes 21600000 | tf_op jit(solution)/shard_map/pallas_call | solution.py:474
  305.1 10.7 %shard_map.281 = (bf16[256,768]{1,0:T(8,128)(2,1)}, f32[256,256]{1,0:T(8,128)}, bf16[256,256]{1,0:T(8,128)(2,1)}, bf16[256,256]{1,0:T(8,128)(2,1)}) custom-call(s32[1]{0:T(128)} %bitcast.1.index_ref, bf16[256,768]{1,0:T(8,128)(2,1)} %get-tuple-element.604.q_ref, s32[256,1]{1,0:T(8,128)} %copy.53.low_ref, s32[256,1]{1,0:T(8,128)} %fusion.19.high_ref, ...), custom_call_target="tpu_custom_call" | custom-call | flops 5500000256 | bytes 18000000 | tf_op jit(solution)/shard_map/pallas_call | solution.py:557
  318.6 4.3 add_convert_fusion.1.refs_0_
  326.1 4.6 collective-permute-done.31.refs_6_
  331.4 4.7 shard_map.282
  336.8 5.2 %shard_map.283 = (f32[384,4480]{1,0:T(8,128)}, f32[384,4480]{1,0:T(8,128)}, f32[4480,384]{1,0:T(8,128)}) custom-call(s32[1]{0:T(128)} %bitcast.25.member_ref, bf16[3,384,768]{2,1,0:T(8,128)(2,1)} %copy-done.1, bf16[3,384,768]{2,1,0:T(8,128)(2,1)} %copy-done.9), custom_call_target="tpu_custom_call" | custom-call | flops 550000000 | bytes 1800000 | tf_op jit(solution)/shard_map/pallas_call | solution.py:673
  345.0 2.9 collective-permute-done.33.other_ref
  347.9 2.8 shard_map.284
  358.8 2.7 collective-permute-done.35
  362.9 14.9 %collective-permute-done.32.refs_1_ = bf16[3,384,768]{2,1,0:T(8,128)(2,1)} collective-permute-done((bf16[3,384,768]{2,1,0:T(8,128)(2,1)}, bf16[3,384,768]{2,1,0:T(8,128)(2,1)}, u32[]{:S(2)}, u32[]{:S(2)}) %collective-permute-start.32) | collective-permute-done | bytes 1769504 | tf_op jit(solution)/shard_map/ppermute | solution.py:44
  379.6 4.6 collective-permute-done.40
  389.0 5.3 %shard_map.285 = (f32[384,4480]{1,0:T(8,128)}, f32[384,4480]{1,0:T(8,128)}, f32[4480,384]{1,0:T(8,128)}) custom-call(s32[1]{0:T(128)} %bitcast.25.member_ref, bf16[3,384,768]{2,1,0:T(8,128)(2,1)} %add_convert_fusion.1.refs_0_, bf16[3,384,768]{2,1,0:T(8,128)(2,1)} %collective-permute-done.32.refs_1_, ...), custom_call_target="tpu_custom_call", output_to_operand_aliasing={{0}: (3, {}), {1}: (4, {}), {2}: (5, {})} | custom-call | flops 550000000 | bytes 1800000 | tf_op jit(solution)/shard_map/pallas_call | solution.py:673
  394.4 8.0 %collective-permute-done.37 = bf16[256,1536]{1,0:T(8,128)(2,1)} collective-permute-done((bf16[256,1536]{1,0:T(8,128)(2,1)}, bf16[256,1536]{1,0:T(8,128)(2,1)}, u32[]{:S(2)}, u32[]{:S(2)}) %collective-permute-start.37) | collective-permute-done | bytes 786464 | tf_op jit(solution)/shard_map/ppermute | solution.py:44
  411.2 10.9 %collective-permute-done.42 = bf16[384,384]{1,0:T(8,128)(2,1)} collective-permute-done((bf16[384,384]{1,0:T(8,128)(2,1)}, bf16[384,384]{1,0:T(8,128)(2,1)}, u32[]{:S(2)}, u32[]{:S(2)}) %collective-permute-start.42) | collective-permute-done | bytes 294944 | tf_op jit(solution)/shard_map/ppermute | solution.py:44
  423.2 7.3 %collective-permute-done.47 = bf16[384,512]{1,0:T(8,128)(2,1)S(1)} collective-permute-done((bf16[384,512]{1,0:T(8,128)(2,1)S(1)}, bf16[384,512]{1,0:T(8,128)(2,1)S(1)}, u32[]{:S(2)}, u32[]{:S(2)}) %collective-permute-start.47) | collective-permute-done | bytes 393248 | tf_op jit(solution)/shard_map/ppermute | solution.py:44
  430.8 3.0 collective-permute-start.50
  433.8 8.0 %collective-permute-done.45 = bf16[192,384]{1,0:T(8,128)(2,1)S(1)} collective-permute-done((bf16[192,384]{1,0:T(8,128)(2,1)S(1)}, bf16[192,384]{1,0:T(8,128)(2,1)S(1)}, u32[]{:S(2)}, u32[]{:S(2)}) %collective-permute-start.45) | collective-permute-done | bytes 147488 | tf_op jit(solution)/shard_map/ppermute | solution.py:44
  441.8 3.4 collective-permute-start.48
  445.2 13.4 %collective-permute-done.50 = bf16[384,256]{1,0:T(8,128)(2,1)S(1)} collective-permute-done((bf16[384,256]{1,0:T(8,128)(2,1)S(1)}, bf16[384,256]{1,0:T(8,128)(2,1)S(1)}, u32[]{:S(2)}, u32[]{:S(2)}) %collective-permute-start.50) | collective-permute-done | bytes 196640 | tf_op jit(solution)/shard_map/ppermute | solution.py:44
  458.8 3.0 collective-permute-start.52
  462.2 4.0 collective-permute-done.53
  468.0 5.3 %shard_map.286 = (f32[384,4480]{1,0:T(8,128)}, f32[384,4480]{1,0:T(8,128)}, f32[4480,384]{1,0:T(8,128)}) custom-call(s32[1]{0:T(128)} %bitcast.25.member_ref, bf16[3,384,768]{2,1,0:T(8,128)(2,1)} %copy-done.2, bf16[3,384,768]{2,1,0:T(8,128)(2,1)} %collective-permute-done.46.refs_1_, ...), custom_call_target="tpu_custom_call", output_to_operand_aliasing={{0}: (3, {}), {1}: (4, {}), {2}: (5, {})} | custom-call | flops 550000000 | bytes 1800000 | tf_op jit(solution)/shard_map/pallas_call | solution.py:673
  476.4 5.5 %collective-permute-done.54 = bf16[384,512]{1,0:T(8,128)(2,1)S(1)} collective-permute-done((bf16[384,512]{1,0:T(8,128)(2,1)S(1)}, bf16[384,512]{1,0:T(8,128)(2,1)S(1)}, u32[]{:S(2)}, u32[]{:S(2)}) %collective-permute-start.54) | collective-permute-done | bytes 393248 | tf_op jit(solution)/shard_map/ppermute | solution.py:44
  (299 shorter events, 113.2 us)
Async XLA Ops:
  7.2 47.7 %all-gather.9.cloned.1.call-start = ((), (), s32[]{:S(2)}) async-start(), calls=%async_computation | async-start | bytes 1966080 | tf_op jit(solution)/shard_map/all_gather | solution.py:830
  14.9 124.5 %all-gather.15.cloned.1.call-start = ((), (), s32[]{:S(2)}) async-start(), calls=%async_computation.3 | async-start | bytes 8847360 | tf_op jit(solution)/shard_map/all_gather | solution.py:892
  15.0 21.2 %collective-permute-start = (bf16[400,1024]{1,0:T(8,128)(2,1)S(1)}, bf16[400,1024]{1,0:T(8,128)(2,1)S(1)}, u32[]{:S(2)}, u32[]{:S(2)}) collective-permute-start(bf16[400,1024]{1,0:T(8,128)(2,1)S(1)} %fusion.5.refs_0_), channel_id=1, source_target_pairs={{0,16},{8,24},{16,0},{24,8},{1,17},{9,25},{17,1},{25,9},{2,18},{10... | collective-permute-start | bytes 2457608 | tf_op jit(solution)/shard_map/ppermute | solution.py:44
  36.2 123.5 %all-gather.13.cloned.1.call-start = ((), (), s32[]{:S(2)}) async-start(), calls=%async_computation.2 | async-start | bytes 8847360 | tf_op jit(solution)/shard_map/all_gather | solution.py:892
  37.0 187.3 %all-gather.11.cloned.1.call-start = ((), (), s32[]{:S(2)}) async-start(), calls=%async_computation.1 | async-start | bytes 8847360 | tf_op jit(solution)/shard_map/all_gather | solution.py:892
  42.3 15.7 %collective-permute-start.2 = (bf16[768,384]{1,0:T(8,128)(2,1)S(1)}, bf16[768,384]{1,0:T(8,128)(2,1)S(1)}, u32[]{:S(2)}, u32[]{:S(2)}) collective-permute-start(bf16[768,384]{1,0:T(8,128)(2,1)S(1)} %convert_element_type.119.refs_0_.refs_2_), channel_id=1, source_target_pairs={{0,16},{8,24},{16,0},{24,8},{1,17},{9,25},{17,1},{25,9},{2,18},{10... | collective-permute-start | bytes 1769480 | tf_op jit(solution)/shard_map/ppermute | solution.py:44
  60.1 13.5 %collective-permute-start.3 = (bf16[2,768,384]{2,1,0:T(8,128)(2,1)}, bf16[2,768,384]{2,1,0:T(8,128)(2,1)S(1)}, u32[]{:S(2)}, u32[]{:S(2)}) collective-permute-start(bf16[2,768,384]{2,1,0:T(8,128)(2,1)} %pad_maximum_fusion.1), channel_id=1, source_target_pairs={{0,8},{8,0},{16,24},{24,16},{1,9},{9,1},{17,25},{25,17},{2,10},{10... | collective-permute-start | bytes 3538952 | tf_op jit(solution)/shard_map/ppermute | solution.py:44
  60.1 37.6 %collective-permute-start.7 = (bf16[4,128,1536]{2,1,0:T(8,128)(2,1)}, bf16[4,128,1536]{2,1,0:T(8,128)(2,1)}, u32[]{:S(2)}, u32[]{:S(2)}) collective-permute-start(bf16[4,128,1536]{2,1,0:T(8,128)(2,1)} %bitcast.51), channel_id=1, source_target_pairs={{0,1},{1,0},{2,3},{3,2},{4,5},{5,4},{6,7},{7,6},{8,9},{9,8},{10,11... | collective-permute-start | bytes 4718600 | tf_op jit(solution)/shard_map/ppermute | solution.py:44
  84.4 21.2 %collective-permute-start.6 = (bf16[128,1536]{1,0:T(8,128)(2,1)}, bf16[128,1536]{1,0:T(8,128)(2,1)S(1)}, u32[]{:S(2)}, u32[]{:S(2)}) collective-permute-start(bf16[128,1536]{1,0:T(8,128)(2,1)} %get-tuple-element.444), channel_id=1, source_target_pairs={{0,1},{1,0},{2,3},{3,2},{4,5},{5,4},{6,7},{7,6},{8,9},{9,8},{10,11... | collective-permute-start | bytes 1179656 | tf_op jit(solution)/shard_map/ppermute | solution.py:44
  86.0 24.6 %collective-permute-start.9 = (bf16[256,1536]{1,0:T(8,128)(2,1)S(1)}, bf16[256,1536]{1,0:T(8,128)(2,1)}, u32[]{:S(2)}, u32[]{:S(2)}) collective-permute-start(bf16[256,1536]{1,0:T(8,128)(2,1)S(1)} %pad_maximum_fusion.3), channel_id=1, source_target_pairs={{0,8},{8,0},{16,24},{24,16},{1,9},{9,1},{17,25},{25,17},{2,10},{10... | collective-permute-start | bytes 2359304 | tf_op jit(solution)/shard_map/ppermute | solution.py:44
  121.0 18.4 %collective-permute-start.10 = (bf16[256,1536]{1,0:T(8,128)(2,1)S(1)}, bf16[256,1536]{1,0:T(8,128)(2,1)S(1)}, u32[]{:S(2)}, u32[]{:S(2)}) collective-permute-start(bf16[256,1536]{1,0:T(8,128)(2,1)S(1)} %constant_dynamic-update-slice_fusion.refs_0_), channel_id=1, source_target_pairs={{0,1},{1,0},{2,3},{3,2},{4,5},{5,4},{6,7},{7,6},{8,9},{9,8},{10,11... | collective-permute-start | bytes 2359304 | tf_op jit(solution)/shard_map/ppermute | solution.py:44
  122.7 35.8 %collective-permute-start.11 = (bf16[256,1536]{1,0:T(8,128)(2,1)S(1)}, bf16[256,1536]{1,0:T(8,128)(2,1)S(1)}, u32[]{:S(2)}, u32[]{:S(2)}) collective-permute-start(bf16[256,1536]{1,0:T(8,128)(2,1)S(1)} %constant_dynamic-update-slice_fusion.refs_0_), channel_id=1, source_target_pairs={{0,4},{2,6},{4,0},{6,2},{1,5},{3,7},{5,1},{7,3},{8,12},{10,14},{12... | collective-permute-start | bytes 2359304 | tf_op jit(solution)/shard_map/ppermute | solution.py:44
  158.5 18.4 %collective-permute-start.12 = (bf16[256,1536]{1,0:T(8,128)(2,1)S(1)}, bf16[256,1536]{1,0:T(8,128)(2,1)S(1)}, u32[]{:S(2)}, u32[]{:S(2)}) collective-permute-start(bf16[256,1536]{1,0:T(8,128)(2,1)S(1)} %collective-permute-done.11.refs_2_.refs_0_), channel_id=1, source_target_pairs={{0,1},{1,0},{2,3},{3,2},{4,5},{5,4},{6,7},{7,6},{8,9},{9,8},{10,11... | collective-permute-start | bytes 2359304 | tf_op jit(solution)/shard_map/ppermute | solution.py:44
  185.8 22.1 %collective-permute-start.13 = (bf16[2,768,1024]{2,1,0:T(8,128)(2,1)}, bf16[2,768,1024]{2,1,0:T(8,128)(2,1)S(1)}, u32[]{:S(2)}, u32[]{:S(2)}) collective-permute-start(bf16[2,768,1024]{2,1,0:T(8,128)(2,1)} %get-tuple-element.497), channel_id=1, source_target_pairs={{0,8},{8,0},{16,24},{24,16},{1,9},{9,1},{17,25},{25,17},{2,10},{10... | collective-permute-start | bytes 9437192 | tf_op jit(solution)/shard_map/ppermute | solution.py:44
  196.2 11.2 %collective-permute-start.14 = (bf16[1024,768]{1,0:T(8,128)(2,1)}, bf16[1024,768]{1,0:T(8,128)(2,1)}, u32[]{:S(2)}, u32[]{:S(2)}) collective-permute-start(bf16[1024,768]{1,0:T(8,128)(2,1)} %get-tuple-element.528.refs_0_), channel_id=1, source_target_pairs={{0,8},{8,0},{16,24},{24,16},{1,9},{9,1},{17,25},{25,17},{2,10},{10... | collective-permute-start | bytes 4718600 | tf_op jit(solution)/shard_map/ppermute | solution.py:44
  196.5 11.1 %collective-permute-start.15 = (bf16[1024,768]{1,0:T(8,128)(2,1)}, bf16[1024,768]{1,0:T(8,128)(2,1)}, u32[]{:S(2)}, u32[]{:S(2)}) collective-permute-start(bf16[1024,768]{1,0:T(8,128)(2,1)} %get-tuple-element.529.refs_1_), channel_id=1, source_target_pairs={{0,8},{8,0},{16,24},{24,16},{1,9},{9,1},{17,25},{25,17},{2,10},{10... | collective-permute-start | bytes 4718600 | tf_op jit(solution)/shard_map/ppermute | solution.py:44
  196.7 11.1 %collective-permute-start.16 = (bf16[1024,768]{1,0:T(8,128)(2,1)}, bf16[1024,768]{1,0:T(8,128)(2,1)}, u32[]{:S(2)}, u32[]{:S(2)}) collective-permute-start(bf16[1024,768]{1,0:T(8,128)(2,1)} %get-tuple-element.530.refs_2_), channel_id=1, source_target_pairs={{0,8},{8,0},{16,24},{24,16},{1,9},{9,1},{17,25},{25,17},{2,10},{10... | collective-permute-start | bytes 4718600 | tf_op jit(solution)/shard_map/ppermute | solution.py:44
  207.1 44.3 %collective-permute-start.17 = (bf16[1024,768]{1,0:T(8,128)(2,1)}, bf16[1024,768]{1,0:T(8,128)(2,1)}, u32[]{:S(2)}, u32[]{:S(2)}) collective-permute-start(bf16[1024,768]{1,0:T(8,128)(2,1)} %get-tuple-element.565.refs_0_), channel_id=1, source_target_pairs={{0,8},{8,0},{16,24},{24,16},{1,9},{9,1},{17,25},{25,17},{2,10},{10... | collective-permute-start | bytes 4718600 | tf_op jit(solution)/shard_map/ppermute | solution.py:44
  207.4 44.1 %collective-permute-start.18 = (bf16[1024,768]{1,0:T(8,128)(2,1)}, bf16[1024,768]{1,0:T(8,128)(2,1)}, u32[]{:S(2)}, u32[]{:S(2)}) collective-permute-start(bf16[1024,768]{1,0:T(8,128)(2,1)} %get-tuple-element.566.refs_1_), channel_id=1, source_target_pairs={{0,8},{8,0},{16,24},{24,16},{1,9},{9,1},{17,25},{25,17},{2,10},{10... | collective-permute-start | bytes 4718600 | tf_op jit(solution)/shard_map/ppermute | solution.py:44
  207.7 44.3 %collective-permute-start.19 = (bf16[1024,768]{1,0:T(8,128)(2,1)}, bf16[1024,768]{1,0:T(8,128)(2,1)}, u32[]{:S(2)}, u32[]{:S(2)}) collective-permute-start(bf16[1024,768]{1,0:T(8,128)(2,1)} %get-tuple-element.567.refs_2_), channel_id=1, source_target_pairs={{0,8},{8,0},{16,24},{24,16},{1,9},{9,1},{17,25},{25,17},{2,10},{10... | collective-permute-start | bytes 4718600 | tf_op jit(solution)/shard_map/ppermute | solution.py:44
  222.9 45.3 %collective-permute-start.21 = (bf16[3,384,768]{2,1,0:T(8,128)(2,1)}, bf16[3,384,768]{2,1,0:T(8,128)(2,1)S(1)}, u32[]{:S(2)}, u32[]{:S(2)}) collective-permute-start(bf16[3,384,768]{2,1,0:T(8,128)(2,1)} %get-tuple-element.534), channel_id=1, source_target_pairs={{0,16},{8,24},{16,0},{24,8},{1,17},{9,25},{17,1},{25,9},{2,18},{10... | collective-permute-start | bytes 5308424 | tf_op jit(solution)/shard_map/ppermute | solution.py:44
  240.5 25.0 %collective-permute-start.22 = (bf16[256,1536]{1,0:T(8,128)(2,1)}, bf16[256,1536]{1,0:T(8,128)(2,1)}, u32[]{:S(2)}, u32[]{:S(2)}) collective-permute-start(bf16[256,1536]{1,0:T(8,128)(2,1)} %get-tuple-element.575), channel_id=1, source_target_pairs={{0,1},{1,0},{2,3},{3,2},{4,5},{5,4},{6,7},{7,6},{8,9},{9,8},{10,11... | collective-permute-start | bytes 2359304 | tf_op jit(solution)/shard_map/ppermute | solution.py:44
  251.4 33.4 %collective-permute-start.26 = (bf16[1024,768]{1,0:T(8,128)(2,1)}, bf16[1024,768]{1,0:T(8,128)(2,1)}, u32[]{:S(2)}, u32[]{:S(2)}) collective-permute-start(bf16[1024,768]{1,0:T(8,128)(2,1)} %get-tuple-element.593.refs_0_), channel_id=1, source_target_pairs={{0,8},{8,0},{16,24},{24,16},{1,9},{9,1},{17,25},{25,17},{2,10},{10... | collective-permute-start | bytes 4718600 | tf_op jit(solution)/shard_map/ppermute | solution.py:44
  251.5 33.3 %collective-permute-start.27 = (bf16[1024,768]{1,0:T(8,128)(2,1)}, bf16[1024,768]{1,0:T(8,128)(2,1)}, u32[]{:S(2)}, u32[]{:S(2)}) collective-permute-start(bf16[1024,768]{1,0:T(8,128)(2,1)} %get-tuple-element.594.refs_1_), channel_id=1, source_target_pairs={{0,8},{8,0},{16,24},{24,16},{1,9},{9,1},{17,25},{25,17},{2,10},{10... | collective-permute-start | bytes 4718600 | tf_op jit(solution)/shard_map/ppermute | solution.py:44
  252.0 32.8 %collective-permute-start.28 = (bf16[1024,768]{1,0:T(8,128)(2,1)}, bf16[1024,768]{1,0:T(8,128)(2,1)}, u32[]{:S(2)}, u32[]{:S(2)}) collective-permute-start(bf16[1024,768]{1,0:T(8,128)(2,1)} %get-tuple-element.595.refs_2_), channel_id=1, source_target_pairs={{0,8},{8,0},{16,24},{24,16},{1,9},{9,1},{17,25},{25,17},{2,10},{10... | collective-permute-start | bytes 4718600 | tf_op jit(solution)/shard_map/ppermute | solution.py:44
  266.8 11.5 %collective-permute-start.24 = (bf16[128,1536]{1,0:T(8,128)(2,1)S(1)}, bf16[128,1536]{1,0:T(8,128)(2,1)S(1)}, u32[]{:S(2)}, u32[]{:S(2)}) collective-permute-start(bf16[128,1536]{1,0:T(8,128)(2,1)S(1)} %add_convert_fusion.5), channel_id=1, source_target_pairs={{0,2},{2,0},{4,6},{6,4},{1,3},{3,1},{5,7},{7,5},{8,10},{10,8},{12,... | collective-permute-start | bytes 1179656 | tf_op jit(solution)/shard_map/ppermute | solution.py:44
  268.2 50.3 %collective-permute-start.20 = (bf16[3,384,768]{2,1,0:T(8,128)(2,1)}, bf16[3,384,768]{2,1,0:T(8,128)(2,1)}, u32[]{:S(2)}, u32[]{:S(2)}) collective-permute-start(bf16[3,384,768]{2,1,0:T(8,128)(2,1)} %get-tuple-element.572), channel_id=1, source_target_pairs={{0,16},{8,24},{16,0},{24,8},{1,17},{9,25},{17,1},{25,9},{2,18},{10... | collective-permute-start | bytes 5308424 | tf_op jit(solution)/shard_map/ppermute | solution.py:44
  278.3 40.3 %collective-permute-start.23 = (bf16[3,384,768]{2,1,0:T(8,128)(2,1)S(1)}, bf16[3,384,768]{2,1,0:T(8,128)(2,1)S(1)}, u32[]{:S(2)}, u32[]{:S(2)}) collective-permute-start(bf16[3,384,768]{2,1,0:T(8,128)(2,1)S(1)} %add_convert_fusion.2.refs_0_), channel_id=1, source_target_pairs={{0,2},{2,0},{4,6},{6,4},{1,3},{3,1},{5,7},{7,5},{8,10},{10,8},{12,... | collective-permute-start | bytes 5308424 | tf_op jit(solution)/shard_map/ppermute | solution.py:44
  284.9 14.7 %collective-permute-start.25 = (bf16[128,1536]{1,0:T(8,128)(2,1)}, bf16[128,1536]{1,0:T(8,128)(2,1)}, u32[]{:S(2)}, u32[]{:S(2)}) collective-permute-start(bf16[128,1536]{1,0:T(8,128)(2,1)} %get-tuple-element.610.refs_0_), channel_id=1, source_target_pairs={{0,1},{1,0},{2,3},{3,2},{4,5},{5,4},{6,7},{7,6},{8,9},{9,8},{10,11... | collective-permute-start | bytes 1179656 | tf_op jit(solution)/shard_map/ppermute | solution.py:44
  303.0 51.4 %collective-permute-start.36 = (bf16[3,384,768]{2,1,0:T(8,128)(2,1)}, bf16[3,384,768]{2,1,0:T(8,128)(2,1)}, u32[]{:S(2)}, u32[]{:S(2)}) collective-permute-start(bf16[3,384,768]{2,1,0:T(8,128)(2,1)} %get-tuple-element.599), channel_id=1, source_target_pairs={{0,16},{8,24},{16,0},{24,8},{1,17},{9,25},{17,1},{25,9},{2,18},{10... | collective-permute-start | bytes 5308424 | tf_op jit(solution)/shard_map/ppermute | solution.py:44
  317.1 13.7 %collective-permute-start.31 = (bf16[256,256]{1,0:T(8,128)(2,1)}, bf16[256,256]{1,0:T(8,128)(2,1)S(1)}, u32[]{:S(2)}, u32[]{:S(2)}) collective-permute-start(bf16[256,256]{1,0:T(8,128)(2,1)} %get-tuple-element.624), channel_id=1, source_target_pairs={{4,0},{6,2},{5,1},{7,3},{12,8},{14,10},{13,9},{15,11},{20,16},{22,... | collective-permute-start | bytes 393224 | tf_op jit(solution)/shard_map/ppermute | solution.py:50
  336.1 41.8 %collective-permute-start.32 = (bf16[3,384,768]{2,1,0:T(8,128)(2,1)}, bf16[3,384,768]{2,1,0:T(8,128)(2,1)}, u32[]{:S(2)}, u32[]{:S(2)}) collective-permute-start(bf16[3,384,768]{2,1,0:T(8,128)(2,1)} %add_convert_fusion.1.refs_0_), channel_id=1, source_target_pairs={{0,2},{2,0},{4,6},{6,4},{1,3},{3,1},{5,7},{7,5},{8,10},{10,8},{12,... | collective-permute-start | bytes 5308424 | tf_op jit(solution)/shard_map/ppermute | solution.py:44
  336.2 11.8 %collective-permute-start.33 = (bf16[128,1536]{1,0:T(8,128)(2,1)}, bf16[128,1536]{1,0:T(8,128)(2,1)}, u32[]{:S(2)}, u32[]{:S(2)}) collective-permute-start(bf16[128,1536]{1,0:T(8,128)(2,1)} %get-tuple-element.645), channel_id=1, source_target_pairs={{0,1},{1,0},{2,3},{3,2},{4,5},{5,4},{6,7},{7,6},{8,9},{9,8},{10,11... | collective-permute-start | bytes 1179656 | tf_op jit(solution)/shard_map/ppermute | solution.py:44
  352.7 25.2 %collective-permute-start.38 = (bf16[768,384]{1,0:T(8,128)(2,1)S(1)}, bf16[768,384]{1,0:T(8,128)(2,1)S(1)}, u32[]{:S(2)}, u32[]{:S(2)}) collective-permute-start(bf16[768,384]{1,0:T(8,128)(2,1)S(1)} %slice.371), channel_id=1, source_target_pairs={{0,16},{8,24},{16,0},{24,8},{1,17},{9,25},{17,1},{25,9},{2,18},{10... | collective-permute-start | bytes 1769480 | tf_op jit(solution)/shard_map/ppermute | solution.py:44
  354.4 29.7 %collective-permute-start.40 = (bf16[384,1024]{1,0:T(8,128)(2,1)S(1)}, bf16[384,1024]{1,0:T(8,128)(2,1)S(1)}, u32[]{:S(2)}, u32[]{:S(2)}) collective-permute-start(bf16[384,1024]{1,0:T(8,128)(2,1)S(1)} %slice.370), channel_id=1, source_target_pairs={{0,16},{8,24},{16,0},{24,8},{1,17},{9,25},{17,1},{25,9},{2,18},{10... | collective-permute-start | bytes 2359304 | tf_op jit(solution)/shard_map/ppermute | solution.py:44
  357.0 73.7 %collective-permute-start.46 = (bf16[3,384,768]{2,1,0:T(8,128)(2,1)S(1)}, bf16[3,384,768]{2,1,0:T(8,128)(2,1)}, u32[]{:S(2)}, u32[]{:S(2)}) collective-permute-start(bf16[3,384,768]{2,1,0:T(8,128)(2,1)S(1)} %add_convert_fusion.refs_0_), channel_id=1, source_target_pairs={{0,2},{2,0},{4,6},{6,4},{1,3},{3,1},{5,7},{7,5},{8,10},{10,8},{12,... | collective-permute-start | bytes 5308424 | tf_op jit(solution)/shard_map/ppermute | solution.py:44
  384.1 18.2 %collective-permute-start.37 = (bf16[256,1536]{1,0:T(8,128)(2,1)}, bf16[256,1536]{1,0:T(8,128)(2,1)}, u32[]{:S(2)}, u32[]{:S(2)}) collective-permute-start(bf16[256,1536]{1,0:T(8,128)(2,1)} %get-tuple-element.666), channel_id=1, source_target_pairs={{0,1},{1,0},{2,3},{3,2},{4,5},{5,4},{6,7},{7,6},{8,9},{9,8},{10,11... | collective-permute-start | bytes 2359304 | tf_op jit(solution)/shard_map/ppermute | solution.py:44
  386.8 35.3 %collective-permute-start.42 = (bf16[384,384]{1,0:T(8,128)(2,1)}, bf16[384,384]{1,0:T(8,128)(2,1)}, u32[]{:S(2)}, u32[]{:S(2)}) collective-permute-start(bf16[384,384]{1,0:T(8,128)(2,1)} %select_convert_fusion.1), channel_id=1, source_target_pairs={{0,2},{2,0},{4,6},{6,4},{1,3},{3,1},{5,7},{7,5},{8,10},{10,8},{12,... | collective-permute-start | bytes 884744 | tf_op jit(solution)/shard_map/ppermute | solution.py:44
  389.0 15.1 %collective-permute-start.43 = (f32[16,1536]{1,0:T(8,128)}, f32[16,1536]{1,0:T(8,128)}, u32[]{:S(2)}, u32[]{:S(2)}) collective-permute-start(f32[16,1536]{1,0:T(8,128)} %select_maximum_fusion), channel_id=1, source_target_pairs={{0,8},{8,0},{16,24},{24,16},{1,9},{9,1},{17,25},{25,17},{2,10},{10... | collective-permute-start | bytes 294920 | tf_op jit(solution)/shard_map/ppermute | solution.py:44
  406.8 23.7 %collective-permute-start.47 = (bf16[384,512]{1,0:T(8,128)(2,1)S(1)}, bf16[384,512]{1,0:T(8,128)(2,1)S(1)}, u32[]{:S(2)}, u32[]{:S(2)}) collective-permute-start(bf16[384,512]{1,0:T(8,128)(2,1)S(1)} %select_convert_fusion), channel_id=1, source_target_pairs={{0,2},{2,0},{4,6},{6,4},{1,3},{3,1},{5,7},{7,5},{8,10},{10,8},{12,... | collective-permute-start | bytes 1179656 | tf_op jit(solution)/shard_map/ppermute | solution.py:44
  408.1 53.8 %collective-permute-start.41 = (bf16[128,1536]{1,0:T(8,128)(2,1)S(1)}, bf16[128,1536]{1,0:T(8,128)(2,1)S(1)}, u32[]{:S(2)}, u32[]{:S(2)}) collective-permute-start(bf16[128,1536]{1,0:T(8,128)(2,1)S(1)} %get-tuple-element.749), channel_id=1, source_target_pairs={{0,2},{2,0},{4,6},{6,4},{1,3},{3,1},{5,7},{7,5},{8,10},{10,8},{12,... | collective-permute-start | bytes 1179656 | tf_op jit(solution)/shard_map/ppermute | solution.py:44
  409.9 48.9 %collective-permute-start.49 = (f32[16,1536]{1,0:T(8,128)S(1)}, f32[16,1536]{1,0:T(8,128)S(1)}, u32[]{:S(2)}, u32[]{:S(2)}) collective-permute-start(f32[16,1536]{1,0:T(8,128)S(1)} %add.248), channel_id=1, source_target_pairs={{0,2},{2,0},{4,6},{6,4},{1,3},{3,1},{5,7},{7,5},{8,10},{10,8},{12,... | collective-permute-start | bytes 294920 | tf_op jit(solution)/shard_map/ppermute | solution.py:44
  430.7 11.1 %collective-permute-start.45 = (bf16[192,384]{1,0:T(8,128)(2,1)S(1)}, bf16[192,384]{1,0:T(8,128)(2,1)S(1)}, u32[]{:S(2)}, u32[]{:S(2)}) collective-permute-start(bf16[192,384]{1,0:T(8,128)(2,1)S(1)} %select_convert_fusion.3), channel_id=1, source_target_pairs={{0,4},{2,6},{4,0},{6,2},{1,5},{3,7},{5,1},{7,3},{8,12},{10,14},{12... | collective-permute-start | bytes 442376 | tf_op jit(solution)/shard_map/ppermute | solution.py:44
  430.8 27.8 %collective-permute-start.50 = (bf16[384,256]{1,0:T(8,128)(2,1)S(1)}, bf16[384,256]{1,0:T(8,128)(2,1)S(1)}, u32[]{:S(2)}, u32[]{:S(2)}) collective-permute-start(bf16[384,256]{1,0:T(8,128)(2,1)S(1)} %select_convert_fusion.2), channel_id=1, source_target_pairs={{0,4},{2,6},{4,0},{6,2},{1,5},{3,7},{5,1},{7,3},{8,12},{10,14},{12... | collective-permute-start | bytes 589832 | tf_op jit(solution)/shard_map/ppermute | solution.py:44
  441.8 20.0 %collective-permute-start.48 = (bf16[192,384]{1,0:T(8,128)(2,1)S(1)}, bf16[192,384]{1,0:T(8,128)(2,1)S(1)}, u32[]{:S(2)}, u32[]{:S(2)}) collective-permute-start(bf16[192,384]{1,0:T(8,128)(2,1)S(1)} %add_convert_fusion.7), channel_id=1, source_target_pairs={{0,4},{2,6},{4,0},{6,2},{1,5},{3,7},{5,1},{7,3},{8,12},{10,14},{12... | collective-permute-start | bytes 442376 | tf_op jit(solution)/shard_map/ppermute | solution.py:44
  461.9 12.0 %collective-permute-start.55 = (bf16[384,384]{1,0:T(8,128)(2,1)S(1)}, bf16[384,384]{1,0:T(8,128)(2,1)S(1)}, u32[]{:S(2)}, u32[]{:S(2)}) collective-permute-start(bf16[384,384]{1,0:T(8,128)(2,1)S(1)} %pad_maximum_fusion.9), channel_id=1, source_target_pairs={{0,2},{2,0},{4,6},{6,4},{1,3},{3,1},{5,7},{7,5},{8,10},{10,8},{12,... | collective-permute-start | bytes 884744 | tf_op jit(solution)/shard_map/ppermute | solution.py:44
  462.1 12.9 %collective-permute-start.51 = (bf16[128,1536]{1,0:T(8,128)(2,1)S(1)}, bf16[128,1536]{1,0:T(8,128)(2,1)S(1)}, u32[]{:S(2)}, u32[]{:S(2)}) collective-permute-start(bf16[128,1536]{1,0:T(8,128)(2,1)S(1)} %add_convert_fusion.3), channel_id=1, source_target_pairs={{0,1},{1,0},{2,3},{3,2},{4,5},{5,4},{6,7},{7,6},{8,9},{9,8},{10,11... | collective-permute-start | bytes 1179656 | tf_op jit(solution)/shard_map/ppermute | solution.py:44
  466.3 15.6 %collective-permute-start.54 = (bf16[384,512]{1,0:T(8,128)(2,1)S(1)}, bf16[384,512]{1,0:T(8,128)(2,1)S(1)}, u32[]{:S(2)}, u32[]{:S(2)}) collective-permute-start(bf16[384,512]{1,0:T(8,128)(2,1)S(1)} %pad_maximum_fusion.8), channel_id=1, source_target_pairs={{0,2},{2,0},{4,6},{6,4},{1,3},{3,1},{5,7},{7,5},{8,10},{10,8},{12,... | collective-permute-start | bytes 1179656 | tf_op jit(solution)/shard_map/ppermute | solution.py:44
  (61 other events, 450.9 us)
Sparse Core Ops, SparseCore 0:
  15.0 39.7 all-gather.8
  57.0 49.6 all-gather.14
  108.9 50.8 all-gather.12
  161.2 52.3 all-gather.10

commit v4 on v3

--- a/solution.py
+++ b/solution.py
@@ -134,7 +134,7 @@
     return pieces
 
 
-SCALE = 0.5
+SCALE = 0.4
 
 
 def cost(us=1):
@@ -183,6 +183,47 @@
         cost_estimate=cost(),
         compiler_params=params(60),
     )(start, *[w_gate] * count, *[w_up] * count, *[w_down] * count)
+
+
+def qkv_pack_body(index_ref, g1_ref, g2_ref, bq_ref, bk_ref, bv_ref, wq_ref, wk_ref, wv_ref, out_ref):
+    shard, at = wq_ref.shape[0], 0
+    for ref in (wq_ref, wk_ref, wv_ref):
+        out_ref[:shard, at : at + ref.shape[1]] = ref[...].astype(bf16)
+        at += ref.shape[1]
+    row = lax.broadcasted_iota(jnp.int32, (16, shard), 0)
+    first, second = g1_ref[...][None, :], g2_ref[...][None, :]
+    gains = jnp.where(row == 0, first, jnp.where(row == 1, second, 0.0))
+    columns = bq_ref.shape[1]
+    from_column = lax.broadcasted_iota(jnp.int32, (columns, HD), 0)
+    to_column = lax.broadcasted_iota(jnp.int32, (columns, HD), 1)
+    spread = (to_column == from_column + columns * index_ref[0]).astype(bf16)
+    biases, at = 0.0, 8
+    for ref in (bq_ref, bk_ref, bv_ref):
+        heads = ref.shape[0]
+        to_row = lax.broadcasted_iota(jnp.int32, (16, heads), 0)
+        from_row = lax.broadcasted_iota(jnp.int32, (16, heads), 1) + at
+        wide = dot_plain(ref[...].astype(bf16), spread).astype(bf16)
+        if heads == 1:
+            row = lax.broadcasted_iota(jnp.int32, (16, HD), 0)
+            biases = biases + jnp.where(row == at, wide.astype(f32), 0.0)
+        else:
+            biases = biases + dot_plain((to_row == from_row).astype(bf16), wide)
+        at += heads
+    out_ref[shard:, :] = jnp.zeros((16, out_ref.shape[1]), bf16)
+    out_ref[shard:, :HD] = (gains[:, :HD] + biases).astype(bf16)
+    out_ref[shard:, HD:shard] = gains[:, HD:].astype(bf16)
+
+
+def qkv_pack(index, g1, g2, b_q, b_k, b_v, w_q, w_k, w_v):
+    width = w_q.shape[1] + w_k.shape[1] + w_v.shape[1]
+    inputs = (g1, g2, b_q, b_k, b_v, w_q, w_k, w_v)
+    return pl.pallas_call(
+        qkv_pack_body,
+        out_shape=jax.ShapeDtypeStruct((w_q.shape[0] + 16, width), bf16),
+        in_specs=[pl.BlockSpec(memory_space=pltpu.SMEM)] + [pl.BlockSpec(memory_space=pltpu.VMEM)] * len(inputs),
+        cost_estimate=cost(2),
+        compiler_params=params(60),
+    )(index, *inputs)
 
 
 def vectors_body(count, heads, index_ref, *refs):
@@ -322,17 +363,31 @@
     count, bases, back, carried, last, filled, at_row, limit_ref, ctx_ref, *refs
 ):
     h_refs, refs = refs[: 2 * len(bases)], refs[2 * len(bases) :]
-    (g_own, g_across, w_ref), refs = refs[:3], refs[3:]
+    (g_own, g_across, w_hbm), refs = refs[:3], refs[3:]
     carry, refs = refs[: 2 * carried], refs[2 * carried + filled :]
-    outs, (act_ref, sems) = refs[:-2], refs[-2:]
-    gate_w, up_w, down_w = (
-        jnp.concatenate([w_ref[i, k] for i in range(count)], axis=0) for k in range(3)
-    )
-    rows = act_ref.shape[1]
-    lane = lax.broadcasted_iota(jnp.int32, (1, act_ref.shape[2]), 1)
-    shown = lane >= limit_ref[0]
+    bufs = None
+    if carried:
+        outs, (w_ref, act_ref, sems, bufs) = refs[:-4], refs[-4:]
+    else:
+        outs, (w_ref, act_ref, sems) = refs[:-3], refs[-3:]
+    rows, width = act_ref.shape[1:]
+    tiles = 3
+    loads = [
+        pltpu.make_async_copy(w_hbm.at[:, k], w_ref.at[:, k], sems.at[k]) for k in range(tiles)
+    ]
+    carries = [
+        pltpu.make_async_copy(ref, bufs.at[k], sems.at[tiles + k]) for k, ref in enumerate(carry)
+    ]
+    for copy in loads + carries:
+        copy.start()
     half = g_own.shape[1]
     chunk = 2 * half
+    lane = lax.broadcasted_iota(jnp.int32, (1, width), 1)
+    shown = lane >= limit_ref[0]
+
+    def weights(k):
+        return jnp.concatenate([w_ref[i, k] for i in range(count)], axis=0)
+
     at = 0
     for which, h_ref in enumerate(h_refs):
         base, g_ref = bases[which // 2], (g_own, g_across)[which % 2]
@@ -341,9 +396,15 @@
             grads_in = jnp.concatenate(
                 [g_ref[ctx_ref[0] ^ (base + 2 * j + k)] for k in range(2)], axis=0
             )
-            gate = dot_plain(rows_in, gate_w)
-            up = dot_plain(rows_in, up_w)
-            d_hidden = dot_plain(grads_in, down_w)
+            if at == 0:
+                loads[0].wait()
+            gate = dot_plain(rows_in, weights(0))
+            if at == 0:
+                loads[1].wait()
+            up = dot_plain(rows_in, weights(1))
+            if at == 0:
+                loads[2].wait()
+            d_hidden = dot_plain(grads_in, weights(2))
             gate_sig = jax.nn.sigmoid(gate)
             activated = gate * gate_sig
             hidden = activated * up
@@ -353,19 +414,22 @@
             act_ref[1, at : at + chunk] = jnp.where(shown, d_up, 0.0).astype(bf16)
             act_ref[2, at : at + chunk] = jnp.where(shown, hidden, 0.0).astype(bf16)
             at += chunk
+    at = tiles + len(carries)
     copies = [
-        pltpu.make_async_copy(act_ref.at[k], outs[k].at[pl.ds(at_row, rows)], sems.at[k])
+        pltpu.make_async_copy(act_ref.at[k], outs[k].at[pl.ds(at_row, rows)], sems.at[at + k])
         for k in range(3)
     ]
     for copy in copies:
         copy.start()
     if back:
-        team = slice(0, 2 * chunk)
-        d_rows = dot_cols(act_ref[0, team], gate_w) + dot_cols(act_ref[1, team], up_w)
-        out_rows = dot_cols(act_ref[2, team], down_w)
+        team = slice(0, 4 * half)
+        d_rows = dot_cols(act_ref[0, team], weights(0)) + dot_cols(act_ref[1, team], weights(1))
+        out_rows = dot_cols(act_ref[2, team], weights(2))
+        for copy in carries:
+            copy.wait()
         if carried:
-            d_rows = d_rows + carry[0][...]
-            out_rows = out_rows + carry[1][...]
+            d_rows = d_rows + bufs[0]
+            out_rows = out_rows + bufs[1]
         if last:
             cuts = ((0, half), (half, 2 * half), (2 * half, 4 * half))
             for group, total in ((outs[3:6], d_rows), (outs[6:], out_rows)):
@@ -391,8 +455,16 @@
     vmem = pl.BlockSpec(memory_space=pltpu.VMEM)
     smem = pl.BlockSpec(memory_space=pltpu.SMEM)
     hbm = pl.BlockSpec(memory_space=pl.ANY)
-    inputs = (*rows_in, *grads_in, weights, *carry)
+    inputs = (*rows_in, *grads_in)
     filled = () if act is None else tuple(act)
+    scratch = [
+        pltpu.VMEM(weights.shape, bf16),
+        pltpu.VMEM((3, some, width), bf16),
+        pltpu.SemaphoreType.DMA((6 + len(carry),)),
+    ]
+    if carry:
+        scratch.append(pltpu.VMEM((2, 4 * half, D), f32))
+    first = 3 + len(inputs) + len(carry)
     return pl.pallas_call(
         functools.partial(
             feed_body, weights.shape[0],
@@ -400,86 +472,79 @@
             back, len(carry) // 2, last, len(filled), 0 if back else total - some,
         ),
         out_shape=tuple(outs),
-        in_specs=[smem, smem] + [vmem] * len(inputs) + [hbm] * len(filled),
+        in_specs=[smem, smem] + [vmem] * len(inputs) + [hbm] * (1 + len(carry) + len(filled)),
         out_specs=tuple([hbm] * 3 + [vmem] * (len(outs) - 3)),
-        scratch_shapes=[pltpu.VMEM((3, some, width), bf16), pltpu.SemaphoreType.DMA((3,))],
-        input_output_aliases={2 + len(inputs) + k: k for k in range(len(filled))},
+        scratch_shapes=scratch,
+        input_output_aliases={first + k: k for k in range(len(filled))},
         compiler_params=params(60),
         cost_estimate=cost((6 if back else 0) + 9 * some / 512),
-    )(limit, ctx, *inputs, *filled)
-
-
-def turn_body(contexts, blocks, index_ref, ctx_ref, *refs):
-    lines, (g_own, g_across, kept_ref, sent_ref) = refs[:-4], refs[-4:]
+    )(limit, ctx, *inputs, weights, *carry, *filled)
+
+
+def turn_body(blocks, dynamic, contexts, index_ref, ctx_ref, *refs):
+    kept_ref, sent_ref = refs[-2:]
     width = D // blocks
     order = fsdp_order(blocks)
-    half = g_own.shape[1]
-
-    def put(which, at, value):
+    values = [(ref, None) for ref in refs[:-2]]
+    if contexts:
+        groups = (range(TEAM), range(TEAM, contexts))
+        values = [(ref, ctx_ref[0] ^ k) for group in groups for ref in refs[:-2] for k in group]
+    at = 0
+    for ref, which in values:
+        value = ref[...] if which is None else ref[which]
         here = slice(at, at + value.shape[0])
+        at += value.shape[0]
         parts = [value[:, i * width : (i + 1) * width] for i in range(blocks)]
-        if blocks > 2:
+        if dynamic:
             parts = xor_blocks(parts, index_ref[0], blocks)
             parts = [parts[i] for i in order]
         for spot in range(blocks // 2):
             lines_at = slice(spot * width, (spot + 1) * width)
-            kept_ref[which, lines_at, here] = parts[spot].T
-            sent_ref[which, lines_at, here] = parts[blocks // 2 + spot].T
-
-    at = 0
-    for ref in lines:
-        put(0, at, ref[...])
-        at += ref.shape[0]
-    at = 0
-    for group in (range(TEAM), range(TEAM, contexts)):
-        for ref in (g_own, g_across):
-            for k in group:
-                put(1, at, ref[ctx_ref[0] ^ k])
-                at += half
-
-
-def turn_rows(index, ctx, rows, grads, n_fsdp):
-    total = sum(r.shape[0] for r in rows)
+            kept_ref[lines_at, here] = parts[spot].T
+            sent_ref[lines_at, here] = parts[blocks // 2 + spot].T
+
+
+def turn_rows(index, ctx, rows, n_fsdp):
+    total = sum(r.size for r in rows) // D
+    contexts = rows[0].shape[0] if rows[0].ndim == 3 else 0
     blocks = n_fsdp
     if D // n_fsdp % LANES:
         blocks = 2
-        rows, grads = (
-            [to_relative(v, index[0], n_fsdp) for v in some] for some in (rows, grads)
-        )
-    smem = pl.BlockSpec(memory_space=pltpu.SMEM)
-    return pl.pallas_call(
-        functools.partial(turn_body, grads[0].shape[0], blocks),
-        out_shape=(jax.ShapeDtypeStruct((2, D // 2, total), bf16),) * 2,
-        in_specs=[smem, smem] + [pl.BlockSpec(memory_space=pltpu.VMEM)] * (len(rows) + 2),
-        cost_estimate=cost(7),
-        compiler_params=params(60),
-    )(index, ctx, *rows, *grads)
-
-
-def weight_body(own_ref, beside_ref, *refs):
-    acts, acts_beside, (near_ref, far_ref) = refs[:3], refs[3:6], refs[6:]
+        rows = [to_relative(v, index[0], n_fsdp) for v in rows]
+    return pl.pallas_call(
+        functools.partial(turn_body, blocks, blocks == n_fsdp, contexts),
+        out_shape=(jax.ShapeDtypeStruct((D // 2, total), bf16),) * 2,
+        in_specs=[pl.BlockSpec(memory_space=pltpu.SMEM), pl.BlockSpec(memory_space=pltpu.SMEM)] + [pl.BlockSpec(memory_space=pltpu.VMEM)] * len(rows),
+        cost_estimate=cost(4),
+        compiler_params=params(60),
+    )(index, ctx, *rows)
+
+
+def weight_body(*refs):
+    own, beside, acts = refs[:2], refs[2:4], refs[4:7]
+    acts_beside, (near_ref, far_ref) = refs[7:10], refs[10:]
     cut = near_ref.shape[1]
     for k in range(3):
-        value = dot_plain(own_ref[k // 2], acts[k][...])
-        value = value + dot_plain(beside_ref[k // 2], acts_beside[k][...])
+        value = dot_plain(own[k // 2][...], acts[k][...])
+        value = value + dot_plain(beside[k // 2][...], acts_beside[k][...])
         near_ref[k] = value[:cut].astype(bf16)
         far_ref[k] = value[cut:].astype(bf16)
 
 
 def weight_grads(own, beside, acts, acts_beside):
     total, width = acts[0].shape
-    left = pl.BlockSpec(own.shape, lambda j: (0, 0, 0), pipeline_mode=pl.Buffered(1))
+    left = pl.BlockSpec(own[0].shape, lambda j: (0, 0), pipeline_mode=pl.Buffered(1))
     right = pl.BlockSpec((total, WIDE), lambda j: (0, j))
     out = pl.BlockSpec((3, D // 4, WIDE), lambda j: (0, 0, j))
     return pl.pallas_call(
         weight_body,
         out_shape=(jax.ShapeDtypeStruct((3, D // 4, width), bf16),) * 2,
         grid=(width // WIDE,),
-        in_specs=[left, left] + [right] * 6,
+        in_specs=[left] * 4 + [right] * 6,
         out_specs=(out, out),
         compiler_params=params(60),
         cost_estimate=cost(12),
-    )(own, beside, *acts, *acts_beside)
+    )(*own, *beside, *acts, *acts_beside)
 
 
 def middle_back_body(
@@ -778,16 +843,10 @@
 
     bias_cols = HD // n_fsdp
 
-    def qkv_pack(g1, g2, b_q, b_k, b_v, *w):
-        biases = jnp.concatenate([b_q, b_k, b_v], axis=0).astype(bf16)
-        spread = jnp.concatenate([biases] * n_fsdp, axis=1)
-        lane = jnp.arange(HD, dtype=jnp.int32)[None, :] // bias_cols
-        spread = jnp.where(lane == my_fsdp, spread, jnp.zeros_like(spread))
-        gains = jnp.pad(jnp.stack([g1, g2]).astype(bf16), ((0, 6), (0, qkv_width - shard)))
-        spread = jnp.pad(spread, ((0, 8 - all_heads), (0, qkv_width - HD)))
-        return stack(jnp.concatenate(w, axis=1).astype(bf16), gains, spread)
-
-    qkv_h = Pieces(run, run(qkv_pack, attn_gain, mlp_gain, b_q, b_k, b_v, w_q, w_k, w_v))
+    index = my_fsdp.astype(jnp.int32).reshape(1)
+    qkv_h = Pieces(
+        run, run(qkv_pack, index, attn_gain, mlp_gain, b_q, b_k, b_v, w_q, w_k, w_v)
+    )
     out_cast = run(lambda w: w.astype(bf16), w_o)
 
     def arrange(values):
@@ -881,7 +940,6 @@
             jnp.concatenate([-sine, sine], axis=1),
         )
 
-    index = my_fsdp.astype(jnp.int32).reshape(1)
     ctx = my_ctx.astype(jnp.int32).reshape(1)
     feed_in = [packed(0)]
     mine_tokens, other_tokens = run(arrange, tokens)
@@ -978,12 +1036,15 @@
 
     carry = feed_team(0, ())
     lines.across_rest()
+    turned_grads, grads_sent = run(lambda *a: turn_rows(*a, n_fsdp), index, ctx, grads)
+    grads_beside = swap(grads_sent, "fsdp", 1)
     carry = feed_team(1, carry)
     lines.pin_rest()
-    turned, turned_sent = run(
-        lambda *a: turn_rows(*a, n_fsdp), index, ctx, lines.team() + lines.rest(), grads
-    )
-    turned_beside = swap(turned_sent, "fsdp", 1)
+    turned_lines, lines_sent = run(
+        lambda *a: turn_rows(*a, n_fsdp), index, ctx, lines.team() + lines.rest()
+    )
+    turned = (turned_lines, turned_grads)
+    turned_beside = (swap(lines_sent, "fsdp", 1), grads_beside)
     feed_rest(0)
     feed_rest(1)
     grads_of(0)
@@ -1125,8 +1186,9 @@
     small = small_step(small)
     small = small_step(small)
     reduce_o.step()
+    arrived = reduce_qkv.sent
     reduce_qkv.step()
-    out_beside = swap(out_beside, "context", 1)
+    out_beside = swap(after(out_beside, arrived), "context", 1)
     other_parts[2] = run.pin(other_parts[2])
     reduce_o.step()
     reduce_qkv.step()

time: 498 us -> 490 us (0.984)
  waiting for transfers between devices: 159 us -> 148 us
  local copies, waits for them, and re-layouts: 22.7 us -> 28.2 us
  Pallas kernels: 192 us -> 197 us
    ppermute x52 -> x53, waiting for transfers between devices: 149 us -> 138 us  [swap(): return lax.ppermute(values, axis_name, [(i, i ^ bit) for i in range(size)])]
    pallas_call x1 -> x3, Pallas kernels: 7.93 us -> 12.1 us  [the longest x2 9.4 us: turn_rows(): pl.pallas_call(functools.partial(turn_body, blocks, blocks == n_fsdp, con...]
    unnamed x96 -> x98, local copies, waits for them, and re-layouts: 9.22 us -> 12.2 us
    ppermute x52 -> x53, starting transfers between devices: 48.5 us -> 47 us  [swap(): return lax.ppermute(values, axis_name, [(i, i ^ bit) for i in range(size)])]
  transfers between devices with their start and end apart: 60 -> 61, of which waited for: 26 -> 23; matrix products, arithmetic and copies ran while one was open for 10% -> 11% of each run, Pallas kernels for 39% -> 40%
where the time goes in v4:
time: 490 us; the launch traced here: 483 us
  Pallas kernels  197 us (40%)
  waiting for transfers between devices  148 us (30%)
  starting transfers between devices  57.7 us (12%)
  other arithmetic  34.6 us (7%)
  local copies, waits for them, and re-layouts  28.2 us (6%)
  between operations  15.2 us (3%)
    ppermute x53, waiting for transfers between devices, swap(): return lax.ppermute(values, axis_name, [(i, i ^ bit) for i in range(size)])  138 us
    pallas_call x6, Pallas kernels, feed(): pl.pallas_call(functools.partial(feed_body, weights.shape[0], ((0,) if ba...  79.2 us
    ppermute x53, starting transfers between devices, swap(): return lax.ppermute(values, axis_name, [(i, i ^ bit) for i in range(size)])  47 us
    pallas_call x3, Pallas kernels, weight_grads(): pl.pallas_call(weight_body, out_shape=(jax.ShapeDtypeStruct((3, D // 4, w...  39.5 us
    pallas_call x3, Pallas kernels, place(): pl.pallas_call(functools.partial(place_body, plan, len(carry)), out_shape...  15.9 us
    unnamed x98, local copies, waits for them, and re-layouts  12.2 us
    pallas_call x3, Pallas kernels, pack(): pl.pallas_call(functools.partial(pack_body, count), out_shape=jax.ShapeDt...  11.1 us
    pallas_call x1, Pallas kernels, attend_back(): pl.pallas_call(functools.partial(attend_back_body, len(weights), len(kv_p...  10.7 us
  transfers between devices with their start and end apart: 61, of which 23 were waited for; matrix products, arithmetic and copies ran while one was open for 11% of the time, Pallas kernels for 40%

profile of v4, /device:TPU:0, one launch (start us, length us, event | category | flops | bytes accessed | tf_op | source)
XLA Modules:
  0.0 483.4 jit_solution(16680489377771922862)
XLA Ops:
  7.2 2.7 shard_map.263.refs_0_
  12.1 3.0 collective-permute-start
  15.1 3.7 shard_map.264
  19.8 3.8 shard_map.265
  23.5 9.8 %collective-permute-done.refs_1_ = bf16[400,1024]{1,0:T(8,128)(2,1)S(1)} collective-permute-done((bf16[400,1024]{1,0:T(8,128)(2,1)S(1)}, bf16[400,1024]{1,0:T(8,128)(2,1)S(1)}, u32[]{:S(2)}, u32[]{:S(2)}) %collective-permute-start) | collective-permute-done | bytes 819232 | tf_op jit(solution)/shard_map/ppermute | solution.py:44
  34.5 3.7 shard_map.266
  45.2 4.7 shard_map.268
  60.1 3.5 collective-permute-start.4
  63.6 4.5 collective-permute-start.5
  74.8 8.9 %shard_map.269 = (bf16[256,768]{1,0:T(8,128)(2,1)}, f32[128,1536]{1,0:T(8,128)}, bf16[128,1536]{1,0:T(8,128)(2,1)}) custom-call(s32[1]{0:T(128)} %bitcast.1.index_ref, bf16[256,768]{1,0:T(8,128)(2,1)} %get-tuple-element.627.q_ref, s32[256,1]{1,0:T(8,128)} %copy.52.low_ref, s32[256,1]{1,0:T(8,128)} %fusion.17.high_ref, s32[1,768]{1,0:T(1,128)} %broadcast_in_dim.76.key_ref, ...), custom_call_target="tpu_custom_call" | custom-call | flops 3520000000 | bytes 11520000 | tf_op jit(solution)/shard_map/pallas_call | solution.py:335
  86.3 8.5 %collective-permute-done.7.refs_3_.refs_1_ = bf16[4,128,1536]{2,1,0:T(8,128)(2,1)S(1)} collective-permute-done((bf16[4,128,1536]{2,1,0:T(8,128)(2,1)S(1)}, bf16[4,128,1536]{2,1,0:T(8,128)(2,1)S(1)}, u32[]{:S(2)}, u32[]{:S(2)}) %collective-permute-start.7) | collective-permute-done | bytes 1572896 | tf_op jit(solution)/shard_map/ppermute | solution.py:44
  94.8 8.0 %collective-permute-done.6.other_ref = bf16[128,1536]{1,0:T(8,128)(2,1)S(1)} collective-permute-done((bf16[128,1536]{1,0:T(8,128)(2,1)}, bf16[128,1536]{1,0:T(8,128)(2,1)S(1)}, u32[]{:S(2)}, u32[]{:S(2)}) %collective-permute-start.6) | collective-permute-done | bytes 393248 | tf_op jit(solution)/shard_map/ppermute | solution.py:44
  103.5 2.5 shard_map.270
  107.8 9.1 %collective-permute-done.8 = bf16[128,1536]{1,0:T(8,128)(2,1)S(1)} collective-permute-done((bf16[128,1536]{1,0:T(8,128)(2,1)}, bf16[128,1536]{1,0:T(8,128)(2,1)S(1)}, u32[]{:S(2)}, u32[]{:S(2)}) %collective-permute-start.8) | collective-permute-done | bytes 393248 | tf_op jit(solution)/shard_map/ppermute | solution.py:44
  119.8 2.6 collective-permute-start.11
  122.4 14.1 %collective-permute-done.10.refs_1_ = bf16[256,1536]{1,0:T(8,128)(2,1)S(1)} collective-permute-done((bf16[256,1536]{1,0:T(8,128)(2,1)S(1)}, bf16[256,1536]{1,0:T(8,128)(2,1)S(1)}, u32[]{:S(2)}, u32[]{:S(2)}) %collective-permute-start.10) | collective-permute-done | bytes 786464 | tf_op jit(solution)/shard_map/ppermute | solution.py:44
  137.4 15.3 %shard_map.271 = (bf16[1024,768]{1,0:T(8,128)(2,1)}, bf16[1024,768]{1,0:T(8,128)(2,1)}, bf16[1024,768]{1,0:T(8,128)(2,1)}, f32[512,1536]{1,0:T(8,128)}, f32[512,1536]{1,0:T(8,128)}) custom-call(s32[1]{0:T(128)} %bitcast.23.limit_ref, s32[1]{0:T(128)} %bitcast.20.ctx_ref, bf16[256,1536]{1,0:T(8,128)(2,1)} %copy-done.31, bf16[256,1536]{1,0:T(8,128)(2,1)} %copy-done.39, ...), custom_call_target="tpu_custom_call" | custom-call | flops 6600000000 | bytes 21600000 | tf_op jit(solution)/shard_map/pallas_call | solution.py:468
  152.7 2.8 collective-permute-done.11.refs_2_.refs_0_
  156.0 4.8 shard_map.272
  160.8 17.0 %shard_map.273 = (bf16[1024,768]{1,0:T(8,128)(2,1)}, bf16[1024,768]{1,0:T(8,128)(2,1)}, bf16[1024,768]{1,0:T(8,128)(2,1)}, f32[512,1536]{1,0:T(8,128)}, f32[512,1536]{1,0:T(8,128)}) custom-call(s32[1]{0:T(128)} %constant.120.clone.1.limit_ref, s32[1]{0:T(128)} %bitcast.20.ctx_ref, bf16[256,1536]{1,0:T(8,128)(2,1)} %copy-done.31, ...), custom_call_target="tpu_custom_call" | custom-call | flops 6600000000 | bytes 21600000 | tf_op jit(solution)/shard_map/pallas_call | solution.py:468
  178.7 4.6 shard_map.274
  183.3 10.4 %shard_map.275 = (bf16[1024,768]{1,0:T(8,128)(2,1)}, bf16[1024,768]{1,0:T(8,128)(2,1)}, bf16[1024,768]{1,0:T(8,128)(2,1)}) custom-call(s32[1]{0:T(128)} %bitcast.23.limit_ref, s32[1]{0:T(128)} %bitcast.20.ctx_ref, bf16[256,1536]{1,0:T(8,128)(2,1)} %copy-done.2, ...), custom_call_target="tpu_custom_call", output_to_operand_aliasing={{0}: (7, {}), {1}: (8, {}), {2}: (9, {})} | custom-call | flops 3960000000 | bytes 12960000 | tf_op jit(solution)/shard_map/pallas_call | solution.py:468
  195.0 10.5 %shard_map.276 = (bf16[1024,768]{1,0:T(8,128)(2,1)}, bf16[1024,768]{1,0:T(8,128)(2,1)}, bf16[1024,768]{1,0:T(8,128)(2,1)}) custom-call(s32[1]{0:T(128)} %constant.120.clone.1.limit_ref, s32[1]{0:T(128)} %bitcast.20.ctx_ref, bf16[256,1536]{1,0:T(8,128)(2,1)} %copy-done.2, ...), custom_call_target="tpu_custom_call", output_to_operand_aliasing={{0}: (7, {}), {1}: (8, {}), {2}: (9, {})} | custom-call | flops 3960000000 | bytes 12960000 | tf_op jit(solution)/shard_map/pallas_call | solution.py:468
  207.9 13.1 %shard_map.277 = (bf16[3,384,768]{2,1,0:T(8,128)(2,1)}, bf16[3,384,768]{2,1,0:T(8,128)(2,1)}) custom-call(bf16[768,1024]{1,0:T(8,128)(2,1)} %get-tuple-element.612.refs_0_, bf16[768,1024]{1,0:T(8,128)(2,1)} %get-tuple-element.613.refs_1_, bf16[768,1024]{1,0:T(8,128)(2,1)} %copy-done.38, bf16[768,1024]{1,0:T(8,128)(2,1)} %copy-done.37, ...), custom_call_target="tpu_custom_call" | custom-call | flops 5280000000 | bytes 17280000 | tf_op jit(solution)/shard_map/pallas_call | solution.py:539
  222.3 15.6 %shard_map.278 = (bf16[1024,768]{1,0:T(8,128)(2,1)}, bf16[1024,768]{1,0:T(8,128)(2,1)}, bf16[1024,768]{1,0:T(8,128)(2,1)}, f32[128,1536]{1,0:T(8,128)}, f32[128,...) custom-call(s32[1]{0:T(128)} %constant.120.clone.1.limit_ref, ...), custom_call_target="tpu_custom_call" | custom-call | flops 6600000000 | bytes 21600000 | tf_op jit(solution)/shard_map/pallas_call | solution.py:468
  239.6 10.4 %shard_map.279 = (bf16[1024,768]{1,0:T(8,128)(2,1)}, bf16[1024,768]{1,0:T(8,128)(2,1)}, bf16[1024,768]{1,0:T(8,128)(2,1)}) custom-call(s32[1]{0:T(128)} %constant.120.clone.1.limit_ref, s32[1]{0:T(128)} %bitcast.20.ctx_ref, bf16[256,1536]{1,0:T(8,128)(2,1)} %copy-done.2, ...), custom_call_target="tpu_custom_call", output_to_operand_aliasing={{0}: (7, {}), {1}: (8, {}), {2}: (9, {})} | custom-call | flops 3960000000 | bytes 12960000 | tf_op jit(solution)/shard_map/pallas_call | solution.py:468
  250.6 13.3 %shard_map.280 = (bf16[3,384,768]{2,1,0:T(8,128)(2,1)}, bf16[3,384,768]{2,1,0:T(8,128)(2,1)}) custom-call(bf16[768,1024]{1,0:T(8,128)(2,1)} %get-tuple-element.612.refs_0_, bf16[768,1024]{1,0:T(8,128)(2,1)} %get-tuple-element.613.refs_1_, bf16[768,1024]{1,0:T(8,128)(2,1)} %copy-done.38, bf16[768,1024]{1,0:T(8,128)(2,1)} %copy-done.37, ...), custom_call_target="tpu_custom_call" | custom-call | flops 5280000000 | bytes 17280000 | tf_op jit(solution)/shard_map/pallas_call | solution.py:539
  268.9 7.8 %collective-permute-done.25.far_ref = bf16[128,1536]{1,0:T(8,128)(2,1)S(1)} collective-permute-done((bf16[128,1536]{1,0:T(8,128)(2,1)S(1)}, bf16[128,1536]{1,0:T(8,128)(2,1)S(1)}, u32[]{:S(2)}, u32[]{:S(2)}) %collective-permute-start.25) | collective-permute-done | bytes 393248 | tf_op jit(solution)/shard_map/ppermute | solution.py:44
  279.0 3.4 shard_map.281
  283.0 13.1 %shard_map.282 = (bf16[3,384,768]{2,1,0:T(8,128)(2,1)}, bf16[3,384,768]{2,1,0:T(8,128)(2,1)}) custom-call(bf16[768,1024]{1,0:T(8,128)(2,1)} %get-tuple-element.612.refs_0_, bf16[768,1024]{1,0:T(8,128)(2,1)} %get-tuple-element.613.refs_1_, bf16[768,1024]{1,0:T(8,128)(2,1)} %copy-done.38, bf16[768,1024]{1,0:T(8,128)(2,1)} %copy-done.37, ...), custom_call_target="tpu_custom_call" | custom-call | flops 5280000000 | bytes 17280000 | tf_op jit(solution)/shard_map/pallas_call | solution.py:539
  301.7 10.7 %shard_map.283 = (bf16[256,768]{1,0:T(8,128)(2,1)}, f32[256,256]{1,0:T(8,128)}, bf16[256,256]{1,0:T(8,128)(2,1)}, bf16[256,256]{1,0:T(8,128)(2,1)}) custom-call(s32[1]{0:T(128)} %bitcast.1.index_ref, bf16[256,768]{1,0:T(8,128)(2,1)} %get-tuple-element.627.q_ref, s32[256,1]{1,0:T(8,128)} %copy.53.low_ref, s32[256,1]{1,0:T(8,128)} %fusion.17.high_ref, ...), custom_call_target="tpu_custom_call" | custom-call | flops 4400000000 | bytes 14400000 | tf_op jit(solution)/shard_map/pallas_call | solution.py:622
  318.2 2.5 add_convert_fusion.1.refs_0_
  322.9 4.7 collective-permute-done.32.refs_6_
  328.3 4.6 shard_map.284
  334.5 5.2 %shard_map.285 = (f32[384,4480]{1,0:T(8,128)}, f32[384,4480]{1,0:T(8,128)}, f32[4480,384]{1,0:T(8,128)}) custom-call(s32[1]{0:T(128)} %bitcast.25.member_ref, bf16[3,384,768]{2,1,0:T(8,128)(2,1)} %copy-done.4, bf16[3,384,768]{2,1,0:T(8,128)(2,1)} %copy-done.12), custom_call_target="tpu_custom_call" | custom-call | flops 440000000 | bytes 1440000 | tf_op jit(solution)/shard_map/pallas_call | solution.py:738
  345.4 2.8 shard_map.286
  354.7 2.4 add_convert_fusion.refs_0_
  361.1 8.8 %collective-permute-done.33.refs_1_ = bf16[3,384,768]{2,1,0:T(8,128)(2,1)} collective-permute-done((bf16[3,384,768]{2,1,0:T(8,128)(2,1)S(1)}, bf16[3,384,768]{2,1,0:T(8,128)(2,1)}, u32[]{:S(2)}, u32[]{:S(2)}) %collective-permute-start.33) | collective-permute-done | bytes 1769504 | tf_op jit(solution)/shard_map/ppermute | solution.py:44
  372.3 10.3 %collective-permute-done.41 = bf16[384,1024]{1,0:T(8,128)(2,1)S(1)} collective-permute-done((bf16[384,1024]{1,0:T(8,128)(2,1)S(1)}, bf16[384,1024]{1,0:T(8,128)(2,1)S(1)}, u32[]{:S(2)}, u32[]{:S(2)}) %collective-permute-start.41) | collective-permute-done | bytes 786464 | tf_op jit(solution)/shard_map/ppermute | solution.py:44
  387.4 5.3 %shard_map.287 = (f32[384,4480]{1,0:T(8,128)}, f32[384,4480]{1,0:T(8,128)}, f32[4480,384]{1,0:T(8,128)}) custom-call(s32[1]{0:T(128)} %bitcast.25.member_ref, bf16[3,384,768]{2,1,0:T(8,128)(2,1)} %copy-done.6, bf16[3,384,768]{2,1,0:T(8,128)(2,1)} %collective-permute-done.33.refs_1_, ...), custom_call_target="tpu_custom_call", output_to_operand_aliasing={{0}: (3, {}), {1}: (4, {}), {2}: (5, {})} | custom-call | flops 440000000 | bytes 1440000 | tf_op jit(solution)/shard_map/pallas_call | solution.py:738
  392.7 8.3 %collective-permute-done.38 = bf16[256,1536]{1,0:T(8,128)(2,1)} collective-permute-done((bf16[256,1536]{1,0:T(8,128)(2,1)}, bf16[256,1536]{1,0:T(8,128)(2,1)}, u32[]{:S(2)}, u32[]{:S(2)}) %collective-permute-start.38) | collective-permute-done | bytes 786464 | tf_op jit(solution)/shard_map/ppermute | solution.py:44
  405.8 15.4 %collective-permute-done.42 = bf16[384,512]{1,0:T(8,128)(2,1)} collective-permute-done((bf16[384,512]{1,0:T(8,128)(2,1)}, bf16[384,512]{1,0:T(8,128)(2,1)}, u32[]{:S(2)}, u32[]{:S(2)}) %collective-permute-start.42) | collective-permute-done | bytes 393248 | tf_op jit(solution)/shard_map/ppermute | solution.py:44
  425.8 3.0 collective-permute-start.51
  428.7 18.0 %collective-permute-done.47 = bf16[192,384]{1,0:T(8,128)(2,1)S(1)} collective-permute-done((bf16[192,384]{1,0:T(8,128)(2,1)S(1)}, bf16[192,384]{1,0:T(8,128)(2,1)S(1)}, u32[]{:S(2)}, u32[]{:S(2)}) %collective-permute-start.47) | collective-permute-done | bytes 147488 | tf_op jit(solution)/shard_map/ppermute | solution.py:44
  446.9 5.9 %collective-permute-done.51 = bf16[384,256]{1,0:T(8,128)(2,1)S(1)} collective-permute-done((bf16[384,256]{1,0:T(8,128)(2,1)S(1)}, bf16[384,256]{1,0:T(8,128)(2,1)S(1)}, u32[]{:S(2)}, u32[]{:S(2)}) %collective-permute-start.51) | collective-permute-done | bytes 196640 | tf_op jit(solution)/shard_map/ppermute | solution.py:44
  452.9 3.0 collective-permute-start.53
  462.2 5.3 %shard_map.288 = (f32[384,4480]{1,0:T(8,128)}, f32[384,4480]{1,0:T(8,128)}, f32[4480,384]{1,0:T(8,128)}) custom-call(s32[1]{0:T(128)} %bitcast.25.member_ref, bf16[3,384,768]{2,1,0:T(8,128)(2,1)} %copy-done.5, bf16[3,384,768]{2,1,0:T(8,128)(2,1)} %collective-permute-done.48.refs_1_, ...), custom_call_target="tpu_custom_call", output_to_operand_aliasing={{0}: (3, {}), {1}: (4, {}), {2}: (5, {})} | custom-call | flops 440000000 | bytes 1440000 | tf_op jit(solution)/shard_map/pallas_call | solution.py:738
  470.6 3.7 collective-permute-done.55
  (292 shorter events, 112.9 us)
Async XLA Ops:
  7.2 44.8 %all-gather.9.cloned.1.call-start = ((), (), s32[]{:S(2)}) async-start(), calls=%async_computation | async-start | bytes 1966080 | tf_op jit(solution)/shard_map/all_gather | solution.py:889
  12.1 124.4 %all-gather.15.cloned.1.call-start = ((), (), s32[]{:S(2)}) async-start(), calls=%async_computation.3 | async-start | bytes 8847360 | tf_op jit(solution)/shard_map/all_gather | solution.py:950
  12.1 21.2 %collective-permute-start = (bf16[400,1024]{1,0:T(8,128)(2,1)S(1)}, bf16[400,1024]{1,0:T(8,128)(2,1)S(1)}, u32[]{:S(2)}, u32[]{:S(2)}) collective-permute-start(bf16[400,1024]{1,0:T(8,128)(2,1)S(1)} %copy-done.9), channel_id=1, source_target_pairs={{0,16},{8,24},{16,0},{24,8},{1,17},{9,25},{17,1},{25,9},{2,18},{10... | collective-permute-start | bytes 2457608 | tf_op jit(solution)/shard_map/ppermute | solution.py:44
  33.4 127.4 %all-gather.13.cloned.1.call-start = ((), (), s32[]{:S(2)}) async-start(), calls=%async_computation.2 | async-start | bytes 8847360 | tf_op jit(solution)/shard_map/all_gather | solution.py:950
  34.1 188.2 %all-gather.11.cloned.1.call-start = ((), (), s32[]{:S(2)}) async-start(), calls=%async_computation.1 | async-start | bytes 8847360 | tf_op jit(solution)/shard_map/all_gather | solution.py:950
  39.1 16.0 %collective-permute-start.2 = (bf16[768,384]{1,0:T(8,128)(2,1)}, bf16[768,384]{1,0:T(8,128)(2,1)}, u32[]{:S(2)}, u32[]{:S(2)}) collective-permute-start(bf16[768,384]{1,0:T(8,128)(2,1)} %convert_element_type.112.refs_0_.refs_2_), channel_id=1, source_target_pairs={{0,16},{8,24},{16,0},{24,8},{1,17},{9,25},{17,1},{25,9},{2,18},{10... | collective-permute-start | bytes 1769480 | tf_op jit(solution)/shard_map/ppermute | solution.py:44
  57.5 14.1 %collective-permute-start.3 = (bf16[2,768,384]{2,1,0:T(8,128)(2,1)}, bf16[2,768,384]{2,1,0:T(8,128)(2,1)}, u32[]{:S(2)}, u32[]{:S(2)}) collective-permute-start(bf16[2,768,384]{2,1,0:T(8,128)(2,1)} %pad_maximum_fusion.1), channel_id=1, source_target_pairs={{0,8},{8,0},{16,24},{24,16},{1,9},{9,1},{17,25},{25,17},{2,10},{10... | collective-permute-start | bytes 3538952 | tf_op jit(solution)/shard_map/ppermute | solution.py:44
  57.5 37.3 %collective-permute-start.7 = (bf16[4,128,1536]{2,1,0:T(8,128)(2,1)S(1)}, bf16[4,128,1536]{2,1,0:T(8,128)(2,1)S(1)}, u32[]{:S(2)}, u32[]{:S(2)}) collective-permute-start(bf16[4,128,1536]{2,1,0:T(8,128)(2,1)S(1)} %bitcast.42), channel_id=1, source_target_pairs={{0,1},{1,0},{2,3},{3,2},{4,5},{5,4},{6,7},{7,6},{8,9},{9,8},{10,11... | collective-permute-start | bytes 4718600 | tf_op jit(solution)/shard_map/ppermute | solution.py:44
  83.7 19.0 %collective-permute-start.6 = (bf16[128,1536]{1,0:T(8,128)(2,1)}, bf16[128,1536]{1,0:T(8,128)(2,1)S(1)}, u32[]{:S(2)}, u32[]{:S(2)}) collective-permute-start(bf16[128,1536]{1,0:T(8,128)(2,1)} %get-tuple-element.457), channel_id=1, source_target_pairs={{0,1},{1,0},{2,3},{3,2},{4,5},{5,4},{6,7},{7,6},{8,9},{9,8},{10,11... | collective-permute-start | bytes 1179656 | tf_op jit(solution)/shard_map/ppermute | solution.py:44
  86.3 21.6 %collective-permute-start.9 = (bf16[256,1536]{1,0:T(8,128)(2,1)}, bf16[256,1536]{1,0:T(8,128)(2,1)}, u32[]{:S(2)}, u32[]{:S(2)}) collective-permute-start(bf16[256,1536]{1,0:T(8,128)(2,1)} %pad_maximum_fusion.3), channel_id=1, source_target_pairs={{0,8},{8,0},{16,24},{24,16},{1,9},{9,1},{17,25},{25,17},{2,10},{10... | collective-permute-start | bytes 2359304 | tf_op jit(solution)/shard_map/ppermute | solution.py:44
  118.1 18.4 %collective-permute-start.10 = (bf16[256,1536]{1,0:T(8,128)(2,1)S(1)}, bf16[256,1536]{1,0:T(8,128)(2,1)S(1)}, u32[]{:S(2)}, u32[]{:S(2)}) collective-permute-start(bf16[256,1536]{1,0:T(8,128)(2,1)S(1)} %constant_dynamic-update-slice_fusion.refs_0_), channel_id=1, source_target_pairs={{0,1},{1,0},{2,3},{3,2},{4,5},{5,4},{6,7},{7,6},{8,9},{9,8},{10,11... | collective-permute-start | bytes 2359304 | tf_op jit(solution)/shard_map/ppermute | solution.py:44
  119.8 35.7 %collective-permute-start.11 = (bf16[256,1536]{1,0:T(8,128)(2,1)S(1)}, bf16[256,1536]{1,0:T(8,128)(2,1)S(1)}, u32[]{:S(2)}, u32[]{:S(2)}) collective-permute-start(bf16[256,1536]{1,0:T(8,128)(2,1)S(1)} %constant_dynamic-update-slice_fusion.refs_0_), channel_id=1, source_target_pairs={{0,4},{2,6},{4,0},{6,2},{1,5},{3,7},{5,1},{7,3},{8,12},{10,14},{12... | collective-permute-start | bytes 2359304 | tf_op jit(solution)/shard_map/ppermute | solution.py:44
  155.5 22.3 %collective-permute-start.12 = (bf16[256,1536]{1,0:T(8,128)(2,1)S(1)}, bf16[256,1536]{1,0:T(8,128)(2,1)S(1)}, u32[]{:S(2)}, u32[]{:S(2)}) collective-permute-start(bf16[256,1536]{1,0:T(8,128)(2,1)S(1)} %collective-permute-done.11.refs_2_.refs_0_), channel_id=1, source_target_pairs={{0,1},{1,0},{2,3},{3,2},{4,5},{5,4},{6,7},{7,6},{8,9},{9,8},{10,11... | collective-permute-start | bytes 2359304 | tf_op jit(solution)/shard_map/ppermute | solution.py:44
  160.8 44.7 %collective-permute-start.14 = (bf16[768,1024]{1,0:T(8,128)(2,1)}, bf16[768,1024]{1,0:T(8,128)(2,1)S(1)}, u32[]{:S(2)}, u32[]{:S(2)}) collective-permute-start(bf16[768,1024]{1,0:T(8,128)(2,1)} %get-tuple-element.514), channel_id=1, source_target_pairs={{0,8},{8,0},{16,24},{24,16},{1,9},{9,1},{17,25},{25,17},{2,10},{10... | collective-permute-start | bytes 4718600 | tf_op jit(solution)/shard_map/ppermute | solution.py:44
  193.7 12.4 %collective-permute-start.15 = (bf16[1024,768]{1,0:T(8,128)(2,1)}, bf16[1024,768]{1,0:T(8,128)(2,1)}, u32[]{:S(2)}, u32[]{:S(2)}) collective-permute-start(bf16[1024,768]{1,0:T(8,128)(2,1)} %get-tuple-element.547.refs_4_), channel_id=1, source_target_pairs={{0,8},{8,0},{16,24},{24,16},{1,9},{9,1},{17,25},{25,17},{2,10},{10... | collective-permute-start | bytes 4718600 | tf_op jit(solution)/shard_map/ppermute | solution.py:44
  194.4 11.8 %collective-permute-start.16 = (bf16[1024,768]{1,0:T(8,128)(2,1)}, bf16[1024,768]{1,0:T(8,128)(2,1)}, u32[]{:S(2)}, u32[]{:S(2)}) collective-permute-start(bf16[1024,768]{1,0:T(8,128)(2,1)} %get-tuple-element.548.refs_5_), channel_id=1, source_target_pairs={{0,8},{8,0},{16,24},{24,16},{1,9},{9,1},{17,25},{25,17},{2,10},{10... | collective-permute-start | bytes 4718600 | tf_op jit(solution)/shard_map/ppermute | solution.py:44
  194.5 12.1 %collective-permute-start.17 = (bf16[1024,768]{1,0:T(8,128)(2,1)}, bf16[1024,768]{1,0:T(8,128)(2,1)}, u32[]{:S(2)}, u32[]{:S(2)}) collective-permute-start(bf16[1024,768]{1,0:T(8,128)(2,1)} %get-tuple-element.549.refs_6_), channel_id=1, source_target_pairs={{0,8},{8,0},{16,24},{24,16},{1,9},{9,1},{17,25},{25,17},{2,10},{10... | collective-permute-start | bytes 4718600 | tf_op jit(solution)/shard_map/ppermute | solution.py:44
  194.9 11.7 %collective-permute-start.13 = (bf16[768,1024]{1,0:T(8,128)(2,1)}, bf16[768,1024]{1,0:T(8,128)(2,1)S(1)}, u32[]{:S(2)}, u32[]{:S(2)}) collective-permute-start(bf16[768,1024]{1,0:T(8,128)(2,1)} %get-tuple-element.513), channel_id=1, source_target_pairs={{0,8},{8,0},{16,24},{24,16},{1,9},{9,1},{17,25},{25,17},{2,10},{10... | collective-permute-start | bytes 4718600 | tf_op jit(solution)/shard_map/ppermute | solution.py:44
  205.5 44.4 %collective-permute-start.18 = (bf16[1024,768]{1,0:T(8,128)(2,1)}, bf16[1024,768]{1,0:T(8,128)(2,1)}, u32[]{:S(2)}, u32[]{:S(2)}) collective-permute-start(bf16[1024,768]{1,0:T(8,128)(2,1)} %get-tuple-element.586.refs_4_), channel_id=1, source_target_pairs={{0,8},{8,0},{16,24},{24,16},{1,9},{9,1},{17,25},{25,17},{2,10},{10... | collective-permute-start | bytes 4718600 | tf_op jit(solution)/shard_map/ppermute | solution.py:44
  206.1 43.9 %collective-permute-start.19 = (bf16[1024,768]{1,0:T(8,128)(2,1)}, bf16[1024,768]{1,0:T(8,128)(2,1)}, u32[]{:S(2)}, u32[]{:S(2)}) collective-permute-start(bf16[1024,768]{1,0:T(8,128)(2,1)} %get-tuple-element.587.refs_5_), channel_id=1, source_target_pairs={{0,8},{8,0},{16,24},{24,16},{1,9},{9,1},{17,25},{25,17},{2,10},{10... | collective-permute-start | bytes 4718600 | tf_op jit(solution)/shard_map/ppermute | solution.py:44
  206.2 44.4 %collective-permute-start.20 = (bf16[1024,768]{1,0:T(8,128)(2,1)}, bf16[1024,768]{1,0:T(8,128)(2,1)}, u32[]{:S(2)}, u32[]{:S(2)}) collective-permute-start(bf16[1024,768]{1,0:T(8,128)(2,1)} %get-tuple-element.588.refs_6_), channel_id=1, source_target_pairs={{0,8},{8,0},{16,24},{24,16},{1,9},{9,1},{17,25},{25,17},{2,10},{10... | collective-permute-start | bytes 4718600 | tf_op jit(solution)/shard_map/ppermute | solution.py:44
  221.0 44.8 %collective-permute-start.22 = (bf16[3,384,768]{2,1,0:T(8,128)(2,1)}, bf16[3,384,768]{2,1,0:T(8,128)(2,1)S(1)}, u32[]{:S(2)}, u32[]{:S(2)}) collective-permute-start(bf16[3,384,768]{2,1,0:T(8,128)(2,1)} %get-tuple-element.553), channel_id=1, source_target_pairs={{0,16},{8,24},{16,0},{24,8},{1,17},{9,25},{17,1},{25,9},{2,18},{10... | collective-permute-start | bytes 5308424 | tf_op jit(solution)/shard_map/ppermute | solution.py:44
  237.9 26.0 %collective-permute-start.23 = (bf16[256,1536]{1,0:T(8,128)(2,1)}, bf16[256,1536]{1,0:T(8,128)(2,1)}, u32[]{:S(2)}, u32[]{:S(2)}) collective-permute-start(bf16[256,1536]{1,0:T(8,128)(2,1)} %get-tuple-element.596), channel_id=1, source_target_pairs={{0,1},{1,0},{2,3},{3,2},{4,5},{5,4},{6,7},{7,6},{8,9},{9,8},{10,11... | collective-permute-start | bytes 2359304 | tf_op jit(solution)/shard_map/ppermute | solution.py:44
  250.0 32.4 %collective-permute-start.27 = (bf16[1024,768]{1,0:T(8,128)(2,1)}, bf16[1024,768]{1,0:T(8,128)(2,1)}, u32[]{:S(2)}, u32[]{:S(2)}) collective-permute-start(bf16[1024,768]{1,0:T(8,128)(2,1)} %get-tuple-element.616.refs_4_), channel_id=1, source_target_pairs={{0,8},{8,0},{16,24},{24,16},{1,9},{9,1},{17,25},{25,17},{2,10},{10... | collective-permute-start | bytes 4718600 | tf_op jit(solution)/shard_map/ppermute | solution.py:44
  250.1 32.3 %collective-permute-start.28 = (bf16[1024,768]{1,0:T(8,128)(2,1)}, bf16[1024,768]{1,0:T(8,128)(2,1)}, u32[]{:S(2)}, u32[]{:S(2)}) collective-permute-start(bf16[1024,768]{1,0:T(8,128)(2,1)} %get-tuple-element.617.refs_5_), channel_id=1, source_target_pairs={{0,8},{8,0},{16,24},{24,16},{1,9},{9,1},{17,25},{25,17},{2,10},{10... | collective-permute-start | bytes 4718600 | tf_op jit(solution)/shard_map/ppermute | solution.py:44
  250.6 31.9 %collective-permute-start.29 = (bf16[1024,768]{1,0:T(8,128)(2,1)}, bf16[1024,768]{1,0:T(8,128)(2,1)}, u32[]{:S(2)}, u32[]{:S(2)}) collective-permute-start(bf16[1024,768]{1,0:T(8,128)(2,1)} %get-tuple-element.618.refs_6_), channel_id=1, source_target_pairs={{0,8},{8,0},{16,24},{24,16},{1,9},{9,1},{17,25},{25,17},{2,10},{10... | collective-permute-start | bytes 4718600 | tf_op jit(solution)/shard_map/ppermute | solution.py:44
  265.2 11.5 %collective-permute-start.25 = (bf16[128,1536]{1,0:T(8,128)(2,1)S(1)}, bf16[128,1536]{1,0:T(8,128)(2,1)S(1)}, u32[]{:S(2)}, u32[]{:S(2)}) collective-permute-start(bf16[128,1536]{1,0:T(8,128)(2,1)S(1)} %add_convert_fusion.5), channel_id=1, source_target_pairs={{0,2},{2,0},{4,6},{6,4},{1,3},{3,1},{5,7},{7,5},{8,10},{10,8},{12,... | collective-permute-start | bytes 1179656 | tf_op jit(solution)/shard_map/ppermute | solution.py:44
  265.8 51.2 %collective-permute-start.21 = (bf16[3,384,768]{2,1,0:T(8,128)(2,1)}, bf16[3,384,768]{2,1,0:T(8,128)(2,1)}, u32[]{:S(2)}, u32[]{:S(2)}) collective-permute-start(bf16[3,384,768]{2,1,0:T(8,128)(2,1)} %get-tuple-element.593), channel_id=1, source_target_pairs={{0,16},{8,24},{16,0},{24,8},{1,17},{9,25},{17,1},{25,9},{2,18},{10... | collective-permute-start | bytes 5308424 | tf_op jit(solution)/shard_map/ppermute | solution.py:44
  276.8 40.3 %collective-permute-start.24 = (bf16[3,384,768]{2,1,0:T(8,128)(2,1)S(1)}, bf16[3,384,768]{2,1,0:T(8,128)(2,1)S(1)}, u32[]{:S(2)}, u32[]{:S(2)}) collective-permute-start(bf16[3,384,768]{2,1,0:T(8,128)(2,1)S(1)} %add_convert_fusion.2.refs_0_), channel_id=1, source_target_pairs={{0,2},{2,0},{4,6},{6,4},{1,3},{3,1},{5,7},{7,5},{8,10},{10,8},{12,... | collective-permute-start | bytes 5308424 | tf_op jit(solution)/shard_map/ppermute | solution.py:44
  282.4 13.7 %collective-permute-start.26 = (bf16[128,1536]{1,0:T(8,128)(2,1)}, bf16[128,1536]{1,0:T(8,128)(2,1)}, u32[]{:S(2)}, u32[]{:S(2)}) collective-permute-start(bf16[128,1536]{1,0:T(8,128)(2,1)} %get-tuple-element.633.refs_0_), channel_id=1, source_target_pairs={{0,1},{1,0},{2,3},{3,2},{4,5},{5,4},{6,7},{7,6},{8,9},{9,8},{10,11... | collective-permute-start | bytes 1179656 | tf_op jit(solution)/shard_map/ppermute | solution.py:44
  299.5 54.6 %collective-permute-start.37 = (bf16[3,384,768]{2,1,0:T(8,128)(2,1)}, bf16[3,384,768]{2,1,0:T(8,128)(2,1)}, u32[]{:S(2)}, u32[]{:S(2)}) collective-permute-start(bf16[3,384,768]{2,1,0:T(8,128)(2,1)} %get-tuple-element.622), channel_id=1, source_target_pairs={{0,16},{8,24},{16,0},{24,8},{1,17},{9,25},{17,1},{25,9},{2,18},{10... | collective-permute-start | bytes 5308424 | tf_op jit(solution)/shard_map/ppermute | solution.py:44
  313.7 13.9 %collective-permute-start.32 = (bf16[256,256]{1,0:T(8,128)(2,1)}, bf16[256,256]{1,0:T(8,128)(2,1)S(1)}, u32[]{:S(2)}, u32[]{:S(2)}) collective-permute-start(bf16[256,256]{1,0:T(8,128)(2,1)} %get-tuple-element.647), channel_id=1, source_target_pairs={{4,0},{6,2},{5,1},{7,3},{12,8},{14,10},{13,9},{15,11},{20,16},{22,... | collective-permute-start | bytes 393224 | tf_op jit(solution)/shard_map/ppermute | solution.py:50
  328.2 41.6 %collective-permute-start.33 = (bf16[3,384,768]{2,1,0:T(8,128)(2,1)S(1)}, bf16[3,384,768]{2,1,0:T(8,128)(2,1)}, u32[]{:S(2)}, u32[]{:S(2)}) collective-permute-start(bf16[3,384,768]{2,1,0:T(8,128)(2,1)S(1)} %add_convert_fusion.1.refs_0_), channel_id=1, source_target_pairs={{0,2},{2,0},{4,6},{6,4},{1,3},{3,1},{5,7},{7,5},{8,10},{10,8},{12,... | collective-permute-start | bytes 5308424 | tf_op jit(solution)/shard_map/ppermute | solution.py:44
  332.9 11.7 %collective-permute-start.34 = (bf16[128,1536]{1,0:T(8,128)(2,1)}, bf16[128,1536]{1,0:T(8,128)(2,1)S(1)}, u32[]{:S(2)}, u32[]{:S(2)}) collective-permute-start(bf16[128,1536]{1,0:T(8,128)(2,1)} %get-tuple-element.668), channel_id=1, source_target_pairs={{0,1},{1,0},{2,3},{3,2},{4,5},{5,4},{6,7},{7,6},{8,9},{9,8},{10,11... | collective-permute-start | bytes 1179656 | tf_op jit(solution)/shard_map/ppermute | solution.py:44
  351.0 18.9 %collective-permute-start.39 = (bf16[768,384]{1,0:T(8,128)(2,1)S(1)}, bf16[768,384]{1,0:T(8,128)(2,1)S(1)}, u32[]{:S(2)}, u32[]{:S(2)}) collective-permute-start(bf16[768,384]{1,0:T(8,128)(2,1)S(1)} %slice.371), channel_id=1, source_target_pairs={{0,16},{8,24},{16,0},{24,8},{1,17},{9,25},{17,1},{25,9},{2,18},{10... | collective-permute-start | bytes 1769480 | tf_op jit(solution)/shard_map/ppermute | solution.py:44
  354.1 28.5 %collective-permute-start.41 = (bf16[384,1024]{1,0:T(8,128)(2,1)S(1)}, bf16[384,1024]{1,0:T(8,128)(2,1)S(1)}, u32[]{:S(2)}, u32[]{:S(2)}) collective-permute-start(bf16[384,1024]{1,0:T(8,128)(2,1)S(1)} %slice.370), channel_id=1, source_target_pairs={{0,16},{8,24},{16,0},{24,8},{1,17},{9,25},{17,1},{25,9},{2,18},{10... | collective-permute-start | bytes 2359304 | tf_op jit(solution)/shard_map/ppermute | solution.py:44
  357.1 68.5 %collective-permute-start.48 = (bf16[3,384,768]{2,1,0:T(8,128)(2,1)S(1)}, bf16[3,384,768]{2,1,0:T(8,128)(2,1)}, u32[]{:S(2)}, u32[]{:S(2)}) collective-permute-start(bf16[3,384,768]{2,1,0:T(8,128)(2,1)S(1)} %add_convert_fusion.refs_0_), channel_id=1, source_target_pairs={{0,2},{2,0},{4,6},{6,4},{1,3},{3,1},{5,7},{7,5},{8,10},{10,8},{12,... | collective-permute-start | bytes 5308424 | tf_op jit(solution)/shard_map/ppermute | solution.py:44
  370.7 16.5 %collective-permute-start.40 = (f32[2,1536]{1,0:T(2,128)S(1)}, f32[2,1536]{1,0:T(2,128)S(1)}, u32[]{:S(2)}, u32[]{:S(2)}) collective-permute-start(f32[2,1536]{1,0:T(2,128)S(1)} %pad_maximum_fusion.12), channel_id=1, source_target_pairs={{0,1},{1,0},{2,3},{3,2},{4,5},{5,4},{6,7},{7,6},{8,9},{9,8},{10,11... | collective-permute-start | bytes 36872 | tf_op jit(solution)/shard_map/ppermute | solution.py:44
  382.6 18.4 %collective-permute-start.38 = (bf16[256,1536]{1,0:T(8,128)(2,1)}, bf16[256,1536]{1,0:T(8,128)(2,1)}, u32[]{:S(2)}, u32[]{:S(2)}) collective-permute-start(bf16[256,1536]{1,0:T(8,128)(2,1)} %get-tuple-element.689), channel_id=1, source_target_pairs={{0,1},{1,0},{2,3},{3,2},{4,5},{5,4},{6,7},{7,6},{8,9},{9,8},{10,11... | collective-permute-start | bytes 2359304 | tf_op jit(solution)/shard_map/ppermute | solution.py:44
  385.2 38.2 %collective-permute-start.44 = (bf16[384,384]{1,0:T(8,128)(2,1)}, bf16[384,384]{1,0:T(8,128)(2,1)}, u32[]{:S(2)}, u32[]{:S(2)}) collective-permute-start(bf16[384,384]{1,0:T(8,128)(2,1)} %select_convert_fusion.1), channel_id=1, source_target_pairs={{0,2},{2,0},{4,6},{6,4},{1,3},{3,1},{5,7},{7,5},{8,10},{10,8},{12,... | collective-permute-start | bytes 884744 | tf_op jit(solution)/shard_map/ppermute | solution.py:44
  387.2 34.1 %collective-permute-start.42 = (bf16[384,512]{1,0:T(8,128)(2,1)}, bf16[384,512]{1,0:T(8,128)(2,1)}, u32[]{:S(2)}, u32[]{:S(2)}) collective-permute-start(bf16[384,512]{1,0:T(8,128)(2,1)} %select_convert_fusion), channel_id=1, source_target_pairs={{0,2},{2,0},{4,6},{6,4},{1,3},{3,1},{5,7},{7,5},{8,10},{10,8},{12,... | collective-permute-start | bytes 1179656 | tf_op jit(solution)/shard_map/ppermute | solution.py:44
  387.3 15.6 %collective-permute-start.45 = (f32[16,1536]{1,0:T(8,128)S(1)}, f32[16,1536]{1,0:T(8,128)S(1)}, u32[]{:S(2)}, u32[]{:S(2)}) collective-permute-start(f32[16,1536]{1,0:T(8,128)S(1)} %select_maximum_fusion), channel_id=1, source_target_pairs={{0,8},{8,0},{16,24},{24,16},{1,9},{9,1},{17,25},{25,17},{2,10},{10... | collective-permute-start | bytes 294920 | tf_op jit(solution)/shard_map/ppermute | solution.py:44
  402.9 18.7 %collective-permute-start.46 = (f32[16,1536]{1,0:T(8,128)S(1)}, f32[16,1536]{1,0:T(8,128)S(1)}, u32[]{:S(2)}, u32[]{:S(2)}) collective-permute-start(f32[16,1536]{1,0:T(8,128)S(1)} %add.237), channel_id=1, source_target_pairs={{0,16},{8,24},{16,0},{24,8},{1,17},{9,25},{17,1},{25,9},{2,18},{10... | collective-permute-start | bytes 294920 | tf_op jit(solution)/shard_map/ppermute | solution.py:44
  421.2 36.3 %collective-permute-start.43 = (bf16[128,1536]{1,0:T(8,128)(2,1)S(1)}, bf16[128,1536]{1,0:T(8,128)(2,1)S(1)}, u32[]{:S(2)}, u32[]{:S(2)}) collective-permute-start(bf16[128,1536]{1,0:T(8,128)(2,1)S(1)} %get-tuple-element.714), channel_id=1, source_target_pairs={{0,2},{2,0},{4,6},{6,4},{1,3},{3,1},{5,7},{7,5},{8,10},{10,8},{12,... | collective-permute-start | bytes 1179656 | tf_op jit(solution)/shard_map/ppermute | solution.py:44
  421.6 31.3 %collective-permute-start.50 = (f32[16,1536]{1,0:T(8,128)S(1)}, f32[16,1536]{1,0:T(8,128)S(1)}, u32[]{:S(2)}, u32[]{:S(2)}) collective-permute-start(f32[16,1536]{1,0:T(8,128)S(1)} %add.238), channel_id=1, source_target_pairs={{0,2},{2,0},{4,6},{6,4},{1,3},{3,1},{5,7},{7,5},{8,10},{10,8},{12,... | collective-permute-start | bytes 294920 | tf_op jit(solution)/shard_map/ppermute | solution.py:44
  425.6 21.1 %collective-permute-start.47 = (bf16[192,384]{1,0:T(8,128)(2,1)S(1)}, bf16[192,384]{1,0:T(8,128)(2,1)S(1)}, u32[]{:S(2)}, u32[]{:S(2)}) collective-permute-start(bf16[192,384]{1,0:T(8,128)(2,1)S(1)} %select_convert_fusion.3), channel_id=1, source_target_pairs={{0,4},{2,6},{4,0},{6,2},{1,5},{3,7},{5,1},{7,3},{8,12},{10,14},{12... | collective-permute-start | bytes 442376 | tf_op jit(solution)/shard_map/ppermute | solution.py:44
  425.8 27.0 %collective-permute-start.51 = (bf16[384,256]{1,0:T(8,128)(2,1)S(1)}, bf16[384,256]{1,0:T(8,128)(2,1)S(1)}, u32[]{:S(2)}, u32[]{:S(2)}) collective-permute-start(bf16[384,256]{1,0:T(8,128)(2,1)S(1)} %select_convert_fusion.2), channel_id=1, source_target_pairs={{0,4},{2,6},{4,0},{6,2},{1,5},{3,7},{5,1},{7,3},{8,12},{10,14},{12... | collective-permute-start | bytes 589832 | tf_op jit(solution)/shard_map/ppermute | solution.py:44
  460.3 14.0 %collective-permute-start.55 = (bf16[384,512]{1,0:T(8,128)(2,1)S(1)}, bf16[384,512]{1,0:T(8,128)(2,1)S(1)}, u32[]{:S(2)}, u32[]{:S(2)}) collective-permute-start(bf16[384,512]{1,0:T(8,128)(2,1)S(1)} %pad_maximum_fusion.8), channel_id=1, source_target_pairs={{0,2},{2,0},{4,6},{6,4},{1,3},{3,1},{5,7},{7,5},{8,10},{10,8},{12,... | collective-permute-start | bytes 1179656 | tf_op jit(solution)/shard_map/ppermute | solution.py:44
  (64 other events, 399.2 us)
Sparse Core Ops, SparseCore 0:
  12.2 39.7 all-gather.8
  54.1 49.6 all-gather.14
  106.0 50.8 all-gather.12
  158.3 51.6 all-gather.10

commit v5 on v4

--- a/solution.py
+++ b/solution.py
@@ -134,7 +134,7 @@
     return pieces
 
 
-SCALE = 0.4
+SCALE = 0.2
 
 
 def cost(us=1):
@@ -989,6 +989,8 @@
     early_beside = run.pin(early_beside)
     attended_beside, normed_beside = early_beside[:, :q_width], early_beside[:, q_width:]
     lines.turn()
+    turned_grads, grads_sent = run(lambda *a: turn_rows(*a, n_fsdp), index, ctx, grads)
+    grads_beside = swap(grads_sent, "fsdp", 1)
     lines.pin_team()
 
     limits = [limit.reshape(1)] + [jnp.zeros((1,), jnp.int32)] * (PARTS - 1)
@@ -1036,8 +1038,6 @@
 
     carry = feed_team(0, ())
     lines.across_rest()
-    turned_grads, grads_sent = run(lambda *a: turn_rows(*a, n_fsdp), index, ctx, grads)
-    grads_beside = swap(grads_sent, "fsdp", 1)
     carry = feed_team(1, carry)
     lines.pin_rest()
     turned_lines, lines_sent = run(

time: 490 us -> 483 us (0.986)
  waiting for transfers between devices: 148 us -> 129 us
  starting transfers between devices: 57.7 us -> 69.6 us
    ppermute x53, waiting for transfers between devices: 138 us -> 122 us  [swap(): return lax.ppermute(values, axis_name, [(i, i ^ bit) for i in range(size)])]
    ppermute x53, starting transfers between devices: 47 us -> 59 us  [swap(): return lax.ppermute(values, axis_name, [(i, i ^ bit) for i in range(size)])]
    unnamed x98 -> x96, local copies, waits for them, and re-layouts: 12.2 us -> 10.6 us
  transfers between devices with their start and end apart: 61 -> 61, of which waited for: 23 -> 25; matrix products, arithmetic and copies ran while one was open for 11% -> 11% of each run, Pallas kernels for 40% -> 41%
where the time goes in v5:
time: 483 us; the launch traced here: 476 us
  Pallas kernels  197 us (41%)
  waiting for transfers between devices  129 us (27%)
  starting transfers between devices  69.6 us (14%)
  other arithmetic  35.3 us (7%)
  local copies, waits for them, and re-layouts  26.7 us (6%)
  between operations  15.2 us (3%)
    ppermute x53, waiting for transfers between devices, swap(): return lax.ppermute(values, axis_name, [(i, i ^ bit) for i in range(size)])  122 us
    pallas_call x6, Pallas kernels, feed(): pl.pallas_call(functools.partial(feed_body, weights.shape[0], ((0,) if ba...  79 us
    ppermute x53, starting transfers between devices, swap(): return lax.ppermute(values, axis_name, [(i, i ^ bit) for i in range(size)])  59 us
    pallas_call x3, Pallas kernels, weight_grads(): pl.pallas_call(weight_body, out_shape=(jax.ShapeDtypeStruct((3, D // 4, w...  39.5 us
    pallas_call x3, Pallas kernels, place(): pl.pallas_call(functools.partial(place_body, plan, len(carry)), out_shape...  15.9 us
    pallas_call x3, Pallas kernels, pack(): pl.pallas_call(functools.partial(pack_body, count), out_shape=jax.ShapeDt...  11.1 us
    pallas_call x1, Pallas kernels, attend_back(): pl.pallas_call(functools.partial(attend_back_body, len(weights), len(kv_p...  10.7 us
    unnamed x96, local copies, waits for them, and re-layouts  10.6 us
  transfers between devices with their start and end apart: 61, of which 25 were waited for; matrix products, arithmetic and copies ran while one was open for 11% of the time, Pallas kernels for 41%

profile of v5, /device:TPU:0, one launch (start us, length us, event | category | flops | bytes accessed | tf_op | source)
XLA Modules:
  0.0 476.1 jit_solution(18025550259362341291)
XLA Ops:
  7.3 2.7 shard_map.263.refs_0_
  11.7 3.0 collective-permute-start
  14.7 3.7 shard_map.264
  19.4 3.8 shard_map.265
  23.1 9.8 %collective-permute-done.refs_1_ = bf16[400,1024]{1,0:T(8,128)(2,1)S(1)} collective-permute-done((bf16[400,1024]{1,0:T(8,128)(2,1)S(1)}, bf16[400,1024]{1,0:T(8,128)(2,1)S(1)}, u32[]{:S(2)}, u32[]{:S(2)}) %collective-permute-start) | collective-permute-done | bytes 819232 | tf_op jit(solution)/shard_map/ppermute | solution.py:44
  34.0 3.7 shard_map.266
  44.6 4.8 shard_map.268
  59.2 3.4 collective-permute-start.4
  62.6 4.5 collective-permute-start.5
  73.7 9.0 %shard_map.269 = (bf16[256,768]{1,0:T(8,128)(2,1)}, f32[128,1536]{1,0:T(8,128)}, bf16[128,1536]{1,0:T(8,128)(2,1)}) custom-call(s32[1]{0:T(128)} %bitcast.1.index_ref, bf16[256,768]{1,0:T(8,128)(2,1)} %get-tuple-element.627.q_ref, s32[256,1]{1,0:T(8,128)} %copy.52.low_ref, s32[256,1]{1,0:T(8,128)} %fusion.17.high_ref, s32[1,768]{1,0:T(1,128)} %broadcast_in_dim.76.key_ref, ...), custom_call_target="tpu_custom_call" | custom-call | flops 1760000000 | bytes 5760000 | tf_op jit(solution)/shard_map/pallas_call | solution.py:335
  85.2 8.7 %collective-permute-done.7.refs_1_.refs_3_ = bf16[4,128,1536]{2,1,0:T(8,128)(2,1)S(1)} collective-permute-done((bf16[4,128,1536]{2,1,0:T(8,128)(2,1)S(1)}, bf16[4,128,1536]{2,1,0:T(8,128)(2,1)S(1)}, u32[]{:S(2)}, u32[]{:S(2)}) %collective-permute-start.7) | collective-permute-done | bytes 1572896 | tf_op jit(solution)/shard_map/ppermute | solution.py:44
  93.9 8.0 %collective-permute-done.6.other_ref = bf16[128,1536]{1,0:T(8,128)(2,1)S(1)} collective-permute-done((bf16[128,1536]{1,0:T(8,128)(2,1)}, bf16[128,1536]{1,0:T(8,128)(2,1)S(1)}, u32[]{:S(2)}, u32[]{:S(2)}) %collective-permute-start.6) | collective-permute-done | bytes 393248 | tf_op jit(solution)/shard_map/ppermute | solution.py:44
  106.8 9.3 %collective-permute-done.8 = bf16[128,1536]{1,0:T(8,128)(2,1)S(1)} collective-permute-done((bf16[128,1536]{1,0:T(8,128)(2,1)}, bf16[128,1536]{1,0:T(8,128)(2,1)S(1)}, u32[]{:S(2)}, u32[]{:S(2)}) %collective-permute-start.8) | collective-permute-done | bytes 393248 | tf_op jit(solution)/shard_map/ppermute | solution.py:44
  121.5 4.9 %shard_map.271 = (bf16[768,1024]{1,0:T(8,128)(2,1)}, bf16[768,1024]{1,0:T(8,128)(2,1)}) custom-call(s32[1]{0:T(128)} %bitcast.1.index_ref, s32[1]{0:T(128)} %bitcast.20.ctx_ref, bf16[4,128,1536]{2,1,0:T(8,128)(2,1)} %bitcast.35, bf16[4,128,1536]{2,1,0:T(8,128)(2,1)} %copy-done.1), custom_call_target="tpu_custom_call" | custom-call | flops 880000000 | bytes 2880000 | tf_op jit(solution)/shard_map/pallas_call | solution.py:514
  126.4 9.3 %collective-permute-done.10.refs_1_ = bf16[256,1536]{1,0:T(8,128)(2,1)} collective-permute-done((bf16[256,1536]{1,0:T(8,128)(2,1)S(1)}, bf16[256,1536]{1,0:T(8,128)(2,1)}, u32[]{:S(2)}, u32[]{:S(2)}) %collective-permute-start.10) | collective-permute-done | bytes 786464 | tf_op jit(solution)/shard_map/ppermute | solution.py:44
  135.7 15.4 %shard_map.272 = (bf16[1024,768]{1,0:T(8,128)(2,1)}, bf16[1024,768]{1,0:T(8,128)(2,1)}, bf16[1024,768]{1,0:T(8,128)(2,1)}, f32[512,1536]{1,0:T(8,128)}, f32[512,1536]{1,0:T(8,128)}) custom-call(s32[1]{0:T(128)} %bitcast.23.limit_ref, s32[1]{0:T(128)} %bitcast.20.ctx_ref, bf16[256,1536]{1,0:T(8,128)(2,1)} %copy-done.12, ...), custom_call_target="tpu_custom_call" | custom-call | flops 3300000000 | bytes 10800000 | tf_op jit(solution)/shard_map/pallas_call | solution.py:468
  151.0 3.7 collective-permute-done.11.refs_2_.refs_0_
  156.9 16.6 %shard_map.273 = (bf16[1024,768]{1,0:T(8,128)(2,1)}, bf16[1024,768]{1,0:T(8,128)(2,1)}, bf16[1024,768]{1,0:T(8,128)(2,1)}, f32[512,1536]{1,0:T(8,128)}, f32[512,1536]{1,0:T(8,128)}) custom-call(s32[1]{0:T(128)} %constant.120.clone.1.limit_ref, s32[1]{0:T(128)} %bitcast.20.ctx_ref, bf16[256,1536]{1,0:T(8,128)(2,1)} %copy-done.12, ...), custom_call_target="tpu_custom_call" | custom-call | flops 3300000000 | bytes 10800000 | tf_op jit(solution)/shard_map/pallas_call | solution.py:468
  174.5 4.7 shard_map.274
  179.1 10.4 %shard_map.275 = (bf16[1024,768]{1,0:T(8,128)(2,1)}, bf16[1024,768]{1,0:T(8,128)(2,1)}, bf16[1024,768]{1,0:T(8,128)(2,1)}) custom-call(s32[1]{0:T(128)} %bitcast.23.limit_ref, s32[1]{0:T(128)} %bitcast.20.ctx_ref, bf16[256,1536]{1,0:T(8,128)(2,1)} %copy-done.6, ...), custom_call_target="tpu_custom_call", output_to_operand_aliasing={{0}: (7, {}), {1}: (8, {}), {2}: (9, {})} | custom-call | flops 1980000000 | bytes 6480000 | tf_op jit(solution)/shard_map/pallas_call | solution.py:468
  190.6 10.6 %shard_map.276 = (bf16[1024,768]{1,0:T(8,128)(2,1)}, bf16[1024,768]{1,0:T(8,128)(2,1)}, bf16[1024,768]{1,0:T(8,128)(2,1)}) custom-call(s32[1]{0:T(128)} %constant.120.clone.1.limit_ref, s32[1]{0:T(128)} %bitcast.20.ctx_ref, bf16[256,1536]{1,0:T(8,128)(2,1)} %copy-done.6, ...), custom_call_target="tpu_custom_call", output_to_operand_aliasing={{0}: (7, {}), {1}: (8, {}), {2}: (9, {})} | custom-call | flops 1980000000 | bytes 6480000 | tf_op jit(solution)/shard_map/pallas_call | solution.py:468
  203.6 13.1 %shard_map.277 = (bf16[3,384,768]{2,1,0:T(8,128)(2,1)}, bf16[3,384,768]{2,1,0:T(8,128)(2,1)}) custom-call(bf16[768,1024]{1,0:T(8,128)(2,1)} %get-tuple-element.612.refs_0_, bf16[768,1024]{1,0:T(8,128)(2,1)} %get-tuple-element.613.refs_1_, bf16[768,1024]{1,0:T(8,128)(2,1)} %copy-done.4, bf16[768,1024]{1,0:T(8,128)(2,1)} %copy-done.3, ...), custom_call_target="tpu_custom_call" | custom-call | flops 2640000000 | bytes 8640000 | tf_op jit(solution)/shard_map/pallas_call | solution.py:539
  217.4 15.6 %shard_map.278 = (bf16[1024,768]{1,0:T(8,128)(2,1)}, bf16[1024,768]{1,0:T(8,128)(2,1)}, bf16[1024,768]{1,0:T(8,128)(2,1)}, f32[128,1536]{1,0:T(8,128)}, f32[128,...) custom-call(s32[1]{0:T(128)} %constant.120.clone.1.limit_ref, ...), custom_call_target="tpu_custom_call" | custom-call | flops 3300000000 | bytes 10800000 | tf_op jit(solution)/shard_map/pallas_call | solution.py:468
  233.9 10.4 %shard_map.279 = (bf16[1024,768]{1,0:T(8,128)(2,1)}, bf16[1024,768]{1,0:T(8,128)(2,1)}, bf16[1024,768]{1,0:T(8,128)(2,1)}) custom-call(s32[1]{0:T(128)} %constant.120.clone.1.limit_ref, s32[1]{0:T(128)} %bitcast.20.ctx_ref, bf16[256,1536]{1,0:T(8,128)(2,1)} %copy-done.6, ...), custom_call_target="tpu_custom_call", output_to_operand_aliasing={{0}: (7, {}), {1}: (8, {}), {2}: (9, {})} | custom-call | flops 1980000000 | bytes 6480000 | tf_op jit(solution)/shard_map/pallas_call | solution.py:468
  245.0 13.3 %shard_map.280 = (bf16[3,384,768]{2,1,0:T(8,128)(2,1)}, bf16[3,384,768]{2,1,0:T(8,128)(2,1)}) custom-call(bf16[768,1024]{1,0:T(8,128)(2,1)} %get-tuple-element.612.refs_0_, bf16[768,1024]{1,0:T(8,128)(2,1)} %get-tuple-element.613.refs_1_, bf16[768,1024]{1,0:T(8,128)(2,1)} %copy-done.4, bf16[768,1024]{1,0:T(8,128)(2,1)} %copy-done.3, ...), custom_call_target="tpu_custom_call" | custom-call | flops 2640000000 | bytes 8640000 | tf_op jit(solution)/shard_map/pallas_call | solution.py:539
  265.0 6.6 %collective-permute-done.25.far_ref = bf16[128,1536]{1,0:T(8,128)(2,1)S(1)} collective-permute-done((bf16[128,1536]{1,0:T(8,128)(2,1)S(1)}, bf16[128,1536]{1,0:T(8,128)(2,1)S(1)}, u32[]{:S(2)}, u32[]{:S(2)}) %collective-permute-start.25) | collective-permute-done | bytes 393248 | tf_op jit(solution)/shard_map/ppermute | solution.py:44
  273.5 3.4 shard_map.281
  281.1 13.1 %shard_map.282 = (bf16[3,384,768]{2,1,0:T(8,128)(2,1)}, bf16[3,384,768]{2,1,0:T(8,128)(2,1)}) custom-call(bf16[768,1024]{1,0:T(8,128)(2,1)} %get-tuple-element.612.refs_0_, bf16[768,1024]{1,0:T(8,128)(2,1)} %get-tuple-element.613.refs_1_, bf16[768,1024]{1,0:T(8,128)(2,1)} %copy-done.4, bf16[768,1024]{1,0:T(8,128)(2,1)} %copy-done.3, ...), custom_call_target="tpu_custom_call" | custom-call | flops 2640000000 | bytes 8640000 | tf_op jit(solution)/shard_map/pallas_call | solution.py:539
  299.4 10.7 %shard_map.283 = (bf16[256,768]{1,0:T(8,128)(2,1)}, f32[256,256]{1,0:T(8,128)}, bf16[256,256]{1,0:T(8,128)(2,1)}, bf16[256,256]{1,0:T(8,128)(2,1)}) custom-call(s32[1]{0:T(128)} %bitcast.1.index_ref, bf16[256,768]{1,0:T(8,128)(2,1)} %get-tuple-element.627.q_ref, s32[256,1]{1,0:T(8,128)} %copy.53.low_ref, s32[256,1]{1,0:T(8,128)} %fusion.17.high_ref, ...), custom_call_target="tpu_custom_call" | custom-call | flops 2200000000 | bytes 7200000 | tf_op jit(solution)/shard_map/pallas_call | solution.py:622
  312.7 6.2 %collective-permute-done.24.refs_1_ = bf16[3,384,768]{2,1,0:T(8,128)(2,1)S(1)} collective-permute-done((bf16[3,384,768]{2,1,0:T(8,128)(2,1)S(1)}, bf16[3,384,768]{2,1,0:T(8,128)(2,1)S(1)}, u32[]{:S(2)}, u32[]{:S(2)}) %collective-permute-start.24) | collective-permute-done | bytes 1769504 | tf_op jit(solution)/shard_map/ppermute | solution.py:44
  327.2 4.6 shard_map.284
  331.9 2.9 collective-permute-start.34
  334.8 5.2 %shard_map.285 = (f32[384,4480]{1,0:T(8,128)}, f32[384,4480]{1,0:T(8,128)}, f32[4480,384]{1,0:T(8,128)}) custom-call(s32[1]{0:T(128)} %bitcast.25.member_ref, bf16[3,384,768]{2,1,0:T(8,128)(2,1)} %copy-done.8, bf16[3,384,768]{2,1,0:T(8,128)(2,1)} %copy-done.15), custom_call_target="tpu_custom_call" | custom-call | flops 220000000 | bytes 720000 | tf_op jit(solution)/shard_map/pallas_call | solution.py:738
  345.5 2.8 shard_map.286
  351.3 2.5 collective-permute-start.39
  355.4 3.6 collective-permute-done.37
  366.2 5.4 %collective-permute-done.39 = bf16[768,384]{1,0:T(8,128)(2,1)S(1)} collective-permute-done((bf16[768,384]{1,0:T(8,128)(2,1)S(1)}, bf16[768,384]{1,0:T(8,128)(2,1)S(1)}, u32[]{:S(2)}, u32[]{:S(2)}) %collective-permute-start.39) | collective-permute-done | bytes 589856 | tf_op jit(solution)/shard_map/ppermute | solution.py:44
  373.9 12.7 %collective-permute-done.41 = bf16[384,1024]{1,0:T(8,128)(2,1)S(1)} collective-permute-done((bf16[384,1024]{1,0:T(8,128)(2,1)S(1)}, bf16[384,1024]{1,0:T(8,128)(2,1)S(1)}, u32[]{:S(2)}, u32[]{:S(2)}) %collective-permute-start.41) | collective-permute-done | bytes 786464 | tf_op jit(solution)/shard_map/ppermute | solution.py:44
  392.3 5.3 %shard_map.287 = (f32[384,4480]{1,0:T(8,128)}, f32[384,4480]{1,0:T(8,128)}, f32[4480,384]{1,0:T(8,128)}) custom-call(s32[1]{0:T(128)} %bitcast.25.member_ref, bf16[3,384,768]{2,1,0:T(8,128)(2,1)} %copy-done.10, bf16[3,384,768]{2,1,0:T(8,128)(2,1)} %collective-permute-done.33.refs_1_, ...), custom_call_target="tpu_custom_call", output_to_operand_aliasing={{0}: (3, {}), {1}: (4, {}), {2}: (5, {})} | custom-call | flops 220000000 | bytes 720000 | tf_op jit(solution)/shard_map/pallas_call | solution.py:738
  397.7 7.1 %collective-permute-done.38 = bf16[256,1536]{1,0:T(8,128)(2,1)} collective-permute-done((bf16[256,1536]{1,0:T(8,128)(2,1)}, bf16[256,1536]{1,0:T(8,128)(2,1)}, u32[]{:S(2)}, u32[]{:S(2)}) %collective-permute-start.38) | collective-permute-done | bytes 786464 | tf_op jit(solution)/shard_map/ppermute | solution.py:44
  409.6 6.8 %collective-permute-done.42 = bf16[384,512]{1,0:T(8,128)(2,1)} collective-permute-done((bf16[384,512]{1,0:T(8,128)(2,1)}, bf16[384,512]{1,0:T(8,128)(2,1)}, u32[]{:S(2)}, u32[]{:S(2)}) %collective-permute-start.42) | collective-permute-done | bytes 393248 | tf_op jit(solution)/shard_map/ppermute | solution.py:44
  420.8 2.7 collective-permute-start.47
  423.9 9.1 %collective-permute-done.47 = bf16[192,384]{1,0:T(8,128)(2,1)S(1)} collective-permute-done((bf16[192,384]{1,0:T(8,128)(2,1)S(1)}, bf16[192,384]{1,0:T(8,128)(2,1)S(1)}, u32[]{:S(2)}, u32[]{:S(2)}) %collective-permute-start.47) | collective-permute-done | bytes 147488 | tf_op jit(solution)/shard_map/ppermute | solution.py:44
  433.1 3.5 collective-permute-start.49
  436.6 7.7 %collective-permute-done.51 = bf16[384,256]{1,0:T(8,128)(2,1)S(1)} collective-permute-done((bf16[384,256]{1,0:T(8,128)(2,1)S(1)}, bf16[384,256]{1,0:T(8,128)(2,1)S(1)}, u32[]{:S(2)}, u32[]{:S(2)}) %collective-permute-start.51) | collective-permute-done | bytes 196640 | tf_op jit(solution)/shard_map/ppermute | solution.py:44
  444.5 3.0 collective-permute-start.53
  450.1 2.9 collective-permute-start.52
  455.7 5.3 %shard_map.288 = (f32[384,4480]{1,0:T(8,128)}, f32[384,4480]{1,0:T(8,128)}, f32[4480,384]{1,0:T(8,128)}) custom-call(s32[1]{0:T(128)} %bitcast.25.member_ref, bf16[3,384,768]{2,1,0:T(8,128)(2,1)} %copy-done.9, bf16[3,384,768]{2,1,0:T(8,128)(2,1)} %collective-permute-done.48.refs_1_, ...), custom_call_target="tpu_custom_call", output_to_operand_aliasing={{0}: (3, {}), {1}: (4, {}), {2}: (5, {})} | custom-call | flops 220000000 | bytes 720000 | tf_op jit(solution)/shard_map/pallas_call | solution.py:738
  (290 shorter events, 125.6 us)
Async XLA Ops:
  7.2 44.4 %all-gather.9.cloned.1.call-start = ((), (), s32[]{:S(2)}) async-start(), calls=%async_computation | async-start | bytes 1966080 | tf_op jit(solution)/shard_map/all_gather | solution.py:889
  11.6 124.0 %all-gather.15.cloned.1.call-start = ((), (), s32[]{:S(2)}) async-start(), calls=%async_computation.3 | async-start | bytes 8847360 | tf_op jit(solution)/shard_map/all_gather | solution.py:950
  11.7 21.2 %collective-permute-start = (bf16[400,1024]{1,0:T(8,128)(2,1)S(1)}, bf16[400,1024]{1,0:T(8,128)(2,1)S(1)}, u32[]{:S(2)}, u32[]{:S(2)}) collective-permute-start(bf16[400,1024]{1,0:T(8,128)(2,1)S(1)} %copy-done.2), channel_id=1, source_target_pairs={{0,16},{8,24},{16,0},{24,8},{1,17},{9,25},{17,1},{25,9},{2,18},{10... | collective-permute-start | bytes 2457608 | tf_op jit(solution)/shard_map/ppermute | solution.py:44
  33.0 124.0 %all-gather.13.cloned.1.call-start = ((), (), s32[]{:S(2)}) async-start(), calls=%async_computation.2 | async-start | bytes 8847360 | tf_op jit(solution)/shard_map/all_gather | solution.py:950
  33.7 183.7 %all-gather.11.cloned.1.call-start = ((), (), s32[]{:S(2)}) async-start(), calls=%async_computation.1 | async-start | bytes 8847360 | tf_op jit(solution)/shard_map/all_gather | solution.py:950
  38.5 15.5 %collective-permute-start.2 = (bf16[768,384]{1,0:T(8,128)(2,1)}, bf16[768,384]{1,0:T(8,128)(2,1)}, u32[]{:S(2)}, u32[]{:S(2)}) collective-permute-start(bf16[768,384]{1,0:T(8,128)(2,1)} %convert_element_type.112.refs_0_.refs_2_), channel_id=1, source_target_pairs={{0,16},{8,24},{16,0},{24,8},{1,17},{9,25},{17,1},{25,9},{2,18},{10... | collective-permute-start | bytes 1769480 | tf_op jit(solution)/shard_map/ppermute | solution.py:44
  56.6 14.0 %collective-permute-start.3 = (bf16[2,768,384]{2,1,0:T(8,128)(2,1)}, bf16[2,768,384]{2,1,0:T(8,128)(2,1)}, u32[]{:S(2)}, u32[]{:S(2)}) collective-permute-start(bf16[2,768,384]{2,1,0:T(8,128)(2,1)} %pad_maximum_fusion.1), channel_id=1, source_target_pairs={{0,8},{8,0},{16,24},{24,16},{1,9},{9,1},{17,25},{25,17},{2,10},{10... | collective-permute-start | bytes 3538952 | tf_op jit(solution)/shard_map/ppermute | solution.py:44
  56.6 37.3 %collective-permute-start.7 = (bf16[4,128,1536]{2,1,0:T(8,128)(2,1)S(1)}, bf16[4,128,1536]{2,1,0:T(8,128)(2,1)S(1)}, u32[]{:S(2)}, u32[]{:S(2)}) collective-permute-start(bf16[4,128,1536]{2,1,0:T(8,128)(2,1)S(1)} %bitcast.42), channel_id=1, source_target_pairs={{0,1},{1,0},{2,3},{3,2},{4,5},{5,4},{6,7},{7,6},{8,9},{9,8},{10,11... | collective-permute-start | bytes 4718600 | tf_op jit(solution)/shard_map/ppermute | solution.py:44
  82.7 19.1 %collective-permute-start.6 = (bf16[128,1536]{1,0:T(8,128)(2,1)}, bf16[128,1536]{1,0:T(8,128)(2,1)S(1)}, u32[]{:S(2)}, u32[]{:S(2)}) collective-permute-start(bf16[128,1536]{1,0:T(8,128)(2,1)} %get-tuple-element.457), channel_id=1, source_target_pairs={{0,1},{1,0},{2,3},{3,2},{4,5},{5,4},{6,7},{7,6},{8,9},{9,8},{10,11... | collective-permute-start | bytes 1179656 | tf_op jit(solution)/shard_map/ppermute | solution.py:44
  85.2 21.6 %collective-permute-start.9 = (bf16[256,1536]{1,0:T(8,128)(2,1)}, bf16[256,1536]{1,0:T(8,128)(2,1)}, u32[]{:S(2)}, u32[]{:S(2)}) collective-permute-start(bf16[256,1536]{1,0:T(8,128)(2,1)} %pad_maximum_fusion.3), channel_id=1, source_target_pairs={{0,8},{8,0},{16,24},{24,16},{1,9},{9,1},{17,25},{25,17},{2,10},{10... | collective-permute-start | bytes 2359304 | tf_op jit(solution)/shard_map/ppermute | solution.py:44
  117.2 18.5 %collective-permute-start.10 = (bf16[256,1536]{1,0:T(8,128)(2,1)S(1)}, bf16[256,1536]{1,0:T(8,128)(2,1)}, u32[]{:S(2)}, u32[]{:S(2)}) collective-permute-start(bf16[256,1536]{1,0:T(8,128)(2,1)S(1)} %constant_dynamic-update-slice_fusion.refs_0_), channel_id=1, source_target_pairs={{0,1},{1,0},{2,3},{3,2},{4,5},{5,4},{6,7},{7,6},{8,9},{9,8},{10,11... | collective-permute-start | bytes 2359304 | tf_op jit(solution)/shard_map/ppermute | solution.py:44
  119.0 35.8 %collective-permute-start.11 = (bf16[256,1536]{1,0:T(8,128)(2,1)S(1)}, bf16[256,1536]{1,0:T(8,128)(2,1)S(1)}, u32[]{:S(2)}, u32[]{:S(2)}) collective-permute-start(bf16[256,1536]{1,0:T(8,128)(2,1)S(1)} %constant_dynamic-update-slice_fusion.refs_0_), channel_id=1, source_target_pairs={{0,4},{2,6},{4,0},{6,2},{1,5},{3,7},{5,1},{7,3},{8,12},{10,14},{12... | collective-permute-start | bytes 2359304 | tf_op jit(solution)/shard_map/ppermute | solution.py:44
  154.8 18.8 %collective-permute-start.12 = (bf16[256,1536]{1,0:T(8,128)(2,1)S(1)}, bf16[256,1536]{1,0:T(8,128)(2,1)S(1)}, u32[]{:S(2)}, u32[]{:S(2)}) collective-permute-start(bf16[256,1536]{1,0:T(8,128)(2,1)S(1)} %collective-permute-done.11.refs_2_.refs_0_), channel_id=1, source_target_pairs={{0,1},{1,0},{2,3},{3,2},{4,5},{5,4},{6,7},{7,6},{8,9},{9,8},{10,11... | collective-permute-start | bytes 2359304 | tf_op jit(solution)/shard_map/ppermute | solution.py:44
  155.1 46.1 %collective-permute-start.14 = (bf16[768,1024]{1,0:T(8,128)(2,1)}, bf16[768,1024]{1,0:T(8,128)(2,1)S(1)}, u32[]{:S(2)}, u32[]{:S(2)}) collective-permute-start(bf16[768,1024]{1,0:T(8,128)(2,1)} %get-tuple-element.514), channel_id=1, source_target_pairs={{0,8},{8,0},{16,24},{24,16},{1,9},{9,1},{17,25},{25,17},{2,10},{10... | collective-permute-start | bytes 4718600 | tf_op jit(solution)/shard_map/ppermute | solution.py:44
  189.7 12.1 %collective-permute-start.16 = (bf16[1024,768]{1,0:T(8,128)(2,1)}, bf16[1024,768]{1,0:T(8,128)(2,1)}, u32[]{:S(2)}, u32[]{:S(2)}) collective-permute-start(bf16[1024,768]{1,0:T(8,128)(2,1)} %get-tuple-element.548.refs_5_), channel_id=1, source_target_pairs={{0,8},{8,0},{16,24},{24,16},{1,9},{9,1},{17,25},{25,17},{2,10},{10... | collective-permute-start | bytes 4718600 | tf_op jit(solution)/shard_map/ppermute | solution.py:44
  201.2 43.1 %collective-permute-start.18 = (bf16[1024,768]{1,0:T(8,128)(2,1)}, bf16[1024,768]{1,0:T(8,128)(2,1)}, u32[]{:S(2)}, u32[]{:S(2)}) collective-permute-start(bf16[1024,768]{1,0:T(8,128)(2,1)} %get-tuple-element.586.refs_4_), channel_id=1, source_target_pairs={{0,8},{8,0},{16,24},{24,16},{1,9},{9,1},{17,25},{25,17},{2,10},{10... | collective-permute-start | bytes 4718600 | tf_op jit(solution)/shard_map/ppermute | solution.py:44
  201.4 43.0 %collective-permute-start.19 = (bf16[1024,768]{1,0:T(8,128)(2,1)}, bf16[1024,768]{1,0:T(8,128)(2,1)}, u32[]{:S(2)}, u32[]{:S(2)}) collective-permute-start(bf16[1024,768]{1,0:T(8,128)(2,1)} %get-tuple-element.587.refs_5_), channel_id=1, source_target_pairs={{0,8},{8,0},{16,24},{24,16},{1,9},{9,1},{17,25},{25,17},{2,10},{10... | collective-permute-start | bytes 4718600 | tf_op jit(solution)/shard_map/ppermute | solution.py:44
  201.8 43.1 %collective-permute-start.20 = (bf16[1024,768]{1,0:T(8,128)(2,1)}, bf16[1024,768]{1,0:T(8,128)(2,1)}, u32[]{:S(2)}, u32[]{:S(2)}) collective-permute-start(bf16[1024,768]{1,0:T(8,128)(2,1)} %get-tuple-element.588.refs_6_), channel_id=1, source_target_pairs={{0,8},{8,0},{16,24},{24,16},{1,9},{9,1},{17,25},{25,17},{2,10},{10... | collective-permute-start | bytes 4718600 | tf_op jit(solution)/shard_map/ppermute | solution.py:44
  216.6 45.3 %collective-permute-start.22 = (bf16[3,384,768]{2,1,0:T(8,128)(2,1)}, bf16[3,384,768]{2,1,0:T(8,128)(2,1)S(1)}, u32[]{:S(2)}, u32[]{:S(2)}) collective-permute-start(bf16[3,384,768]{2,1,0:T(8,128)(2,1)} %get-tuple-element.553), channel_id=1, source_target_pairs={{0,16},{8,24},{16,0},{24,8},{1,17},{9,25},{17,1},{25,9},{2,18},{10... | collective-permute-start | bytes 5308424 | tf_op jit(solution)/shard_map/ppermute | solution.py:44
  233.1 25.2 %collective-permute-start.23 = (bf16[256,1536]{1,0:T(8,128)(2,1)}, bf16[256,1536]{1,0:T(8,128)(2,1)}, u32[]{:S(2)}, u32[]{:S(2)}) collective-permute-start(bf16[256,1536]{1,0:T(8,128)(2,1)} %get-tuple-element.596), channel_id=1, source_target_pairs={{0,1},{1,0},{2,3},{3,2},{4,5},{5,4},{6,7},{7,6},{8,9},{9,8},{10,11... | collective-permute-start | bytes 2359304 | tf_op jit(solution)/shard_map/ppermute | solution.py:44
  244.3 34.9 %collective-permute-start.27 = (bf16[1024,768]{1,0:T(8,128)(2,1)}, bf16[1024,768]{1,0:T(8,128)(2,1)}, u32[]{:S(2)}, u32[]{:S(2)}) collective-permute-start(bf16[1024,768]{1,0:T(8,128)(2,1)} %get-tuple-element.616.refs_4_), channel_id=1, source_target_pairs={{0,8},{8,0},{16,24},{24,16},{1,9},{9,1},{17,25},{25,17},{2,10},{10... | collective-permute-start | bytes 4718600 | tf_op jit(solution)/shard_map/ppermute | solution.py:44
  244.4 36.7 %collective-permute-start.28 = (bf16[1024,768]{1,0:T(8,128)(2,1)}, bf16[1024,768]{1,0:T(8,128)(2,1)}, u32[]{:S(2)}, u32[]{:S(2)}) collective-permute-start(bf16[1024,768]{1,0:T(8,128)(2,1)} %get-tuple-element.617.refs_5_), channel_id=1, source_target_pairs={{0,8},{8,0},{16,24},{24,16},{1,9},{9,1},{17,25},{25,17},{2,10},{10... | collective-permute-start | bytes 4718600 | tf_op jit(solution)/shard_map/ppermute | solution.py:44
  244.9 36.2 %collective-permute-start.29 = (bf16[1024,768]{1,0:T(8,128)(2,1)}, bf16[1024,768]{1,0:T(8,128)(2,1)}, u32[]{:S(2)}, u32[]{:S(2)}) collective-permute-start(bf16[1024,768]{1,0:T(8,128)(2,1)} %get-tuple-element.618.refs_6_), channel_id=1, source_target_pairs={{0,8},{8,0},{16,24},{24,16},{1,9},{9,1},{17,25},{25,17},{2,10},{10... | collective-permute-start | bytes 4718600 | tf_op jit(solution)/shard_map/ppermute | solution.py:44
  276.9 17.4 %collective-permute-start.26 = (bf16[128,1536]{1,0:T(8,128)(2,1)}, bf16[128,1536]{1,0:T(8,128)(2,1)}, u32[]{:S(2)}, u32[]{:S(2)}) collective-permute-start(bf16[128,1536]{1,0:T(8,128)(2,1)} %get-tuple-element.633.refs_0_), channel_id=1, source_target_pairs={{0,1},{1,0},{2,3},{3,2},{4,5},{5,4},{6,7},{7,6},{8,9},{9,8},{10,11... | collective-permute-start | bytes 1179656 | tf_op jit(solution)/shard_map/ppermute | solution.py:44
  277.6 41.3 %collective-permute-start.24 = (bf16[3,384,768]{2,1,0:T(8,128)(2,1)S(1)}, bf16[3,384,768]{2,1,0:T(8,128)(2,1)S(1)}, u32[]{:S(2)}, u32[]{:S(2)}) collective-permute-start(bf16[3,384,768]{2,1,0:T(8,128)(2,1)S(1)} %add_convert_fusion.2.refs_0_), channel_id=1, source_target_pairs={{0,2},{2,0},{4,6},{6,4},{1,3},{3,1},{5,7},{7,5},{8,10},{10,8},{12,... | collective-permute-start | bytes 5308424 | tf_op jit(solution)/shard_map/ppermute | solution.py:44
  279.2 41.9 %collective-permute-start.21 = (bf16[3,384,768]{2,1,0:T(8,128)(2,1)}, bf16[3,384,768]{2,1,0:T(8,128)(2,1)}, u32[]{:S(2)}, u32[]{:S(2)}) collective-permute-start(bf16[3,384,768]{2,1,0:T(8,128)(2,1)} %get-tuple-element.593), channel_id=1, source_target_pairs={{0,16},{8,24},{16,0},{24,8},{1,17},{9,25},{17,1},{25,9},{2,18},{10... | collective-permute-start | bytes 5308424 | tf_op jit(solution)/shard_map/ppermute | solution.py:44
  297.6 61.4 %collective-permute-start.37 = (bf16[3,384,768]{2,1,0:T(8,128)(2,1)}, bf16[3,384,768]{2,1,0:T(8,128)(2,1)}, u32[]{:S(2)}, u32[]{:S(2)}) collective-permute-start(bf16[3,384,768]{2,1,0:T(8,128)(2,1)} %get-tuple-element.622), channel_id=1, source_target_pairs={{0,16},{8,24},{16,0},{24,8},{1,17},{9,25},{17,1},{25,9},{2,18},{10... | collective-permute-start | bytes 5308424 | tf_op jit(solution)/shard_map/ppermute | solution.py:44
  310.1 15.7 %collective-permute-start.31 = (bf16[256,256]{1,0:T(8,128)(2,1)}, bf16[256,256]{1,0:T(8,128)(2,1)S(1)}, u32[]{:S(2)}, u32[]{:S(2)}) collective-permute-start(bf16[256,256]{1,0:T(8,128)(2,1)} %get-tuple-element.646), channel_id=1, source_target_pairs={{2,0},{4,2},{6,4},{3,1},{5,3},{7,5},{10,8},{12,10},{14,12},{11,9},... | collective-permute-start | bytes 393224 | tf_op jit(solution)/shard_map/ppermute | solution.py:50
  311.4 14.4 %collective-permute-start.32 = (bf16[256,256]{1,0:T(8,128)(2,1)}, bf16[256,256]{1,0:T(8,128)(2,1)S(1)}, u32[]{:S(2)}, u32[]{:S(2)}) collective-permute-start(bf16[256,256]{1,0:T(8,128)(2,1)} %get-tuple-element.647), channel_id=1, source_target_pairs={{4,0},{6,2},{5,1},{7,3},{12,8},{14,10},{13,9},{15,11},{20,16},{22,... | collective-permute-start | bytes 393224 | tf_op jit(solution)/shard_map/ppermute | solution.py:50
  325.8 40.3 %collective-permute-start.33 = (bf16[3,384,768]{2,1,0:T(8,128)(2,1)S(1)}, bf16[3,384,768]{2,1,0:T(8,128)(2,1)}, u32[]{:S(2)}, u32[]{:S(2)}) collective-permute-start(bf16[3,384,768]{2,1,0:T(8,128)(2,1)S(1)} %add_convert_fusion.1.refs_0_), channel_id=1, source_target_pairs={{0,2},{2,0},{4,6},{6,4},{1,3},{3,1},{5,7},{7,5},{8,10},{10,8},{12,... | collective-permute-start | bytes 5308424 | tf_op jit(solution)/shard_map/ppermute | solution.py:44
  331.9 12.8 %collective-permute-start.34 = (bf16[128,1536]{1,0:T(8,128)(2,1)}, bf16[128,1536]{1,0:T(8,128)(2,1)S(1)}, u32[]{:S(2)}, u32[]{:S(2)}) collective-permute-start(bf16[128,1536]{1,0:T(8,128)(2,1)} %get-tuple-element.668), channel_id=1, source_target_pairs={{0,1},{1,0},{2,3},{3,2},{4,5},{5,4},{6,7},{7,6},{8,9},{9,8},{10,11... | collective-permute-start | bytes 1179656 | tf_op jit(solution)/shard_map/ppermute | solution.py:44
  348.2 15.5 %collective-permute-start.36 = (bf16[128,1536]{1,0:T(8,128)(2,1)}, bf16[128,1536]{1,0:T(8,128)(2,1)}, u32[]{:S(2)}, u32[]{:S(2)}) collective-permute-start(bf16[128,1536]{1,0:T(8,128)(2,1)} %get-tuple-element.683), channel_id=1, source_target_pairs={{0,1},{1,0},{2,3},{3,2},{4,5},{5,4},{6,7},{7,6},{8,9},{9,8},{10,11... | collective-permute-start | bytes 1179656 | tf_op jit(solution)/shard_map/ppermute | solution.py:44
  351.3 20.2 %collective-permute-start.39 = (bf16[768,384]{1,0:T(8,128)(2,1)S(1)}, bf16[768,384]{1,0:T(8,128)(2,1)S(1)}, u32[]{:S(2)}, u32[]{:S(2)}) collective-permute-start(bf16[768,384]{1,0:T(8,128)(2,1)S(1)} %slice.371), channel_id=1, source_target_pairs={{0,16},{8,24},{16,0},{24,8},{1,17},{9,25},{17,1},{25,9},{2,18},{10... | collective-permute-start | bytes 1769480 | tf_op jit(solution)/shard_map/ppermute | solution.py:44
  359.0 27.6 %collective-permute-start.41 = (bf16[384,1024]{1,0:T(8,128)(2,1)S(1)}, bf16[384,1024]{1,0:T(8,128)(2,1)S(1)}, u32[]{:S(2)}, u32[]{:S(2)}) collective-permute-start(bf16[384,1024]{1,0:T(8,128)(2,1)S(1)} %slice.370), channel_id=1, source_target_pairs={{0,16},{8,24},{16,0},{24,8},{1,17},{9,25},{17,1},{25,9},{2,18},{10... | collective-permute-start | bytes 2359304 | tf_op jit(solution)/shard_map/ppermute | solution.py:44
  363.4 57.5 %collective-permute-start.48 = (bf16[3,384,768]{2,1,0:T(8,128)(2,1)S(1)}, bf16[3,384,768]{2,1,0:T(8,128)(2,1)}, u32[]{:S(2)}, u32[]{:S(2)}) collective-permute-start(bf16[3,384,768]{2,1,0:T(8,128)(2,1)S(1)} %add_convert_fusion.refs_0_), channel_id=1, source_target_pairs={{0,2},{2,0},{4,6},{6,4},{1,3},{3,1},{5,7},{7,5},{8,10},{10,8},{12,... | collective-permute-start | bytes 5308424 | tf_op jit(solution)/shard_map/ppermute | solution.py:44
  372.4 19.8 %collective-permute-start.40 = (f32[2,1536]{1,0:T(2,128)S(1)}, f32[2,1536]{1,0:T(2,128)S(1)}, u32[]{:S(2)}, u32[]{:S(2)}) collective-permute-start(f32[2,1536]{1,0:T(2,128)S(1)} %pad_maximum_fusion.12), channel_id=1, source_target_pairs={{0,1},{1,0},{2,3},{3,2},{4,5},{5,4},{6,7},{7,6},{8,9},{9,8},{10,11... | collective-permute-start | bytes 36872 | tf_op jit(solution)/shard_map/ppermute | solution.py:44
  386.6 18.2 %collective-permute-start.38 = (bf16[256,1536]{1,0:T(8,128)(2,1)}, bf16[256,1536]{1,0:T(8,128)(2,1)}, u32[]{:S(2)}, u32[]{:S(2)}) collective-permute-start(bf16[256,1536]{1,0:T(8,128)(2,1)} %get-tuple-element.689), channel_id=1, source_target_pairs={{0,1},{1,0},{2,3},{3,2},{4,5},{5,4},{6,7},{7,6},{8,9},{9,8},{10,11... | collective-permute-start | bytes 2359304 | tf_op jit(solution)/shard_map/ppermute | solution.py:44
  390.2 28.4 %collective-permute-start.44 = (bf16[384,384]{1,0:T(8,128)(2,1)}, bf16[384,384]{1,0:T(8,128)(2,1)}, u32[]{:S(2)}, u32[]{:S(2)}) collective-permute-start(bf16[384,384]{1,0:T(8,128)(2,1)} %select_convert_fusion.1), channel_id=1, source_target_pairs={{0,2},{2,0},{4,6},{6,4},{1,3},{3,1},{5,7},{7,5},{8,10},{10,8},{12,... | collective-permute-start | bytes 884744 | tf_op jit(solution)/shard_map/ppermute | solution.py:44
  390.7 25.8 %collective-permute-start.42 = (bf16[384,512]{1,0:T(8,128)(2,1)}, bf16[384,512]{1,0:T(8,128)(2,1)}, u32[]{:S(2)}, u32[]{:S(2)}) collective-permute-start(bf16[384,512]{1,0:T(8,128)(2,1)} %select_convert_fusion), channel_id=1, source_target_pairs={{0,2},{2,0},{4,6},{6,4},{1,3},{3,1},{5,7},{7,5},{8,10},{10,8},{12,... | collective-permute-start | bytes 1179656 | tf_op jit(solution)/shard_map/ppermute | solution.py:44
  392.3 14.4 %collective-permute-start.45 = (f32[16,1536]{1,0:T(8,128)S(1)}, f32[16,1536]{1,0:T(8,128)S(1)}, u32[]{:S(2)}, u32[]{:S(2)}) collective-permute-start(f32[16,1536]{1,0:T(8,128)S(1)} %select_maximum_fusion), channel_id=1, source_target_pairs={{0,8},{8,0},{16,24},{24,16},{1,9},{9,1},{17,25},{25,17},{2,10},{10... | collective-permute-start | bytes 294920 | tf_op jit(solution)/shard_map/ppermute | solution.py:44
  416.4 33.5 %collective-permute-start.43 = (bf16[128,1536]{1,0:T(8,128)(2,1)S(1)}, bf16[128,1536]{1,0:T(8,128)(2,1)S(1)}, u32[]{:S(2)}, u32[]{:S(2)}) collective-permute-start(bf16[128,1536]{1,0:T(8,128)(2,1)S(1)} %get-tuple-element.714), channel_id=1, source_target_pairs={{0,2},{2,0},{4,6},{6,4},{1,3},{3,1},{5,7},{7,5},{8,10},{10,8},{12,... | collective-permute-start | bytes 1179656 | tf_op jit(solution)/shard_map/ppermute | solution.py:44
  418.2 26.2 %collective-permute-start.50 = (f32[16,1536]{1,0:T(8,128)S(1)}, f32[16,1536]{1,0:T(8,128)S(1)}, u32[]{:S(2)}, u32[]{:S(2)}) collective-permute-start(f32[16,1536]{1,0:T(8,128)S(1)} %add.238), channel_id=1, source_target_pairs={{0,2},{2,0},{4,6},{6,4},{1,3},{3,1},{5,7},{7,5},{8,10},{10,8},{12,... | collective-permute-start | bytes 294920 | tf_op jit(solution)/shard_map/ppermute | solution.py:44
  420.8 12.2 %collective-permute-start.47 = (bf16[192,384]{1,0:T(8,128)(2,1)S(1)}, bf16[192,384]{1,0:T(8,128)(2,1)S(1)}, u32[]{:S(2)}, u32[]{:S(2)}) collective-permute-start(bf16[192,384]{1,0:T(8,128)(2,1)S(1)} %select_convert_fusion.3), channel_id=1, source_target_pairs={{0,4},{2,6},{4,0},{6,2},{1,5},{3,7},{5,1},{7,3},{8,12},{10,14},{12... | collective-permute-start | bytes 442376 | tf_op jit(solution)/shard_map/ppermute | solution.py:44
  423.6 20.7 %collective-permute-start.51 = (bf16[384,256]{1,0:T(8,128)(2,1)S(1)}, bf16[384,256]{1,0:T(8,128)(2,1)S(1)}, u32[]{:S(2)}, u32[]{:S(2)}) collective-permute-start(bf16[384,256]{1,0:T(8,128)(2,1)S(1)} %select_convert_fusion.2), channel_id=1, source_target_pairs={{0,4},{2,6},{4,0},{6,2},{1,5},{3,7},{5,1},{7,3},{8,12},{10,14},{12... | collective-permute-start | bytes 589832 | tf_op jit(solution)/shard_map/ppermute | solution.py:44
  433.1 14.4 %collective-permute-start.49 = (bf16[192,384]{1,0:T(8,128)(2,1)S(1)}, bf16[192,384]{1,0:T(8,128)(2,1)S(1)}, u32[]{:S(2)}, u32[]{:S(2)}) collective-permute-start(bf16[192,384]{1,0:T(8,128)(2,1)S(1)} %add_convert_fusion.7), channel_id=1, source_target_pairs={{0,4},{2,6},{4,0},{6,2},{1,5},{3,7},{5,1},{7,3},{8,12},{10,14},{12... | collective-permute-start | bytes 442376 | tf_op jit(solution)/shard_map/ppermute | solution.py:44
  447.6 14.6 %collective-permute-start.56 = (bf16[384,384]{1,0:T(8,128)(2,1)S(1)}, bf16[384,384]{1,0:T(8,128)(2,1)S(1)}, u32[]{:S(2)}, u32[]{:S(2)}) collective-permute-start(bf16[384,384]{1,0:T(8,128)(2,1)S(1)} %pad_maximum_fusion.9), channel_id=1, source_target_pairs={{0,2},{2,0},{4,6},{6,4},{1,3},{3,1},{5,7},{7,5},{8,10},{10,8},{12,... | collective-permute-start | bytes 884744 | tf_op jit(solution)/shard_map/ppermute | solution.py:44
  450.1 13.2 %collective-permute-start.52 = (bf16[128,1536]{1,0:T(8,128)(2,1)S(1)}, bf16[128,1536]{1,0:T(8,128)(2,1)S(1)}, u32[]{:S(2)}, u32[]{:S(2)}) collective-permute-start(bf16[128,1536]{1,0:T(8,128)(2,1)S(1)} %add_convert_fusion.3), channel_id=1, source_target_pairs={{0,1},{1,0},{2,3},{3,2},{4,5},{5,4},{6,7},{7,6},{8,9},{9,8},{10,11... | collective-permute-start | bytes 1179656 | tf_op jit(solution)/shard_map/ppermute | solution.py:44
  453.8 13.2 %collective-permute-start.55 = (bf16[384,512]{1,0:T(8,128)(2,1)S(1)}, bf16[384,512]{1,0:T(8,128)(2,1)S(1)}, u32[]{:S(2)}, u32[]{:S(2)}) collective-permute-start(bf16[384,512]{1,0:T(8,128)(2,1)S(1)} %pad_maximum_fusion.8), channel_id=1, source_target_pairs={{0,2},{2,0},{4,6},{6,4},{1,3},{3,1},{5,7},{7,5},{8,10},{10,8},{12,... | collective-permute-start | bytes 1179656 | tf_op jit(solution)/shard_map/ppermute | solution.py:44
  (63 other events, 389.6 us)
Sparse Core Ops, SparseCore 0:
  11.8 39.7 all-gather.8
  53.7 49.6 all-gather.14
  105.6 51.2 all-gather.12
  158.4 51.5 all-gather.10

commit v6 on v5

--- a/solution.py
+++ b/solution.py
@@ -1163,7 +1163,6 @@
     )
     d_qkv_beside = swap(d_qkv, "fsdp", 1)
     dn_other = swap(dn_other, "tensor", 1)
-    placed = place_part(0, ())
     reduce_qkv = Reduce(0, d_qkv, d_qkv_beside, normed_rel, normed_beside)
     reduce_qkv.first()
     d_inputs, grad_gain_one = run(
@@ -1172,6 +1171,7 @@
     d_inputs_other = swap(d_inputs, "tensor", 1)
     add_far(2)
     d_inputs_other = run.pin(d_inputs_other)
+    placed = place_part(0, ())
     other_parts[1] = run.pin(other_parts[1])
     reduce_o.step()
     gain_rows = run(stack, grad_gain_one, grad_gain_two)

time: 483 us -> 484 us (level)
  transfers between devices with their start and end apart: 61 -> 61, of which waited for: 25 -> 25; matrix products, arithmetic and copies ran while one was open for 11% -> 12% of each run, Pallas kernels for 41% -> 41%
where the time goes in v6:
time: 484 us; the launch traced here: 477 us
  Pallas kernels  197 us (41%)
  waiting for transfers between devices  127 us (26%)
  starting transfers between devices  67.3 us (14%)
  other arithmetic  37.1 us (8%)
  local copies, waits for them, and re-layouts  29.9 us (6%)
  between operations  15.1 us (3%)
    ppermute x53, waiting for transfers between devices, swap(): return lax.ppermute(values, axis_name, [(i, i ^ bit) for i in range(size)])  120 us
    pallas_call x6, Pallas kernels, feed(): pl.pallas_call(functools.partial(feed_body, weights.shape[0], ((0,) if ba...  78.9 us
    ppermute x53, starting transfers between devices, swap(): return lax.ppermute(values, axis_name, [(i, i ^ bit) for i in range(size)])  56.4 us
    pallas_call x3, Pallas kernels, weight_grads(): pl.pallas_call(weight_body, out_shape=(jax.ShapeDtypeStruct((3, D // 4, w...  39.4 us
    pallas_call x3, Pallas kernels, place(): pl.pallas_call(functools.partial(place_body, plan, len(carry)), out_shape...  15.8 us
    pallas_call x3, Pallas kernels, pack(): pl.pallas_call(functools.partial(pack_body, count), out_shape=jax.ShapeDt...  11.1 us
    unnamed x96, local copies, waits for them, and re-layouts  11 us
    ppermute x4, starting transfers between devices, shift(): return lax.ppermute(values, axis_name, pairs)  10.8 us
  transfers between devices with their start and end apart: 61, of which 25 were waited for; matrix products, arithmetic and copies ran while one was open for 12% of the time, Pallas kernels for 41%

profile of v6, /device:TPU:0, one launch (start us, length us, event | category | flops | bytes accessed | tf_op | source)
XLA Modules:
  0.0 477.2 jit_solution(2406692481010589633)
XLA Ops:
  7.3 2.7 shard_map.263.refs_0_
  11.7 3.0 collective-permute-start
  14.7 3.7 shard_map.264
  19.3 3.7 shard_map.265
  23.1 9.9 %collective-permute-done.refs_1_ = bf16[400,1024]{1,0:T(8,128)(2,1)S(1)} collective-permute-done((bf16[400,1024]{1,0:T(8,128)(2,1)S(1)}, bf16[400,1024]{1,0:T(8,128)(2,1)S(1)}, u32[]{:S(2)}, u32[]{:S(2)}) %collective-permute-start) | collective-permute-done | bytes 819232 | tf_op jit(solution)/shard_map/ppermute | solution.py:44
  34.0 3.7 shard_map.266
  44.6 4.7 shard_map.268
  59.2 3.4 collective-permute-start.4
  62.6 4.5 collective-permute-start.5
  73.8 9.0 %shard_map.269 = (bf16[256,768]{1,0:T(8,128)(2,1)}, f32[128,1536]{1,0:T(8,128)}, bf16[128,1536]{1,0:T(8,128)(2,1)}) custom-call(s32[1]{0:T(128)} %bitcast.1.index_ref, bf16[256,768]{1,0:T(8,128)(2,1)} %get-tuple-element.627.q_ref, s32[256,1]{1,0:T(8,128)} %copy.52.low_ref, s32[256,1]{1,0:T(8,128)} %fusion.17.high_ref, s32[1,768]{1,0:T(1,128)} %broadcast_in_dim.76.key_ref, ...), custom_call_target="tpu_custom_call" | custom-call | flops 1760000000 | bytes 5760000 | tf_op jit(solution)/shard_map/pallas_call | solution.py:335
  85.2 8.7 %collective-permute-done.7.refs_1_.refs_3_ = bf16[4,128,1536]{2,1,0:T(8,128)(2,1)S(1)} collective-permute-done((bf16[4,128,1536]{2,1,0:T(8,128)(2,1)S(1)}, bf16[4,128,1536]{2,1,0:T(8,128)(2,1)S(1)}, u32[]{:S(2)}, u32[]{:S(2)}) %collective-permute-start.7) | collective-permute-done | bytes 1572896 | tf_op jit(solution)/shard_map/ppermute | solution.py:44
  93.9 8.0 %collective-permute-done.6.other_ref = bf16[128,1536]{1,0:T(8,128)(2,1)S(1)} collective-permute-done((bf16[128,1536]{1,0:T(8,128)(2,1)}, bf16[128,1536]{1,0:T(8,128)(2,1)S(1)}, u32[]{:S(2)}, u32[]{:S(2)}) %collective-permute-start.6) | collective-permute-done | bytes 393248 | tf_op jit(solution)/shard_map/ppermute | solution.py:44
  102.6 2.5 shard_map.270
  106.8 9.3 %collective-permute-done.8 = bf16[128,1536]{1,0:T(8,128)(2,1)S(1)} collective-permute-done((bf16[128,1536]{1,0:T(8,128)(2,1)}, bf16[128,1536]{1,0:T(8,128)(2,1)S(1)}, u32[]{:S(2)}, u32[]{:S(2)}) %collective-permute-start.8) | collective-permute-done | bytes 393248 | tf_op jit(solution)/shard_map/ppermute | solution.py:44
  121.5 4.9 %shard_map.271 = (bf16[768,1024]{1,0:T(8,128)(2,1)}, bf16[768,1024]{1,0:T(8,128)(2,1)}) custom-call(s32[1]{0:T(128)} %bitcast.1.index_ref, s32[1]{0:T(128)} %bitcast.20.ctx_ref, bf16[4,128,1536]{2,1,0:T(8,128)(2,1)} %bitcast.35, bf16[4,128,1536]{2,1,0:T(8,128)(2,1)} %copy-done.1), custom_call_target="tpu_custom_call" | custom-call | flops 880000000 | bytes 2880000 | tf_op jit(solution)/shard_map/pallas_call | solution.py:514
  126.4 9.3 %collective-permute-done.10.refs_1_ = bf16[256,1536]{1,0:T(8,128)(2,1)} collective-permute-done((bf16[256,1536]{1,0:T(8,128)(2,1)S(1)}, bf16[256,1536]{1,0:T(8,128)(2,1)}, u32[]{:S(2)}, u32[]{:S(2)}) %collective-permute-start.10) | collective-permute-done | bytes 786464 | tf_op jit(solution)/shard_map/ppermute | solution.py:44
  135.7 15.4 %shard_map.272 = (bf16[1024,768]{1,0:T(8,128)(2,1)}, bf16[1024,768]{1,0:T(8,128)(2,1)}, bf16[1024,768]{1,0:T(8,128)(2,1)}, f32[512,1536]{1,0:T(8,128)}, f32[512,1536]{1,0:T(8,128)}) custom-call(s32[1]{0:T(128)} %bitcast.23.limit_ref, s32[1]{0:T(128)} %bitcast.20.ctx_ref, bf16[256,1536]{1,0:T(8,128)(2,1)} %copy-done.12, ...), custom_call_target="tpu_custom_call" | custom-call | flops 3300000000 | bytes 10800000 | tf_op jit(solution)/shard_map/pallas_call | solution.py:468
  151.0 3.7 collective-permute-done.11.refs_2_.refs_0_
  157.0 16.6 %shard_map.273 = (bf16[1024,768]{1,0:T(8,128)(2,1)}, bf16[1024,768]{1,0:T(8,128)(2,1)}, bf16[1024,768]{1,0:T(8,128)(2,1)}, f32[512,1536]{1,0:T(8,128)}, f32[512,1536]{1,0:T(8,128)}) custom-call(s32[1]{0:T(128)} %constant.120.clone.1.limit_ref, s32[1]{0:T(128)} %bitcast.20.ctx_ref, bf16[256,1536]{1,0:T(8,128)(2,1)} %copy-done.12, ...), custom_call_target="tpu_custom_call" | custom-call | flops 3300000000 | bytes 10800000 | tf_op jit(solution)/shard_map/pallas_call | solution.py:468
  174.4 4.7 shard_map.274
  179.1 10.4 %shard_map.275 = (bf16[1024,768]{1,0:T(8,128)(2,1)}, bf16[1024,768]{1,0:T(8,128)(2,1)}, bf16[1024,768]{1,0:T(8,128)(2,1)}) custom-call(s32[1]{0:T(128)} %bitcast.23.limit_ref, s32[1]{0:T(128)} %bitcast.20.ctx_ref, bf16[256,1536]{1,0:T(8,128)(2,1)} %copy-done.6, ...), custom_call_target="tpu_custom_call", output_to_operand_aliasing={{0}: (7, {}), {1}: (8, {}), {2}: (9, {})} | custom-call | flops 1980000000 | bytes 6480000 | tf_op jit(solution)/shard_map/pallas_call | solution.py:468
  190.7 10.6 %shard_map.276 = (bf16[1024,768]{1,0:T(8,128)(2,1)}, bf16[1024,768]{1,0:T(8,128)(2,1)}, bf16[1024,768]{1,0:T(8,128)(2,1)}) custom-call(s32[1]{0:T(128)} %constant.120.clone.1.limit_ref, s32[1]{0:T(128)} %bitcast.20.ctx_ref, bf16[256,1536]{1,0:T(8,128)(2,1)} %copy-done.6, ...), custom_call_target="tpu_custom_call", output_to_operand_aliasing={{0}: (7, {}), {1}: (8, {}), {2}: (9, {})} | custom-call | flops 1980000000 | bytes 6480000 | tf_op jit(solution)/shard_map/pallas_call | solution.py:468
  203.6 13.1 %shard_map.277 = (bf16[3,384,768]{2,1,0:T(8,128)(2,1)}, bf16[3,384,768]{2,1,0:T(8,128)(2,1)}) custom-call(bf16[768,1024]{1,0:T(8,128)(2,1)} %get-tuple-element.612.refs_0_, bf16[768,1024]{1,0:T(8,128)(2,1)} %get-tuple-element.613.refs_1_, bf16[768,1024]{1,0:T(8,128)(2,1)} %copy-done.4, bf16[768,1024]{1,0:T(8,128)(2,1)} %copy-done.3, ...), custom_call_target="tpu_custom_call" | custom-call | flops 2640000000 | bytes 8640000 | tf_op jit(solution)/shard_map/pallas_call | solution.py:539
  217.4 15.6 %shard_map.278 = (bf16[1024,768]{1,0:T(8,128)(2,1)}, bf16[1024,768]{1,0:T(8,128)(2,1)}, bf16[1024,768]{1,0:T(8,128)(2,1)}, f32[128,1536]{1,0:T(8,128)}, f32[128,...) custom-call(s32[1]{0:T(128)} %constant.120.clone.1.limit_ref, ...), custom_call_target="tpu_custom_call" | custom-call | flops 3300000000 | bytes 10800000 | tf_op jit(solution)/shard_map/pallas_call | solution.py:468
  233.8 10.4 %shard_map.279 = (bf16[1024,768]{1,0:T(8,128)(2,1)}, bf16[1024,768]{1,0:T(8,128)(2,1)}, bf16[1024,768]{1,0:T(8,128)(2,1)}) custom-call(s32[1]{0:T(128)} %constant.120.clone.1.limit_ref, s32[1]{0:T(128)} %bitcast.20.ctx_ref, bf16[256,1536]{1,0:T(8,128)(2,1)} %copy-done.6, ...), custom_call_target="tpu_custom_call", output_to_operand_aliasing={{0}: (7, {}), {1}: (8, {}), {2}: (9, {})} | custom-call | flops 1980000000 | bytes 6480000 | tf_op jit(solution)/shard_map/pallas_call | solution.py:468
  244.9 13.3 %shard_map.280 = (bf16[3,384,768]{2,1,0:T(8,128)(2,1)}, bf16[3,384,768]{2,1,0:T(8,128)(2,1)}) custom-call(bf16[768,1024]{1,0:T(8,128)(2,1)} %get-tuple-element.612.refs_0_, bf16[768,1024]{1,0:T(8,128)(2,1)} %get-tuple-element.613.refs_1_, bf16[768,1024]{1,0:T(8,128)(2,1)} %copy-done.4, bf16[768,1024]{1,0:T(8,128)(2,1)} %copy-done.3, ...), custom_call_target="tpu_custom_call" | custom-call | flops 2640000000 | bytes 8640000 | tf_op jit(solution)/shard_map/pallas_call | solution.py:539
  265.0 6.6 %collective-permute-done.25.far_ref = bf16[128,1536]{1,0:T(8,128)(2,1)S(1)} collective-permute-done((bf16[128,1536]{1,0:T(8,128)(2,1)S(1)}, bf16[128,1536]{1,0:T(8,128)(2,1)S(1)}, u32[]{:S(2)}, u32[]{:S(2)}) %collective-permute-start.25) | collective-permute-done | bytes 393248 | tf_op jit(solution)/shard_map/ppermute | solution.py:44
  273.5 3.4 shard_map.281
  281.1 13.0 %shard_map.282 = (bf16[3,384,768]{2,1,0:T(8,128)(2,1)}, bf16[3,384,768]{2,1,0:T(8,128)(2,1)}) custom-call(bf16[768,1024]{1,0:T(8,128)(2,1)} %get-tuple-element.612.refs_0_, bf16[768,1024]{1,0:T(8,128)(2,1)} %get-tuple-element.613.refs_1_, bf16[768,1024]{1,0:T(8,128)(2,1)} %copy-done.4, bf16[768,1024]{1,0:T(8,128)(2,1)} %copy-done.3, ...), custom_call_target="tpu_custom_call" | custom-call | flops 2640000000 | bytes 8640000 | tf_op jit(solution)/shard_map/pallas_call | solution.py:539
  299.3 10.7 %shard_map.283 = (bf16[256,768]{1,0:T(8,128)(2,1)}, f32[256,256]{1,0:T(8,128)}, bf16[256,256]{1,0:T(8,128)(2,1)}, bf16[256,256]{1,0:T(8,128)(2,1)}) custom-call(s32[1]{0:T(128)} %bitcast.1.index_ref, bf16[256,768]{1,0:T(8,128)(2,1)} %get-tuple-element.627.q_ref, s32[256,1]{1,0:T(8,128)} %copy.53.low_ref, s32[256,1]{1,0:T(8,128)} %fusion.17.high_ref, ...), custom_call_target="tpu_custom_call" | custom-call | flops 2200000000 | bytes 7200000 | tf_op jit(solution)/shard_map/pallas_call | solution.py:622
  312.9 6.0 %collective-permute-done.24.refs_1_ = bf16[3,384,768]{2,1,0:T(8,128)(2,1)S(1)} collective-permute-done((bf16[3,384,768]{2,1,0:T(8,128)(2,1)S(1)}, bf16[3,384,768]{2,1,0:T(8,128)(2,1)S(1)}, u32[]{:S(2)}, u32[]{:S(2)}) %collective-permute-start.24) | collective-permute-done | bytes 1769504 | tf_op jit(solution)/shard_map/ppermute | solution.py:44
  321.1 2.5 add_convert_fusion.1.refs_0_
  327.7 4.7 shard_map.284
  332.4 2.9 collective-permute-start.34
  339.1 6.1 %collective-permute-done.34.other_ref = bf16[128,1536]{1,0:T(8,128)(2,1)S(1)} collective-permute-done((bf16[128,1536]{1,0:T(8,128)(2,1)}, bf16[128,1536]{1,0:T(8,128)(2,1)S(1)}, u32[]{:S(2)}, u32[]{:S(2)}) %collective-permute-start.34) | collective-permute-done | bytes 393248 | tf_op jit(solution)/shard_map/ppermute | solution.py:44
  345.9 2.8 shard_map.285
  365.7 5.1 %shard_map.286 = (f32[384,4480]{1,0:T(8,128)}, f32[384,4480]{1,0:T(8,128)}, f32[4480,384]{1,0:T(8,128)}) custom-call(s32[1]{0:T(128)} %bitcast.25.member_ref, bf16[3,384,768]{2,1,0:T(8,128)(2,1)} %copy-done.8, bf16[3,384,768]{2,1,0:T(8,128)(2,1)} %copy-done.14), custom_call_target="tpu_custom_call" | custom-call | flops 220000000 | bytes 720000 | tf_op jit(solution)/shard_map/pallas_call | solution.py:738
  375.4 11.3 %collective-permute-done.41 = bf16[384,1024]{1,0:T(8,128)(2,1)} collective-permute-done((bf16[384,1024]{1,0:T(8,128)(2,1)}, bf16[384,1024]{1,0:T(8,128)(2,1)}, u32[]{:S(2)}, u32[]{:S(2)}) %collective-permute-start.41) | collective-permute-done | bytes 786464 | tf_op jit(solution)/shard_map/ppermute | solution.py:44
  393.6 5.3 %shard_map.287 = (f32[384,4480]{1,0:T(8,128)}, f32[384,4480]{1,0:T(8,128)}, f32[4480,384]{1,0:T(8,128)}) custom-call(s32[1]{0:T(128)} %bitcast.25.member_ref, bf16[3,384,768]{2,1,0:T(8,128)(2,1)} %copy-done.10, bf16[3,384,768]{2,1,0:T(8,128)(2,1)} %collective-permute-done.33.refs_1_, ...), custom_call_target="tpu_custom_call", output_to_operand_aliasing={{0}: (3, {}), {1}: (4, {}), {2}: (5, {})} | custom-call | flops 220000000 | bytes 720000 | tf_op jit(solution)/shard_map/pallas_call | solution.py:738
  398.9 6.2 %collective-permute-done.38 = bf16[256,1536]{1,0:T(8,128)(2,1)} collective-permute-done((bf16[256,1536]{1,0:T(8,128)(2,1)}, bf16[256,1536]{1,0:T(8,128)(2,1)}, u32[]{:S(2)}, u32[]{:S(2)}) %collective-permute-start.38) | collective-permute-done | bytes 786464 | tf_op jit(solution)/shard_map/ppermute | solution.py:44
  410.1 6.7 %collective-permute-done.42 = bf16[384,512]{1,0:T(8,128)(2,1)} collective-permute-done((bf16[384,512]{1,0:T(8,128)(2,1)}, bf16[384,512]{1,0:T(8,128)(2,1)}, u32[]{:S(2)}, u32[]{:S(2)}) %collective-permute-start.42) | collective-permute-done | bytes 393248 | tf_op jit(solution)/shard_map/ppermute | solution.py:44
  421.2 3.6 collective-permute-start.47
  425.0 8.1 %collective-permute-done.47 = bf16[192,384]{1,0:T(8,128)(2,1)S(1)} collective-permute-done((bf16[192,384]{1,0:T(8,128)(2,1)S(1)}, bf16[192,384]{1,0:T(8,128)(2,1)S(1)}, u32[]{:S(2)}, u32[]{:S(2)}) %collective-permute-start.47) | collective-permute-done | bytes 147488 | tf_op jit(solution)/shard_map/ppermute | solution.py:44
  433.1 3.5 collective-permute-start.49
  436.6 8.8 %collective-permute-done.51 = bf16[384,256]{1,0:T(8,128)(2,1)S(1)} collective-permute-done((bf16[384,256]{1,0:T(8,128)(2,1)S(1)}, bf16[384,256]{1,0:T(8,128)(2,1)S(1)}, u32[]{:S(2)}, u32[]{:S(2)}) %collective-permute-start.51) | collective-permute-done | bytes 196640 | tf_op jit(solution)/shard_map/ppermute | solution.py:44
  445.6 3.0 collective-permute-start.53
  451.2 3.6 collective-permute-done.54
  456.7 5.3 %shard_map.288 = (f32[384,4480]{1,0:T(8,128)}, f32[384,4480]{1,0:T(8,128)}, f32[4480,384]{1,0:T(8,128)}) custom-call(s32[1]{0:T(128)} %bitcast.25.member_ref, bf16[3,384,768]{2,1,0:T(8,128)(2,1)} %copy-done.9, bf16[3,384,768]{2,1,0:T(8,128)(2,1)} %collective-permute-done.48.refs_1_, ...), custom_call_target="tpu_custom_call", output_to_operand_aliasing={{0}: (3, {}), {1}: (4, {}), {2}: (5, {})} | custom-call | flops 220000000 | bytes 720000 | tf_op jit(solution)/shard_map/pallas_call | solution.py:738
  (289 shorter events, 128.2 us)
Async XLA Ops:
  7.2 44.4 %all-gather.9.cloned.1.call-start = ((), (), s32[]{:S(2)}) async-start(), calls=%async_computation | async-start | bytes 1966080 | tf_op jit(solution)/shard_map/all_gather | solution.py:889
  11.6 124.0 %all-gather.15.cloned.1.call-start = ((), (), s32[]{:S(2)}) async-start(), calls=%async_computation.3 | async-start | bytes 8847360 | tf_op jit(solution)/shard_map/all_gather | solution.py:950
  11.7 21.2 %collective-permute-start = (bf16[400,1024]{1,0:T(8,128)(2,1)S(1)}, bf16[400,1024]{1,0:T(8,128)(2,1)S(1)}, u32[]{:S(2)}, u32[]{:S(2)}) collective-permute-start(bf16[400,1024]{1,0:T(8,128)(2,1)S(1)} %copy-done.2), channel_id=1, source_target_pairs={{0,16},{8,24},{16,0},{24,8},{1,17},{9,25},{17,1},{25,9},{2,18},{10... | collective-permute-start | bytes 2457608 | tf_op jit(solution)/shard_map/ppermute | solution.py:44
  33.0 124.0 %all-gather.13.cloned.1.call-start = ((), (), s32[]{:S(2)}) async-start(), calls=%async_computation.2 | async-start | bytes 8847360 | tf_op jit(solution)/shard_map/all_gather | solution.py:950
  33.7 183.7 %all-gather.11.cloned.1.call-start = ((), (), s32[]{:S(2)}) async-start(), calls=%async_computation.1 | async-start | bytes 8847360 | tf_op jit(solution)/shard_map/all_gather | solution.py:950
  38.5 15.5 %collective-permute-start.2 = (bf16[768,384]{1,0:T(8,128)(2,1)}, bf16[768,384]{1,0:T(8,128)(2,1)}, u32[]{:S(2)}, u32[]{:S(2)}) collective-permute-start(bf16[768,384]{1,0:T(8,128)(2,1)} %convert_element_type.112.refs_0_.refs_2_), channel_id=1, source_target_pairs={{0,16},{8,24},{16,0},{24,8},{1,17},{9,25},{17,1},{25,9},{2,18},{10... | collective-permute-start | bytes 1769480 | tf_op jit(solution)/shard_map/ppermute | solution.py:44
  56.6 14.0 %collective-permute-start.3 = (bf16[2,768,384]{2,1,0:T(8,128)(2,1)}, bf16[2,768,384]{2,1,0:T(8,128)(2,1)}, u32[]{:S(2)}, u32[]{:S(2)}) collective-permute-start(bf16[2,768,384]{2,1,0:T(8,128)(2,1)} %pad_maximum_fusion.1), channel_id=1, source_target_pairs={{0,8},{8,0},{16,24},{24,16},{1,9},{9,1},{17,25},{25,17},{2,10},{10... | collective-permute-start | bytes 3538952 | tf_op jit(solution)/shard_map/ppermute | solution.py:44
  56.6 37.3 %collective-permute-start.7 = (bf16[4,128,1536]{2,1,0:T(8,128)(2,1)S(1)}, bf16[4,128,1536]{2,1,0:T(8,128)(2,1)S(1)}, u32[]{:S(2)}, u32[]{:S(2)}) collective-permute-start(bf16[4,128,1536]{2,1,0:T(8,128)(2,1)S(1)} %bitcast.42), channel_id=1, source_target_pairs={{0,1},{1,0},{2,3},{3,2},{4,5},{5,4},{6,7},{7,6},{8,9},{9,8},{10,11... | collective-permute-start | bytes 4718600 | tf_op jit(solution)/shard_map/ppermute | solution.py:44
  82.8 19.1 %collective-permute-start.6 = (bf16[128,1536]{1,0:T(8,128)(2,1)}, bf16[128,1536]{1,0:T(8,128)(2,1)S(1)}, u32[]{:S(2)}, u32[]{:S(2)}) collective-permute-start(bf16[128,1536]{1,0:T(8,128)(2,1)} %get-tuple-element.457), channel_id=1, source_target_pairs={{0,1},{1,0},{2,3},{3,2},{4,5},{5,4},{6,7},{7,6},{8,9},{9,8},{10,11... | collective-permute-start | bytes 1179656 | tf_op jit(solution)/shard_map/ppermute | solution.py:44
  85.2 21.6 %collective-permute-start.9 = (bf16[256,1536]{1,0:T(8,128)(2,1)}, bf16[256,1536]{1,0:T(8,128)(2,1)}, u32[]{:S(2)}, u32[]{:S(2)}) collective-permute-start(bf16[256,1536]{1,0:T(8,128)(2,1)} %pad_maximum_fusion.3), channel_id=1, source_target_pairs={{0,8},{8,0},{16,24},{24,16},{1,9},{9,1},{17,25},{25,17},{2,10},{10... | collective-permute-start | bytes 2359304 | tf_op jit(solution)/shard_map/ppermute | solution.py:44
  117.2 18.5 %collective-permute-start.10 = (bf16[256,1536]{1,0:T(8,128)(2,1)S(1)}, bf16[256,1536]{1,0:T(8,128)(2,1)}, u32[]{:S(2)}, u32[]{:S(2)}) collective-permute-start(bf16[256,1536]{1,0:T(8,128)(2,1)S(1)} %constant_dynamic-update-slice_fusion.refs_0_), channel_id=1, source_target_pairs={{0,1},{1,0},{2,3},{3,2},{4,5},{5,4},{6,7},{7,6},{8,9},{9,8},{10,11... | collective-permute-start | bytes 2359304 | tf_op jit(solution)/shard_map/ppermute | solution.py:44
  119.0 35.8 %collective-permute-start.11 = (bf16[256,1536]{1,0:T(8,128)(2,1)S(1)}, bf16[256,1536]{1,0:T(8,128)(2,1)S(1)}, u32[]{:S(2)}, u32[]{:S(2)}) collective-permute-start(bf16[256,1536]{1,0:T(8,128)(2,1)S(1)} %constant_dynamic-update-slice_fusion.refs_0_), channel_id=1, source_target_pairs={{0,4},{2,6},{4,0},{6,2},{1,5},{3,7},{5,1},{7,3},{8,12},{10,14},{12... | collective-permute-start | bytes 2359304 | tf_op jit(solution)/shard_map/ppermute | solution.py:44
  154.8 18.8 %collective-permute-start.12 = (bf16[256,1536]{1,0:T(8,128)(2,1)S(1)}, bf16[256,1536]{1,0:T(8,128)(2,1)S(1)}, u32[]{:S(2)}, u32[]{:S(2)}) collective-permute-start(bf16[256,1536]{1,0:T(8,128)(2,1)S(1)} %collective-permute-done.11.refs_2_.refs_0_), channel_id=1, source_target_pairs={{0,1},{1,0},{2,3},{3,2},{4,5},{5,4},{6,7},{7,6},{8,9},{9,8},{10,11... | collective-permute-start | bytes 2359304 | tf_op jit(solution)/shard_map/ppermute | solution.py:44
  155.1 46.1 %collective-permute-start.14 = (bf16[768,1024]{1,0:T(8,128)(2,1)}, bf16[768,1024]{1,0:T(8,128)(2,1)S(1)}, u32[]{:S(2)}, u32[]{:S(2)}) collective-permute-start(bf16[768,1024]{1,0:T(8,128)(2,1)} %get-tuple-element.514), channel_id=1, source_target_pairs={{0,8},{8,0},{16,24},{24,16},{1,9},{9,1},{17,25},{25,17},{2,10},{10... | collective-permute-start | bytes 4718600 | tf_op jit(solution)/shard_map/ppermute | solution.py:44
  189.8 12.1 %collective-permute-start.16 = (bf16[1024,768]{1,0:T(8,128)(2,1)}, bf16[1024,768]{1,0:T(8,128)(2,1)}, u32[]{:S(2)}, u32[]{:S(2)}) collective-permute-start(bf16[1024,768]{1,0:T(8,128)(2,1)} %get-tuple-element.548.refs_5_), channel_id=1, source_target_pairs={{0,8},{8,0},{16,24},{24,16},{1,9},{9,1},{17,25},{25,17},{2,10},{10... | collective-permute-start | bytes 4718600 | tf_op jit(solution)/shard_map/ppermute | solution.py:44
  201.2 43.0 %collective-permute-start.18 = (bf16[1024,768]{1,0:T(8,128)(2,1)}, bf16[1024,768]{1,0:T(8,128)(2,1)}, u32[]{:S(2)}, u32[]{:S(2)}) collective-permute-start(bf16[1024,768]{1,0:T(8,128)(2,1)} %get-tuple-element.586.refs_4_), channel_id=1, source_target_pairs={{0,8},{8,0},{16,24},{24,16},{1,9},{9,1},{17,25},{25,17},{2,10},{10... | collective-permute-start | bytes 4718600 | tf_op jit(solution)/shard_map/ppermute | solution.py:44
  201.5 42.9 %collective-permute-start.19 = (bf16[1024,768]{1,0:T(8,128)(2,1)}, bf16[1024,768]{1,0:T(8,128)(2,1)}, u32[]{:S(2)}, u32[]{:S(2)}) collective-permute-start(bf16[1024,768]{1,0:T(8,128)(2,1)} %get-tuple-element.587.refs_5_), channel_id=1, source_target_pairs={{0,8},{8,0},{16,24},{24,16},{1,9},{9,1},{17,25},{25,17},{2,10},{10... | collective-permute-start | bytes 4718600 | tf_op jit(solution)/shard_map/ppermute | solution.py:44
  201.8 43.0 %collective-permute-start.20 = (bf16[1024,768]{1,0:T(8,128)(2,1)}, bf16[1024,768]{1,0:T(8,128)(2,1)}, u32[]{:S(2)}, u32[]{:S(2)}) collective-permute-start(bf16[1024,768]{1,0:T(8,128)(2,1)} %get-tuple-element.588.refs_6_), channel_id=1, source_target_pairs={{0,8},{8,0},{16,24},{24,16},{1,9},{9,1},{17,25},{25,17},{2,10},{10... | collective-permute-start | bytes 4718600 | tf_op jit(solution)/shard_map/ppermute | solution.py:44
  216.6 45.3 %collective-permute-start.22 = (bf16[3,384,768]{2,1,0:T(8,128)(2,1)}, bf16[3,384,768]{2,1,0:T(8,128)(2,1)S(1)}, u32[]{:S(2)}, u32[]{:S(2)}) collective-permute-start(bf16[3,384,768]{2,1,0:T(8,128)(2,1)} %get-tuple-element.553), channel_id=1, source_target_pairs={{0,16},{8,24},{16,0},{24,8},{1,17},{9,25},{17,1},{25,9},{2,18},{10... | collective-permute-start | bytes 5308424 | tf_op jit(solution)/shard_map/ppermute | solution.py:44
  233.0 25.2 %collective-permute-start.23 = (bf16[256,1536]{1,0:T(8,128)(2,1)}, bf16[256,1536]{1,0:T(8,128)(2,1)}, u32[]{:S(2)}, u32[]{:S(2)}) collective-permute-start(bf16[256,1536]{1,0:T(8,128)(2,1)} %get-tuple-element.596), channel_id=1, source_target_pairs={{0,1},{1,0},{2,3},{3,2},{4,5},{5,4},{6,7},{7,6},{8,9},{9,8},{10,11... | collective-permute-start | bytes 2359304 | tf_op jit(solution)/shard_map/ppermute | solution.py:44
  244.2 35.0 %collective-permute-start.27 = (bf16[1024,768]{1,0:T(8,128)(2,1)}, bf16[1024,768]{1,0:T(8,128)(2,1)}, u32[]{:S(2)}, u32[]{:S(2)}) collective-permute-start(bf16[1024,768]{1,0:T(8,128)(2,1)} %get-tuple-element.616.refs_4_), channel_id=1, source_target_pairs={{0,8},{8,0},{16,24},{24,16},{1,9},{9,1},{17,25},{25,17},{2,10},{10... | collective-permute-start | bytes 4718600 | tf_op jit(solution)/shard_map/ppermute | solution.py:44
  244.3 36.8 %collective-permute-start.28 = (bf16[1024,768]{1,0:T(8,128)(2,1)}, bf16[1024,768]{1,0:T(8,128)(2,1)}, u32[]{:S(2)}, u32[]{:S(2)}) collective-permute-start(bf16[1024,768]{1,0:T(8,128)(2,1)} %get-tuple-element.617.refs_5_), channel_id=1, source_target_pairs={{0,8},{8,0},{16,24},{24,16},{1,9},{9,1},{17,25},{25,17},{2,10},{10... | collective-permute-start | bytes 4718600 | tf_op jit(solution)/shard_map/ppermute | solution.py:44
  244.8 36.3 %collective-permute-start.29 = (bf16[1024,768]{1,0:T(8,128)(2,1)}, bf16[1024,768]{1,0:T(8,128)(2,1)}, u32[]{:S(2)}, u32[]{:S(2)}) collective-permute-start(bf16[1024,768]{1,0:T(8,128)(2,1)} %get-tuple-element.618.refs_6_), channel_id=1, source_target_pairs={{0,8},{8,0},{16,24},{24,16},{1,9},{9,1},{17,25},{25,17},{2,10},{10... | collective-permute-start | bytes 4718600 | tf_op jit(solution)/shard_map/ppermute | solution.py:44
  259.6 12.0 %collective-permute-start.25 = (bf16[128,1536]{1,0:T(8,128)(2,1)S(1)}, bf16[128,1536]{1,0:T(8,128)(2,1)S(1)}, u32[]{:S(2)}, u32[]{:S(2)}) collective-permute-start(bf16[128,1536]{1,0:T(8,128)(2,1)S(1)} %add_convert_fusion.5), channel_id=1, source_target_pairs={{0,2},{2,0},{4,6},{6,4},{1,3},{3,1},{5,7},{7,5},{8,10},{10,8},{12,... | collective-permute-start | bytes 1179656 | tf_op jit(solution)/shard_map/ppermute | solution.py:44
  276.9 17.3 %collective-permute-start.26 = (bf16[128,1536]{1,0:T(8,128)(2,1)}, bf16[128,1536]{1,0:T(8,128)(2,1)}, u32[]{:S(2)}, u32[]{:S(2)}) collective-permute-start(bf16[128,1536]{1,0:T(8,128)(2,1)} %get-tuple-element.633.refs_0_), channel_id=1, source_target_pairs={{0,1},{1,0},{2,3},{3,2},{4,5},{5,4},{6,7},{7,6},{8,9},{9,8},{10,11... | collective-permute-start | bytes 1179656 | tf_op jit(solution)/shard_map/ppermute | solution.py:44
  277.6 41.3 %collective-permute-start.24 = (bf16[3,384,768]{2,1,0:T(8,128)(2,1)S(1)}, bf16[3,384,768]{2,1,0:T(8,128)(2,1)S(1)}, u32[]{:S(2)}, u32[]{:S(2)}) collective-permute-start(bf16[3,384,768]{2,1,0:T(8,128)(2,1)S(1)} %add_convert_fusion.2.refs_0_), channel_id=1, source_target_pairs={{0,2},{2,0},{4,6},{6,4},{1,3},{3,1},{5,7},{7,5},{8,10},{10,8},{12,... | collective-permute-start | bytes 5308424 | tf_op jit(solution)/shard_map/ppermute | solution.py:44
  279.3 41.9 %collective-permute-start.21 = (bf16[3,384,768]{2,1,0:T(8,128)(2,1)}, bf16[3,384,768]{2,1,0:T(8,128)(2,1)}, u32[]{:S(2)}, u32[]{:S(2)}) collective-permute-start(bf16[3,384,768]{2,1,0:T(8,128)(2,1)} %get-tuple-element.593), channel_id=1, source_target_pairs={{0,16},{8,24},{16,0},{24,8},{1,17},{9,25},{17,1},{25,9},{2,18},{10... | collective-permute-start | bytes 5308424 | tf_op jit(solution)/shard_map/ppermute | solution.py:44
  295.5 63.2 %collective-permute-start.37 = (bf16[3,384,768]{2,1,0:T(8,128)(2,1)}, bf16[3,384,768]{2,1,0:T(8,128)(2,1)}, u32[]{:S(2)}, u32[]{:S(2)}) collective-permute-start(bf16[3,384,768]{2,1,0:T(8,128)(2,1)} %get-tuple-element.622), channel_id=1, source_target_pairs={{0,16},{8,24},{16,0},{24,8},{1,17},{9,25},{17,1},{25,9},{2,18},{10... | collective-permute-start | bytes 5308424 | tf_op jit(solution)/shard_map/ppermute | solution.py:44
  310.1 16.9 %collective-permute-start.31 = (bf16[256,256]{1,0:T(8,128)(2,1)}, bf16[256,256]{1,0:T(8,128)(2,1)S(1)}, u32[]{:S(2)}, u32[]{:S(2)}) collective-permute-start(bf16[256,256]{1,0:T(8,128)(2,1)} %get-tuple-element.646), channel_id=1, source_target_pairs={{2,0},{4,2},{6,4},{3,1},{5,3},{7,5},{10,8},{12,10},{14,12},{11,9},... | collective-permute-start | bytes 393224 | tf_op jit(solution)/shard_map/ppermute | solution.py:50
  311.4 15.6 %collective-permute-start.32 = (bf16[256,256]{1,0:T(8,128)(2,1)}, bf16[256,256]{1,0:T(8,128)(2,1)S(1)}, u32[]{:S(2)}, u32[]{:S(2)}) collective-permute-start(bf16[256,256]{1,0:T(8,128)(2,1)} %get-tuple-element.647), channel_id=1, source_target_pairs={{4,0},{6,2},{5,1},{7,3},{12,8},{14,10},{13,9},{15,11},{20,16},{22,... | collective-permute-start | bytes 393224 | tf_op jit(solution)/shard_map/ppermute | solution.py:50
  327.0 43.8 %collective-permute-start.33 = (bf16[3,384,768]{2,1,0:T(8,128)(2,1)S(1)}, bf16[3,384,768]{2,1,0:T(8,128)(2,1)}, u32[]{:S(2)}, u32[]{:S(2)}) collective-permute-start(bf16[3,384,768]{2,1,0:T(8,128)(2,1)S(1)} %add_convert_fusion.1.refs_0_), channel_id=1, source_target_pairs={{0,2},{2,0},{4,6},{6,4},{1,3},{3,1},{5,7},{7,5},{8,10},{10,8},{12,... | collective-permute-start | bytes 5308424 | tf_op jit(solution)/shard_map/ppermute | solution.py:44
  332.4 12.8 %collective-permute-start.34 = (bf16[128,1536]{1,0:T(8,128)(2,1)}, bf16[128,1536]{1,0:T(8,128)(2,1)S(1)}, u32[]{:S(2)}, u32[]{:S(2)}) collective-permute-start(bf16[128,1536]{1,0:T(8,128)(2,1)} %get-tuple-element.668), channel_id=1, source_target_pairs={{0,1},{1,0},{2,3},{3,2},{4,5},{5,4},{6,7},{7,6},{8,9},{9,8},{10,11... | collective-permute-start | bytes 1179656 | tf_op jit(solution)/shard_map/ppermute | solution.py:44
  348.7 14.3 %collective-permute-start.36 = (bf16[128,1536]{1,0:T(8,128)(2,1)}, bf16[128,1536]{1,0:T(8,128)(2,1)S(1)}, u32[]{:S(2)}, u32[]{:S(2)}) collective-permute-start(bf16[128,1536]{1,0:T(8,128)(2,1)} %get-tuple-element.679), channel_id=1, source_target_pairs={{0,1},{1,0},{2,3},{3,2},{4,5},{5,4},{6,7},{7,6},{8,9},{9,8},{10,11... | collective-permute-start | bytes 1179656 | tf_op jit(solution)/shard_map/ppermute | solution.py:44
  352.6 18.8 %collective-permute-start.39 = (bf16[768,384]{1,0:T(8,128)(2,1)}, bf16[768,384]{1,0:T(8,128)(2,1)}, u32[]{:S(2)}, u32[]{:S(2)}) collective-permute-start(bf16[768,384]{1,0:T(8,128)(2,1)} %slice.371), channel_id=1, source_target_pairs={{0,16},{8,24},{16,0},{24,8},{1,17},{9,25},{17,1},{25,9},{2,18},{10... | collective-permute-start | bytes 1769480 | tf_op jit(solution)/shard_map/ppermute | solution.py:44
  358.7 28.0 %collective-permute-start.41 = (bf16[384,1024]{1,0:T(8,128)(2,1)}, bf16[384,1024]{1,0:T(8,128)(2,1)}, u32[]{:S(2)}, u32[]{:S(2)}) collective-permute-start(bf16[384,1024]{1,0:T(8,128)(2,1)} %slice.370), channel_id=1, source_target_pairs={{0,16},{8,24},{16,0},{24,8},{1,17},{9,25},{17,1},{25,9},{2,18},{10... | collective-permute-start | bytes 2359304 | tf_op jit(solution)/shard_map/ppermute | solution.py:44
  362.9 58.3 %collective-permute-start.48 = (bf16[3,384,768]{2,1,0:T(8,128)(2,1)S(1)}, bf16[3,384,768]{2,1,0:T(8,128)(2,1)}, u32[]{:S(2)}, u32[]{:S(2)}) collective-permute-start(bf16[3,384,768]{2,1,0:T(8,128)(2,1)S(1)} %add_convert_fusion.refs_0_), channel_id=1, source_target_pairs={{0,2},{2,0},{4,6},{6,4},{1,3},{3,1},{5,7},{7,5},{8,10},{10,8},{12,... | collective-permute-start | bytes 5308424 | tf_op jit(solution)/shard_map/ppermute | solution.py:44
  373.6 19.9 %collective-permute-start.40 = (f32[2,1536]{1,0:T(2,128)S(1)}, f32[2,1536]{1,0:T(2,128)S(1)}, u32[]{:S(2)}, u32[]{:S(2)}) collective-permute-start(f32[2,1536]{1,0:T(2,128)S(1)} %pad_maximum_fusion.12), channel_id=1, source_target_pairs={{0,1},{1,0},{2,3},{3,2},{4,5},{5,4},{6,7},{7,6},{8,9},{9,8},{10,11... | collective-permute-start | bytes 36872 | tf_op jit(solution)/shard_map/ppermute | solution.py:44
  386.7 18.4 %collective-permute-start.38 = (bf16[256,1536]{1,0:T(8,128)(2,1)}, bf16[256,1536]{1,0:T(8,128)(2,1)}, u32[]{:S(2)}, u32[]{:S(2)}) collective-permute-start(bf16[256,1536]{1,0:T(8,128)(2,1)} %get-tuple-element.689), channel_id=1, source_target_pairs={{0,1},{1,0},{2,3},{3,2},{4,5},{5,4},{6,7},{7,6},{8,9},{9,8},{10,11... | collective-permute-start | bytes 2359304 | tf_op jit(solution)/shard_map/ppermute | solution.py:44
  391.4 27.5 %collective-permute-start.44 = (bf16[384,384]{1,0:T(8,128)(2,1)}, bf16[384,384]{1,0:T(8,128)(2,1)}, u32[]{:S(2)}, u32[]{:S(2)}) collective-permute-start(bf16[384,384]{1,0:T(8,128)(2,1)} %select_convert_fusion.1), channel_id=1, source_target_pairs={{0,2},{2,0},{4,6},{6,4},{1,3},{3,1},{5,7},{7,5},{8,10},{10,8},{12,... | collective-permute-start | bytes 884744 | tf_op jit(solution)/shard_map/ppermute | solution.py:44
  391.9 24.9 %collective-permute-start.42 = (bf16[384,512]{1,0:T(8,128)(2,1)}, bf16[384,512]{1,0:T(8,128)(2,1)}, u32[]{:S(2)}, u32[]{:S(2)}) collective-permute-start(bf16[384,512]{1,0:T(8,128)(2,1)} %select_convert_fusion), channel_id=1, source_target_pairs={{0,2},{2,0},{4,6},{6,4},{1,3},{3,1},{5,7},{7,5},{8,10},{10,8},{12,... | collective-permute-start | bytes 1179656 | tf_op jit(solution)/shard_map/ppermute | solution.py:44
  393.5 13.4 %collective-permute-start.45 = (f32[16,1536]{1,0:T(8,128)S(1)}, f32[16,1536]{1,0:T(8,128)S(1)}, u32[]{:S(2)}, u32[]{:S(2)}) collective-permute-start(f32[16,1536]{1,0:T(8,128)S(1)} %select_maximum_fusion), channel_id=1, source_target_pairs={{0,8},{8,0},{16,24},{24,16},{1,9},{9,1},{17,25},{25,17},{2,10},{10... | collective-permute-start | bytes 294920 | tf_op jit(solution)/shard_map/ppermute | solution.py:44
  416.8 33.7 %collective-permute-start.43 = (bf16[128,1536]{1,0:T(8,128)(2,1)S(1)}, bf16[128,1536]{1,0:T(8,128)(2,1)S(1)}, u32[]{:S(2)}, u32[]{:S(2)}) collective-permute-start(bf16[128,1536]{1,0:T(8,128)(2,1)S(1)} %get-tuple-element.714), channel_id=1, source_target_pairs={{0,2},{2,0},{4,6},{6,4},{1,3},{3,1},{5,7},{7,5},{8,10},{10,8},{12,... | collective-permute-start | bytes 1179656 | tf_op jit(solution)/shard_map/ppermute | solution.py:44
  418.2 27.3 %collective-permute-start.50 = (f32[16,1536]{1,0:T(8,128)S(1)}, f32[16,1536]{1,0:T(8,128)S(1)}, u32[]{:S(2)}, u32[]{:S(2)}) collective-permute-start(f32[16,1536]{1,0:T(8,128)S(1)} %add.238), channel_id=1, source_target_pairs={{0,2},{2,0},{4,6},{6,4},{1,3},{3,1},{5,7},{7,5},{8,10},{10,8},{12,... | collective-permute-start | bytes 294920 | tf_op jit(solution)/shard_map/ppermute | solution.py:44
  424.9 20.5 %collective-permute-start.51 = (bf16[384,256]{1,0:T(8,128)(2,1)S(1)}, bf16[384,256]{1,0:T(8,128)(2,1)S(1)}, u32[]{:S(2)}, u32[]{:S(2)}) collective-permute-start(bf16[384,256]{1,0:T(8,128)(2,1)S(1)} %select_convert_fusion.2), channel_id=1, source_target_pairs={{0,4},{2,6},{4,0},{6,2},{1,5},{3,7},{5,1},{7,3},{8,12},{10,14},{12... | collective-permute-start | bytes 589832 | tf_op jit(solution)/shard_map/ppermute | solution.py:44
  433.1 15.5 %collective-permute-start.49 = (bf16[192,384]{1,0:T(8,128)(2,1)S(1)}, bf16[192,384]{1,0:T(8,128)(2,1)S(1)}, u32[]{:S(2)}, u32[]{:S(2)}) collective-permute-start(bf16[192,384]{1,0:T(8,128)(2,1)S(1)} %add_convert_fusion.7), channel_id=1, source_target_pairs={{0,4},{2,6},{4,0},{6,2},{1,5},{3,7},{5,1},{7,3},{8,12},{10,14},{12... | collective-permute-start | bytes 442376 | tf_op jit(solution)/shard_map/ppermute | solution.py:44
  448.7 14.5 %collective-permute-start.56 = (bf16[384,384]{1,0:T(8,128)(2,1)S(1)}, bf16[384,384]{1,0:T(8,128)(2,1)S(1)}, u32[]{:S(2)}, u32[]{:S(2)}) collective-permute-start(bf16[384,384]{1,0:T(8,128)(2,1)S(1)} %pad_maximum_fusion.9), channel_id=1, source_target_pairs={{0,2},{2,0},{4,6},{6,4},{1,3},{3,1},{5,7},{7,5},{8,10},{10,8},{12,... | collective-permute-start | bytes 884744 | tf_op jit(solution)/shard_map/ppermute | solution.py:44
  450.7 13.7 %collective-permute-start.52 = (bf16[128,1536]{1,0:T(8,128)(2,1)S(1)}, bf16[128,1536]{1,0:T(8,128)(2,1)S(1)}, u32[]{:S(2)}, u32[]{:S(2)}) collective-permute-start(bf16[128,1536]{1,0:T(8,128)(2,1)S(1)} %add_convert_fusion.3), channel_id=1, source_target_pairs={{0,1},{1,0},{2,3},{3,2},{4,5},{5,4},{6,7},{7,6},{8,9},{9,8},{10,11... | collective-permute-start | bytes 1179656 | tf_op jit(solution)/shard_map/ppermute | solution.py:44
  454.8 13.2 %collective-permute-start.55 = (bf16[384,512]{1,0:T(8,128)(2,1)S(1)}, bf16[384,512]{1,0:T(8,128)(2,1)S(1)}, u32[]{:S(2)}, u32[]{:S(2)}) collective-permute-start(bf16[384,512]{1,0:T(8,128)(2,1)S(1)} %pad_maximum_fusion.8), channel_id=1, source_target_pairs={{0,2},{2,0},{4,6},{6,4},{1,3},{3,1},{5,7},{7,5},{8,10},{10,8},{12,... | collective-permute-start | bytes 1179656 | tf_op jit(solution)/shard_map/ppermute | solution.py:44
  (62 other events, 372.1 us)
Sparse Core Ops, SparseCore 0:
  11.8 39.7 all-gather.8
  53.7 49.6 all-gather.14
  105.6 51.2 all-gather.12
  158.4 51.5 all-gather.10
